TPU v7x, 32 devices: a whole 2x2x4 slice. The times are simulated.
32 devices in a mesh: req: 16 (over z, y, core), tp: 2 (over x).
Axes of the slice: x: 2, y: 2, z: 4, core: 2. Of those that a mesh axis runs over, the one named last changes fastest.
Arguments:
- queries: bfloat16 [1024, 2048], P('req', 'tp'), may hold values from -18 to 18
- fresh_key_value: bfloat16 [1024, 1024], P('req', 'tp'), may hold values from -6 to 6
- key_value_cache: bfloat16 [64, 128, 1024], P('req', None, 'tp'), may hold values from -12.2 to 12.2
- request_page_index: int32 [144, 4], P('req'), may hold values from 0 to 3
- cache_length_rows: int32 [144], P('req'), may hold values from 2 to 512, as said below
- residual: bfloat16 [1024, 2048], P('req'), may hold values from -12.8 to 12.8
- w_out: bfloat16 [2048, 2048], P('tp'), may hold values from -0.125 to 0.125
- gain_in: float32 [2048], replicated, may hold values from 0.5 to 1.5
- route_ids: int32 [1024, 8], P('req'), may hold values from 0 to 15, all different within a row; in each aligned block of 32 rows (0 to 31, 32 to 63, ...) at most 32 rows name the same one
- route_weights: float32 [1024, 8], P('req'), may hold values from 0.1 to 1
- expert_home: int32 [16], replicated, may hold values from 0 to 15, each once
- w_gate: bfloat16 [16, 2048, 768], P('req', None, 'tp'), may hold values from -0.125 to 0.125
- w_up: bfloat16 [16, 2048, 768], P('req', None, 'tp'), may hold values from -0.125 to 0.125
- w_down: bfloat16 [16, 768, 2048], P('req', 'tp'), may hold values from -0.21875 to 0.21875
- gain_out: float32 [2048], replicated, may hold values from 0.5 to 1.5
Outputs:
- normed: bfloat16 [1024, 2048], P(('req', 'tp'))
Inputs may be any that keep to these rules, and one draw needn't show every extreme that they name: `route_ids`: each row names 8 different experts; in each aligned block of 32 rows no expert is named by more than 32 rows, and in some block some expert by exactly 32. `expert_home`: each expert is held by exactly one group. `request_page_index`: entries number pages among the 4 pages of the request's own group; a page may be named by several requests and entries. `cache_length_rows`: in every group one request has exactly 512 cached tokens.
All inputs are finite; a program needn't handle non-finite values.
Results may differ from a plain program's by a relative error of at most 0.0058.
Values may be sent and summed in bfloat16 or wider, within the bound.
No kernel may reach another device: no remote copies, remote signals or barrier semaphores. Data moves between devices by JAX's collectives and lax.ppermute only.
A program may use at most 64 MiB of HBM per device.

v0:
```python
import jax
import jax.numpy as jnp
from jax import lax
from jax.sharding import PartitionSpec as P

HEAD_WIDTH = 128
TOPK = 8
PRE_DEV = 56


EPSILON = 1e-06


def rms_scale(value_rows, gain_row):
    mean_square = jnp.mean(value_rows * value_rows, axis=-1, keepdims=True)
    return value_rows * lax.rsqrt(mean_square + EPSILON) * gain_row


def softmax_rounded(scores):
    row_peak = jnp.max(scores, axis=-1, keepdims=True)
    weights = jnp.exp(scores - row_peak)
    return (weights / jnp.sum(weights, axis=-1, keepdims=True)).astype(jnp.bfloat16)


def group_attention(queries, fresh_key_value, page_pool, page_rows, lengths):
    tokens_here = queries.shape[0]
    kv_heads = fresh_key_value.shape[1] // (2 * HEAD_WIDTH)
    group_size = queries.shape[1] // (HEAD_WIDTH * kv_heads)
    score_scale = HEAD_WIDTH ** (-0.5)
    split_query = queries.reshape(tokens_here, kv_heads, group_size, HEAD_WIDTH)
    fresh_kv = fresh_key_value.reshape(tokens_here, kv_heads, 2, HEAD_WIDTH)
    gathered_pages = page_pool[page_rows]
    cached = gathered_pages.reshape(page_rows.shape[0], -1, kv_heads, 2, HEAD_WIDTH)
    places = jnp.arange(cached.shape[1], dtype=jnp.int32)
    prefill_query = split_query[:PRE_DEV]
    prefill_fresh = fresh_kv[:PRE_DEV]
    cache_scores = (
        jnp.einsum(
            "ikgd,ckd->kgic", prefill_query, cached[0, :, :, 0], preferred_element_type=jnp.float32
        )
        * score_scale
    )
    cache_scores = jnp.where(places < lengths[0], cache_scores, -jnp.inf)
    block_scores = (
        jnp.einsum(
            "ikgd,jkd->kgij",
            prefill_query,
            prefill_fresh[:, :, 0],
            preferred_element_type=jnp.float32,
        )
        * score_scale
    )
    causal = jnp.arange(PRE_DEV)[:, None] >= jnp.arange(PRE_DEV)[None, :]
    block_scores = jnp.where(causal, block_scores, -jnp.inf)
    prefill_probs = softmax_rounded(jnp.concatenate([cache_scores, block_scores], axis=3))
    prefill_values = jnp.concatenate([cached[0, :, :, 1], prefill_fresh[:, :, 1]], axis=0)
    prefill_out = jnp.einsum(
        "kgic,ckd->ikgd", prefill_probs, prefill_values, preferred_element_type=jnp.float32
    )
    decode_query = split_query[PRE_DEV:]
    decode_fresh = fresh_kv[PRE_DEV:]
    decode_scores = (
        jnp.einsum(
            "rkgd,rckd->rkgc", decode_query, cached[1:, :, :, 0], preferred_element_type=jnp.float32
        )
        * score_scale
    )
    decode_scores = jnp.where(
        places[None, None, None, :] < lengths[1:, None, None, None], decode_scores, -jnp.inf
    )
    own_scores = (
        jnp.einsum(
            "rkgd,rkd->rkg", decode_query, decode_fresh[:, :, 0], preferred_element_type=jnp.float32
        )[..., None]
        * score_scale
    )
    decode_probs = softmax_rounded(jnp.concatenate([decode_scores, own_scores], axis=3))
    decode_values = jnp.concatenate([cached[1:, :, :, 1], decode_fresh[:, None, :, 1]], axis=1)
    decode_out = jnp.einsum(
        "rkgc,rckd->rkgd", decode_probs, decode_values, preferred_element_type=jnp.float32
    )
    joined = jnp.concatenate([prefill_out, decode_out], axis=0)
    return joined.reshape(tokens_here, -1).astype(jnp.bfloat16)


def slot_positions(block_owner, experts, capacity):
    flat_owner = block_owner.reshape(-1)
    onehot = (flat_owner[:, None] == jnp.arange(experts, dtype=jnp.int32)[None, :]).astype(
        jnp.int32
    )
    earlier = jnp.cumsum(onehot, axis=0) - onehot
    slot_index = jnp.sum(earlier * onehot, axis=1)
    return (flat_owner * capacity + slot_index).reshape(block_owner.shape)


def place_matrix(positions, slots_total):
    matches = positions[None, :, :] == jnp.arange(slots_total, dtype=jnp.int32)[:, None, None]
    return jnp.any(matches, axis=2).astype(jnp.bfloat16)


def local(
    queries,
    fresh_key_value,
    key_value_cache,
    request_page_index,
    cache_length_rows,
    residual,
    w_out,
    gain_in,
    route_ids,
    route_weights,
    expert_home,
    w_gate,
    w_up,
    w_down,
    gain_out,
):
    tp_size = lax.axis_size("tp")
    req_size = lax.axis_size("req")
    tp_index = lax.axis_index("tp")
    model_width = residual.shape[1]
    tokens_here = residual.shape[0]
    quarter = tokens_here // tp_size
    experts = expert_home.shape[0]
    capacity = min(quarter, max(2, 2 * quarter * TOPK // experts))
    context = group_attention(
        queries, fresh_key_value, key_value_cache, request_page_index, cache_length_rows
    )
    head_terms = jnp.dot(context, w_out, preferred_element_type=jnp.float32)
    state = residual.astype(jnp.float32) + lax.psum(head_terms, "tp")
    owners = jnp.sum(
        jnp.where(
            route_ids[:, :, None] == jnp.arange(experts, dtype=jnp.int32)[None, None, :],
            expert_home[None, None, :],
            0,
        ),
        axis=2,
    )
    shares = route_weights / jnp.sum(route_weights, axis=1, keepdims=True)
    own_start = tp_index * quarter
    own_state = lax.dynamic_slice_in_dim(state, own_start, quarter, 0)
    own_shares = lax.dynamic_slice_in_dim(shares, own_start, quarter, 0)
    normed_all = rms_scale(state, gain_in).astype(jnp.bfloat16)
    positions_all = jax.vmap(lambda block_owner: slot_positions(block_owner, experts, capacity))(
        owners.reshape(tp_size, quarter, TOPK)
    )
    placing = jax.vmap(lambda positions: place_matrix(positions, experts * capacity))(positions_all)
    outgoing = jnp.einsum(
        "qmi,qid->qmd",
        placing,
        normed_all.reshape(tp_size, quarter, model_width),
        preferred_element_type=jnp.float32,
    )
    outgoing = outgoing.astype(jnp.bfloat16).reshape(tp_size, experts, capacity, model_width)
    incoming = lax.all_to_all(outgoing, "req", split_axis=1, concat_axis=1, tiled=True)
    own_positions = lax.dynamic_index_in_dim(positions_all, tp_index, 0, keepdims=False)
    expert_rows = incoming.reshape(-1, model_width)
    gate_proj = jnp.dot(expert_rows, w_gate[0], preferred_element_type=jnp.float32)
    up_proj = jnp.dot(expert_rows, w_up[0], preferred_element_type=jnp.float32)
    inner_units = (jax.nn.silu(gate_proj) * up_proj).astype(jnp.bfloat16)
    summed = lax.psum_scatter(
        jnp.dot(inner_units, w_down[0], preferred_element_type=jnp.float32).astype(jnp.bfloat16),
        "tp",
        scatter_dimension=0,
        tiled=True,
    )
    results = summed.reshape(req_size, capacity, model_width)
    returned = lax.all_to_all(results, "req", split_axis=0, concat_axis=0, tiled=True).reshape(
        -1, model_width
    )
    picked = returned[own_positions]
    mixture = jnp.sum(own_shares[:, :, None] * picked.astype(jnp.float32), axis=1)
    return rms_scale(own_state + mixture, gain_out).astype(jnp.bfloat16)


def solution(mesh):
    return jax.shard_map(
        local,
        mesh=mesh,
        in_specs=(
            P("req", "tp"),
            P("req", "tp"),
            P("req", None, "tp"),
            P("req", None),
            P("req"),
            P("req", None),
            P("tp", None),
            P(),
            P("req", None),
            P("req", None),
            P(),
            P("req", None, "tp"),
            P("req", None, "tp"),
            P("req", "tp", None),
            P(),
        ),
        out_specs=P(("req", "tp"), None),
        check_vma=False,
    )
```

profile of v0, /device:TPU:0, one launch (start us, length us, event | category | flops | bytes accessed | tf_op | source)
XLA Modules:
  0.0 308.4 jit_solution(11618750523219073472)
XLA Ops:
  6.5 0.8 compare_select_fusion.1
  7.5 5.4 %gather_fusion = bf16[36,128,512]{2,1,0:T(8,128)(2,1)} fusion(bf16[4,128,512]{2,1,0:T(8,128)(2,1)} %param.17, s32[1024]{0:T(1024)S(1)} %pad_clamp_fusion.1), kind=kCustom, calls=%fused_computation | custom fusion | bytes 9437328 | tf_op jit(solution)/shard_map/gather | solution.py:32
  13.0 7.7 %reshape.139 = bf16[9,512,2,2,128]{4,3,2,1,0:T(2,128)(2,1)} reshape(bf16[36,128,512]{2,1,0:T(8,128)(2,1)} %gather_fusion) | data formatting | bytes 9437184 | tf_op jit(solution)/shard_map/reshape | solution.py:33
  20.7 10.0 %fusion.46 = (bf16[8,512,2,1,128]{4,3,2,1,0:T(2,128)(2,1)}, bf16[8,512,2,1,128]{4,3,2,1,0:T(2,128)(2,1)}) fusion(bf16[9,512,2,2,128]{4,3,2,1,0:T(2,128)(2,1)} %reshape.139), kind=kLoop, calls=%fused_computation.93 | loop fusion | bytes 8388608 | tf_op jit(solution)/shard_map/slice | solution.py:64
  30.7 2.1 fusion.45
  33.2 2.9 fusion.48
  36.4 2.7 copy.146
  39.3 0.5 fusion
  39.8 0.4 slice-done.1
  40.5 0.4 fusion.49
  40.9 0.3 fusion.50
  41.2 0.3 fusion.23
  41.6 0.5 fusion.21
  42.3 3.9 %fusion.51 = f32[64,2048]{1,0:T(8,128)} fusion(bf16[64,1024]{1,0:T(8,128)(2,1)S(1)} %convert_element_type.42, bf16[1024,2048]{1,0:T(8,128)(2,1)} %param.21), kind=kOutput, calls=%fused_computation.98 | convolution fusion | flops 268435456 | bytes 4849664 | tf_op jit(solution)/shard_map/dot_general | solution.py:129
  46.5 1.2 reduce-window.6
  47.7 0.2 slice_reduce_fusion
  48.4 0.4 fusion.22
  48.8 28.9 %all-reduce.2.cloned.1.call-done = f32[64,2048]{1,0:T(8,128)} async-done(((f32[64,2048]{1,0:T(8,128)}), f32[64,2048]{1,0:T(8,128)}) %all-reduce.2.cloned.1.call-update) | async-done | bytes 524304 | tf_op jit(solution)/shard_map/psum | solution.py:130
  77.7 1.2 multiply_reduce_fusion
  79.0 1.3 convolution_convert_fusion.1
  80.3 0.6 copy.95
  80.9 97.7 %all_to_all.10 = bf16[2,16,32,2048]{3,2,0,1:T(8,128)(2,1)S(1)} all-to-all(bf16[2,16,32,2048]{3,2,0,1:T(8,128)(2,1)S(1)} %copy.95), channel_id=1, replica_groups=mesh['req'=16,'tp'=2] {'req'}, dimensions={1} | all-to-all | bytes 8388608 | tf_op jit(solution)/shard_map/all_to_all | solution.py:155
  178.6 0.6 copy.96
  179.2 2.0 copy-done.1
  181.2 3.6 %fusion.9 = f32[1024,384]{1,0:T(8,128)} fusion(bf16[1024,2048]{1,0:T(8,128)(2,1)S(1)} %bitcast.118, bf16[1,2048,384]{2,1,0:T(8,128)(2,1)S(1)} %copy-done.8), kind=kOutput, calls=%fused_computation.16 | convolution fusion | flops 1610612736 | bytes 7340032 | tf_op jit(solution)/shard_map/dot_general | solution.py:158
  184.7 9.6 %convolution_convert_fusion = bf16[1024,2048]{1,0:T(8,128)(2,1)} fusion(bf16[1,384,2048]{2,1,0:T(8,128)(2,1)S(1)} %copy-done, f32[1024,384]{1,0:T(8,128)} %fusion.9, bf16[1024,2048]{1,0:T(8,128)(2,1)} %bitcast.119, bf16[1,2048,384]{2,1,0:T(8,128)(2,1)} %param.27), kind=kOutput, calls=%fused_computation.2 | convolution fusion | flops 3225681920 | bytes 13107200 | tf_op jit(solution)/shard_map/dot_general | solution.py:162
  194.3 54.1 %reduce-scatter.2.cloned.1.call-done = bf16[512,2048]{1,0:T(8,128)(2,1)} async-done(((bf16[1024,2048]{1,0:T(8,128)(2,1)}), bf16[512,2048]{1,0:T(8,128)(2,1)}) %reduce-scatter.2.cloned.1.call-update) | async-done | bytes 2097168 | tf_op jit(solution)/shard_map/reduce_scatter | solution.py:161
  248.4 5.8 %all-to-all-start.1 = ((bf16[16,32,2048]{2,1,0:T(8,128)(2,1)}), bf16[16,32,2048]{2,1,0:T(8,128)(2,1)}, u32[]{:S(2)}, u32[]{:S(2)}) async-start(bf16[16,32,2048]{2,1,0:T(8,128)(2,1)} %bitcast.121), calls=%async_computation.2 | async-start | bytes 4194304 | tf_op jit(solution)/shard_map/all_to_all | solution.py:168
  254.6 40.8 %all-to-all-done.1 = bf16[16,32,2048]{2,1,0:T(8,128)(2,1)} async-done(((bf16[16,32,2048]{2,1,0:T(8,128)(2,1)}), bf16[16,32,2048]{2,1,0:T(8,128)(2,1)}, u32[]{:S(2)}, u32[]{:S(2)}) %all-to-all-start.1) | async-done | bytes 2097184 | tf_op jit(solution)/shard_map/all_to_all | solution.py:168
  295.4 4.2 %gather_fusion.1 = bf16[256,2048]{1,0:T(8,128)(2,1)S(1)} fusion(bf16[512,2048]{1,0:T(8,128)(2,1)} %bitcast.33, s32[1024]{0:T(1024)S(1)} %pad_clamp_fusion), kind=kCustom, calls=%fused_computation.1 | custom fusion | bytes 2098176 | tf_op jit(solution)/shard_map/gather | solution.py:171
  299.7 1.0 fusion.5
  300.8 0.8 multiply_convert_fusion.2
  (77 shorter events, 2.8 us)
Async XLA Ops:
  6.5 178.2 %copy-start = (bf16[1,384,2048]{2,1,0:T(8,128)(2,1)S(1)}, bf16[1,384,2048]{2,1,0:T(8,128)(2,1)}, u32[]{:S(2)}) copy-start(bf16[1,384,2048]{2,1,0:T(8,128)(2,1)} %param.28) | copy-start | bytes 4718596
  6.5 71.1 %all-reduce.2.cloned.1.call-start = ((), (), s32[]{:S(2)}) async-start(), calls=%async_computation.3 | async-start | bytes 1048576 | tf_op jit(solution)/shard_map/psum | solution.py:130
  30.7 2.2 slice-start
  30.7 2.2 copy-start.9
  30.7 2.3 slice-start.2
  39.3 0.9 slice-start.1
  39.3 1.0 slice-start.3
  42.2 4.0 %copy-start.6 = (s32[64,8]{0,1:T(8,128)S(1)}, s32[64,8]{0,1:T(8,128)}, u32[]{:S(2)}) copy-start(s32[64,8]{0,1:T(8,128)} %param.23) | copy-start | bytes 6148
  42.3 4.0 %copy-start.7 = (s32[16]{0:T(128)S(1)}, s32[16]{0:T(128)}, u32[]{:S(2)}) copy-start(s32[16]{0:T(128)} %param.25) | copy-start | bytes 196
  42.3 35.4 %copy-start.2 = (bf16[64,2048]{1,0:T(8,128)(2,1)S(1)}, bf16[64,2048]{1,0:T(8,128)(2,1)}, u32[]{:S(2)}) copy-start(bf16[64,2048]{1,0:T(8,128)(2,1)} %param.20) | copy-start | bytes 786436
  46.2 32.7 %copy-start.4 = (f32[2048]{0:T(1024)S(1)}, f32[2048]{0:T(1024)}, u32[]{:S(2)}) copy-start(f32[2048]{0:T(1024)} %param.22) | copy-start | bytes 24580
  46.2 202.2 %reduce-scatter.2.cloned.1.call-start = ((), (), s32[]{:S(2)}) async-start(), calls=%async_computation.4 | async-start | bytes 6291456 | tf_op jit(solution)/shard_map/reduce_scatter | solution.py:161
  178.6 2.6 copy-start.8
  179.2 2.0 copy-start.1
  248.4 5.9 %copy-start.3 = (f32[64,8]{0,1:T(8,128)S(1)}, f32[64,8]{0,1:T(8,128)}, u32[]{:S(2)}) copy-start(f32[64,8]{0,1:T(8,128)} %param.24) | copy-start | bytes 6148
  248.4 47.0 %all-to-all-start.1 = ((bf16[16,32,2048]{2,1,0:T(8,128)(2,1)}), bf16[16,32,2048]{2,1,0:T(8,128)(2,1)}, u32[]{:S(2)}, u32[]{:S(2)}) async-start(bf16[16,32,2048]{2,1,0:T(8,128)(2,1)} %bitcast.121), calls=%async_computation.2 | async-start | bytes 4194304 | tf_op jit(solution)/shard_map/all_to_all | solution.py:168
  295.4 5.4 %copy-start.5 = (f32[2048]{0:T(1024)S(1)}, f32[2048]{0:T(1024)}, u32[]{:S(2)}) copy-start(f32[2048]{0:T(1024)} %param.29) | copy-start | bytes 24580
Sparse Core Ops, SparseCore 0:
  46.3 31.3 all-reduce.1
  194.4 53.9 reduce-scatter.1
where the time goes:
time: 315 us; the launch traced here: 308 us
  waiting for transfers between devices  124 us (39%)
  blocking collectives  97.7 us (31%)
  local copies, waits for them, and re-layouts  37.6 us (12%)
  matrix products  23 us (7%)
  between operations  13.8 us (4%)
  other arithmetic  6.55 us (2%)
  starting transfers between devices  5.86 us (2%)
    all_to_all x1, blocking collectives, local(): lax.all_to_all(outgoing, 'req', split_axis=1, concat_axis=1, tiled=True)  97.7 us
    reduce_scatter x1, waiting for transfers between devices, local(): lax.psum_scatter(jnp.dot(inner_units, w_down[0], preferred_element_type=j...  54.1 us
    all_to_all x1, waiting for transfers between devices, local(): lax.all_to_all(results, 'req', split_axis=0, concat_axis=0, tiled=True)  40.8 us
    psum x1, waiting for transfers between devices, local(): state = residual.astype(jnp.float32) + lax.psum(head_terms, 'tp')  28.9 us
    slice x1, local copies, waits for them, and re-layouts, group_attention(): cached[1:, :, :, 0]  10 us
    dot_general x1, matrix products, local(): jnp.dot(inner_units, w_down[0], preferred_element_type=jnp.float32)  9.55 us
    reshape x1, local copies, waits for them, and re-layouts, group_attention(): gathered_pages.reshape(page_rows.shape[0], -1, kv_heads, 2, HEAD_WIDTH)  7.7 us
  transfers between devices with their start and end apart: 3, of which 3 were waited for; matrix products, arithmetic and copies ran while one was open for 1% of the time, Pallas kernels for 0%

commit v1 on v0

--- a/solution.py
+++ b/solution.py
@@ -1,6 +1,10 @@
+import functools
+
 import jax
 import jax.numpy as jnp
 from jax import lax
+from jax.experimental import pallas as pl
+from jax.experimental.pallas import tpu as pltpu
 from jax.sharding import PartitionSpec as P
 
 HEAD_WIDTH = 128
@@ -98,7 +102,7 @@
     return jnp.any(matches, axis=2).astype(jnp.bfloat16)
 
 
-def local(
+def local_sparse(
     queries,
     fresh_key_value,
     key_value_cache,
@@ -173,9 +177,377 @@
     return rms_scale(own_state + mixture, gain_out).astype(jnp.bfloat16)
 
 
+ALL = ("req", "tp")
+MASKED = -1e30
+VMEM_BYTES = 40 * 1024 * 1024
+
+
+def vmem():
+    return pl.BlockSpec(memory_space=pltpu.VMEM)
+
+
+def smem():
+    return pl.BlockSpec(memory_space=pltpu.SMEM)
+
+
+def multiplicity(page_rows, length, pool_pages, page_tokens):
+    rows = page_rows[0].shape[0]
+    lane = lax.broadcasted_iota(jnp.int32, (rows, page_tokens), 1)
+    parts = []
+    for page in range(pool_pages):
+        count = jnp.zeros((rows, page_tokens), jnp.float32)
+        for slot, named in enumerate(page_rows):
+            hit = (named == page) & (lane + slot * page_tokens < length)
+            count = count + jnp.where(hit, 1.0, 0.0)
+        parts.append(count)
+    return jnp.concatenate(parts, axis=1)
+
+
+def attention_kernel(
+    pages_ref, lengths_ref, tp_ref, q_ref, fresh_ref, cache_ref, residual_ref, w_hbm,
+    own_ref, send_ref, w_ref, context_ref, terms_ref, w_sem,
+):
+    fetch = pltpu.make_async_copy(w_hbm, w_ref, w_sem)
+    fetch.start()
+    tokens = q_ref.shape[0]
+    pool_pages, page_tokens, _ = cache_ref.shape
+    requests, slots = pages_ref.shape
+    kv_heads = fresh_ref.shape[1] // (2 * HEAD_WIDTH)
+    group = q_ref.shape[1] // (HEAD_WIDTH * kv_heads)
+    decodes = requests - 1
+    row = lax.broadcasted_iota(jnp.int32, (decodes, page_tokens), 0)
+
+    def by_row(read):
+        value = jnp.zeros((decodes, page_tokens), jnp.int32)
+        for j in range(decodes):
+            value = jnp.where(row == j, read(j + 1), value)
+        return value
+
+    full = lambda scalar: jnp.full((decodes, page_tokens), scalar, jnp.int32)
+    first = multiplicity(
+        [full(pages_ref[0, s]) for s in range(slots)], full(lengths_ref[0]), pool_pages, page_tokens
+    )
+    later = multiplicity(
+        [by_row(lambda j, s=s: pages_ref[j, s]) for s in range(slots)],
+        by_row(lambda j: lengths_ref[j]),
+        pool_pages,
+        page_tokens,
+    )
+    count = jnp.concatenate([first] * (PRE_DEV // decodes) + [later], axis=0)
+    query_place = lax.broadcasted_iota(jnp.int32, (tokens, tokens), 0)
+    key_place = lax.broadcasted_iota(jnp.int32, (tokens, tokens), 1)
+    seen = (key_place == query_place) | ((key_place <= query_place) & (query_place < PRE_DEV))
+    visible = jnp.concatenate([count] * group, axis=0)
+    seen = jnp.concatenate([jnp.where(seen, 1.0, 0.0)] * group, axis=0)
+    scale = HEAD_WIDTH**-0.5
+    contract_last = (((1,), (1,)), ((), ()))
+    for k in range(kv_heads):
+        key_at, value_at = 2 * k * HEAD_WIDTH, (2 * k + 1) * HEAD_WIDTH
+        query = jnp.concatenate(
+            [
+                q_ref[:, (k * group + g) * HEAD_WIDTH : (k * group + g + 1) * HEAD_WIDTH]
+                for g in range(group)
+            ],
+            axis=0,
+        )
+        keys = cache_ref[:, :, key_at : key_at + HEAD_WIDTH].reshape(-1, HEAD_WIDTH)
+        values = cache_ref[:, :, value_at : value_at + HEAD_WIDTH].reshape(-1, HEAD_WIDTH)
+        old = lax.dot_general(query, keys, contract_last, preferred_element_type=jnp.float32)
+        new = lax.dot_general(
+            query,
+            fresh_ref[:, key_at : key_at + HEAD_WIDTH],
+            contract_last,
+            preferred_element_type=jnp.float32,
+        )
+        old = jnp.where(visible > 0, old * scale, MASKED)
+        new = jnp.where(seen > 0, new * scale, MASKED)
+        peak = jnp.maximum(
+            jnp.max(old, axis=1, keepdims=True), jnp.max(new, axis=1, keepdims=True)
+        )
+        old = jnp.exp(old - peak) * visible
+        new = jnp.exp(new - peak) * seen
+        inverse = 1.0 / (
+            jnp.sum(old, axis=1, keepdims=True) + jnp.sum(new, axis=1, keepdims=True)
+        )
+        mixed = jnp.dot(
+            (old * inverse).astype(jnp.bfloat16), values, preferred_element_type=jnp.float32
+        ) + jnp.dot(
+            (new * inverse).astype(jnp.bfloat16),
+            fresh_ref[:, value_at : value_at + HEAD_WIDTH],
+            preferred_element_type=jnp.float32,
+        )
+        mixed = mixed.astype(jnp.bfloat16)
+        for g in range(group):
+            h = k * group + g
+            context_ref[:, h * HEAD_WIDTH : (h + 1) * HEAD_WIDTH] = mixed[
+                g * tokens : (g + 1) * tokens
+            ]
+    fetch.wait()
+    half = tokens // 2
+    width = terms_ref.shape[1]
+    block = 512
+    own_at = pl.multiple_of(tp_ref[0] * half, half)
+    other_at = pl.multiple_of((1 - tp_ref[0]) * half, half)
+    for at in range(0, width, block):
+        cols = slice(at, at + block)
+        terms_ref[:, cols] = jnp.dot(
+            context_ref[...], w_ref[:, cols], preferred_element_type=jnp.float32
+        )
+    own_ref[...] = terms_ref[pl.ds(own_at, half), :] + residual_ref[
+        pl.ds(own_at, half), :
+    ].astype(jnp.float32)
+    send_ref[...] = terms_ref[pl.ds(other_at, half), :].astype(jnp.bfloat16)
+
+
+def attention_terms(pages, lengths, tp_index, queries, fresh, cache, residual, w_out):
+    tokens, width = residual.shape
+    half = tokens // 2
+    return pl.pallas_call(
+        attention_kernel,
+        out_shape=(
+            jax.ShapeDtypeStruct((half, width), jnp.float32),
+            jax.ShapeDtypeStruct((half, width), jnp.bfloat16),
+        ),
+        in_specs=[smem(), smem(), smem(), vmem(), vmem(), vmem(), vmem(),
+                  pl.BlockSpec(memory_space=pl.ANY)],
+        out_specs=(vmem(), vmem()),
+        scratch_shapes=[
+            pltpu.VMEM(w_out.shape, jnp.bfloat16),
+            pltpu.VMEM(queries.shape, jnp.bfloat16),
+            pltpu.VMEM((tokens, width), jnp.float32),
+            pltpu.SemaphoreType.DMA,
+        ],
+        compiler_params=pltpu.CompilerParams(vmem_limit_bytes=VMEM_BYTES),
+        name="attention_terms",
+    )(pages, lengths, tp_index, queries, fresh, cache, residual, w_out)
+
+
+def norm_kernel(own_ref, got_ref, gain_ref, state_ref, a_ref, b_ref):
+    state = own_ref[...] + got_ref[...].astype(jnp.float32)
+    state_ref[...] = state
+    normed = rms_scale(state, gain_ref[...]).astype(jnp.bfloat16)
+    wide = a_ref.shape[1]
+    a_ref[...] = normed[:, :wide]
+    b_ref[...] = normed[:, wide:]
+
+
+def norm_rows(own, got, gain, wide):
+    rows, width = own.shape
+    return pl.pallas_call(
+        norm_kernel,
+        out_shape=(
+            jax.ShapeDtypeStruct((rows, width), jnp.float32),
+            jax.ShapeDtypeStruct((rows, wide), jnp.bfloat16),
+            jax.ShapeDtypeStruct((rows, width - wide), jnp.bfloat16),
+        ),
+        in_specs=[vmem()] * 3,
+        out_specs=(vmem(),) * 3,
+        name="norm_rows",
+    )(own, got, gain)
+
+
+def expert_kernel(*refs):
+    (a0, a1, a2, a3, b0, b1, b2, b3, share_ref, wg0, wu0, wd0, wg1, wu1, wd1) = refs[:15]
+    (oa0, oa1, oa2, oa3, ob0, ob1, ob2, ob3, x_ref, h0_ref, h1_ref) = refs[15:]
+    a_in, b_in = (a0, a1, a2, a3), (b0, b1, b2, b3)
+    a_out, b_out = (oa0, oa1, oa2, oa3), (ob0, ob1, ob2, ob3)
+    rows, width = x_ref.shape
+    wide = a0.shape[1]
+    quad = rows // 4
+    unit = quad // 4
+    for i in range(4):
+        x_ref[i * quad : (i + 1) * quad, :wide] = a_in[i][...]
+        for j in range(4):
+            at = i * quad + j * unit
+            x_ref[at : at + unit, wide:] = b_in[j][i * unit : (i + 1) * unit, :]
+    for wg, wu, h_ref in ((wg0, wu0, h0_ref), (wg1, wu1, h1_ref)):
+        gate = jnp.dot(x_ref[...], wg[...], preferred_element_type=jnp.float32)
+        up = jnp.dot(x_ref[...], wu[...], preferred_element_type=jnp.float32)
+        h_ref[...] = (gate / (1.0 + jnp.exp(-gate)) * up).astype(jnp.bfloat16)
+    share0, share1 = share_ref[:, 0:1], share_ref[:, 1:2]
+    block = 128
+    for at in range(0, width, block):
+        cols = slice(at, at + block)
+        down = share0 * jnp.dot(h0_ref[...], wd0[:, cols], preferred_element_type=jnp.float32)
+        down = down + share1 * jnp.dot(
+            h1_ref[...], wd1[:, cols], preferred_element_type=jnp.float32
+        )
+        if at < wide:
+            for i in range(4):
+                a_out[i][:, cols] = down[i * quad : (i + 1) * quad].astype(a_out[i].dtype)
+        else:
+            there = slice(at - wide, at - wide + block)
+            for i in range(4):
+                for j in range(4):
+                    row = i * quad + j * unit
+                    b_out[j][i * unit : (i + 1) * unit, there] = down[row : row + unit].astype(
+                        b_out[j].dtype
+                    )
+
+
+def expert_rows(a_parts, b_parts, shares, weights, partner_weights):
+    quad, wide = a_parts[0].shape
+    narrow = b_parts[0].shape[1]
+    width = wide + narrow
+    rows = 4 * quad
+    hidden = weights[0].shape[1]
+    kinds = (jnp.float32, jnp.bfloat16, jnp.bfloat16, jnp.bfloat16)
+    return pl.pallas_call(
+        expert_kernel,
+        out_shape=tuple(jax.ShapeDtypeStruct((quad, wide), kind) for kind in kinds)
+        + tuple(jax.ShapeDtypeStruct((quad, narrow), kind) for kind in kinds),
+        in_specs=[vmem()] * 15,
+        out_specs=(vmem(),) * 8,
+        scratch_shapes=[
+            pltpu.VMEM((rows, width), jnp.bfloat16),
+            pltpu.VMEM((rows, hidden), jnp.bfloat16),
+            pltpu.VMEM((rows, hidden), jnp.bfloat16),
+        ],
+        compiler_params=pltpu.CompilerParams(vmem_limit_bytes=VMEM_BYTES),
+        cost_estimate=pl.CostEstimate(
+            flops=12 * rows * width * hidden, bytes_accessed=16 * rows * width, transcendentals=0
+        ),
+        name="expert_rows",
+    )(*a_parts, *b_parts, shares, *weights, *partner_weights)
+
+
+def sum_kernel(own_ref, g1, g2, g3, o0, o1, o2, o3):
+    unit = o0.shape[0]
+    for i, out in enumerate((o0, o1, o2, o3)):
+        rows = slice(i * unit, (i + 1) * unit)
+        total = own_ref[rows, :]
+        for got in (g1, g2, g3):
+            total = total + got[rows, :].astype(jnp.float32)
+        out[...] = total.astype(out.dtype)
+
+
+def sum_rows(own, got):
+    quad, width = own.shape
+    unit = quad // 4
+    kinds = (jnp.float32, jnp.bfloat16, jnp.bfloat16, jnp.bfloat16)
+    return pl.pallas_call(
+        sum_kernel,
+        out_shape=tuple(jax.ShapeDtypeStruct((unit, width), kind) for kind in kinds),
+        in_specs=[vmem()] * 4,
+        out_specs=(vmem(),) * 4,
+        name="sum_rows",
+    )(own, *got)
+
+
+def final_kernel(state_ref, a0, a1, a2, a3, b0, b1, b2, b3, gain_ref, out_ref):
+    wide = a0.shape[1]
+    mixed_a = a0[...]
+    for got in (a1, a2, a3):
+        mixed_a = mixed_a + got[...].astype(jnp.float32)
+    mixed_b = b0[...]
+    for got in (b1, b2, b3):
+        mixed_b = mixed_b + got[...].astype(jnp.float32)
+    total = state_ref[...] + jnp.concatenate([mixed_a, mixed_b], axis=1)
+    out_ref[...] = rms_scale(total, gain_ref[...]).astype(jnp.bfloat16)
+
+
+def final_rows(state, a_parts, b_parts, gain):
+    return pl.pallas_call(
+        final_kernel,
+        out_shape=jax.ShapeDtypeStruct(state.shape, jnp.bfloat16),
+        in_specs=[vmem()] * 10,
+        out_specs=vmem(),
+        name="final_rows",
+    )(state, *a_parts, *b_parts, gain)
+
+
+def place(z, y, c, x):
+    return ((z * 2 + y) * 2 + c) * 2 + x
+
+
+def swap(value, dz, dy, dc, dx):
+    pairs = [
+        (place(z, y, c, x), place(z ^ dz, y ^ dy, c ^ dc, x ^ dx))
+        for z in range(4)
+        for y in range(2)
+        for c in range(2)
+        for x in range(2)
+    ]
+    return lax.ppermute(value, ALL, pairs)
+
+
+PLANE = ((0, 0), (0, 1), (1, 0), (1, 1))
+
+
+def swap_z(pieces):
+    return tuple(swap(piece, d, 0, 0, 0) for d, piece in zip((1, 2, 3), pieces))
+
+
+def swap_plane(pieces):
+    return tuple(swap(piece, 0, dy, 0, dx) for (dy, dx), piece in zip(PLANE[1:], pieces))
+
+
+def local_dense(
+    queries, fresh_key_value, key_value_cache, request_page_index, cache_length_rows, residual,
+    w_out, gain_in, route_ids, route_weights, expert_home, w_gate, w_up, w_down, gain_out,
+):
+    tp_index = lax.axis_index("tp")
+    req_index = lax.axis_index("req")
+    tokens, width = residual.shape
+    half = tokens // 2
+    wide = (width * 11 // 16) // 128 * 128
+    groups = expert_home.shape[0]
+    weights = (w_gate[0], w_up[0], w_down[0])
+    partner_weights = tuple(swap(w, 0, 0, 1, 0) for w in weights)
+    own_start = tp_index * half
+    ids = lax.dynamic_slice_in_dim(route_ids, own_start, half, 0)
+    routed = lax.dynamic_slice_in_dim(route_weights, own_start, half, 0)
+    shares = routed / jnp.sum(routed, axis=1, keepdims=True)
+    by_expert = jnp.sum(
+        jnp.where(
+            ids[:, :, None] == jnp.arange(groups, dtype=jnp.int32)[None, None, :],
+            shares[:, :, None],
+            0.0,
+        ),
+        axis=1,
+    )
+    homes = expert_home[:, None] == jnp.arange(groups, dtype=jnp.int32)[None, :]
+    by_home = jnp.sum(jnp.where(homes[None], by_expert[:, :, None], 0.0), axis=1)
+    every_share = lax.all_gather(by_home, ALL, axis=0, tiled=False)
+    core = req_index % 2
+    spots = [
+        (((req_index // 4) ^ dz) * 2 + (((req_index // 2) % 2) ^ dy)) * 4 + core * 2 + (tp_index ^ dx)
+        for dy, dx in PLANE
+        for dz in range(4)
+    ]
+    near_share = every_share[jnp.stack(spots)].reshape(16 * half, groups)
+    column = jnp.arange(groups, dtype=jnp.int32)[None, :]
+    pair_share = jnp.stack(
+        [
+            jnp.sum(jnp.where(column == req_index, near_share, 0.0), axis=1),
+            jnp.sum(jnp.where(column == (req_index ^ 1), near_share, 0.0), axis=1),
+        ],
+        axis=1,
+    )
+
+    own_state, sent = attention_terms(
+        request_page_index, cache_length_rows, tp_index.reshape(1).astype(jnp.int32),
+        queries, fresh_key_value, key_value_cache, residual, w_out,
+    )
+    got = swap(sent, 0, 0, 0, 1)
+    state, rows_a, rows_b = norm_rows(own_state, got, gain_in[None, :], wide)
+    column_a = jnp.concatenate((rows_a,) + swap_z((rows_a,) * 3), axis=0)
+    column_b = jnp.concatenate((rows_b,) + swap_plane((rows_b,) * 3), axis=0)
+    all_a = (column_a,) + swap_plane((column_a,) * 3)
+    all_b = (column_b,) + swap_z((column_b,) * 3)
+    parts = expert_rows(all_a, all_b, pair_share, weights, partner_weights)
+    part_a, part_b = parts[:4], parts[4:]
+    near_a = sum_rows(part_a[0], swap_plane(part_a[1:]))
+    near_b = sum_rows(part_b[0], swap_z(part_b[1:]))
+    last_a = (near_a[0],) + swap_z(near_a[1:])
+    last_b = (near_b[0],) + swap_plane(near_b[1:])
+    return final_rows(state, last_a, last_b, gain_out[None, :])
+
+
 def solution(mesh):
+    dense = mesh.shape["req"] == 16 and mesh.shape["tp"] == 2
     return jax.shard_map(
-        local,
+        local_dense if dense else local_sparse,
         mesh=mesh,
         in_specs=(
             P("req", "tp"),

time: 315 us -> 199 us (0.63); the launches traced: 308 us -> 199 us
  waiting for transfers between devices: 124 us -> 57.2 us
  blocking collectives: 97.7 us -> 71.1 us
  matrix products: 23 us -> 0 us
  Pallas kernels: 0 us -> 23 us
  starting transfers between devices: 5.86 us -> 24.6 us
  local copies, waits for them, and re-layouts: 37.6 us -> 21 us
  between operations: 13.8 us -> 0.25 us
  other arithmetic: 6.55 us -> 1.41 us
    all_to_all x1 -> x0, blocking collectives: 97.7 us -> none  [local(): lax.all_to_all(outgoing, 'req', split_axis=1, concat_axis=1, tiled=True)]
    all_gather x0 -> x1, blocking collectives: none -> 71.1 us  [local_dense(): every_share = lax.all_gather(by_home, ALL, axis=0, tiled=False)]
    ppermute x0 -> x28, waiting for transfers between devices: none -> 57.2 us  [swap(): return lax.ppermute(value, ALL, pairs)]
    reduce_scatter x1 -> x0, waiting for transfers between devices: 54.1 us -> none  [local(): lax.psum_scatter(jnp.dot(inner_units, w_down[0], preferred_element_type=j...]
    all_to_all x1 -> x0, waiting for transfers between devices: 40.8 us -> none  [local(): lax.all_to_all(results, 'req', split_axis=0, concat_axis=0, tiled=True)]
    psum x1 -> x0, waiting for transfers between devices: 28.9 us -> none  [local(): state = residual.astype(jnp.float32) + lax.psum(head_terms, 'tp')]
    ppermute x0 -> x28, starting transfers between devices: none -> 24.6 us  [swap(): return lax.ppermute(value, ALL, pairs)]
    dot_general x10 -> x0, matrix products: 23 us -> none  [the longest x1 9.55 us: local(): jnp.dot(inner_units, w_down[0], preferred_element_type=jnp.float32)]
  transfers between devices with their start and end apart: 3 -> 28, of which waited for: 3 -> 14; matrix products, arithmetic and copies ran while one was open for 1% -> 3% of each run, Pallas kernels for 0% -> 3%
where the time goes in v1:
time: 199 us
  blocking collectives  71.1 us (36%)
  waiting for transfers between devices  57.2 us (29%)
  starting transfers between devices  24.6 us (12%)
  Pallas kernels  23 us (12%)
  local copies, waits for them, and re-layouts  21 us (11%)
    all_gather x1, blocking collectives, local_dense(): every_share = lax.all_gather(by_home, ALL, axis=0, tiled=False)  71.1 us
    ppermute x28, waiting for transfers between devices, swap(): return lax.ppermute(value, ALL, pairs)  57.2 us
    ppermute x28, starting transfers between devices, swap(): return lax.ppermute(value, ALL, pairs)  24.6 us
    unnamed x71, local copies, waits for them, and re-layouts  18.4 us
    pallas_call x1, Pallas kernels, expert_rows(): pl.pallas_call(expert_kernel, out_shape=tuple((jax.ShapeDtypeStruct((quad...  11.9 us
    pallas_call x2, Pallas kernels, sum_rows(): pl.pallas_call(sum_kernel, out_shape=tuple((jax.ShapeDtypeStruct((unit, w...  4.13 us
  transfers between devices with their start and end apart: 28, of which 14 were waited for; matrix products, arithmetic and copies ran while one was open for 3% of the time, Pallas kernels for 3%

profile of v1, /device:TPU:0, one launch (start us, length us, event | category | flops | bytes accessed | tf_op | source)
XLA Modules:
  0.0 198.6 jit_solution(13454724965112267958)
XLA Ops:
  0.8 2.2 %copy-done.1 = bf16[1024,2048]{1,0:T(8,128)(2,1)S(1)} copy-done((bf16[1024,2048]{1,0:T(8,128)(2,1)S(1)}, bf16[1024,2048]{1,0:T(8,128)(2,1)}, u32[]{:S(2)}) %copy-start.1) | copy-done | bytes 4194328
  3.0 1.0 copy-done.3
  4.0 0.9 copy-done.5
  7.4 3.0 %attention_terms.1 = (f32[32,2048]{1,0:T(8,128)S(1)}, bf16[32,2048]{1,0:T(8,128)(2,1)S(1)}) custom-call(s32[9,4]{1,0:T(8,128)S(1)} %copy.28.pages_ref, s32[9]{0:T(128)S(1)} %copy-done.9, s32[1]{0:T(128)} %bitcast.tp_ref, bf16[64,1024]{1,0:T(8,128)(2,1)S(1)} %copy-done.7, bf16[64,512]{1,0:T(8,128)(2,1)S(1)} %copy-done.8, bf16[4,128,512]{2,1,0:T(8,128)(2,1)S(1)} %copy-done.3, ...), custom_call_target="tpu_custom_call" | custom-call | tf_op jit(solution)/shard_map/attention_terms/pallas_call | solution.py:305
  11.1 2.9 %collective-permute-start = (bf16[32,2048]{1,0:T(8,128)(2,1)S(1)}, bf16[32,2048]{1,0:T(8,128)(2,1)S(1)}, u32[]{:S(2)}, u32[]{:S(2)}) collective-permute-start(bf16[32,2048]{1,0:T(8,128)(2,1)S(1)} %get-tuple-element.27), channel_id=1, source_target_pairs={{0,1},{1,0},{2,3},{3,2},{4,5},{5,4},{6,7},{7,6},{8,9},{9,8},{10,11... | collective-permute-start | bytes 393224 | tf_op jit(solution)/shard_map/ppermute | solution.py:471
  14.9 2.6 %collective-permute-done.got_ref = bf16[32,2048]{1,0:T(8,128)(2,1)S(1)} collective-permute-done((bf16[32,2048]{1,0:T(8,128)(2,1)S(1)}, bf16[32,2048]{1,0:T(8,128)(2,1)S(1)}, u32[]{:S(2)}, u32[]{:S(2)}) %collective-permute-start) | collective-permute-done | bytes 131104 | tf_op jit(solution)/shard_map/ppermute | solution.py:471
  18.2 1.8 norm_rows.1
  20.0 2.7 %collective-permute-start.9 = (bf16[32,640]{1,0:T(8,128)(2,1)}, bf16[32,640]{1,0:T(8,128)(2,1)S(1)}, u32[]{:S(2)}, u32[]{:S(2)}) collective-permute-start(bf16[32,640]{1,0:T(8,128)(2,1)} %get-tuple-element.30), channel_id=1, source_target_pairs={{0,5},{1,4},{2,7},{3,6},{4,1},{5,0},{6,3},{7,2},{8,13},{9,12},{10,... | collective-permute-start | bytes 122888 | tf_op jit(solution)/shard_map/ppermute | solution.py:471
  25.0 2.0 %collective-permute-done.7 = bf16[32,640]{1,0:T(8,128)(2,1)S(1)} collective-permute-done((bf16[32,640]{1,0:T(8,128)(2,1)}, bf16[32,640]{1,0:T(8,128)(2,1)S(1)}, u32[]{:S(2)}, u32[]{:S(2)}) %collective-permute-start.7) | collective-permute-done | bytes 40992 | tf_op jit(solution)/shard_map/ppermute | solution.py:471
  27.5 3.7 %collective-permute-done.8 = bf16[32,640]{1,0:T(8,128)(2,1)S(1)} collective-permute-done((bf16[32,640]{1,0:T(8,128)(2,1)}, bf16[32,640]{1,0:T(8,128)(2,1)S(1)}, u32[]{:S(2)}, u32[]{:S(2)}) %collective-permute-start.8) | collective-permute-done | bytes 40992 | tf_op jit(solution)/shard_map/ppermute | solution.py:471
  31.2 3.6 %collective-permute-start.3 = (bf16[32,1408]{1,0:T(8,128)(2,1)}, bf16[32,1408]{1,0:T(8,128)(2,1)S(1)}, u32[]{:S(2)}, u32[]{:S(2)}) collective-permute-start(bf16[32,1408]{1,0:T(8,128)(2,1)} %get-tuple-element.29), channel_id=1, source_target_pairs={{0,24},{1,25},{2,26},{3,27},{4,28},{5,29},{6,30},{7,31},{8,16},{9,... | collective-permute-start | bytes 270344 | tf_op jit(solution)/shard_map/ppermute | solution.py:471
  34.9 5.0 %collective-permute-done.1 = bf16[32,1408]{1,0:T(8,128)(2,1)S(1)} collective-permute-done((bf16[32,1408]{1,0:T(8,128)(2,1)}, bf16[32,1408]{1,0:T(8,128)(2,1)S(1)}, u32[]{:S(2)}, u32[]{:S(2)}) %collective-permute-start.1) | collective-permute-done | bytes 90144 | tf_op jit(solution)/shard_map/ppermute | solution.py:471
  39.9 10.8 %collective-permute-done.2 = bf16[32,1408]{1,0:T(8,128)(2,1)S(1)} collective-permute-done((bf16[32,1408]{1,0:T(8,128)(2,1)}, bf16[32,1408]{1,0:T(8,128)(2,1)S(1)}, u32[]{:S(2)}, u32[]{:S(2)}) %collective-permute-start.2) | collective-permute-done | bytes 90144 | tf_op jit(solution)/shard_map/ppermute | solution.py:471
  51.2 6.8 %collective-permute-done.12.refs_7_ = bf16[128,640]{1,0:T(8,128)(2,1)S(1)} collective-permute-done((bf16[128,640]{1,0:T(8,128)(2,1)S(1)}, bf16[128,640]{1,0:T(8,128)(2,1)S(1)}, u32[]{:S(2)}, u32[]{:S(2)}) %collective-permute-start.12) | collective-permute-done | bytes 163872 | tf_op jit(solution)/shard_map/ppermute | solution.py:471
  58.8 2.2 %collective-permute-done.11.refs_6_ = bf16[128,640]{1,0:T(8,128)(2,1)S(1)} collective-permute-done((bf16[128,640]{1,0:T(8,128)(2,1)S(1)}, bf16[128,640]{1,0:T(8,128)(2,1)S(1)}, u32[]{:S(2)}, u32[]{:S(2)}) %collective-permute-start.11) | collective-permute-done | bytes 163872 | tf_op jit(solution)/shard_map/ppermute | solution.py:471
  61.8 5.2 %collective-permute-done.10.refs_5_ = bf16[128,640]{1,0:T(8,128)(2,1)S(1)} collective-permute-done((bf16[128,640]{1,0:T(8,128)(2,1)S(1)}, bf16[128,640]{1,0:T(8,128)(2,1)S(1)}, u32[]{:S(2)}, u32[]{:S(2)}) %collective-permute-start.10) | collective-permute-done | bytes 163872 | tf_op jit(solution)/shard_map/ppermute | solution.py:471
  68.2 1.4 collective-permute-done.6.refs_3_
  70.3 71.1 %all-gather.1 = f32[32,32,16]{1,2,0:T(8,128)} all-gather(f32[1,32,16]{1,2,0:T(8,128)S(1)} %bitcast.27), channel_id=2, replica_groups=mesh['req'=16,'tp'=2] {'req','tp'}, dimensions={0}, use_global_device_ids=true | all-gather | bytes 67584 | tf_op jit(solution)/shard_map/all_gather | solution.py:511
  141.4 2.2 %gather_fusion = f32[16,32,16]{1,2,0:T(8,128)} fusion(f32[32,32,16]{1,2,0:T(8,128)} %all-gather.1, s32[1024]{0:T(1024)S(1)} %pad_clamp_fusion), kind=kCustom, calls=%fused_computation | custom fusion | bytes 65600 | tf_op jit(solution)/shard_map/gather | solution.py:518
  143.6 1.0 select_reduce_fusion.1
  147.7 11.9 %expert_rows.1 = (f32[128,1408]{1,0:T(8,128)S(1)}, bf16[128,1408]{1,0:T(8,128)(2,1)S(1)}, bf16[128,1408]{1,0:T(8,128)(2,1)S(1)}, bf16[128,1408]{1,0:T(8,128)(2,1...) custom-call(bf16[128,1408]{1,0:T(8,128)(2,1)S(1)} %constant_dynamic-, ...), custom_call_target="tpu_custom_call" | custom-call | flops 4831838208 | bytes 16777216 | tf_op jit(solution)/shard_map/expert_rows/pallas_call | solution.py:395
  162.1 2.6 %collective-permute-start.18 = (bf16[128,1408]{1,0:T(8,128)(2,1)S(1)}, bf16[128,1408]{1,0:T(8,128)(2,1)S(1)}, u32[]{:S(2)}, u32[]{:S(2)}) collective-permute-start(bf16[128,1408]{1,0:T(8,128)(2,1)S(1)} %get-tuple-element.34), channel_id=1, source_target_pairs={{0,5},{1,4},{2,7},{3,6},{4,1},{5,0},{6,3},{7,2},{8,13},{9,12},{10,... | collective-permute-start | bytes 1081352 | tf_op jit(solution)/shard_map/ppermute | solution.py:471
  164.8 7.8 %collective-permute-done.16.g1 = bf16[128,1408]{1,0:T(8,128)(2,1)S(1)} collective-permute-done((bf16[128,1408]{1,0:T(8,128)(2,1)S(1)}, bf16[128,1408]{1,0:T(8,128)(2,1)S(1)}, u32[]{:S(2)}, u32[]{:S(2)}) %collective-permute-start.16) | collective-permute-done | bytes 360480 | tf_op jit(solution)/shard_map/ppermute | solution.py:471
  172.5 3.9 %collective-permute-done.17.g2 = bf16[128,1408]{1,0:T(8,128)(2,1)S(1)} collective-permute-done((bf16[128,1408]{1,0:T(8,128)(2,1)S(1)}, bf16[128,1408]{1,0:T(8,128)(2,1)S(1)}, u32[]{:S(2)}, u32[]{:S(2)}) %collective-permute-start.17) | collective-permute-done | bytes 360480 | tf_op jit(solution)/shard_map/ppermute | solution.py:471
  177.2 2.2 %sum_rows.2 = (f32[32,1408]{1,0:T(8,128)}, bf16[32,1408]{1,0:T(8,128)(2,1)}, bf16[32,1408]{1,0:T(8,128)(2,1)}, bf16[32,1408]{1,0:T(8,128)(2,1)}) custom-call(f32[128,1408]{1,0:T(8,128)} %copy-done.2, bf16[128,1408]{1,0:T(8,128)(2,1)} %copy-done.17, bf16[128,1408]{1,0:T(8,128)(2,1)} %copy-done.18, bf16[128,1408]{1,0:T(8,128)(2,1)} %copy-done.19), custom_call_target="tpu_custom_call" | custom-call | tf_op jit(solution)/shard_map/sum_rows/pallas_call | solution.py:428
  180.0 3.9 %collective-permute-start.21 = (bf16[32,1408]{1,0:T(8,128)(2,1)}, bf16[32,1408]{1,0:T(8,128)(2,1)S(1)}, u32[]{:S(2)}, u32[]{:S(2)}) collective-permute-start(bf16[32,1408]{1,0:T(8,128)(2,1)} %get-tuple-element.38), channel_id=1, source_target_pairs={{0,24},{1,25},{2,26},{3,27},{4,28},{5,29},{6,30},{7,31},{8,16},{9,... | collective-permute-start | bytes 270344 | tf_op jit(solution)/shard_map/ppermute | solution.py:471
  184.6 1.9 sum_rows.3
  186.5 1.7 collective-permute-start.25
  188.5 2.2 %collective-permute-done.25.b1 = bf16[32,640]{1,0:T(8,128)(2,1)S(1)} collective-permute-done((bf16[32,640]{1,0:T(8,128)(2,1)}, bf16[32,640]{1,0:T(8,128)(2,1)S(1)}, u32[]{:S(2)}, u32[]{:S(2)}) %collective-permute-start.25) | collective-permute-done | bytes 40992 | tf_op jit(solution)/shard_map/ppermute | solution.py:471
  190.7 1.5 collective-permute-start.27
  192.7 3.2 %collective-permute-done.27.b3 = bf16[32,640]{1,0:T(8,128)(2,1)S(1)} collective-permute-done((bf16[32,640]{1,0:T(8,128)(2,1)}, bf16[32,640]{1,0:T(8,128)(2,1)S(1)}, u32[]{:S(2)}, u32[]{:S(2)}) %collective-permute-start.27) | collective-permute-done | bytes 40992 | tf_op jit(solution)/shard_map/ppermute | solution.py:471
  196.6 2.0 %final_rows.1 = bf16[32,2048]{1,0:T(8,128)(2,1)} custom-call(f32[32,2048]{1,0:T(8,128)} %get-tuple-element.28.state_ref, f32[32,1408]{1,0:T(8,128)} %get-tuple-element.35.a0, bf16[32,1408]{1,0:T(8,128)(2,1)} %copy-done.24, bf16[32,1408]{1,0:T(8,128)(2,1)} %copy-done.25, bf16[32,1408]{1,0:T(8,128)(2,1)} %copy-done.26, f32[32,640]{1,0:T(8,128)} %get-tuple-element.43.b0, ...), custom_call_target="tpu_custom_call" | custom-call | tf_op jit(solution)/shard_map/final_rows/pallas_call | solution.py:450
  (120 shorter events, 21.3 us)
Async XLA Ops:
  0.0 58.7 %copy-start = (s32[64,8]{0,1:T(8,128)S(1)}, s32[64,8]{0,1:T(8,128)}, u32[]{:S(2)}) copy-start(s32[64,8]{0,1:T(8,128)} %param.23) | copy-start | bytes 6148
  7.4 7.2 %copy-start.31 = (s32[16]{0:T(128)S(1)}, s32[16]{0:T(128)}, u32[]{:S(2)}) copy-start(s32[16]{0:T(128)} %param.25) | copy-start | bytes 196
  7.4 7.3 %copy-start.30 = (f32[64,8]{0,1:T(8,128)S(1)}, f32[64,8]{0,1:T(8,128)}, u32[]{:S(2)}) copy-start(f32[64,8]{0,1:T(8,128)} %param.24) | copy-start | bytes 6148
  11.1 6.4 %collective-permute-start = (bf16[32,2048]{1,0:T(8,128)(2,1)S(1)}, bf16[32,2048]{1,0:T(8,128)(2,1)S(1)}, u32[]{:S(2)}, u32[]{:S(2)}) collective-permute-start(bf16[32,2048]{1,0:T(8,128)(2,1)S(1)} %get-tuple-element.27), channel_id=1, source_target_pairs={{0,1},{1,0},{2,3},{3,2},{4,5},{5,4},{6,7},{7,6},{8,9},{9,8},{10,11... | collective-permute-start | bytes 393224 | tf_op jit(solution)/shard_map/ppermute | solution.py:471
  14.1 130.9 %collective-permute-start.13 = (bf16[2048,384]{1,0:T(8,128)(2,1)S(1)}, bf16[2048,384]{1,0:T(8,128)(2,1)}, u32[]{:S(2)}, u32[]{:S(2)}) collective-permute-start(bf16[2048,384]{1,0:T(8,128)(2,1)S(1)} %bitcast.25), channel_id=1, source_target_pairs={{0,2},{1,3},{2,0},{3,1},{4,6},{5,7},{6,4},{7,5},{8,10},{9,11},{10,... | collective-permute-start | bytes 4718600 | tf_op jit(solution)/shard_map/ppermute | solution.py:471
  14.1 130.9 %collective-permute-start.14 = (bf16[2048,384]{1,0:T(8,128)(2,1)}, bf16[2048,384]{1,0:T(8,128)(2,1)}, u32[]{:S(2)}, u32[]{:S(2)}) collective-permute-start(bf16[2048,384]{1,0:T(8,128)(2,1)} %bitcast.21.refs_10_), channel_id=1, source_target_pairs={{0,2},{1,3},{2,0},{3,1},{4,6},{5,7},{6,4},{7,5},{8,10},{9,11},{10,... | collective-permute-start | bytes 4718600 | tf_op jit(solution)/shard_map/ppermute | solution.py:471
  14.6 130.4 %collective-permute-start.15 = (bf16[384,2048]{1,0:T(8,128)(2,1)}, bf16[384,2048]{1,0:T(8,128)(2,1)}, u32[]{:S(2)}, u32[]{:S(2)}) collective-permute-start(bf16[384,2048]{1,0:T(8,128)(2,1)} %bitcast.22.refs_11_), channel_id=1, source_target_pairs={{0,2},{1,3},{2,0},{3,1},{4,6},{5,7},{6,4},{7,5},{8,10},{9,11},{10,... | collective-permute-start | bytes 4718600 | tf_op jit(solution)/shard_map/ppermute | solution.py:471
  20.0 14.7 %collective-permute-start.9 = (bf16[32,640]{1,0:T(8,128)(2,1)}, bf16[32,640]{1,0:T(8,128)(2,1)S(1)}, u32[]{:S(2)}, u32[]{:S(2)}) collective-permute-start(bf16[32,640]{1,0:T(8,128)(2,1)} %get-tuple-element.30), channel_id=1, source_target_pairs={{0,5},{1,4},{2,7},{3,6},{4,1},{5,0},{6,3},{7,2},{8,13},{9,12},{10,... | collective-permute-start | bytes 122888 | tf_op jit(solution)/shard_map/ppermute | solution.py:471
  22.7 4.2 %collective-permute-start.7 = (bf16[32,640]{1,0:T(8,128)(2,1)}, bf16[32,640]{1,0:T(8,128)(2,1)S(1)}, u32[]{:S(2)}, u32[]{:S(2)}) collective-permute-start(bf16[32,640]{1,0:T(8,128)(2,1)} %get-tuple-element.30), channel_id=1, source_target_pairs={{0,1},{1,0},{2,3},{3,2},{4,5},{5,4},{6,7},{7,6},{8,9},{9,8},{10,11... | collective-permute-start | bytes 122888 | tf_op jit(solution)/shard_map/ppermute | solution.py:471
  27.0 4.2 %collective-permute-start.8 = (bf16[32,640]{1,0:T(8,128)(2,1)}, bf16[32,640]{1,0:T(8,128)(2,1)S(1)}, u32[]{:S(2)}, u32[]{:S(2)}) collective-permute-start(bf16[32,640]{1,0:T(8,128)(2,1)} %get-tuple-element.30), channel_id=1, source_target_pairs={{0,4},{1,5},{2,6},{3,7},{4,0},{5,1},{6,2},{7,3},{8,12},{9,13},{10,... | collective-permute-start | bytes 122888 | tf_op jit(solution)/shard_map/ppermute | solution.py:471
  31.2 20.0 %collective-permute-start.3 = (bf16[32,1408]{1,0:T(8,128)(2,1)}, bf16[32,1408]{1,0:T(8,128)(2,1)S(1)}, u32[]{:S(2)}, u32[]{:S(2)}) collective-permute-start(bf16[32,1408]{1,0:T(8,128)(2,1)} %get-tuple-element.29), channel_id=1, source_target_pairs={{0,24},{1,25},{2,26},{3,27},{4,28},{5,29},{6,30},{7,31},{8,16},{9,... | collective-permute-start | bytes 270344 | tf_op jit(solution)/shard_map/ppermute | solution.py:471
  34.8 5.1 %collective-permute-start.1 = (bf16[32,1408]{1,0:T(8,128)(2,1)}, bf16[32,1408]{1,0:T(8,128)(2,1)S(1)}, u32[]{:S(2)}, u32[]{:S(2)}) collective-permute-start(bf16[32,1408]{1,0:T(8,128)(2,1)} %get-tuple-element.29), channel_id=1, source_target_pairs={{0,8},{1,9},{2,10},{3,11},{4,12},{5,13},{6,14},{7,15},{8,0},{9,1},... | collective-permute-start | bytes 270344 | tf_op jit(solution)/shard_map/ppermute | solution.py:471
  39.9 10.8 %collective-permute-start.2 = (bf16[32,1408]{1,0:T(8,128)(2,1)}, bf16[32,1408]{1,0:T(8,128)(2,1)S(1)}, u32[]{:S(2)}, u32[]{:S(2)}) collective-permute-start(bf16[32,1408]{1,0:T(8,128)(2,1)} %get-tuple-element.29), channel_id=1, source_target_pairs={{0,16},{1,17},{2,18},{3,19},{4,20},{5,21},{6,22},{7,23},{8,24},{9,... | collective-permute-start | bytes 270344 | tf_op jit(solution)/shard_map/ppermute | solution.py:471
  50.7 7.3 %collective-permute-start.12 = (bf16[128,640]{1,0:T(8,128)(2,1)S(1)}, bf16[128,640]{1,0:T(8,128)(2,1)S(1)}, u32[]{:S(2)}, u32[]{:S(2)}) collective-permute-start(bf16[128,640]{1,0:T(8,128)(2,1)S(1)} %constant_dynamic-update-slice_fusion.4.refs_4_), channel_id=1, source_target_pairs={{0,24},{1,25},{2,26},{3,27},{4,28},{5,29},{6,30},{7,31},{8,16},{9,... | collective-permute-start | bytes 491528 | tf_op jit(solution)/shard_map/ppermute | solution.py:471
  51.2 9.8 %collective-permute-start.11 = (bf16[128,640]{1,0:T(8,128)(2,1)S(1)}, bf16[128,640]{1,0:T(8,128)(2,1)S(1)}, u32[]{:S(2)}, u32[]{:S(2)}) collective-permute-start(bf16[128,640]{1,0:T(8,128)(2,1)S(1)} %constant_dynamic-update-slice_fusion.4.refs_4_), channel_id=1, source_target_pairs={{0,16},{1,17},{2,18},{3,19},{4,20},{5,21},{6,22},{7,23},{8,24},{9,... | collective-permute-start | bytes 491528 | tf_op jit(solution)/shard_map/ppermute | solution.py:471
  58.0 86.7 %copy-start.11 = (bf16[128,640]{1,0:T(8,128)(2,1)}, bf16[128,640]{1,0:T(8,128)(2,1)S(1)}, u32[]{:S(2)}) copy-start(bf16[128,640]{1,0:T(8,128)(2,1)S(1)} %collective-permute-done.12.refs_7_) | copy-start | bytes 491524
  58.1 11.5 %collective-permute-start.6 = (bf16[128,1408]{1,0:T(8,128)(2,1)S(1)}, bf16[128,1408]{1,0:T(8,128)(2,1)S(1)}, u32[]{:S(2)}, u32[]{:S(2)}) collective-permute-start(bf16[128,1408]{1,0:T(8,128)(2,1)S(1)} %constant_dynamic-update-slice_fusion.refs_0_), channel_id=1, source_target_pairs={{0,5},{1,4},{2,7},{3,6},{4,1},{5,0},{6,3},{7,2},{8,13},{9,12},{10,... | collective-permute-start | bytes 1081352 | tf_op jit(solution)/shard_map/ppermute | solution.py:471
  61.7 5.3 %collective-permute-start.10 = (bf16[128,640]{1,0:T(8,128)(2,1)S(1)}, bf16[128,640]{1,0:T(8,128)(2,1)S(1)}, u32[]{:S(2)}, u32[]{:S(2)}) collective-permute-start(bf16[128,640]{1,0:T(8,128)(2,1)S(1)} %constant_dynamic-update-slice_fusion.4.refs_4_), channel_id=1, source_target_pairs={{0,8},{1,9},{2,10},{3,11},{4,12},{5,13},{6,14},{7,15},{8,0},{9,1},... | collective-permute-start | bytes 491528 | tf_op jit(solution)/shard_map/ppermute | solution.py:471
  67.7 77.3 %collective-permute-start.5 = (bf16[128,1408]{1,0:T(8,128)(2,1)S(1)}, bf16[128,1408]{1,0:T(8,128)(2,1)S(1)}, u32[]{:S(2)}, u32[]{:S(2)}) collective-permute-start(bf16[128,1408]{1,0:T(8,128)(2,1)S(1)} %constant_dynamic-update-slice_fusion.refs_0_), channel_id=1, source_target_pairs={{0,4},{1,5},{2,6},{3,7},{4,0},{5,1},{6,2},{7,3},{8,12},{9,13},{10,... | collective-permute-start | bytes 1081352 | tf_op jit(solution)/shard_map/ppermute | solution.py:471
  69.5 75.4 %collective-permute-start.4 = (bf16[128,1408]{1,0:T(8,128)(2,1)S(1)}, bf16[128,1408]{1,0:T(8,128)(2,1)S(1)}, u32[]{:S(2)}, u32[]{:S(2)}) collective-permute-start(bf16[128,1408]{1,0:T(8,128)(2,1)S(1)} %constant_dynamic-update-slice_fusion.refs_0_), channel_id=1, source_target_pairs={{0,1},{1,0},{2,3},{3,2},{4,5},{5,4},{6,7},{7,6},{8,9},{9,8},{10,11... | collective-permute-start | bytes 1081352 | tf_op jit(solution)/shard_map/ppermute | solution.py:471
  161.3 11.3 %collective-permute-start.16 = (bf16[128,1408]{1,0:T(8,128)(2,1)S(1)}, bf16[128,1408]{1,0:T(8,128)(2,1)S(1)}, u32[]{:S(2)}, u32[]{:S(2)}) collective-permute-start(bf16[128,1408]{1,0:T(8,128)(2,1)S(1)} %get-tuple-element.32), channel_id=1, source_target_pairs={{0,1},{1,0},{2,3},{3,2},{4,5},{5,4},{6,7},{7,6},{8,9},{9,8},{10,11... | collective-permute-start | bytes 1081352 | tf_op jit(solution)/shard_map/ppermute | solution.py:471
  162.1 14.3 %collective-permute-start.17 = (bf16[128,1408]{1,0:T(8,128)(2,1)S(1)}, bf16[128,1408]{1,0:T(8,128)(2,1)S(1)}, u32[]{:S(2)}, u32[]{:S(2)}) collective-permute-start(bf16[128,1408]{1,0:T(8,128)(2,1)S(1)} %get-tuple-element.33), channel_id=1, source_target_pairs={{0,4},{1,5},{2,6},{3,7},{4,0},{5,1},{6,2},{7,3},{8,12},{9,13},{10,... | collective-permute-start | bytes 1081352 | tf_op jit(solution)/shard_map/ppermute | solution.py:471
  162.1 14.3 %collective-permute-start.18 = (bf16[128,1408]{1,0:T(8,128)(2,1)S(1)}, bf16[128,1408]{1,0:T(8,128)(2,1)S(1)}, u32[]{:S(2)}, u32[]{:S(2)}) collective-permute-start(bf16[128,1408]{1,0:T(8,128)(2,1)S(1)} %get-tuple-element.34), channel_id=1, source_target_pairs={{0,5},{1,4},{2,7},{3,6},{4,1},{5,0},{6,3},{7,2},{8,13},{9,12},{10,... | collective-permute-start | bytes 1081352 | tf_op jit(solution)/shard_map/ppermute | solution.py:471
  164.7 15.2 %collective-permute-start.22 = (bf16[128,640]{1,0:T(8,128)(2,1)}, bf16[128,640]{1,0:T(8,128)(2,1)S(1)}, u32[]{:S(2)}, u32[]{:S(2)}) collective-permute-start(bf16[128,640]{1,0:T(8,128)(2,1)} %get-tuple-element.40), channel_id=1, source_target_pairs={{0,8},{1,9},{2,10},{3,11},{4,12},{5,13},{6,14},{7,15},{8,0},{9,1},... | collective-permute-start | bytes 491528 | tf_op jit(solution)/shard_map/ppermute | solution.py:471
  164.8 19.1 %collective-permute-start.23 = (bf16[128,640]{1,0:T(8,128)(2,1)}, bf16[128,640]{1,0:T(8,128)(2,1)S(1)}, u32[]{:S(2)}, u32[]{:S(2)}) collective-permute-start(bf16[128,640]{1,0:T(8,128)(2,1)} %get-tuple-element.41), channel_id=1, source_target_pairs={{0,16},{1,17},{2,18},{3,19},{4,20},{5,21},{6,22},{7,23},{8,24},{9,... | collective-permute-start | bytes 491528 | tf_op jit(solution)/shard_map/ppermute | solution.py:471
  172.5 11.3 %collective-permute-start.24 = (bf16[128,640]{1,0:T(8,128)(2,1)}, bf16[128,640]{1,0:T(8,128)(2,1)S(1)}, u32[]{:S(2)}, u32[]{:S(2)}) collective-permute-start(bf16[128,640]{1,0:T(8,128)(2,1)} %get-tuple-element.42), channel_id=1, source_target_pairs={{0,24},{1,25},{2,26},{3,27},{4,28},{5,29},{6,30},{7,31},{8,16},{9,... | collective-permute-start | bytes 491528 | tf_op jit(solution)/shard_map/ppermute | solution.py:471
  179.5 16.4 %collective-permute-start.19 = (bf16[32,1408]{1,0:T(8,128)(2,1)}, bf16[32,1408]{1,0:T(8,128)(2,1)S(1)}, u32[]{:S(2)}, u32[]{:S(2)}) collective-permute-start(bf16[32,1408]{1,0:T(8,128)(2,1)} %get-tuple-element.36), channel_id=1, source_target_pairs={{0,8},{1,9},{2,10},{3,11},{4,12},{5,13},{6,14},{7,15},{8,0},{9,1},... | collective-permute-start | bytes 270344 | tf_op jit(solution)/shard_map/ppermute | solution.py:471
  179.5 16.4 %collective-permute-start.20 = (bf16[32,1408]{1,0:T(8,128)(2,1)}, bf16[32,1408]{1,0:T(8,128)(2,1)S(1)}, u32[]{:S(2)}, u32[]{:S(2)}) collective-permute-start(bf16[32,1408]{1,0:T(8,128)(2,1)} %get-tuple-element.37), channel_id=1, source_target_pairs={{0,16},{1,17},{2,18},{3,19},{4,20},{5,21},{6,22},{7,23},{8,24},{9,... | collective-permute-start | bytes 270344 | tf_op jit(solution)/shard_map/ppermute | solution.py:471
  180.0 15.9 %collective-permute-start.21 = (bf16[32,1408]{1,0:T(8,128)(2,1)}, bf16[32,1408]{1,0:T(8,128)(2,1)S(1)}, u32[]{:S(2)}, u32[]{:S(2)}) collective-permute-start(bf16[32,1408]{1,0:T(8,128)(2,1)} %get-tuple-element.38), channel_id=1, source_target_pairs={{0,24},{1,25},{2,26},{3,27},{4,28},{5,29},{6,30},{7,31},{8,16},{9,... | collective-permute-start | bytes 270344 | tf_op jit(solution)/shard_map/ppermute | solution.py:471
  186.5 4.2 %collective-permute-start.25 = (bf16[32,640]{1,0:T(8,128)(2,1)}, bf16[32,640]{1,0:T(8,128)(2,1)S(1)}, u32[]{:S(2)}, u32[]{:S(2)}) collective-permute-start(bf16[32,640]{1,0:T(8,128)(2,1)} %get-tuple-element.44), channel_id=1, source_target_pairs={{0,1},{1,0},{2,3},{3,2},{4,5},{5,4},{6,7},{7,6},{8,9},{9,8},{10,11... | collective-permute-start | bytes 122888 | tf_op jit(solution)/shard_map/ppermute | solution.py:471
  188.3 4.4 %collective-permute-start.26 = (bf16[32,640]{1,0:T(8,128)(2,1)}, bf16[32,640]{1,0:T(8,128)(2,1)S(1)}, u32[]{:S(2)}, u32[]{:S(2)}) collective-permute-start(bf16[32,640]{1,0:T(8,128)(2,1)} %get-tuple-element.45), channel_id=1, source_target_pairs={{0,4},{1,5},{2,6},{3,7},{4,0},{5,1},{6,2},{7,3},{8,12},{9,13},{10,... | collective-permute-start | bytes 122888 | tf_op jit(solution)/shard_map/ppermute | solution.py:471
  190.7 5.1 %collective-permute-start.27 = (bf16[32,640]{1,0:T(8,128)(2,1)}, bf16[32,640]{1,0:T(8,128)(2,1)S(1)}, u32[]{:S(2)}, u32[]{:S(2)}) collective-permute-start(bf16[32,640]{1,0:T(8,128)(2,1)} %get-tuple-element.46), channel_id=1, source_target_pairs={{0,5},{1,4},{2,7},{3,6},{4,1},{5,0},{6,3},{7,2},{8,13},{9,12},{10,... | collective-permute-start | bytes 122888 | tf_op jit(solution)/shard_map/ppermute | solution.py:471
  (28 other events, 42.1 us)

commit v2 on v1

--- a/solution.py
+++ b/solution.py
@@ -179,7 +179,9 @@
 
 ALL = ("req", "tp")
 MASKED = -1e30
-VMEM_BYTES = 40 * 1024 * 1024
+LANES = 128
+MIB = 1024 * 1024
+SMALL = pltpu.CompilerParams(vmem_limit_bytes=8 * MIB)
 
 
 def vmem():
@@ -188,6 +190,18 @@
 
 def smem():
     return pl.BlockSpec(memory_space=pltpu.SMEM)
+
+
+def hbm():
+    return pl.BlockSpec(memory_space=pltpu.HBM)
+
+
+def stay(value):
+    return pltpu.with_memory_space_constraint(value, pltpu.HBM)
+
+
+def barrier(*values):
+    return lax.optimization_barrier(values)
 
 
 def multiplicity(page_rows, length, pool_pages, page_tokens):
@@ -203,12 +217,44 @@
     return jnp.concatenate(parts, axis=1)
 
 
+def pack_shares(ids, routed, home_ref):
+    groups = home_ref.shape[0]
+    rows = ids.shape[0]
+    lane = lax.broadcasted_iota(jnp.int32, (rows, LANES), 1)
+    shares = routed / jnp.sum(routed, axis=1, keepdims=True)
+    by_expert = jnp.zeros((rows, LANES), jnp.float32)
+    for k in range(ids.shape[1]):
+        by_expert = by_expert + jnp.where(lane == ids[:, k : k + 1], shares[:, k : k + 1], 0.0)
+    by_home = jnp.zeros((rows, LANES), jnp.float32)
+    for e in range(groups):
+        mine = (lane == home_ref[e]) | (lane == home_ref[e] + groups)
+        by_home = by_home + jnp.where(mine, by_expert[:, e : e + 1], 0.0)
+    rounded = by_home.astype(jnp.bfloat16).astype(jnp.float32)
+    return jnp.where(lane < groups, rounded, by_home - rounded).astype(jnp.bfloat16)
+
+
 def attention_kernel(
-    pages_ref, lengths_ref, tp_ref, q_ref, fresh_ref, cache_ref, residual_ref, w_hbm,
-    own_ref, send_ref, w_ref, context_ref, terms_ref, w_sem,
+    pages_ref, lengths_ref, tp_ref, home_ref, q_hbm, fresh_hbm, cache_hbm, residual_hbm, ids_hbm,
+    routed_hbm, w_hbm, own_ref, send_ref, pack_ref,
+    q_ref, fresh_ref, cache_ref, residual_ref, ids_ref, routed_ref, w_ref, context_ref, terms_ref,
+    sems,
 ):
-    fetch = pltpu.make_async_copy(w_hbm, w_ref, w_sem)
-    fetch.start()
+    fetches = [
+        pltpu.make_async_copy(source, target, sems.at[i])
+        for i, (source, target) in enumerate(
+            (
+                (q_hbm, q_ref),
+                (cache_hbm, cache_ref),
+                (fresh_hbm, fresh_ref),
+                (ids_hbm, ids_ref),
+                (routed_hbm, routed_ref),
+                (residual_hbm, residual_ref),
+                (w_hbm, w_ref),
+            )
+        )
+    ]
+    for fetch in fetches:
+        fetch.start()
     tokens = q_ref.shape[0]
     pool_pages, page_tokens, _ = cache_ref.shape
     requests, slots = pages_ref.shape
@@ -240,6 +286,8 @@
     visible = jnp.concatenate([count] * group, axis=0)
     seen = jnp.concatenate([jnp.where(seen, 1.0, 0.0)] * group, axis=0)
     scale = HEAD_WIDTH**-0.5
+    for fetch in fetches[:3]:
+        fetch.wait()
     contract_last = (((1,), (1,)), ((), ()))
     for k in range(kv_heads):
         key_at, value_at = 2 * k * HEAD_WIDTH, (2 * k + 1) * HEAD_WIDTH
@@ -282,12 +330,18 @@
             context_ref[:, h * HEAD_WIDTH : (h + 1) * HEAD_WIDTH] = mixed[
                 g * tokens : (g + 1) * tokens
             ]
-    fetch.wait()
     half = tokens // 2
     width = terms_ref.shape[1]
     block = 512
     own_at = pl.multiple_of(tp_ref[0] * half, half)
     other_at = pl.multiple_of((1 - tp_ref[0]) * half, half)
+    for fetch in fetches[3:5]:
+        fetch.wait()
+    pack_ref[...] = pack_shares(
+        ids_ref[pl.ds(own_at, half), :], routed_ref[pl.ds(own_at, half), :], home_ref
+    )
+    for fetch in fetches[5:]:
+        fetch.wait()
     for at in range(0, width, block):
         cols = slice(at, at + block)
         terms_ref[:, cols] = jnp.dot(
@@ -299,79 +353,113 @@
     send_ref[...] = terms_ref[pl.ds(other_at, half), :].astype(jnp.bfloat16)
 
 
-def attention_terms(pages, lengths, tp_index, queries, fresh, cache, residual, w_out):
+def attention_terms(
+    pages, lengths, tp_index, home, queries, fresh, cache, residual, ids, routed, w_out
+):
     tokens, width = residual.shape
     half = tokens // 2
+    moved = (queries, fresh, cache, residual, ids, routed, w_out)
     return pl.pallas_call(
         attention_kernel,
         out_shape=(
             jax.ShapeDtypeStruct((half, width), jnp.float32),
             jax.ShapeDtypeStruct((half, width), jnp.bfloat16),
+            jax.ShapeDtypeStruct((half, LANES), jnp.bfloat16),
         ),
-        in_specs=[smem(), smem(), smem(), vmem(), vmem(), vmem(), vmem(),
-                  pl.BlockSpec(memory_space=pl.ANY)],
-        out_specs=(vmem(), vmem()),
-        scratch_shapes=[
-            pltpu.VMEM(w_out.shape, jnp.bfloat16),
+        in_specs=[smem()] * 4 + [hbm()] * 7,
+        out_specs=(vmem(),) * 3,
+        scratch_shapes=[pltpu.VMEM(v.shape, v.dtype) for v in moved]
+        + [
             pltpu.VMEM(queries.shape, jnp.bfloat16),
             pltpu.VMEM((tokens, width), jnp.float32),
-            pltpu.SemaphoreType.DMA,
+            pltpu.SemaphoreType.DMA((7,)),
         ],
-        compiler_params=pltpu.CompilerParams(vmem_limit_bytes=VMEM_BYTES),
+        compiler_params=pltpu.CompilerParams(vmem_limit_bytes=40 * MIB),
         name="attention_terms",
-    )(pages, lengths, tp_index, queries, fresh, cache, residual, w_out)
-
-
-def norm_kernel(own_ref, got_ref, gain_ref, state_ref, a_ref, b_ref):
+    )(stay(pages), stay(lengths), tp_index, stay(home), *[stay(v) for v in moved])
+
+
+def norm_kernel(own_ref, got_ref, pack_ref, gain_ref, state_ref, a_ref, b_ref):
     state = own_ref[...] + got_ref[...].astype(jnp.float32)
     state_ref[...] = state
     normed = rms_scale(state, gain_ref[...]).astype(jnp.bfloat16)
-    wide = a_ref.shape[1]
-    a_ref[...] = normed[:, :wide]
+    wide = a_ref.shape[1] - LANES
+    a_ref[:, :wide] = normed[:, :wide]
+    a_ref[:, wide:] = pack_ref[...]
     b_ref[...] = normed[:, wide:]
 
 
-def norm_rows(own, got, gain, wide):
+def norm_rows(own, got, pack, gain, wide):
     rows, width = own.shape
     return pl.pallas_call(
         norm_kernel,
         out_shape=(
             jax.ShapeDtypeStruct((rows, width), jnp.float32),
-            jax.ShapeDtypeStruct((rows, wide), jnp.bfloat16),
+            jax.ShapeDtypeStruct((rows, wide + LANES), jnp.bfloat16),
             jax.ShapeDtypeStruct((rows, width - wide), jnp.bfloat16),
         ),
-        in_specs=[vmem()] * 3,
+        in_specs=[vmem()] * 4,
         out_specs=(vmem(),) * 3,
+        compiler_params=SMALL,
         name="norm_rows",
-    )(own, got, gain)
-
-
-def expert_kernel(*refs):
-    (a0, a1, a2, a3, b0, b1, b2, b3, share_ref, wg0, wu0, wd0, wg1, wu1, wd1) = refs[:15]
-    (oa0, oa1, oa2, oa3, ob0, ob1, ob2, ob3, x_ref, h0_ref, h1_ref) = refs[15:]
+    )(own, got, pack, gain)
+
+
+def expert_kernel(
+    group_ref, a0, a1, a2, a3, b0, b1, b2, b3, wg0, wu0, wd0, wg1, wu1, wd1,
+    oa0, oa1, oa2, oa3, ob0, ob1, ob2, ob3,
+    x_ref, w0_ref, w1_ref, down_ref, h_ref, sems,
+):
     a_in, b_in = (a0, a1, a2, a3), (b0, b1, b2, b3)
     a_out, b_out = (oa0, oa1, oa2, oa3), (ob0, ob1, ob2, ob3)
     rows, width = x_ref.shape
-    wide = a0.shape[1]
+    hidden = wg0.shape[1]
+    wide = oa0.shape[1]
     quad = rows // 4
     unit = quad // 4
+    fetches = [
+        pltpu.make_async_copy(source, target, sems.at[i])
+        for i, (source, target) in enumerate(
+            (
+                (wg0, w0_ref.at[:, :hidden]),
+                (wu0, w0_ref.at[:, hidden:]),
+                (wg1, w1_ref.at[:, :hidden]),
+                (wu1, w1_ref.at[:, hidden:]),
+                (wd0, down_ref.at[:hidden, :]),
+                (wd1, down_ref.at[hidden:, :]),
+            )
+        )
+    ]
+    for fetch in fetches:
+        fetch.start()
+    lane = lax.broadcasted_iota(jnp.int32, (rows, LANES), 1)
+    packed = jnp.concatenate([a[:, wide:] for a in a_in], axis=0).astype(jnp.float32)
+    groups = group_ref[2]
     for i in range(4):
-        x_ref[i * quad : (i + 1) * quad, :wide] = a_in[i][...]
+        x_ref[i * quad : (i + 1) * quad, :wide] = a_in[i][:, :wide]
         for j in range(4):
             at = i * quad + j * unit
             x_ref[at : at + unit, wide:] = b_in[j][i * unit : (i + 1) * unit, :]
-    for wg, wu, h_ref in ((wg0, wu0, h0_ref), (wg1, wu1, h1_ref)):
-        gate = jnp.dot(x_ref[...], wg[...], preferred_element_type=jnp.float32)
-        up = jnp.dot(x_ref[...], wu[...], preferred_element_type=jnp.float32)
-        h_ref[...] = (gate / (1.0 + jnp.exp(-gate)) * up).astype(jnp.bfloat16)
-    share0, share1 = share_ref[:, 0:1], share_ref[:, 1:2]
-    block = 128
+    for e, w_ref in enumerate((w0_ref, w1_ref)):
+        group = group_ref[e]
+        share = jnp.sum(
+            jnp.where((lane == group) | (lane == group + groups), packed, 0.0),
+            axis=1,
+            keepdims=True,
+        )
+        fetches[2 * e].wait()
+        fetches[2 * e + 1].wait()
+        both = jnp.dot(x_ref[...], w_ref[...], preferred_element_type=jnp.float32)
+        gate, up = both[:, :hidden], both[:, hidden:]
+        h_ref[:, e * hidden : (e + 1) * hidden] = (
+            share * up * (gate / (1.0 + jnp.exp(-gate)))
+        ).astype(jnp.bfloat16)
+    fetches[4].wait()
+    fetches[5].wait()
+    block = 256
     for at in range(0, width, block):
         cols = slice(at, at + block)
-        down = share0 * jnp.dot(h0_ref[...], wd0[:, cols], preferred_element_type=jnp.float32)
-        down = down + share1 * jnp.dot(
-            h1_ref[...], wd1[:, cols], preferred_element_type=jnp.float32
-        )
+        down = jnp.dot(h_ref[...], down_ref[:, cols], preferred_element_type=jnp.float32)
         if at < wide:
             for i in range(4):
                 a_out[i][:, cols] = down[i * quad : (i + 1) * quad].astype(a_out[i].dtype)
@@ -385,9 +473,9 @@
                     )
 
 
-def expert_rows(a_parts, b_parts, shares, weights, partner_weights):
-    quad, wide = a_parts[0].shape
-    narrow = b_parts[0].shape[1]
+def expert_rows(group, a_parts, b_parts, weights, partner_weights):
+    quad, narrow = b_parts[0].shape
+    wide = a_parts[0].shape[1] - LANES
     width = wide + narrow
     rows = 4 * quad
     hidden = weights[0].shape[1]
@@ -396,19 +484,22 @@
         expert_kernel,
         out_shape=tuple(jax.ShapeDtypeStruct((quad, wide), kind) for kind in kinds)
         + tuple(jax.ShapeDtypeStruct((quad, narrow), kind) for kind in kinds),
-        in_specs=[vmem()] * 15,
+        in_specs=[smem()] + [vmem()] * 8 + [hbm()] * 6,
         out_specs=(vmem(),) * 8,
         scratch_shapes=[
             pltpu.VMEM((rows, width), jnp.bfloat16),
-            pltpu.VMEM((rows, hidden), jnp.bfloat16),
-            pltpu.VMEM((rows, hidden), jnp.bfloat16),
+            pltpu.VMEM((width, 2 * hidden), jnp.bfloat16),
+            pltpu.VMEM((width, 2 * hidden), jnp.bfloat16),
+            pltpu.VMEM((2 * hidden, width), jnp.bfloat16),
+            pltpu.VMEM((rows, 2 * hidden), jnp.bfloat16),
+            pltpu.SemaphoreType.DMA((6,)),
         ],
-        compiler_params=pltpu.CompilerParams(vmem_limit_bytes=VMEM_BYTES),
+        compiler_params=pltpu.CompilerParams(vmem_limit_bytes=40 * MIB),
         cost_estimate=pl.CostEstimate(
             flops=12 * rows * width * hidden, bytes_accessed=16 * rows * width, transcendentals=0
         ),
         name="expert_rows",
-    )(*a_parts, *b_parts, shares, *weights, *partner_weights)
+    )(group, *a_parts, *b_parts, *[stay(w) for w in weights + partner_weights])
 
 
 def sum_kernel(own_ref, g1, g2, g3, o0, o1, o2, o3):
@@ -430,6 +521,7 @@
         out_shape=tuple(jax.ShapeDtypeStruct((unit, width), kind) for kind in kinds),
         in_specs=[vmem()] * 4,
         out_specs=(vmem(),) * 4,
+        compiler_params=SMALL,
         name="sum_rows",
     )(own, *got)
 
@@ -452,6 +544,7 @@
         out_shape=jax.ShapeDtypeStruct(state.shape, jnp.bfloat16),
         in_specs=[vmem()] * 10,
         out_specs=vmem(),
+        compiler_params=SMALL,
         name="final_rows",
     )(state, *a_parts, *b_parts, gain)
 
@@ -490,58 +583,32 @@
     req_index = lax.axis_index("req")
     tokens, width = residual.shape
     half = tokens // 2
-    wide = (width * 11 // 16) // 128 * 128
+    wide = width * 5 // 8
     groups = expert_home.shape[0]
     weights = (w_gate[0], w_up[0], w_down[0])
     partner_weights = tuple(swap(w, 0, 0, 1, 0) for w in weights)
-    own_start = tp_index * half
-    ids = lax.dynamic_slice_in_dim(route_ids, own_start, half, 0)
-    routed = lax.dynamic_slice_in_dim(route_weights, own_start, half, 0)
-    shares = routed / jnp.sum(routed, axis=1, keepdims=True)
-    by_expert = jnp.sum(
-        jnp.where(
-            ids[:, :, None] == jnp.arange(groups, dtype=jnp.int32)[None, None, :],
-            shares[:, :, None],
-            0.0,
-        ),
-        axis=1,
-    )
-    homes = expert_home[:, None] == jnp.arange(groups, dtype=jnp.int32)[None, :]
-    by_home = jnp.sum(jnp.where(homes[None], by_expert[:, :, None], 0.0), axis=1)
-    every_share = lax.all_gather(by_home, ALL, axis=0, tiled=False)
-    core = req_index % 2
-    spots = [
-        (((req_index // 4) ^ dz) * 2 + (((req_index // 2) % 2) ^ dy)) * 4 + core * 2 + (tp_index ^ dx)
-        for dy, dx in PLANE
-        for dz in range(4)
-    ]
-    near_share = every_share[jnp.stack(spots)].reshape(16 * half, groups)
-    column = jnp.arange(groups, dtype=jnp.int32)[None, :]
-    pair_share = jnp.stack(
-        [
-            jnp.sum(jnp.where(column == req_index, near_share, 0.0), axis=1),
-            jnp.sum(jnp.where(column == (req_index ^ 1), near_share, 0.0), axis=1),
-        ],
-        axis=1,
-    )
-
-    own_state, sent = attention_terms(
-        request_page_index, cache_length_rows, tp_index.reshape(1).astype(jnp.int32),
-        queries, fresh_key_value, key_value_cache, residual, w_out,
+    own_state, sent, pack = attention_terms(
+        request_page_index, cache_length_rows, tp_index.reshape(1).astype(jnp.int32), expert_home,
+        queries, fresh_key_value, key_value_cache, residual, route_ids, route_weights, w_out,
     )
     got = swap(sent, 0, 0, 0, 1)
-    state, rows_a, rows_b = norm_rows(own_state, got, gain_in[None, :], wide)
-    column_a = jnp.concatenate((rows_a,) + swap_z((rows_a,) * 3), axis=0)
-    column_b = jnp.concatenate((rows_b,) + swap_plane((rows_b,) * 3), axis=0)
-    all_a = (column_a,) + swap_plane((column_a,) * 3)
-    all_b = (column_b,) + swap_z((column_b,) * 3)
-    parts = expert_rows(all_a, all_b, pair_share, weights, partner_weights)
+    state, rows_a, rows_b = norm_rows(own_state, got, pack, gain_in[None, :], wide)
+    more_a, more_b, partner_weights = barrier(
+        swap_z((rows_a,) * 3), swap_plane((rows_b,) * 3), partner_weights
+    )
+    column_a, column_b = barrier(
+        jnp.concatenate((rows_a,) + more_a, axis=0), jnp.concatenate((rows_b,) + more_b, axis=0)
+    )
+    more_a, more_b = barrier(swap_plane((column_a,) * 3), swap_z((column_b,) * 3))
+    group = jnp.stack([req_index, req_index ^ 1, groups]).astype(jnp.int32)
+    parts = expert_rows(
+        group, (column_a,) + more_a, (column_b,) + more_b, weights, partner_weights
+    )
     part_a, part_b = parts[:4], parts[4:]
-    near_a = sum_rows(part_a[0], swap_plane(part_a[1:]))
-    near_b = sum_rows(part_b[0], swap_z(part_b[1:]))
-    last_a = (near_a[0],) + swap_z(near_a[1:])
-    last_b = (near_b[0],) + swap_plane(near_b[1:])
-    return final_rows(state, last_a, last_b, gain_out[None, :])
+    more_a, more_b = barrier(swap_plane(part_a[1:]), swap_z(part_b[1:]))
+    near_a, near_b = barrier(sum_rows(part_a[0], more_a), sum_rows(part_b[0], more_b))
+    more_a, more_b = barrier(swap_z(near_a[1:]), swap_plane(near_b[1:]))
+    return final_rows(state, (near_a[0],) + more_a, (near_b[0],) + more_b, gain_out[None, :])
 
 
 def solution(mesh):

time: 199 us -> 96.4 us (0.48)
  blocking collectives: 71.1 us -> 0 us
  waiting for transfers between devices: 57.2 us -> 34.7 us
  starting transfers between devices: 24.6 us -> 41.1 us
  local copies, waits for them, and re-layouts: 21 us -> 5.25 us
  Pallas kernels: 23 us -> 14.8 us
    all_gather x1 -> x0, blocking collectives: 71.1 us -> none  [local_dense(): every_share = lax.all_gather(by_home, ALL, axis=0, tiled=False)]
    ppermute x28, waiting for transfers between devices: 57.2 us -> 34.7 us  [swap(): return lax.ppermute(value, ALL, pairs)]
    ppermute x28, starting transfers between devices: 24.6 us -> 41.1 us  [swap(): return lax.ppermute(value, ALL, pairs)]
    unnamed x71 -> x9, local copies, waits for them, and re-layouts: 18.4 us -> 5.25 us
    pallas_call x2, Pallas kernels: 4.13 us -> 0.26 us  [sum_rows(): pl.pallas_call(sum_kernel, out_shape=tuple((jax.ShapeDtypeStruct((unit, w...]
    pallas_call x1, Pallas kernels: 11.9 us -> 8.97 us  [expert_rows(): pl.pallas_call(expert_kernel, out_shape=tuple((jax.ShapeDtypeStruct((quad...]
    gather x1 -> x0, local copies, waits for them, and re-layouts: 2.16 us -> none  [local_dense(): near_share = every_share[jnp.stack(spots)].reshape(16 * half, groups)]
  transfers between devices with their start and end apart: 28 -> 28, of which waited for: 14 -> 12; matrix products, arithmetic and copies ran while one was open for 3% -> 4% of each run, Pallas kernels for 3% -> 5%
where the time goes in v2:
time: 96.4 us; the launch traced here: 96.1 us
  starting transfers between devices  41.1 us (43%)
  waiting for transfers between devices  34.7 us (36%)
  Pallas kernels  14.8 us (15%)
  local copies, waits for them, and re-layouts  5.25 us (5%)
    ppermute x28, starting transfers between devices, swap(): return lax.ppermute(value, ALL, pairs)  41.1 us
    ppermute x28, waiting for transfers between devices, swap(): return lax.ppermute(value, ALL, pairs)  34.7 us
    pallas_call x1, Pallas kernels, expert_rows(): pl.pallas_call(expert_kernel, out_shape=tuple((jax.ShapeDtypeStruct((quad...  8.97 us
    unnamed x9, local copies, waits for them, and re-layouts  5.25 us
    pallas_call x1, Pallas kernels, attention_terms(): pl.pallas_call(attention_kernel, out_shape=(jax.ShapeDtypeStruct((half, w...  4.59 us
  transfers between devices with their start and end apart: 28, of which 12 were waited for; matrix products, arithmetic and copies ran while one was open for 4% of the time, Pallas kernels for 5%

profile of v2, /device:TPU:0, one launch (start us, length us, event | category | flops | bytes accessed | tf_op | source)
XLA Modules:
  0.0 96.1 jit_solution(8520384454235519622)
XLA Ops:
  1.0 1.4 %copy.16.pages_ref = s32[9,4]{1,0:T(8,128)} copy(s32[9,4]{0,1:T(4,128)} %param.18) | data formatting | bytes 288 | tf_op args[3]
  2.3 1.4 %copy.17.ids_hbm = s32[64,8]{1,0:T(8,128)} copy(s32[64,8]{0,1:T(8,128)} %param.23) | data formatting | bytes 4096 | tf_op args[8]
  3.7 1.4 %copy.18.routed_hbm = f32[64,8]{1,0:T(8,128)} copy(f32[64,8]{0,1:T(8,128)} %param.24) | data formatting | bytes 4096 | tf_op args[9]
  5.1 4.6 %attention_terms.1 = (f32[32,2048]{1,0:T(8,128)S(1)}, bf16[32,2048]{1,0:T(8,128)(2,1)S(1)}, bf16[32,128]{1,0:T(8,128)(2,1)S(1)}) custom-call(s32[9,4]{1,0:T(8,128)} %copy.16.pages_ref, s32[9]{0:T(128)} %lengths_ref.1, s32[1]{0:T(128)} %bitcast.tp_ref, s32[16]{0:T(128)} %home_ref.1, bf16[64,1024]{1,0:T(8,128)(2,1)} %q_hbm.1, bf16[64,512]{1,0:T(8,128)(2,1)} %fresh_hbm.1, ...), custom_call_target="tpu_custom_call" | custom-call | tf_op jit(solution)/shard_map/attention_terms/pallas_call | solution.py:362
  9.7 2.6 %collective-permute-start = (bf16[32,2048]{1,0:T(8,128)(2,1)S(1)}, bf16[32,2048]{1,0:T(8,128)(2,1)S(1)}, u32[]{:S(2)}, u32[]{:S(2)}) collective-permute-start(bf16[32,2048]{1,0:T(8,128)(2,1)S(1)} %get-tuple-element.65), channel_id=1, source_target_pairs={{0,1},{1,0},{2,3},{3,2},{4,5},{5,4},{6,7},{7,6},{8,9},{9,8},{10,11... | collective-permute-start | bytes 393224 | tf_op jit(solution)/shard_map/ppermute | solution.py:564
  12.2 4.2 %collective-permute-done.got_ref = bf16[32,2048]{1,0:T(8,128)(2,1)S(1)} collective-permute-done((bf16[32,2048]{1,0:T(8,128)(2,1)S(1)}, bf16[32,2048]{1,0:T(8,128)(2,1)S(1)}, u32[]{:S(2)}, u32[]{:S(2)}) %collective-permute-start) | collective-permute-done | bytes 131104 | tf_op jit(solution)/shard_map/ppermute | solution.py:564
  16.5 2.8 %collective-permute-start.6 = (bf16[32,768]{1,0:T(8,128)(2,1)S(1)}, bf16[32,768]{1,0:T(8,128)(2,1)S(1)}, u32[]{:S(2)}, u32[]{:S(2)}) collective-permute-start(bf16[32,768]{1,0:T(8,128)(2,1)S(1)} %get-tuple-element.69), channel_id=1, source_target_pairs={{0,5},{1,4},{2,7},{3,6},{4,1},{5,0},{6,3},{7,2},{8,13},{9,12},{10,... | collective-permute-start | bytes 147464 | tf_op jit(solution)/shard_map/ppermute | solution.py:564
  19.8 1.8 %collective-permute-done.6 = bf16[32,768]{1,0:T(8,128)(2,1)S(1)} collective-permute-done((bf16[32,768]{1,0:T(8,128)(2,1)S(1)}, bf16[32,768]{1,0:T(8,128)(2,1)S(1)}, u32[]{:S(2)}, u32[]{:S(2)}) %collective-permute-start.6) | collective-permute-done | bytes 49184 | tf_op jit(solution)/shard_map/ppermute | solution.py:564
  21.6 3.9 %collective-permute-start.3 = (bf16[32,1408]{1,0:T(8,128)(2,1)S(1)}, bf16[32,1408]{1,0:T(8,128)(2,1)S(1)}, u32[]{:S(2)}, u32[]{:S(2)}) collective-permute-start(bf16[32,1408]{1,0:T(8,128)(2,1)S(1)} %get-tuple-element.68), channel_id=1, source_target_pairs={{0,24},{1,25},{2,26},{3,27},{4,28},{5,29},{6,30},{7,31},{8,16},{9,... | collective-permute-start | bytes 270344 | tf_op jit(solution)/shard_map/ppermute | solution.py:564
  25.5 1.4 %collective-permute-start.4 = (bf16[32,768]{1,0:T(8,128)(2,1)S(1)}, bf16[32,768]{1,0:T(8,128)(2,1)S(1)}, u32[]{:S(2)}, u32[]{:S(2)}) collective-permute-start(bf16[32,768]{1,0:T(8,128)(2,1)S(1)} %get-tuple-element.69), channel_id=1, source_target_pairs={{0,1},{1,0},{2,3},{3,2},{4,5},{5,4},{6,7},{7,6},{8,9},{9,8},{10,11... | collective-permute-start | bytes 147464 | tf_op jit(solution)/shard_map/ppermute | solution.py:564
  26.9 2.7 %collective-permute-done.4 = bf16[32,768]{1,0:T(8,128)(2,1)S(1)} collective-permute-done((bf16[32,768]{1,0:T(8,128)(2,1)S(1)}, bf16[32,768]{1,0:T(8,128)(2,1)S(1)}, u32[]{:S(2)}, u32[]{:S(2)}) %collective-permute-start.4) | collective-permute-done | bytes 49184 | tf_op jit(solution)/shard_map/ppermute | solution.py:564
  30.1 1.6 %collective-permute-start.1 = (bf16[32,1408]{1,0:T(8,128)(2,1)S(1)}, bf16[32,1408]{1,0:T(8,128)(2,1)S(1)}, u32[]{:S(2)}, u32[]{:S(2)}) collective-permute-start(bf16[32,1408]{1,0:T(8,128)(2,1)S(1)} %get-tuple-element.68), channel_id=1, source_target_pairs={{0,8},{1,9},{2,10},{3,11},{4,12},{5,13},{6,14},{7,15},{8,0},{9,1},... | collective-permute-start | bytes 270344 | tf_op jit(solution)/shard_map/ppermute | solution.py:564
  31.7 3.5 %collective-permute-done.2 = bf16[32,1408]{1,0:T(8,128)(2,1)S(1)} collective-permute-done((bf16[32,1408]{1,0:T(8,128)(2,1)S(1)}, bf16[32,1408]{1,0:T(8,128)(2,1)S(1)}, u32[]{:S(2)}, u32[]{:S(2)}) %collective-permute-start.2) | collective-permute-done | bytes 90144 | tf_op jit(solution)/shard_map/ppermute | solution.py:564
  35.6 1.1 %copy-done.2 = bf16[2048,384]{1,0:T(8,128)(2,1)} copy-done((bf16[2048,384]{1,0:T(8,128)(2,1)}, bf16[2048,384]{1,0:T(8,128)(2,1)S(1)}, u32[]{:S(2)}) %copy-start.2) | copy-done | bytes 1572888
  36.8 2.0 %collective-permute-start.15 = (bf16[128,768]{1,0:T(8,128)(2,1)S(1)}, bf16[128,768]{1,0:T(8,128)(2,1)S(1)}, u32[]{:S(2)}, u32[]{:S(2)}) collective-permute-start(bf16[128,768]{1,0:T(8,128)(2,1)S(1)} %pad_maximum_fusion.1.b0), channel_id=1, source_target_pairs={{0,24},{1,25},{2,26},{3,27},{4,28},{5,29},{6,30},{7,31},{8,16},{9,... | collective-permute-start | bytes 589832 | tf_op jit(solution)/shard_map/ppermute | solution.py:564
  38.7 2.1 %collective-permute-start.12 = (bf16[128,1408]{1,0:T(8,128)(2,1)S(1)}, bf16[128,1408]{1,0:T(8,128)(2,1)S(1)}, u32[]{:S(2)}, u32[]{:S(2)}) collective-permute-start(bf16[128,1408]{1,0:T(8,128)(2,1)S(1)} %pad_maximum_fusion.a0), channel_id=1, source_target_pairs={{0,5},{1,4},{2,7},{3,6},{4,1},{5,0},{6,3},{7,2},{8,13},{9,12},{10,... | collective-permute-start | bytes 1081352 | tf_op jit(solution)/shard_map/ppermute | solution.py:564
  42.4 3.9 %collective-permute-done.15.b3 = bf16[128,768]{1,0:T(8,128)(2,1)S(1)} collective-permute-done((bf16[128,768]{1,0:T(8,128)(2,1)S(1)}, bf16[128,768]{1,0:T(8,128)(2,1)S(1)}, u32[]{:S(2)}, u32[]{:S(2)}) %collective-permute-start.15) | collective-permute-done | bytes 196640 | tf_op jit(solution)/shard_map/ppermute | solution.py:564
  46.3 4.9 %collective-permute-start.13 = (bf16[128,768]{1,0:T(8,128)(2,1)S(1)}, bf16[128,768]{1,0:T(8,128)(2,1)S(1)}, u32[]{:S(2)}, u32[]{:S(2)}) collective-permute-start(bf16[128,768]{1,0:T(8,128)(2,1)S(1)} %pad_maximum_fusion.1.b0), channel_id=1, source_target_pairs={{0,8},{1,9},{2,10},{3,11},{4,12},{5,13},{6,14},{7,15},{8,0},{9,1},... | collective-permute-start | bytes 589832 | tf_op jit(solution)/shard_map/ppermute | solution.py:564
  51.2 1.5 %collective-permute-done.14.b2 = bf16[128,768]{1,0:T(8,128)(2,1)S(1)} collective-permute-done((bf16[128,768]{1,0:T(8,128)(2,1)S(1)}, bf16[128,768]{1,0:T(8,128)(2,1)S(1)}, u32[]{:S(2)}, u32[]{:S(2)}) %collective-permute-start.14) | collective-permute-done | bytes 196640 | tf_op jit(solution)/shard_map/ppermute | solution.py:564
  52.8 2.1 %collective-permute-done.13.b1 = bf16[128,768]{1,0:T(8,128)(2,1)S(1)} collective-permute-done((bf16[128,768]{1,0:T(8,128)(2,1)S(1)}, bf16[128,768]{1,0:T(8,128)(2,1)S(1)}, u32[]{:S(2)}, u32[]{:S(2)}) %collective-permute-start.13) | collective-permute-done | bytes 196640 | tf_op jit(solution)/shard_map/ppermute | solution.py:564
  54.9 9.0 %expert_rows.1 = (f32[128,1280]{1,0:T(8,128)S(1)}, bf16[128,1280]{1,0:T(8,128)(2,1)S(1)}, bf16[128,1280]{1,0:T(8,128)(2,1)S(1)}, bf16[128,1280]{1,0:T(8,128)(2,1...) custom-call(s32[3]{0:T(128)S(1)} %pad_add_fusion.group_ref, ...), custom_call_target="tpu_custom_call" | custom-call | flops 4831838208 | bytes 16777216 | tf_op jit(solution)/shard_map/expert_rows/pallas_call | solution.py:483
  63.9 2.0 %collective-permute-start.19 = (bf16[128,768]{1,0:T(8,128)(2,1)S(1)}, bf16[128,768]{1,0:T(8,128)(2,1)S(1)}, u32[]{:S(2)}, u32[]{:S(2)}) collective-permute-start(bf16[128,768]{1,0:T(8,128)(2,1)S(1)} %get-tuple-element.91), channel_id=1, source_target_pairs={{0,8},{1,9},{2,10},{3,11},{4,12},{5,13},{6,14},{7,15},{8,0},{9,1},... | collective-permute-start | bytes 589832 | tf_op jit(solution)/shard_map/ppermute | solution.py:564
  65.9 1.1 %collective-permute-start.16 = (bf16[128,1280]{1,0:T(8,128)(2,1)S(1)}, bf16[128,1280]{1,0:T(8,128)(2,1)S(1)}, u32[]{:S(2)}, u32[]{:S(2)}) collective-permute-start(bf16[128,1280]{1,0:T(8,128)(2,1)S(1)} %get-tuple-element.88), channel_id=1, source_target_pairs={{0,1},{1,0},{2,3},{3,2},{4,5},{5,4},{6,7},{7,6},{8,9},{9,8},{10,11... | collective-permute-start | bytes 983048 | tf_op jit(solution)/shard_map/ppermute | solution.py:564
  67.0 1.6 %collective-permute-start.17 = (bf16[128,1280]{1,0:T(8,128)(2,1)S(1)}, bf16[128,1280]{1,0:T(8,128)(2,1)S(1)}, u32[]{:S(2)}, u32[]{:S(2)}) collective-permute-start(bf16[128,1280]{1,0:T(8,128)(2,1)S(1)} %get-tuple-element.89), channel_id=1, source_target_pairs={{0,4},{1,5},{2,6},{3,7},{4,0},{5,1},{6,2},{7,3},{8,12},{9,13},{10,... | collective-permute-start | bytes 983048 | tf_op jit(solution)/shard_map/ppermute | solution.py:564
  70.1 1.6 %collective-permute-done.19.g1 = bf16[128,768]{1,0:T(8,128)(2,1)S(1)} collective-permute-done((bf16[128,768]{1,0:T(8,128)(2,1)S(1)}, bf16[128,768]{1,0:T(8,128)(2,1)S(1)}, u32[]{:S(2)}, u32[]{:S(2)}) %collective-permute-start.19) | collective-permute-done | bytes 196640 | tf_op jit(solution)/shard_map/ppermute | solution.py:564
  71.7 1.6 %collective-permute-start.21 = (bf16[128,768]{1,0:T(8,128)(2,1)S(1)}, bf16[128,768]{1,0:T(8,128)(2,1)S(1)}, u32[]{:S(2)}, u32[]{:S(2)}) collective-permute-start(bf16[128,768]{1,0:T(8,128)(2,1)S(1)} %get-tuple-element.93), channel_id=1, source_target_pairs={{0,24},{1,25},{2,26},{3,27},{4,28},{5,29},{6,30},{7,31},{8,16},{9,... | collective-permute-start | bytes 589832 | tf_op jit(solution)/shard_map/ppermute | solution.py:564
  73.3 9.0 %collective-permute-done.20.g2 = bf16[128,768]{1,0:T(8,128)(2,1)S(1)} collective-permute-done((bf16[128,768]{1,0:T(8,128)(2,1)S(1)}, bf16[128,768]{1,0:T(8,128)(2,1)S(1)}, u32[]{:S(2)}, u32[]{:S(2)}) %collective-permute-start.20) | collective-permute-done | bytes 196640 | tf_op jit(solution)/shard_map/ppermute | solution.py:564
  82.6 1.7 %collective-permute-start.25 = (bf16[32,768]{1,0:T(8,128)(2,1)S(1)}, bf16[32,768]{1,0:T(8,128)(2,1)S(1)}, u32[]{:S(2)}, u32[]{:S(2)}) collective-permute-start(bf16[32,768]{1,0:T(8,128)(2,1)S(1)} %get-tuple-element.113), channel_id=1, source_target_pairs={{0,1},{1,0},{2,3},{3,2},{4,5},{5,4},{6,7},{7,6},{8,9},{9,8},{10,11... | collective-permute-start | bytes 147464 | tf_op jit(solution)/shard_map/ppermute | solution.py:564
  84.3 2.7 %collective-permute-start.22 = (bf16[32,1280]{1,0:T(8,128)(2,1)S(1)}, bf16[32,1280]{1,0:T(8,128)(2,1)S(1)}, u32[]{:S(2)}, u32[]{:S(2)}) collective-permute-start(bf16[32,1280]{1,0:T(8,128)(2,1)S(1)} %get-tuple-element.110), channel_id=1, source_target_pairs={{0,8},{1,9},{2,10},{3,11},{4,12},{5,13},{6,14},{7,15},{8,0},{9,1},... | collective-permute-start | bytes 245768 | tf_op jit(solution)/shard_map/ppermute | solution.py:564
  87.0 2.4 %collective-permute-start.24 = (bf16[32,1280]{1,0:T(8,128)(2,1)S(1)}, bf16[32,1280]{1,0:T(8,128)(2,1)S(1)}, u32[]{:S(2)}, u32[]{:S(2)}) collective-permute-start(bf16[32,1280]{1,0:T(8,128)(2,1)S(1)} %get-tuple-element.112), channel_id=1, source_target_pairs={{0,24},{1,25},{2,26},{3,27},{4,28},{5,29},{6,30},{7,31},{8,16},{9,... | collective-permute-start | bytes 245768 | tf_op jit(solution)/shard_map/ppermute | solution.py:564
  91.2 2.3 %collective-permute-done.26.b2 = bf16[32,768]{1,0:T(8,128)(2,1)S(1)} collective-permute-done((bf16[32,768]{1,0:T(8,128)(2,1)S(1)}, bf16[32,768]{1,0:T(8,128)(2,1)S(1)}, u32[]{:S(2)}, u32[]{:S(2)}) %collective-permute-start.26) | collective-permute-done | bytes 49184 | tf_op jit(solution)/shard_map/ppermute | solution.py:564
  93.4 1.9 %collective-permute-done.27.b3 = bf16[32,768]{1,0:T(8,128)(2,1)S(1)} collective-permute-done((bf16[32,768]{1,0:T(8,128)(2,1)S(1)}, bf16[32,768]{1,0:T(8,128)(2,1)S(1)}, u32[]{:S(2)}, u32[]{:S(2)}) %collective-permute-start.27) | collective-permute-done | bytes 49184 | tf_op jit(solution)/shard_map/ppermute | solution.py:564
  (42 shorter events, 8.7 us)
Async XLA Ops:
  0.0 35.6 %collective-permute-start.7 = (bf16[2048,384]{1,0:T(8,128)(2,1)}, bf16[2048,384]{1,0:T(8,128)(2,1)S(1)}, u32[]{:S(2)}, u32[]{:S(2)}) collective-permute-start(bf16[2048,384]{1,0:T(8,128)(2,1)} %bitcast.10), channel_id=1, source_target_pairs={{0,2},{1,3},{2,0},{3,1},{4,6},{5,7},{6,4},{7,5},{8,10},{9,11},{10,... | collective-permute-start | bytes 4718600 | tf_op jit(solution)/shard_map/ppermute | solution.py:564
  0.5 35.1 %collective-permute-start.8 = (bf16[2048,384]{1,0:T(8,128)(2,1)}, bf16[2048,384]{1,0:T(8,128)(2,1)}, u32[]{:S(2)}, u32[]{:S(2)}) collective-permute-start(bf16[2048,384]{1,0:T(8,128)(2,1)} %bitcast.12), channel_id=1, source_target_pairs={{0,2},{1,3},{2,0},{3,1},{4,6},{5,7},{6,4},{7,5},{8,10},{9,11},{10,... | collective-permute-start | bytes 4718600 | tf_op jit(solution)/shard_map/ppermute | solution.py:564
  0.5 35.1 %collective-permute-start.9 = (bf16[384,2048]{1,0:T(8,128)(2,1)}, bf16[384,2048]{1,0:T(8,128)(2,1)}, u32[]{:S(2)}, u32[]{:S(2)}) collective-permute-start(bf16[384,2048]{1,0:T(8,128)(2,1)} %bitcast.14), channel_id=1, source_target_pairs={{0,2},{1,3},{2,0},{3,1},{4,6},{5,7},{6,4},{7,5},{8,10},{9,11},{10,... | collective-permute-start | bytes 4718600 | tf_op jit(solution)/shard_map/ppermute | solution.py:564
  5.1 11.3 %copy-start.1 = (f32[2048]{0:T(1024)S(1)}, f32[2048]{0:T(1024)}, u32[]{:S(2)}) copy-start(f32[2048]{0:T(1024)} %param.22) | copy-start | bytes 24580
  9.7 6.7 %collective-permute-start = (bf16[32,2048]{1,0:T(8,128)(2,1)S(1)}, bf16[32,2048]{1,0:T(8,128)(2,1)S(1)}, u32[]{:S(2)}, u32[]{:S(2)}) collective-permute-start(bf16[32,2048]{1,0:T(8,128)(2,1)S(1)} %get-tuple-element.65), channel_id=1, source_target_pairs={{0,1},{1,0},{2,3},{3,2},{4,5},{5,4},{6,7},{7,6},{8,9},{9,8},{10,11... | collective-permute-start | bytes 393224 | tf_op jit(solution)/shard_map/ppermute | solution.py:564
  16.5 5.1 %collective-permute-start.6 = (bf16[32,768]{1,0:T(8,128)(2,1)S(1)}, bf16[32,768]{1,0:T(8,128)(2,1)S(1)}, u32[]{:S(2)}, u32[]{:S(2)}) collective-permute-start(bf16[32,768]{1,0:T(8,128)(2,1)S(1)} %get-tuple-element.69), channel_id=1, source_target_pairs={{0,5},{1,4},{2,7},{3,6},{4,1},{5,0},{6,3},{7,2},{8,13},{9,12},{10,... | collective-permute-start | bytes 147464 | tf_op jit(solution)/shard_map/ppermute | solution.py:564
  19.3 6.2 %collective-permute-start.5 = (bf16[32,768]{1,0:T(8,128)(2,1)S(1)}, bf16[32,768]{1,0:T(8,128)(2,1)S(1)}, u32[]{:S(2)}, u32[]{:S(2)}) collective-permute-start(bf16[32,768]{1,0:T(8,128)(2,1)S(1)} %get-tuple-element.69), channel_id=1, source_target_pairs={{0,4},{1,5},{2,6},{3,7},{4,0},{5,1},{6,2},{7,3},{8,12},{9,13},{10,... | collective-permute-start | bytes 147464 | tf_op jit(solution)/shard_map/ppermute | solution.py:564
  21.6 8.5 %collective-permute-start.3 = (bf16[32,1408]{1,0:T(8,128)(2,1)S(1)}, bf16[32,1408]{1,0:T(8,128)(2,1)S(1)}, u32[]{:S(2)}, u32[]{:S(2)}) collective-permute-start(bf16[32,1408]{1,0:T(8,128)(2,1)S(1)} %get-tuple-element.68), channel_id=1, source_target_pairs={{0,24},{1,25},{2,26},{3,27},{4,28},{5,29},{6,30},{7,31},{8,16},{9,... | collective-permute-start | bytes 270344 | tf_op jit(solution)/shard_map/ppermute | solution.py:564
  25.5 4.1 %collective-permute-start.4 = (bf16[32,768]{1,0:T(8,128)(2,1)S(1)}, bf16[32,768]{1,0:T(8,128)(2,1)S(1)}, u32[]{:S(2)}, u32[]{:S(2)}) collective-permute-start(bf16[32,768]{1,0:T(8,128)(2,1)S(1)} %get-tuple-element.69), channel_id=1, source_target_pairs={{0,1},{1,0},{2,3},{3,2},{4,5},{5,4},{6,7},{7,6},{8,9},{9,8},{10,11... | collective-permute-start | bytes 147464 | tf_op jit(solution)/shard_map/ppermute | solution.py:564
  29.6 5.5 %collective-permute-start.2 = (bf16[32,1408]{1,0:T(8,128)(2,1)S(1)}, bf16[32,1408]{1,0:T(8,128)(2,1)S(1)}, u32[]{:S(2)}, u32[]{:S(2)}) collective-permute-start(bf16[32,1408]{1,0:T(8,128)(2,1)S(1)} %get-tuple-element.68), channel_id=1, source_target_pairs={{0,16},{1,17},{2,18},{3,19},{4,20},{5,21},{6,22},{7,23},{8,24},{9,... | collective-permute-start | bytes 270344 | tf_op jit(solution)/shard_map/ppermute | solution.py:564
  30.1 5.5 %collective-permute-start.1 = (bf16[32,1408]{1,0:T(8,128)(2,1)S(1)}, bf16[32,1408]{1,0:T(8,128)(2,1)S(1)}, u32[]{:S(2)}, u32[]{:S(2)}) collective-permute-start(bf16[32,1408]{1,0:T(8,128)(2,1)S(1)} %get-tuple-element.68), channel_id=1, source_target_pairs={{0,8},{1,9},{2,10},{3,11},{4,12},{5,13},{6,14},{7,15},{8,0},{9,1},... | collective-permute-start | bytes 270344 | tf_op jit(solution)/shard_map/ppermute | solution.py:564
  35.6 1.2 %copy-start.2 = (bf16[2048,384]{1,0:T(8,128)(2,1)}, bf16[2048,384]{1,0:T(8,128)(2,1)S(1)}, u32[]{:S(2)}) copy-start(bf16[2048,384]{1,0:T(8,128)(2,1)S(1)} %collective-permute-done.7.wg1) | copy-start | bytes 4718596
  36.8 9.5 %collective-permute-start.15 = (bf16[128,768]{1,0:T(8,128)(2,1)S(1)}, bf16[128,768]{1,0:T(8,128)(2,1)S(1)}, u32[]{:S(2)}, u32[]{:S(2)}) collective-permute-start(bf16[128,768]{1,0:T(8,128)(2,1)S(1)} %pad_maximum_fusion.1.b0), channel_id=1, source_target_pairs={{0,24},{1,25},{2,26},{3,27},{4,28},{5,29},{6,30},{7,31},{8,16},{9,... | collective-permute-start | bytes 589832 | tf_op jit(solution)/shard_map/ppermute | solution.py:564
  38.7 16.1 %collective-permute-start.12 = (bf16[128,1408]{1,0:T(8,128)(2,1)S(1)}, bf16[128,1408]{1,0:T(8,128)(2,1)S(1)}, u32[]{:S(2)}, u32[]{:S(2)}) collective-permute-start(bf16[128,1408]{1,0:T(8,128)(2,1)S(1)} %pad_maximum_fusion.a0), channel_id=1, source_target_pairs={{0,5},{1,4},{2,7},{3,6},{4,1},{5,0},{6,3},{7,2},{8,13},{9,12},{10,... | collective-permute-start | bytes 1081352 | tf_op jit(solution)/shard_map/ppermute | solution.py:564
  40.9 14.0 %collective-permute-start.11 = (bf16[128,1408]{1,0:T(8,128)(2,1)S(1)}, bf16[128,1408]{1,0:T(8,128)(2,1)S(1)}, u32[]{:S(2)}, u32[]{:S(2)}) collective-permute-start(bf16[128,1408]{1,0:T(8,128)(2,1)S(1)} %pad_maximum_fusion.a0), channel_id=1, source_target_pairs={{0,4},{1,5},{2,6},{3,7},{4,0},{5,1},{6,2},{7,3},{8,12},{9,13},{10,... | collective-permute-start | bytes 1081352 | tf_op jit(solution)/shard_map/ppermute | solution.py:564
  41.6 13.2 %collective-permute-start.10 = (bf16[128,1408]{1,0:T(8,128)(2,1)S(1)}, bf16[128,1408]{1,0:T(8,128)(2,1)S(1)}, u32[]{:S(2)}, u32[]{:S(2)}) collective-permute-start(bf16[128,1408]{1,0:T(8,128)(2,1)S(1)} %pad_maximum_fusion.a0), channel_id=1, source_target_pairs={{0,1},{1,0},{2,3},{3,2},{4,5},{5,4},{6,7},{7,6},{8,9},{9,8},{10,11... | collective-permute-start | bytes 1081352 | tf_op jit(solution)/shard_map/ppermute | solution.py:564
  42.2 10.5 %collective-permute-start.14 = (bf16[128,768]{1,0:T(8,128)(2,1)S(1)}, bf16[128,768]{1,0:T(8,128)(2,1)S(1)}, u32[]{:S(2)}, u32[]{:S(2)}) collective-permute-start(bf16[128,768]{1,0:T(8,128)(2,1)S(1)} %pad_maximum_fusion.1.b0), channel_id=1, source_target_pairs={{0,16},{1,17},{2,18},{3,19},{4,20},{5,21},{6,22},{7,23},{8,24},{9,... | collective-permute-start | bytes 589832 | tf_op jit(solution)/shard_map/ppermute | solution.py:564
  46.3 8.6 %collective-permute-start.13 = (bf16[128,768]{1,0:T(8,128)(2,1)S(1)}, bf16[128,768]{1,0:T(8,128)(2,1)S(1)}, u32[]{:S(2)}, u32[]{:S(2)}) collective-permute-start(bf16[128,768]{1,0:T(8,128)(2,1)S(1)} %pad_maximum_fusion.1.b0), channel_id=1, source_target_pairs={{0,8},{1,9},{2,10},{3,11},{4,12},{5,13},{6,14},{7,15},{8,0},{9,1},... | collective-permute-start | bytes 589832 | tf_op jit(solution)/shard_map/ppermute | solution.py:564
  63.9 31.4 %copy-start = (f32[2048]{0:T(1024)S(1)}, f32[2048]{0:T(1024)}, u32[]{:S(2)}) copy-start(f32[2048]{0:T(1024)} %param.29) | copy-start | bytes 24580
  63.9 7.8 %collective-permute-start.19 = (bf16[128,768]{1,0:T(8,128)(2,1)S(1)}, bf16[128,768]{1,0:T(8,128)(2,1)S(1)}, u32[]{:S(2)}, u32[]{:S(2)}) collective-permute-start(bf16[128,768]{1,0:T(8,128)(2,1)S(1)} %get-tuple-element.91), channel_id=1, source_target_pairs={{0,8},{1,9},{2,10},{3,11},{4,12},{5,13},{6,14},{7,15},{8,0},{9,1},... | collective-permute-start | bytes 589832 | tf_op jit(solution)/shard_map/ppermute | solution.py:564
  65.9 16.4 %collective-permute-start.16 = (bf16[128,1280]{1,0:T(8,128)(2,1)S(1)}, bf16[128,1280]{1,0:T(8,128)(2,1)S(1)}, u32[]{:S(2)}, u32[]{:S(2)}) collective-permute-start(bf16[128,1280]{1,0:T(8,128)(2,1)S(1)} %get-tuple-element.88), channel_id=1, source_target_pairs={{0,1},{1,0},{2,3},{3,2},{4,5},{5,4},{6,7},{7,6},{8,9},{9,8},{10,11... | collective-permute-start | bytes 983048 | tf_op jit(solution)/shard_map/ppermute | solution.py:564
  67.0 15.3 %collective-permute-start.17 = (bf16[128,1280]{1,0:T(8,128)(2,1)S(1)}, bf16[128,1280]{1,0:T(8,128)(2,1)S(1)}, u32[]{:S(2)}, u32[]{:S(2)}) collective-permute-start(bf16[128,1280]{1,0:T(8,128)(2,1)S(1)} %get-tuple-element.89), channel_id=1, source_target_pairs={{0,4},{1,5},{2,6},{3,7},{4,0},{5,1},{6,2},{7,3},{8,12},{9,13},{10,... | collective-permute-start | bytes 983048 | tf_op jit(solution)/shard_map/ppermute | solution.py:564
  68.6 13.7 %collective-permute-start.18 = (bf16[128,1280]{1,0:T(8,128)(2,1)S(1)}, bf16[128,1280]{1,0:T(8,128)(2,1)S(1)}, u32[]{:S(2)}, u32[]{:S(2)}) collective-permute-start(bf16[128,1280]{1,0:T(8,128)(2,1)S(1)} %get-tuple-element.90), channel_id=1, source_target_pairs={{0,5},{1,4},{2,7},{3,6},{4,1},{5,0},{6,3},{7,2},{8,13},{9,12},{10,... | collective-permute-start | bytes 983048 | tf_op jit(solution)/shard_map/ppermute | solution.py:564
  69.4 12.9 %collective-permute-start.20 = (bf16[128,768]{1,0:T(8,128)(2,1)S(1)}, bf16[128,768]{1,0:T(8,128)(2,1)S(1)}, u32[]{:S(2)}, u32[]{:S(2)}) collective-permute-start(bf16[128,768]{1,0:T(8,128)(2,1)S(1)} %get-tuple-element.92), channel_id=1, source_target_pairs={{0,16},{1,17},{2,18},{3,19},{4,20},{5,21},{6,22},{7,23},{8,24},{9,... | collective-permute-start | bytes 589832 | tf_op jit(solution)/shard_map/ppermute | solution.py:564
  71.7 10.6 %collective-permute-start.21 = (bf16[128,768]{1,0:T(8,128)(2,1)S(1)}, bf16[128,768]{1,0:T(8,128)(2,1)S(1)}, u32[]{:S(2)}, u32[]{:S(2)}) collective-permute-start(bf16[128,768]{1,0:T(8,128)(2,1)S(1)} %get-tuple-element.93), channel_id=1, source_target_pairs={{0,24},{1,25},{2,26},{3,27},{4,28},{5,29},{6,30},{7,31},{8,16},{9,... | collective-permute-start | bytes 589832 | tf_op jit(solution)/shard_map/ppermute | solution.py:564
  82.6 7.7 %collective-permute-start.25 = (bf16[32,768]{1,0:T(8,128)(2,1)S(1)}, bf16[32,768]{1,0:T(8,128)(2,1)S(1)}, u32[]{:S(2)}, u32[]{:S(2)}) collective-permute-start(bf16[32,768]{1,0:T(8,128)(2,1)S(1)} %get-tuple-element.113), channel_id=1, source_target_pairs={{0,1},{1,0},{2,3},{3,2},{4,5},{5,4},{6,7},{7,6},{8,9},{9,8},{10,11... | collective-permute-start | bytes 147464 | tf_op jit(solution)/shard_map/ppermute | solution.py:564
  84.3 11.0 %collective-permute-start.22 = (bf16[32,1280]{1,0:T(8,128)(2,1)S(1)}, bf16[32,1280]{1,0:T(8,128)(2,1)S(1)}, u32[]{:S(2)}, u32[]{:S(2)}) collective-permute-start(bf16[32,1280]{1,0:T(8,128)(2,1)S(1)} %get-tuple-element.110), channel_id=1, source_target_pairs={{0,8},{1,9},{2,10},{3,11},{4,12},{5,13},{6,14},{7,15},{8,0},{9,1},... | collective-permute-start | bytes 245768 | tf_op jit(solution)/shard_map/ppermute | solution.py:564
  87.0 8.3 %collective-permute-start.23 = (bf16[32,1280]{1,0:T(8,128)(2,1)S(1)}, bf16[32,1280]{1,0:T(8,128)(2,1)S(1)}, u32[]{:S(2)}, u32[]{:S(2)}) collective-permute-start(bf16[32,1280]{1,0:T(8,128)(2,1)S(1)} %get-tuple-element.111), channel_id=1, source_target_pairs={{0,16},{1,17},{2,18},{3,19},{4,20},{5,21},{6,22},{7,23},{8,24},{9,... | collective-permute-start | bytes 245768 | tf_op jit(solution)/shard_map/ppermute | solution.py:564
  87.0 8.3 %collective-permute-start.24 = (bf16[32,1280]{1,0:T(8,128)(2,1)S(1)}, bf16[32,1280]{1,0:T(8,128)(2,1)S(1)}, u32[]{:S(2)}, u32[]{:S(2)}) collective-permute-start(bf16[32,1280]{1,0:T(8,128)(2,1)S(1)} %get-tuple-element.112), channel_id=1, source_target_pairs={{0,24},{1,25},{2,26},{3,27},{4,28},{5,29},{6,30},{7,31},{8,16},{9,... | collective-permute-start | bytes 245768 | tf_op jit(solution)/shard_map/ppermute | solution.py:564
  89.3 4.1 %collective-permute-start.26 = (bf16[32,768]{1,0:T(8,128)(2,1)S(1)}, bf16[32,768]{1,0:T(8,128)(2,1)S(1)}, u32[]{:S(2)}, u32[]{:S(2)}) collective-permute-start(bf16[32,768]{1,0:T(8,128)(2,1)S(1)} %get-tuple-element.114), channel_id=1, source_target_pairs={{0,4},{1,5},{2,6},{3,7},{4,0},{5,1},{6,2},{7,3},{8,12},{9,13},{10,... | collective-permute-start | bytes 147464 | tf_op jit(solution)/shard_map/ppermute | solution.py:564
  90.3 5.0 %collective-permute-start.27 = (bf16[32,768]{1,0:T(8,128)(2,1)S(1)}, bf16[32,768]{1,0:T(8,128)(2,1)S(1)}, u32[]{:S(2)}, u32[]{:S(2)}) collective-permute-start(bf16[32,768]{1,0:T(8,128)(2,1)S(1)} %get-tuple-element.115), channel_id=1, source_target_pairs={{0,5},{1,4},{2,7},{3,6},{4,1},{5,0},{6,3},{7,2},{8,13},{9,12},{10,... | collective-permute-start | bytes 147464 | tf_op jit(solution)/shard_map/ppermute | solution.py:564

commit v3 on v2

--- a/solution.py
+++ b/solution.py
@@ -219,25 +219,28 @@
 
 def pack_shares(ids, routed, home_ref):
     groups = home_ref.shape[0]
-    rows = ids.shape[0]
-    lane = lax.broadcasted_iota(jnp.int32, (rows, LANES), 1)
-    shares = routed / jnp.sum(routed, axis=1, keepdims=True)
-    by_expert = jnp.zeros((rows, LANES), jnp.float32)
-    for k in range(ids.shape[1]):
-        by_expert = by_expert + jnp.where(lane == ids[:, k : k + 1], shares[:, k : k + 1], 0.0)
-    by_home = jnp.zeros((rows, LANES), jnp.float32)
+    choices, tokens = ids.shape
+    spot = lax.broadcasted_iota(jnp.int32, (groups, tokens), 0)
+    shares = routed / jnp.sum(routed, axis=0, keepdims=True)
+    by_expert = jnp.zeros((groups, tokens), jnp.float32)
+    for k in range(choices):
+        by_expert = by_expert + jnp.where(spot == ids[k : k + 1, :], shares[k : k + 1, :], 0.0)
+    by_home = jnp.zeros((groups, tokens), jnp.float32)
     for e in range(groups):
-        mine = (lane == home_ref[e]) | (lane == home_ref[e] + groups)
-        by_home = by_home + jnp.where(mine, by_expert[:, e : e + 1], 0.0)
+        by_home = by_home + jnp.where(spot == home_ref[e], by_expert[e : e + 1, :], 0.0)
     rounded = by_home.astype(jnp.bfloat16).astype(jnp.float32)
-    return jnp.where(lane < groups, rounded, by_home - rounded).astype(jnp.bfloat16)
+    tall = jnp.concatenate(
+        [rounded, by_home - rounded, jnp.zeros((LANES - 2 * groups, tokens), jnp.float32)], axis=0
+    )
+    square = jnp.concatenate([tall, jnp.zeros((LANES, LANES - tokens), jnp.float32)], axis=1)
+    return jnp.transpose(square)
 
 
 def attention_kernel(
     pages_ref, lengths_ref, tp_ref, home_ref, q_hbm, fresh_hbm, cache_hbm, residual_hbm, ids_hbm,
     routed_hbm, w_hbm, own_ref, send_ref, pack_ref,
     q_ref, fresh_ref, cache_ref, residual_ref, ids_ref, routed_ref, w_ref, context_ref, terms_ref,
-    sems,
+    every_ref, sems,
 ):
     fetches = [
         pltpu.make_async_copy(source, target, sems.at[i])
@@ -257,7 +260,7 @@
         fetch.start()
     tokens = q_ref.shape[0]
     pool_pages, page_tokens, _ = cache_ref.shape
-    requests, slots = pages_ref.shape
+    slots, requests = pages_ref.shape
     kv_heads = fresh_ref.shape[1] // (2 * HEAD_WIDTH)
     group = q_ref.shape[1] // (HEAD_WIDTH * kv_heads)
     decodes = requests - 1
@@ -271,10 +274,10 @@
 
     full = lambda scalar: jnp.full((decodes, page_tokens), scalar, jnp.int32)
     first = multiplicity(
-        [full(pages_ref[0, s]) for s in range(slots)], full(lengths_ref[0]), pool_pages, page_tokens
+        [full(pages_ref[s, 0]) for s in range(slots)], full(lengths_ref[0]), pool_pages, page_tokens
     )
     later = multiplicity(
-        [by_row(lambda j, s=s: pages_ref[j, s]) for s in range(slots)],
+        [by_row(lambda j, s=s: pages_ref[s, j]) for s in range(slots)],
         by_row(lambda j: lengths_ref[j]),
         pool_pages,
         page_tokens,
@@ -337,9 +340,8 @@
     other_at = pl.multiple_of((1 - tp_ref[0]) * half, half)
     for fetch in fetches[3:5]:
         fetch.wait()
-    pack_ref[...] = pack_shares(
-        ids_ref[pl.ds(own_at, half), :], routed_ref[pl.ds(own_at, half), :], home_ref
-    )
+    every_ref[...] = pack_shares(ids_ref[...], routed_ref[...], home_ref)
+    pack_ref[...] = every_ref[pl.ds(own_at, half), :].astype(jnp.bfloat16)
     for fetch in fetches[5:]:
         fetch.wait()
     for at in range(0, width, block):
@@ -358,7 +360,7 @@
 ):
     tokens, width = residual.shape
     half = tokens // 2
-    moved = (queries, fresh, cache, residual, ids, routed, w_out)
+    moved = (queries, fresh, cache, residual, ids.T, routed.T, w_out)
     return pl.pallas_call(
         attention_kernel,
         out_shape=(
@@ -372,31 +374,34 @@
         + [
             pltpu.VMEM(queries.shape, jnp.bfloat16),
             pltpu.VMEM((tokens, width), jnp.float32),
+            pltpu.VMEM((LANES, LANES), jnp.float32),
             pltpu.SemaphoreType.DMA((7,)),
         ],
         compiler_params=pltpu.CompilerParams(vmem_limit_bytes=40 * MIB),
         name="attention_terms",
-    )(stay(pages), stay(lengths), tp_index, stay(home), *[stay(v) for v in moved])
-
-
-def norm_kernel(own_ref, got_ref, pack_ref, gain_ref, state_ref, a_ref, b_ref):
+    )(stay(pages.T), stay(lengths), tp_index, stay(home), *[stay(v) for v in moved])
+
+
+def norm_kernel(own_ref, got_ref, pack_ref, gain_ref, state_ref, rows_ref, far_ref):
     state = own_ref[...] + got_ref[...].astype(jnp.float32)
     state_ref[...] = state
     normed = rms_scale(state, gain_ref[...]).astype(jnp.bfloat16)
-    wide = a_ref.shape[1] - LANES
-    a_ref[:, :wide] = normed[:, :wide]
-    a_ref[:, wide:] = pack_ref[...]
-    b_ref[...] = normed[:, wide:]
-
-
-def norm_rows(own, got, pack, gain, wide):
+    width = state.shape[1]
+    far = far_ref.shape[0]
+    rows_ref[:, :width] = normed
+    rows_ref[:, width:] = pack_ref[...]
+    far_ref[:, :width] = normed[:far]
+    far_ref[:, width:] = pack_ref[:far, :]
+
+
+def norm_rows(own, got, pack, gain, far):
     rows, width = own.shape
     return pl.pallas_call(
         norm_kernel,
         out_shape=(
             jax.ShapeDtypeStruct((rows, width), jnp.float32),
-            jax.ShapeDtypeStruct((rows, wide + LANES), jnp.bfloat16),
-            jax.ShapeDtypeStruct((rows, width - wide), jnp.bfloat16),
+            jax.ShapeDtypeStruct((rows, width + LANES), jnp.bfloat16),
+            jax.ShapeDtypeStruct((far, width + LANES), jnp.bfloat16),
         ),
         in_specs=[vmem()] * 4,
         out_specs=(vmem(),) * 3,
@@ -405,18 +410,61 @@
     )(own, got, pack, gain)
 
 
-def expert_kernel(
-    group_ref, a0, a1, a2, a3, b0, b1, b2, b3, wg0, wu0, wd0, wg1, wu1, wd1,
-    oa0, oa1, oa2, oa3, ob0, ob1, ob2, ob3,
-    x_ref, w0_ref, w1_ref, down_ref, h_ref, sems,
+def relay_kernel(r0, r1, r2, r3, z1, z2, z3, plane_ref, column_ref):
+    far = z1.shape[0]
+    near = r0.shape[0] - far
+    for j, piece in enumerate((z1, z2, z3)):
+        plane_ref[j * far : (j + 1) * far, :] = piece[...]
+    for i, piece in enumerate((r0, r1, r2, r3)):
+        column_ref[i * near : (i + 1) * near, :] = piece[far:, :]
+
+
+def relay_rows(rows, far):
+    height, width = far[0].shape
+    near = rows[0].shape[0] - height
+    return pl.pallas_call(
+        relay_kernel,
+        out_shape=(
+            jax.ShapeDtypeStruct((3 * height, width), jnp.bfloat16),
+            jax.ShapeDtypeStruct((4 * near, width), jnp.bfloat16),
+        ),
+        in_specs=[vmem()] * 7,
+        out_specs=(vmem(),) * 2,
+        compiler_params=SMALL,
+        name="relay_rows",
+    )(*rows, *far)
+
+
+def hidden_units(group_ref, x_ref, w_refs, h_ref, ready):
+    rows = x_ref.shape[0]
+    width = w_refs[0].shape[0]
+    hidden = h_ref.shape[1] // 2
+    groups = group_ref[2]
+    lane = lax.broadcasted_iota(jnp.int32, (rows, LANES), 1)
+    packed = x_ref[:, width:].astype(jnp.float32)
+    for e, w_ref in enumerate(w_refs):
+        group = group_ref[e]
+        share = jnp.sum(
+            jnp.where((lane == group) | (lane == group + groups), packed, 0.0),
+            axis=1,
+            keepdims=True,
+        )
+        ready(e)
+        both = jnp.dot(x_ref[:, :width], w_ref[...], preferred_element_type=jnp.float32)
+        gate, up = both[:, :hidden], both[:, hidden:]
+        h_ref[:, e * hidden : (e + 1) * hidden] = (
+            share * up * (gate / (1.0 + jnp.exp(-gate)))
+        ).astype(jnp.bfloat16)
+
+
+DOWN_BLOCK = 512
+
+
+def near_kernel(
+    group_ref, r0, r1, r2, r3, z1, z2, z3, wg0, wu0, wd0, wg1, wu1, wd1,
+    out_ref, w0_ref, w1_ref, down_ref, x_ref, h_ref, sems,
 ):
-    a_in, b_in = (a0, a1, a2, a3), (b0, b1, b2, b3)
-    a_out, b_out = (oa0, oa1, oa2, oa3), (ob0, ob1, ob2, ob3)
-    rows, width = x_ref.shape
     hidden = wg0.shape[1]
-    wide = oa0.shape[1]
-    quad = rows // 4
-    unit = quad // 4
     fetches = [
         pltpu.make_async_copy(source, target, sems.at[i])
         for i, (source, target) in enumerate(
@@ -432,121 +480,169 @@
     ]
     for fetch in fetches:
         fetch.start()
-    lane = lax.broadcasted_iota(jnp.int32, (rows, LANES), 1)
-    packed = jnp.concatenate([a[:, wide:] for a in a_in], axis=0).astype(jnp.float32)
-    groups = group_ref[2]
-    for i in range(4):
-        x_ref[i * quad : (i + 1) * quad, :wide] = a_in[i][:, :wide]
-        for j in range(4):
-            at = i * quad + j * unit
-            x_ref[at : at + unit, wide:] = b_in[j][i * unit : (i + 1) * unit, :]
-    for e, w_ref in enumerate((w0_ref, w1_ref)):
-        group = group_ref[e]
-        share = jnp.sum(
-            jnp.where((lane == group) | (lane == group + groups), packed, 0.0),
-            axis=1,
-            keepdims=True,
-        )
+    at = 0
+    for piece in (r0, r1, r2, r3, z1, z2, z3):
+        x_ref[at : at + piece.shape[0], :] = piece[...]
+        at += piece.shape[0]
+    if at < x_ref.shape[0]:
+        x_ref[at:, :] = jnp.zeros((x_ref.shape[0] - at, x_ref.shape[1]), jnp.bfloat16)
+
+    def ready(e):
         fetches[2 * e].wait()
         fetches[2 * e + 1].wait()
-        both = jnp.dot(x_ref[...], w_ref[...], preferred_element_type=jnp.float32)
-        gate, up = both[:, :hidden], both[:, hidden:]
-        h_ref[:, e * hidden : (e + 1) * hidden] = (
-            share * up * (gate / (1.0 + jnp.exp(-gate)))
-        ).astype(jnp.bfloat16)
+
+    hidden_units(group_ref, x_ref, (w0_ref, w1_ref), h_ref, ready)
     fetches[4].wait()
     fetches[5].wait()
-    block = 256
-    for at in range(0, width, block):
-        cols = slice(at, at + block)
+    for col in range(0, down_ref.shape[1], DOWN_BLOCK):
+        cols = slice(col, col + DOWN_BLOCK)
         down = jnp.dot(h_ref[...], down_ref[:, cols], preferred_element_type=jnp.float32)
-        if at < wide:
-            for i in range(4):
-                a_out[i][:, cols] = down[i * quad : (i + 1) * quad].astype(a_out[i].dtype)
-        else:
-            there = slice(at - wide, at - wide + block)
-            for i in range(4):
-                for j in range(4):
-                    row = i * quad + j * unit
-                    b_out[j][i * unit : (i + 1) * unit, there] = down[row : row + unit].astype(
-                        b_out[j].dtype
-                    )
-
-
-def expert_rows(group, a_parts, b_parts, weights, partner_weights):
-    quad, narrow = b_parts[0].shape
-    wide = a_parts[0].shape[1] - LANES
-    width = wide + narrow
-    rows = 4 * quad
-    hidden = weights[0].shape[1]
+        out_ref[:, cols] = down[:at]
+
+
+def expert_cost(rows, width, hidden):
+    return pl.CostEstimate(
+        flops=12 * rows * width * hidden,
+        bytes_accessed=12 * width * hidden,
+        transcendentals=2 * rows * hidden,
+    )
+
+
+def near_rows(group, rows, far, weights, partner_weights):
+    height = 4 * rows[0].shape[0] + 3 * far[0].shape[0]
+    padded = -(-height // 16) * 16
+    width, hidden = weights[0].shape
+    return pl.pallas_call(
+        near_kernel,
+        out_shape=(
+            jax.ShapeDtypeStruct((height, width), jnp.float32),
+            jax.ShapeDtypeStruct((width, 2 * hidden), jnp.bfloat16),
+            jax.ShapeDtypeStruct((width, 2 * hidden), jnp.bfloat16),
+            jax.ShapeDtypeStruct((2 * hidden, width), jnp.bfloat16),
+        ),
+        in_specs=[smem()] + [vmem()] * 7 + [hbm()] * 6,
+        out_specs=(vmem(),) * 4,
+        scratch_shapes=[
+            pltpu.VMEM((padded, width + LANES), jnp.bfloat16),
+            pltpu.VMEM((padded, 2 * hidden), jnp.bfloat16),
+            pltpu.SemaphoreType.DMA((6,)),
+        ],
+        compiler_params=pltpu.CompilerParams(vmem_limit_bytes=24 * MIB),
+        cost_estimate=expert_cost(height, width, hidden),
+        name="near_rows",
+    )(group, *rows, *far, *[stay(w) for w in weights + partner_weights])
+
+
+def piece_kernel(count, group_ref, *refs):
+    pieces, (w0_ref, w1_ref, down_ref) = refs[:count], refs[count : count + 3]
+    outs, (x_ref, h_ref) = refs[count + 3 : 2 * count + 3], refs[2 * count + 3 :]
+    height = pieces[0].shape[0]
+    for i, piece in enumerate(pieces):
+        x_ref[i * height : (i + 1) * height, :] = piece[...]
+    at = count * height
+    if at < x_ref.shape[0]:
+        x_ref[at:, :] = jnp.zeros((x_ref.shape[0] - at, x_ref.shape[1]), jnp.bfloat16)
+    hidden_units(group_ref, x_ref, (w0_ref, w1_ref), h_ref, lambda e: None)
+    for col in range(0, down_ref.shape[1], DOWN_BLOCK):
+        cols = slice(col, col + DOWN_BLOCK)
+        down = jnp.dot(h_ref[...], down_ref[:, cols], preferred_element_type=jnp.float32)
+        for i, out in enumerate(outs):
+            out[:, cols] = down[i * height : (i + 1) * height].astype(jnp.bfloat16)
+
+
+def piece_rows(group, pieces, w0, w1, down):
+    count = len(pieces)
+    height = count * pieces[0].shape[0]
+    padded = -(-height // 16) * 16
+    width, hidden = w0.shape[0], w0.shape[1] // 2
+    return pl.pallas_call(
+        functools.partial(piece_kernel, count),
+        out_shape=tuple(
+            jax.ShapeDtypeStruct((piece.shape[0], width), jnp.bfloat16) for piece in pieces
+        ),
+        in_specs=[smem()] + [vmem()] * (count + 3),
+        out_specs=(vmem(),) * count,
+        scratch_shapes=[
+            pltpu.VMEM((padded, width + LANES), jnp.bfloat16),
+            pltpu.VMEM((padded, 2 * hidden), jnp.bfloat16),
+        ],
+        compiler_params=pltpu.CompilerParams(vmem_limit_bytes=24 * MIB),
+        cost_estimate=expert_cost(height, width, hidden),
+        name="piece_rows",
+    )(group, *pieces, w0, w1, down)
+
+
+def plane_sum_kernel(near_ref, g1, g2, g3, m1, m2, m3):
+    far = m1.shape[0]
+    start = near_ref.shape[0] - 3 * far
+    for j, out in enumerate((m1, m2, m3)):
+        rows = slice(j * far, (j + 1) * far)
+        total = near_ref[start + j * far : start + (j + 1) * far, :]
+        for got in (g1, g2, g3):
+            total = total + got[rows, :].astype(jnp.float32)
+        out[...] = total.astype(jnp.bfloat16)
+
+
+def plane_sum(near, got):
+    far, width = got[0].shape[0] // 3, got[0].shape[1]
+    return pl.pallas_call(
+        plane_sum_kernel,
+        out_shape=tuple(jax.ShapeDtypeStruct((far, width), jnp.bfloat16) for _ in range(3)),
+        in_specs=[vmem()] * 4,
+        out_specs=(vmem(),) * 3,
+        compiler_params=SMALL,
+        name="plane_sum",
+    )(near, *got)
+
+
+def column_sum_kernel(near_ref, g1, g2, g3, own_ref, m1, m2, m3):
+    rows = own_ref.shape[0]
+    near = g1.shape[0] // 4
+    far = rows - near
+    for i, out in enumerate((own_ref, m1, m2, m3)):
+        out[:far, :] = near_ref[i * rows : i * rows + far, :].astype(out.dtype)
+        total = near_ref[i * rows + far : (i + 1) * rows, :]
+        for got in (g1, g2, g3):
+            total = total + got[i * near : (i + 1) * near, :].astype(jnp.float32)
+        out[far:, :] = total.astype(out.dtype)
+
+
+def column_sum(near, got, rows):
+    width = near.shape[1]
     kinds = (jnp.float32, jnp.bfloat16, jnp.bfloat16, jnp.bfloat16)
     return pl.pallas_call(
-        expert_kernel,
-        out_shape=tuple(jax.ShapeDtypeStruct((quad, wide), kind) for kind in kinds)
-        + tuple(jax.ShapeDtypeStruct((quad, narrow), kind) for kind in kinds),
-        in_specs=[smem()] + [vmem()] * 8 + [hbm()] * 6,
-        out_specs=(vmem(),) * 8,
-        scratch_shapes=[
-            pltpu.VMEM((rows, width), jnp.bfloat16),
-            pltpu.VMEM((width, 2 * hidden), jnp.bfloat16),
-            pltpu.VMEM((width, 2 * hidden), jnp.bfloat16),
-            pltpu.VMEM((2 * hidden, width), jnp.bfloat16),
-            pltpu.VMEM((rows, 2 * hidden), jnp.bfloat16),
-            pltpu.SemaphoreType.DMA((6,)),
-        ],
-        compiler_params=pltpu.CompilerParams(vmem_limit_bytes=40 * MIB),
-        cost_estimate=pl.CostEstimate(
-            flops=12 * rows * width * hidden, bytes_accessed=16 * rows * width, transcendentals=0
-        ),
-        name="expert_rows",
-    )(group, *a_parts, *b_parts, *[stay(w) for w in weights + partner_weights])
-
-
-def sum_kernel(own_ref, g1, g2, g3, o0, o1, o2, o3):
-    unit = o0.shape[0]
-    for i, out in enumerate((o0, o1, o2, o3)):
-        rows = slice(i * unit, (i + 1) * unit)
-        total = own_ref[rows, :]
-        for got in (g1, g2, g3):
-            total = total + got[rows, :].astype(jnp.float32)
-        out[...] = total.astype(out.dtype)
-
-
-def sum_rows(own, got):
-    quad, width = own.shape
-    unit = quad // 4
-    kinds = (jnp.float32, jnp.bfloat16, jnp.bfloat16, jnp.bfloat16)
-    return pl.pallas_call(
-        sum_kernel,
-        out_shape=tuple(jax.ShapeDtypeStruct((unit, width), kind) for kind in kinds),
+        column_sum_kernel,
+        out_shape=tuple(jax.ShapeDtypeStruct((rows, width), kind) for kind in kinds),
         in_specs=[vmem()] * 4,
         out_specs=(vmem(),) * 4,
         compiler_params=SMALL,
-        name="sum_rows",
-    )(own, *got)
-
-
-def final_kernel(state_ref, a0, a1, a2, a3, b0, b1, b2, b3, gain_ref, out_ref):
-    wide = a0.shape[1]
-    mixed_a = a0[...]
-    for got in (a1, a2, a3):
-        mixed_a = mixed_a + got[...].astype(jnp.float32)
-    mixed_b = b0[...]
-    for got in (b1, b2, b3):
-        mixed_b = mixed_b + got[...].astype(jnp.float32)
-    total = state_ref[...] + jnp.concatenate([mixed_a, mixed_b], axis=1)
-    out_ref[...] = rms_scale(total, gain_ref[...]).astype(jnp.bfloat16)
-
-
-def final_rows(state, a_parts, b_parts, gain):
+        name="column_sum",
+    )(near, *got)
+
+
+def final_kernel(state_ref, own_ref, p1, p2, p3, z1, z2, z3, gain_ref, out_ref, total_ref):
+    total = state_ref[...] + own_ref[...]
+    for got in (p1, p2, p3):
+        total = total + got[...].astype(jnp.float32)
+    total_ref[...] = total
+    far = z1.shape[0]
+    part = total_ref[:far, :]
+    for got in (z1, z2, z3):
+        part = part + got[...].astype(jnp.float32)
+    total_ref[:far, :] = part
+    out_ref[...] = rms_scale(total_ref[...], gain_ref[...]).astype(jnp.bfloat16)
+
+
+def final_rows(state, own, plane, column, gain):
     return pl.pallas_call(
         final_kernel,
         out_shape=jax.ShapeDtypeStruct(state.shape, jnp.bfloat16),
-        in_specs=[vmem()] * 10,
+        in_specs=[vmem()] * 9,
         out_specs=vmem(),
+        scratch_shapes=[pltpu.VMEM(state.shape, jnp.float32)],
         compiler_params=SMALL,
         name="final_rows",
-    )(state, *a_parts, *b_parts, gain)
+    )(state, own, *plane, *column, gain)
 
 
 def place(z, y, c, x):
@@ -583,7 +679,7 @@
     req_index = lax.axis_index("req")
     tokens, width = residual.shape
     half = tokens // 2
-    wide = width * 5 // 8
+    far = half * 3 // 4
     groups = expert_home.shape[0]
     weights = (w_gate[0], w_up[0], w_down[0])
     partner_weights = tuple(swap(w, 0, 0, 1, 0) for w in weights)
@@ -591,24 +687,21 @@
         request_page_index, cache_length_rows, tp_index.reshape(1).astype(jnp.int32), expert_home,
         queries, fresh_key_value, key_value_cache, residual, route_ids, route_weights, w_out,
     )
-    got = swap(sent, 0, 0, 0, 1)
-    state, rows_a, rows_b = norm_rows(own_state, got, pack, gain_in[None, :], wide)
-    more_a, more_b, partner_weights = barrier(
-        swap_z((rows_a,) * 3), swap_plane((rows_b,) * 3), partner_weights
-    )
-    column_a, column_b = barrier(
-        jnp.concatenate((rows_a,) + more_a, axis=0), jnp.concatenate((rows_b,) + more_b, axis=0)
-    )
-    more_a, more_b = barrier(swap_plane((column_a,) * 3), swap_z((column_b,) * 3))
+    got, partner_weights = barrier(swap(sent, 0, 0, 0, 1), partner_weights)
     group = jnp.stack([req_index, req_index ^ 1, groups]).astype(jnp.int32)
-    parts = expert_rows(
-        group, (column_a,) + more_a, (column_b,) + more_b, weights, partner_weights
-    )
-    part_a, part_b = parts[:4], parts[4:]
-    more_a, more_b = barrier(swap_plane(part_a[1:]), swap_z(part_b[1:]))
-    near_a, near_b = barrier(sum_rows(part_a[0], more_a), sum_rows(part_b[0], more_b))
-    more_a, more_b = barrier(swap_z(near_a[1:]), swap_plane(near_b[1:]))
-    return final_rows(state, (near_a[0],) + more_a, (near_b[0],) + more_b, gain_out[None, :])
+    state, rows, far_rows = norm_rows(own_state, got, pack, gain_in[None, :], far)
+    z_rows, plane_rows = barrier(swap_z((far_rows,) * 3), swap_plane((rows,) * 3))
+    plane_rows = (rows,) + plane_rows
+    onward_plane, onward_z = relay_rows(plane_rows, z_rows)
+    z_pieces = swap_z((onward_z,) * 3)
+    plane_pieces = swap_plane((onward_plane,) * 3)
+    near, w0, w1, down = near_rows(group, plane_rows, z_rows, weights, partner_weights)
+    z_parts = piece_rows(group, z_pieces, w0, w1, down)
+    plane_parts = tuple(piece_rows(group, (piece,), w0, w1, down)[0] for piece in plane_pieces)
+    own, *near_sums = column_sum(near, swap_z(z_parts), half)
+    far_sums = plane_sum(near, swap_plane(plane_parts))
+    last_z, last_plane = barrier(swap_z(far_sums), swap_plane(near_sums))
+    return final_rows(state, own, last_plane, last_z, gain_out[None, :])
 
 
 def solution(mesh):

time: 96.4 us -> 86.3 us (0.90)
  waiting for transfers between devices: 34.7 us -> 26 us
  Pallas kernels: 14.8 us -> 20.5 us
  local copies, waits for them, and re-layouts: 5.25 us -> 1.17 us
  starting transfers between devices: 41.1 us -> 38.3 us
    ppermute x28, waiting for transfers between devices: 34.7 us -> 26 us  [swap(): return lax.ppermute(value, ALL, pairs)]
    pallas_call x3 -> x8, Pallas kernels: 9.23 us -> 15.1 us  [the longest x4 9.4 us: piece_rows(): pl.pallas_call(functools.partial(piece_kernel, count), out_shape=tuple((j...]
    unnamed x9 -> x8, local copies, waits for them, and re-layouts: 5.25 us -> 1.17 us
    ppermute x28, starting transfers between devices: 41.1 us -> 38.3 us  [swap(): return lax.ppermute(value, ALL, pairs)]
  transfers between devices with their start and end apart: 28 -> 28, of which waited for: 12 -> 6; matrix products, arithmetic and copies ran while one was open for 4% -> 0% of each run, Pallas kernels for 5% -> 23%
where the time goes in v3:
time: 86.3 us; the launch traced here: 86.1 us
  starting transfers between devices  38.3 us (44%)
  waiting for transfers between devices  26 us (30%)
  Pallas kernels  20.5 us (24%)
  local copies, waits for them, and re-layouts  1.17 us (1%)
    ppermute x28, starting transfers between devices, swap(): return lax.ppermute(value, ALL, pairs)  38.3 us
    ppermute x28, waiting for transfers between devices, swap(): return lax.ppermute(value, ALL, pairs)  26 us
    pallas_call x4, Pallas kernels, piece_rows(): pl.pallas_call(functools.partial(piece_kernel, count), out_shape=tuple((j...  9.4 us
    pallas_call x1, Pallas kernels, near_rows(): pl.pallas_call(near_kernel, out_shape=(jax.ShapeDtypeStruct((height, widt...  5.44 us
    pallas_call x1, Pallas kernels, attention_terms(): pl.pallas_call(attention_kernel, out_shape=(jax.ShapeDtypeStruct((half, w...  4.33 us
  transfers between devices with their start and end apart: 28, of which 6 were waited for; matrix products, arithmetic and copies ran while one was open for 0% of the time, Pallas kernels for 23%

profile of v3, /device:TPU:0, one launch (start us, length us, event | category | flops | bytes accessed | tf_op | source)
XLA Modules:
  0.0 86.1 jit_solution(17406775369427587389)
XLA Ops:
  1.0 4.3 %attention_terms.1 = (f32[32,2048]{1,0:T(8,128)S(1)}, bf16[32,2048]{1,0:T(8,128)(2,1)S(1)}, bf16[32,128]{1,0:T(8,128)(2,1)S(1)}) custom-call(s32[4,9]{1,0:T(4,128)} %bitcast.21, s32[9]{0:T(128)} %lengths_ref.1, s32[1]{0:T(128)} %bitcast.1.tp_ref, s32[16]{0:T(128)} %home_ref.1, bf16[64,1024]{1,0:T(8,128)(2,1)} %q_hbm.1, bf16[64,512]{1,0:T(8,128)(2,1)} %fresh_hbm.1, ...), custom_call_target="tpu_custom_call" | custom-call | tf_op jit(solution)/shard_map/attention_terms/pallas_call | solution.py:364
  5.3 2.6 %collective-permute-start = (bf16[32,2048]{1,0:T(8,128)(2,1)S(1)}, bf16[32,2048]{1,0:T(8,128)(2,1)S(1)}, u32[]{:S(2)}, u32[]{:S(2)}) collective-permute-start(bf16[32,2048]{1,0:T(8,128)(2,1)S(1)} %get-tuple-element.44), channel_id=1, source_target_pairs={{0,1},{1,0},{2,3},{3,2},{4,5},{5,4},{6,7},{7,6},{8,9},{9,8},{10,11... | collective-permute-start | bytes 393224 | tf_op jit(solution)/shard_map/ppermute | solution.py:660
  7.9 4.2 %collective-permute-done.got_ref = bf16[32,2048]{1,0:T(8,128)(2,1)S(1)} collective-permute-done((bf16[32,2048]{1,0:T(8,128)(2,1)S(1)}, bf16[32,2048]{1,0:T(8,128)(2,1)S(1)}, u32[]{:S(2)}, u32[]{:S(2)}) %collective-permute-start) | collective-permute-done | bytes 131104 | tf_op jit(solution)/shard_map/ppermute | solution.py:660
  12.1 1.2 %copy-done.3 = bf16[2048,384]{1,0:T(8,128)(2,1)} copy-done((bf16[2048,384]{1,0:T(8,128)(2,1)}, bf16[2048,384]{1,0:T(8,128)(2,1)S(1)}, u32[]{:S(2)}) %copy-start.3) | copy-done | bytes 1572888
  13.4 1.9 %collective-permute-start.4 = (bf16[24,2176]{1,0:T(8,128)(2,1)S(1)}, bf16[24,2176]{1,0:T(8,128)(2,1)S(1)}, u32[]{:S(2)}, u32[]{:S(2)}) collective-permute-start(bf16[24,2176]{1,0:T(8,128)(2,1)S(1)} %get-tuple-element.49), channel_id=1, source_target_pairs={{0,8},{1,9},{2,10},{3,11},{4,12},{5,13},{6,14},{7,15},{8,0},{9,1},... | collective-permute-start | bytes 313352 | tf_op jit(solution)/shard_map/ppermute | solution.py:660
  15.3 1.5 %collective-permute-start.7 = (bf16[32,2176]{1,0:T(8,128)(2,1)S(1)}, bf16[32,2176]{1,0:T(8,128)(2,1)S(1)}, u32[]{:S(2)}, u32[]{:S(2)}) collective-permute-start(bf16[32,2176]{1,0:T(8,128)(2,1)S(1)} %get-tuple-element.48.r0), channel_id=1, source_target_pairs={{0,1},{1,0},{2,3},{3,2},{4,5},{5,4},{6,7},{7,6},{8,9},{9,8},{10,11... | collective-permute-start | bytes 417800 | tf_op jit(solution)/shard_map/ppermute | solution.py:660
  16.7 1.5 %collective-permute-start.8 = (bf16[32,2176]{1,0:T(8,128)(2,1)S(1)}, bf16[32,2176]{1,0:T(8,128)(2,1)S(1)}, u32[]{:S(2)}, u32[]{:S(2)}) collective-permute-start(bf16[32,2176]{1,0:T(8,128)(2,1)S(1)} %get-tuple-element.48.r0), channel_id=1, source_target_pairs={{0,4},{1,5},{2,6},{3,7},{4,0},{5,1},{6,2},{7,3},{8,12},{9,13},{10,... | collective-permute-start | bytes 417800 | tf_op jit(solution)/shard_map/ppermute | solution.py:660
  18.7 2.6 %collective-permute-start.5 = (bf16[24,2176]{1,0:T(8,128)(2,1)S(1)}, bf16[24,2176]{1,0:T(8,128)(2,1)S(1)}, u32[]{:S(2)}, u32[]{:S(2)}) collective-permute-start(bf16[24,2176]{1,0:T(8,128)(2,1)S(1)} %get-tuple-element.49), channel_id=1, source_target_pairs={{0,16},{1,17},{2,18},{3,19},{4,20},{5,21},{6,22},{7,23},{8,24},{9,... | collective-permute-start | bytes 313352 | tf_op jit(solution)/shard_map/ppermute | solution.py:660
  22.0 6.6 %collective-permute-done.5.z2 = bf16[24,2176]{1,0:T(8,128)(2,1)S(1)} collective-permute-done((bf16[24,2176]{1,0:T(8,128)(2,1)S(1)}, bf16[24,2176]{1,0:T(8,128)(2,1)S(1)}, u32[]{:S(2)}, u32[]{:S(2)}) %collective-permute-start.5) | collective-permute-done | bytes 104480 | tf_op jit(solution)/shard_map/ppermute | solution.py:660
  28.6 1.7 %collective-permute-start.10 = (bf16[32,2176]{1,0:T(8,128)(2,1)S(1)}, bf16[32,2176]{1,0:T(8,128)(2,1)S(1)}, u32[]{:S(2)}, u32[]{:S(2)}) collective-permute-start(bf16[32,2176]{1,0:T(8,128)(2,1)S(1)} %get-tuple-element.60), channel_id=1, source_target_pairs={{0,8},{1,9},{2,10},{3,11},{4,12},{5,13},{6,14},{7,15},{8,0},{9,1},... | collective-permute-start | bytes 417800 | tf_op jit(solution)/shard_map/ppermute | solution.py:660
  30.3 1.5 %collective-permute-start.16 = (bf16[72,2176]{1,0:T(8,128)(2,1)S(1)}, bf16[72,2176]{1,0:T(8,128)(2,1)S(1)}, u32[]{:S(2)}, u32[]{:S(2)}) collective-permute-start(bf16[72,2176]{1,0:T(8,128)(2,1)S(1)} %get-tuple-element.68), channel_id=1, source_target_pairs={{0,1},{1,0},{2,3},{3,2},{4,5},{5,4},{6,7},{7,6},{8,9},{9,8},{10,11... | collective-permute-start | bytes 940040 | tf_op jit(solution)/shard_map/ppermute | solution.py:660
  31.9 1.5 %collective-permute-start.11 = (bf16[32,2176]{1,0:T(8,128)(2,1)S(1)}, bf16[32,2176]{1,0:T(8,128)(2,1)S(1)}, u32[]{:S(2)}, u32[]{:S(2)}) collective-permute-start(bf16[32,2176]{1,0:T(8,128)(2,1)S(1)} %get-tuple-element.60), channel_id=1, source_target_pairs={{0,16},{1,17},{2,18},{3,19},{4,20},{5,21},{6,22},{7,23},{8,24},{9,... | collective-permute-start | bytes 417800 | tf_op jit(solution)/shard_map/ppermute | solution.py:660
  33.4 1.2 %collective-permute-start.12 = (bf16[32,2176]{1,0:T(8,128)(2,1)S(1)}, bf16[32,2176]{1,0:T(8,128)(2,1)S(1)}, u32[]{:S(2)}, u32[]{:S(2)}) collective-permute-start(bf16[32,2176]{1,0:T(8,128)(2,1)S(1)} %get-tuple-element.60), channel_id=1, source_target_pairs={{0,24},{1,25},{2,26},{3,27},{4,28},{5,29},{6,30},{7,31},{8,16},{9,... | collective-permute-start | bytes 417800 | tf_op jit(solution)/shard_map/ppermute | solution.py:660
  34.7 1.5 %collective-permute-start.18 = (bf16[72,2176]{1,0:T(8,128)(2,1)S(1)}, bf16[72,2176]{1,0:T(8,128)(2,1)S(1)}, u32[]{:S(2)}, u32[]{:S(2)}) collective-permute-start(bf16[72,2176]{1,0:T(8,128)(2,1)S(1)} %get-tuple-element.68), channel_id=1, source_target_pairs={{0,4},{1,5},{2,6},{3,7},{4,0},{5,1},{6,2},{7,3},{8,12},{9,13},{10,... | collective-permute-start | bytes 940040 | tf_op jit(solution)/shard_map/ppermute | solution.py:660
  36.2 1.5 %collective-permute-start.20 = (bf16[72,2176]{1,0:T(8,128)(2,1)S(1)}, bf16[72,2176]{1,0:T(8,128)(2,1)S(1)}, u32[]{:S(2)}, u32[]{:S(2)}) collective-permute-start(bf16[72,2176]{1,0:T(8,128)(2,1)S(1)} %get-tuple-element.68), channel_id=1, source_target_pairs={{0,5},{1,4},{2,7},{3,6},{4,1},{5,0},{6,3},{7,2},{8,13},{9,12},{10,... | collective-permute-start | bytes 940040 | tf_op jit(solution)/shard_map/ppermute | solution.py:660
  37.7 5.4 %near_rows.1 = (f32[200,2048]{1,0:T(8,128)S(1)}, bf16[2048,768]{1,0:T(8,128)(2,1)S(1)}, bf16[2048,768]{1,0:T(8,128)(2,1)S(1)}, bf16[768,2048]{1,0:T(8,128)(2,1)S(1)}) custom-call(s32[3]{0:T(128)S(1)} %pad_add_fusion.group_ref, bf16[32,2176]{1,0:T(8,128)(2,1)S(1)} %get-tuple-element.48.r0, bf16[32,2176]{1,0:T(8,128)(2,1)S(1)} %collective-permute-done.7.r1, ...), custom_call_target="tpu_custom_call" | custom-call | flops 1887436800 | bytes 9437184 | tf_op jit(solution)/shard_map/near_rows/pallas_call | solution.py:515
  43.6 2.3 %piece_rows.4 = (bf16[32,2048]{1,0:T(8,128)(2,1)S(1)}, bf16[32,2048]{1,0:T(8,128)(2,1)S(1)}, bf16[32,2048]{1,0:T(8,128)(2,1)S(1)}) custom-call(s32[3]{0:T(128)S(1)} %pad_add_fusion.group_ref, bf16[32,2176]{1,0:T(8,128)(2,1)S(1)} %collective-permute-done.10.refs_0_, bf16[32,2176]{1,0:T(8,128)(2,1)S(1)} %collective-permute-done.11.refs_1_, ...), custom_call_target="tpu_custom_call" | custom-call | flops 905969664 | bytes 9437184 | tf_op jit(solution)/shard_map/piece_rows/pallas_call | solution.py:558
  45.9 2.2 %collective-permute-start.13 = (bf16[32,2048]{1,0:T(8,128)(2,1)S(1)}, bf16[32,2048]{1,0:T(8,128)(2,1)S(1)}, u32[]{:S(2)}, u32[]{:S(2)}) collective-permute-start(bf16[32,2048]{1,0:T(8,128)(2,1)S(1)} %get-tuple-element.64), channel_id=1, source_target_pairs={{0,8},{1,9},{2,10},{3,11},{4,12},{5,13},{6,14},{7,15},{8,0},{9,1},... | collective-permute-start | bytes 393224 | tf_op jit(solution)/shard_map/ppermute | solution.py:660
  48.1 2.4 %piece_rows.5 = bf16[72,2048]{1,0:T(8,128)(2,1)S(1)} custom-call(s32[3]{0:T(128)S(1)} %pad_add_fusion.group_ref, bf16[72,2176]{1,0:T(8,128)(2,1)S(1)} %collective-permute-done.16.refs_0_, bf16[2048,768]{1,0:T(8,128)(2,1)S(1)} %get-tuple-element.61.refs_3_.refs_1_, bf16[2048,768]{1,0:T(8,128)(2,1)S(1)} %get-tuple-element.62.refs_4_.refs_2_, ...), custom_call_target="tpu_custom_call" | custom-call | flops 679477248 | bytes 9437184 | tf_op jit(solution)/shard_map/piece_rows/pallas_call | solution.py:558
  51.3 2.4 %piece_rows.6 = bf16[72,2048]{1,0:T(8,128)(2,1)S(1)} custom-call(s32[3]{0:T(128)S(1)} %pad_add_fusion.group_ref, bf16[72,2176]{1,0:T(8,128)(2,1)S(1)} %collective-permute-done.18.refs_0_, bf16[2048,768]{1,0:T(8,128)(2,1)S(1)} %get-tuple-element.61.refs_3_.refs_1_, bf16[2048,768]{1,0:T(8,128)(2,1)S(1)} %get-tuple-element.62.refs_4_.refs_2_, ...), custom_call_target="tpu_custom_call" | custom-call | flops 679477248 | bytes 9437184 | tf_op jit(solution)/shard_map/piece_rows/pallas_call | solution.py:558
  53.7 1.4 %collective-permute-start.19 = (bf16[72,2048]{1,0:T(8,128)(2,1)S(1)}, bf16[72,2048]{1,0:T(8,128)(2,1)S(1)}, u32[]{:S(2)}, u32[]{:S(2)}) collective-permute-start(bf16[72,2048]{1,0:T(8,128)(2,1)S(1)} %piece_rows.6), channel_id=1, source_target_pairs={{0,4},{1,5},{2,6},{3,7},{4,0},{5,1},{6,2},{7,3},{8,12},{9,13},{10,... | collective-permute-start | bytes 884744 | tf_op jit(solution)/shard_map/ppermute | solution.py:660
  55.1 2.4 %piece_rows.7 = bf16[72,2048]{1,0:T(8,128)(2,1)S(1)} custom-call(s32[3]{0:T(128)S(1)} %pad_add_fusion.group_ref, bf16[72,2176]{1,0:T(8,128)(2,1)S(1)} %collective-permute-done.20.refs_0_, bf16[2048,768]{1,0:T(8,128)(2,1)S(1)} %get-tuple-element.61.refs_3_.refs_1_, bf16[2048,768]{1,0:T(8,128)(2,1)S(1)} %get-tuple-element.62.refs_4_.refs_2_, ...), custom_call_target="tpu_custom_call" | custom-call | flops 679477248 | bytes 9437184 | tf_op jit(solution)/shard_map/piece_rows/pallas_call | solution.py:558
  57.5 1.4 %collective-permute-start.21 = (bf16[72,2048]{1,0:T(8,128)(2,1)S(1)}, bf16[72,2048]{1,0:T(8,128)(2,1)S(1)}, u32[]{:S(2)}, u32[]{:S(2)}) collective-permute-start(bf16[72,2048]{1,0:T(8,128)(2,1)S(1)} %piece_rows.7), channel_id=1, source_target_pairs={{0,5},{1,4},{2,7},{3,6},{4,1},{5,0},{6,3},{7,2},{8,13},{9,12},{10,... | collective-permute-start | bytes 884744 | tf_op jit(solution)/shard_map/ppermute | solution.py:660
  58.9 1.3 %collective-permute-start.14 = (bf16[32,2048]{1,0:T(8,128)(2,1)S(1)}, bf16[32,2048]{1,0:T(8,128)(2,1)S(1)}, u32[]{:S(2)}, u32[]{:S(2)}) collective-permute-start(bf16[32,2048]{1,0:T(8,128)(2,1)S(1)} %get-tuple-element.65), channel_id=1, source_target_pairs={{0,16},{1,17},{2,18},{3,19},{4,20},{5,21},{6,22},{7,23},{8,24},{9,... | collective-permute-start | bytes 393224 | tf_op jit(solution)/shard_map/ppermute | solution.py:660
  60.2 1.4 %collective-permute-start.15 = (bf16[32,2048]{1,0:T(8,128)(2,1)S(1)}, bf16[32,2048]{1,0:T(8,128)(2,1)S(1)}, u32[]{:S(2)}, u32[]{:S(2)}) collective-permute-start(bf16[32,2048]{1,0:T(8,128)(2,1)S(1)} %get-tuple-element.66), channel_id=1, source_target_pairs={{0,24},{1,25},{2,26},{3,27},{4,28},{5,29},{6,30},{7,31},{8,16},{9,... | collective-permute-start | bytes 393224 | tf_op jit(solution)/shard_map/ppermute | solution.py:660
  61.7 7.8 %collective-permute-done.14.g2 = bf16[32,2048]{1,0:T(8,128)(2,1)S(1)} collective-permute-done((bf16[32,2048]{1,0:T(8,128)(2,1)S(1)}, bf16[32,2048]{1,0:T(8,128)(2,1)S(1)}, u32[]{:S(2)}, u32[]{:S(2)}) %collective-permute-start.14) | collective-permute-done | bytes 131104 | tf_op jit(solution)/shard_map/ppermute | solution.py:660
  70.2 1.5 %collective-permute-start.26 = (bf16[32,2048]{1,0:T(8,128)(2,1)S(1)}, bf16[32,2048]{1,0:T(8,128)(2,1)S(1)}, u32[]{:S(2)}, u32[]{:S(2)}) collective-permute-start(bf16[32,2048]{1,0:T(8,128)(2,1)S(1)} %get-tuple-element.73), channel_id=1, source_target_pairs={{0,4},{1,5},{2,6},{3,7},{4,0},{5,1},{6,2},{7,3},{8,12},{9,13},{10,... | collective-permute-start | bytes 393224 | tf_op jit(solution)/shard_map/ppermute | solution.py:660
  71.7 1.4 %collective-permute-start.27 = (bf16[32,2048]{1,0:T(8,128)(2,1)S(1)}, bf16[32,2048]{1,0:T(8,128)(2,1)S(1)}, u32[]{:S(2)}, u32[]{:S(2)}) collective-permute-start(bf16[32,2048]{1,0:T(8,128)(2,1)S(1)} %get-tuple-element.74), channel_id=1, source_target_pairs={{0,5},{1,4},{2,7},{3,6},{4,1},{5,0},{6,3},{7,2},{8,13},{9,12},{10,... | collective-permute-start | bytes 393224 | tf_op jit(solution)/shard_map/ppermute | solution.py:660
  73.3 2.5 %collective-permute-start.22 = (bf16[24,2048]{1,0:T(8,128)(2,1)S(1)}, bf16[24,2048]{1,0:T(8,128)(2,1)S(1)}, u32[]{:S(2)}, u32[]{:S(2)}) collective-permute-start(bf16[24,2048]{1,0:T(8,128)(2,1)S(1)} %get-tuple-element.69), channel_id=1, source_target_pairs={{0,8},{1,9},{2,10},{3,11},{4,12},{5,13},{6,14},{7,15},{8,0},{9,1},... | collective-permute-start | bytes 294920 | tf_op jit(solution)/shard_map/ppermute | solution.py:660
  75.8 1.1 %collective-permute-start.23 = (bf16[24,2048]{1,0:T(8,128)(2,1)S(1)}, bf16[24,2048]{1,0:T(8,128)(2,1)S(1)}, u32[]{:S(2)}, u32[]{:S(2)}) collective-permute-start(bf16[24,2048]{1,0:T(8,128)(2,1)S(1)} %get-tuple-element.70), channel_id=1, source_target_pairs={{0,16},{1,17},{2,18},{3,19},{4,20},{5,21},{6,22},{7,23},{8,24},{9,... | collective-permute-start | bytes 294920 | tf_op jit(solution)/shard_map/ppermute | solution.py:660
  76.9 1.4 %collective-permute-start.24 = (bf16[24,2048]{1,0:T(8,128)(2,1)S(1)}, bf16[24,2048]{1,0:T(8,128)(2,1)S(1)}, u32[]{:S(2)}, u32[]{:S(2)}) collective-permute-start(bf16[24,2048]{1,0:T(8,128)(2,1)S(1)} %get-tuple-element.71), channel_id=1, source_target_pairs={{0,24},{1,25},{2,26},{3,27},{4,28},{5,29},{6,30},{7,31},{8,16},{9,... | collective-permute-start | bytes 294920 | tf_op jit(solution)/shard_map/ppermute | solution.py:660
  79.4 5.9 %collective-permute-done.23.z2 = bf16[24,2048]{1,0:T(8,128)(2,1)S(1)} collective-permute-done((bf16[24,2048]{1,0:T(8,128)(2,1)S(1)}, bf16[24,2048]{1,0:T(8,128)(2,1)S(1)}, u32[]{:S(2)}, u32[]{:S(2)}) %collective-permute-start.23) | collective-permute-done | bytes 98336 | tf_op jit(solution)/shard_map/ppermute | solution.py:660
  (44 shorter events, 6.5 us)
Async XLA Ops:
  0.0 12.0 %collective-permute-start.1 = (bf16[2048,384]{1,0:T(8,128)(2,1)}, bf16[2048,384]{1,0:T(8,128)(2,1)S(1)}, u32[]{:S(2)}, u32[]{:S(2)}) collective-permute-start(bf16[2048,384]{1,0:T(8,128)(2,1)} %bitcast.13), channel_id=1, source_target_pairs={{0,2},{1,3},{2,0},{3,1},{4,6},{5,7},{6,4},{7,5},{8,10},{9,11},{10,... | collective-permute-start | bytes 4718600 | tf_op jit(solution)/shard_map/ppermute | solution.py:660
  0.5 11.6 %collective-permute-start.2 = (bf16[2048,384]{1,0:T(8,128)(2,1)}, bf16[2048,384]{1,0:T(8,128)(2,1)S(1)}, u32[]{:S(2)}, u32[]{:S(2)}) collective-permute-start(bf16[2048,384]{1,0:T(8,128)(2,1)} %bitcast.15), channel_id=1, source_target_pairs={{0,2},{1,3},{2,0},{3,1},{4,6},{5,7},{6,4},{7,5},{8,10},{9,11},{10,... | collective-permute-start | bytes 4718600 | tf_op jit(solution)/shard_map/ppermute | solution.py:660
  0.5 11.5 %collective-permute-start.3 = (bf16[384,2048]{1,0:T(8,128)(2,1)}, bf16[384,2048]{1,0:T(8,128)(2,1)}, u32[]{:S(2)}, u32[]{:S(2)}) collective-permute-start(bf16[384,2048]{1,0:T(8,128)(2,1)} %bitcast.17), channel_id=1, source_target_pairs={{0,2},{1,3},{2,0},{3,1},{4,6},{5,7},{6,4},{7,5},{8,10},{9,11},{10,... | collective-permute-start | bytes 4718600 | tf_op jit(solution)/shard_map/ppermute | solution.py:660
  1.0 12.3 %copy-start.1 = (f32[2048]{0:T(1024)S(1)}, f32[2048]{0:T(1024)}, u32[]{:S(2)}) copy-start(f32[2048]{0:T(1024)} %param.22) | copy-start | bytes 24580
  5.3 6.7 %collective-permute-start = (bf16[32,2048]{1,0:T(8,128)(2,1)S(1)}, bf16[32,2048]{1,0:T(8,128)(2,1)S(1)}, u32[]{:S(2)}, u32[]{:S(2)}) collective-permute-start(bf16[32,2048]{1,0:T(8,128)(2,1)S(1)} %get-tuple-element.44), channel_id=1, source_target_pairs={{0,1},{1,0},{2,3},{3,2},{4,5},{5,4},{6,7},{7,6},{8,9},{9,8},{10,11... | collective-permute-start | bytes 393224 | tf_op jit(solution)/shard_map/ppermute | solution.py:660
  12.0 25.7 %copy-start.2 = (bf16[2048,384]{1,0:T(8,128)(2,1)}, bf16[2048,384]{1,0:T(8,128)(2,1)S(1)}, u32[]{:S(2)}) copy-start(bf16[2048,384]{1,0:T(8,128)(2,1)S(1)} %collective-permute-done.1.wg1) | copy-start | bytes 4718596
  12.0 1.2 %copy-start.3 = (bf16[2048,384]{1,0:T(8,128)(2,1)}, bf16[2048,384]{1,0:T(8,128)(2,1)S(1)}, u32[]{:S(2)}) copy-start(bf16[2048,384]{1,0:T(8,128)(2,1)S(1)} %collective-permute-done.2.wu1) | copy-start | bytes 4718596
  13.4 8.0 %collective-permute-start.4 = (bf16[24,2176]{1,0:T(8,128)(2,1)S(1)}, bf16[24,2176]{1,0:T(8,128)(2,1)S(1)}, u32[]{:S(2)}, u32[]{:S(2)}) collective-permute-start(bf16[24,2176]{1,0:T(8,128)(2,1)S(1)} %get-tuple-element.49), channel_id=1, source_target_pairs={{0,8},{1,9},{2,10},{3,11},{4,12},{5,13},{6,14},{7,15},{8,0},{9,1},... | collective-permute-start | bytes 313352 | tf_op jit(solution)/shard_map/ppermute | solution.py:660
  15.3 13.3 %collective-permute-start.7 = (bf16[32,2176]{1,0:T(8,128)(2,1)S(1)}, bf16[32,2176]{1,0:T(8,128)(2,1)S(1)}, u32[]{:S(2)}, u32[]{:S(2)}) collective-permute-start(bf16[32,2176]{1,0:T(8,128)(2,1)S(1)} %get-tuple-element.48.r0), channel_id=1, source_target_pairs={{0,1},{1,0},{2,3},{3,2},{4,5},{5,4},{6,7},{7,6},{8,9},{9,8},{10,11... | collective-permute-start | bytes 417800 | tf_op jit(solution)/shard_map/ppermute | solution.py:660
  16.7 11.8 %collective-permute-start.8 = (bf16[32,2176]{1,0:T(8,128)(2,1)S(1)}, bf16[32,2176]{1,0:T(8,128)(2,1)S(1)}, u32[]{:S(2)}, u32[]{:S(2)}) collective-permute-start(bf16[32,2176]{1,0:T(8,128)(2,1)S(1)} %get-tuple-element.48.r0), channel_id=1, source_target_pairs={{0,4},{1,5},{2,6},{3,7},{4,0},{5,1},{6,2},{7,3},{8,12},{9,13},{10,... | collective-permute-start | bytes 417800 | tf_op jit(solution)/shard_map/ppermute | solution.py:660
  18.3 10.3 %collective-permute-start.9 = (bf16[32,2176]{1,0:T(8,128)(2,1)S(1)}, bf16[32,2176]{1,0:T(8,128)(2,1)S(1)}, u32[]{:S(2)}, u32[]{:S(2)}) collective-permute-start(bf16[32,2176]{1,0:T(8,128)(2,1)S(1)} %get-tuple-element.48.r0), channel_id=1, source_target_pairs={{0,5},{1,4},{2,7},{3,6},{4,1},{5,0},{6,3},{7,2},{8,13},{9,12},{10,... | collective-permute-start | bytes 417800 | tf_op jit(solution)/shard_map/ppermute | solution.py:660
  18.7 9.8 %collective-permute-start.5 = (bf16[24,2176]{1,0:T(8,128)(2,1)S(1)}, bf16[24,2176]{1,0:T(8,128)(2,1)S(1)}, u32[]{:S(2)}, u32[]{:S(2)}) collective-permute-start(bf16[24,2176]{1,0:T(8,128)(2,1)S(1)} %get-tuple-element.49), channel_id=1, source_target_pairs={{0,16},{1,17},{2,18},{3,19},{4,20},{5,21},{6,22},{7,23},{8,24},{9,... | collective-permute-start | bytes 313352 | tf_op jit(solution)/shard_map/ppermute | solution.py:660
  21.3 7.2 %collective-permute-start.6 = (bf16[24,2176]{1,0:T(8,128)(2,1)S(1)}, bf16[24,2176]{1,0:T(8,128)(2,1)S(1)}, u32[]{:S(2)}, u32[]{:S(2)}) collective-permute-start(bf16[24,2176]{1,0:T(8,128)(2,1)S(1)} %get-tuple-element.49), channel_id=1, source_target_pairs={{0,24},{1,25},{2,26},{3,27},{4,28},{5,29},{6,30},{7,31},{8,16},{9,... | collective-permute-start | bytes 313352 | tf_op jit(solution)/shard_map/ppermute | solution.py:660
  28.6 7.6 %collective-permute-start.10 = (bf16[32,2176]{1,0:T(8,128)(2,1)S(1)}, bf16[32,2176]{1,0:T(8,128)(2,1)S(1)}, u32[]{:S(2)}, u32[]{:S(2)}) collective-permute-start(bf16[32,2176]{1,0:T(8,128)(2,1)S(1)} %get-tuple-element.60), channel_id=1, source_target_pairs={{0,8},{1,9},{2,10},{3,11},{4,12},{5,13},{6,14},{7,15},{8,0},{9,1},... | collective-permute-start | bytes 417800 | tf_op jit(solution)/shard_map/ppermute | solution.py:660
  30.3 17.8 %collective-permute-start.16 = (bf16[72,2176]{1,0:T(8,128)(2,1)S(1)}, bf16[72,2176]{1,0:T(8,128)(2,1)S(1)}, u32[]{:S(2)}, u32[]{:S(2)}) collective-permute-start(bf16[72,2176]{1,0:T(8,128)(2,1)S(1)} %get-tuple-element.68), channel_id=1, source_target_pairs={{0,1},{1,0},{2,3},{3,2},{4,5},{5,4},{6,7},{7,6},{8,9},{9,8},{10,11... | collective-permute-start | bytes 940040 | tf_op jit(solution)/shard_map/ppermute | solution.py:660
  31.9 11.7 %collective-permute-start.11 = (bf16[32,2176]{1,0:T(8,128)(2,1)S(1)}, bf16[32,2176]{1,0:T(8,128)(2,1)S(1)}, u32[]{:S(2)}, u32[]{:S(2)}) collective-permute-start(bf16[32,2176]{1,0:T(8,128)(2,1)S(1)} %get-tuple-element.60), channel_id=1, source_target_pairs={{0,16},{1,17},{2,18},{3,19},{4,20},{5,21},{6,22},{7,23},{8,24},{9,... | collective-permute-start | bytes 417800 | tf_op jit(solution)/shard_map/ppermute | solution.py:660
  33.4 10.2 %collective-permute-start.12 = (bf16[32,2176]{1,0:T(8,128)(2,1)S(1)}, bf16[32,2176]{1,0:T(8,128)(2,1)S(1)}, u32[]{:S(2)}, u32[]{:S(2)}) collective-permute-start(bf16[32,2176]{1,0:T(8,128)(2,1)S(1)} %get-tuple-element.60), channel_id=1, source_target_pairs={{0,24},{1,25},{2,26},{3,27},{4,28},{5,29},{6,30},{7,31},{8,16},{9,... | collective-permute-start | bytes 417800 | tf_op jit(solution)/shard_map/ppermute | solution.py:660
  34.7 16.6 %collective-permute-start.18 = (bf16[72,2176]{1,0:T(8,128)(2,1)S(1)}, bf16[72,2176]{1,0:T(8,128)(2,1)S(1)}, u32[]{:S(2)}, u32[]{:S(2)}) collective-permute-start(bf16[72,2176]{1,0:T(8,128)(2,1)S(1)} %get-tuple-element.68), channel_id=1, source_target_pairs={{0,4},{1,5},{2,6},{3,7},{4,0},{5,1},{6,2},{7,3},{8,12},{9,13},{10,... | collective-permute-start | bytes 940040 | tf_op jit(solution)/shard_map/ppermute | solution.py:660
  36.2 18.9 %collective-permute-start.20 = (bf16[72,2176]{1,0:T(8,128)(2,1)S(1)}, bf16[72,2176]{1,0:T(8,128)(2,1)S(1)}, u32[]{:S(2)}, u32[]{:S(2)}) collective-permute-start(bf16[72,2176]{1,0:T(8,128)(2,1)S(1)} %get-tuple-element.68), channel_id=1, source_target_pairs={{0,5},{1,4},{2,7},{3,6},{4,1},{5,0},{6,3},{7,2},{8,13},{9,12},{10,... | collective-permute-start | bytes 940040 | tf_op jit(solution)/shard_map/ppermute | solution.py:660
  45.9 14.3 %collective-permute-start.13 = (bf16[32,2048]{1,0:T(8,128)(2,1)S(1)}, bf16[32,2048]{1,0:T(8,128)(2,1)S(1)}, u32[]{:S(2)}, u32[]{:S(2)}) collective-permute-start(bf16[32,2048]{1,0:T(8,128)(2,1)S(1)} %get-tuple-element.64), channel_id=1, source_target_pairs={{0,8},{1,9},{2,10},{3,11},{4,12},{5,13},{6,14},{7,15},{8,0},{9,1},... | collective-permute-start | bytes 393224 | tf_op jit(solution)/shard_map/ppermute | solution.py:660
  50.5 21.2 %collective-permute-start.17 = (bf16[72,2048]{1,0:T(8,128)(2,1)S(1)}, bf16[72,2048]{1,0:T(8,128)(2,1)S(1)}, u32[]{:S(2)}, u32[]{:S(2)}) collective-permute-start(bf16[72,2048]{1,0:T(8,128)(2,1)S(1)} %piece_rows.5), channel_id=1, source_target_pairs={{0,1},{1,0},{2,3},{3,2},{4,5},{5,4},{6,7},{7,6},{8,9},{9,8},{10,11... | collective-permute-start | bytes 884744 | tf_op jit(solution)/shard_map/ppermute | solution.py:660
  53.7 19.5 %collective-permute-start.19 = (bf16[72,2048]{1,0:T(8,128)(2,1)S(1)}, bf16[72,2048]{1,0:T(8,128)(2,1)S(1)}, u32[]{:S(2)}, u32[]{:S(2)}) collective-permute-start(bf16[72,2048]{1,0:T(8,128)(2,1)S(1)} %piece_rows.6), channel_id=1, source_target_pairs={{0,4},{1,5},{2,6},{3,7},{4,0},{5,1},{6,2},{7,3},{8,12},{9,13},{10,... | collective-permute-start | bytes 884744 | tf_op jit(solution)/shard_map/ppermute | solution.py:660
  57.5 15.7 %collective-permute-start.21 = (bf16[72,2048]{1,0:T(8,128)(2,1)S(1)}, bf16[72,2048]{1,0:T(8,128)(2,1)S(1)}, u32[]{:S(2)}, u32[]{:S(2)}) collective-permute-start(bf16[72,2048]{1,0:T(8,128)(2,1)S(1)} %piece_rows.7), channel_id=1, source_target_pairs={{0,5},{1,4},{2,7},{3,6},{4,1},{5,0},{6,3},{7,2},{8,13},{9,12},{10,... | collective-permute-start | bytes 884744 | tf_op jit(solution)/shard_map/ppermute | solution.py:660
  58.9 10.5 %collective-permute-start.14 = (bf16[32,2048]{1,0:T(8,128)(2,1)S(1)}, bf16[32,2048]{1,0:T(8,128)(2,1)S(1)}, u32[]{:S(2)}, u32[]{:S(2)}) collective-permute-start(bf16[32,2048]{1,0:T(8,128)(2,1)S(1)} %get-tuple-element.65), channel_id=1, source_target_pairs={{0,16},{1,17},{2,18},{3,19},{4,20},{5,21},{6,22},{7,23},{8,24},{9,... | collective-permute-start | bytes 393224 | tf_op jit(solution)/shard_map/ppermute | solution.py:660
  60.2 9.2 %collective-permute-start.15 = (bf16[32,2048]{1,0:T(8,128)(2,1)S(1)}, bf16[32,2048]{1,0:T(8,128)(2,1)S(1)}, u32[]{:S(2)}, u32[]{:S(2)}) collective-permute-start(bf16[32,2048]{1,0:T(8,128)(2,1)S(1)} %get-tuple-element.66), channel_id=1, source_target_pairs={{0,24},{1,25},{2,26},{3,27},{4,28},{5,29},{6,30},{7,31},{8,16},{9,... | collective-permute-start | bytes 393224 | tf_op jit(solution)/shard_map/ppermute | solution.py:660
  69.6 15.7 %copy-start = (f32[2048]{0:T(1024)S(1)}, f32[2048]{0:T(1024)}, u32[]{:S(2)}) copy-start(f32[2048]{0:T(1024)} %param.29) | copy-start | bytes 24580
  69.6 7.3 %collective-permute-start.25 = (bf16[32,2048]{1,0:T(8,128)(2,1)S(1)}, bf16[32,2048]{1,0:T(8,128)(2,1)S(1)}, u32[]{:S(2)}, u32[]{:S(2)}) collective-permute-start(bf16[32,2048]{1,0:T(8,128)(2,1)S(1)} %get-tuple-element.72), channel_id=1, source_target_pairs={{0,1},{1,0},{2,3},{3,2},{4,5},{5,4},{6,7},{7,6},{8,9},{9,8},{10,11... | collective-permute-start | bytes 393224 | tf_op jit(solution)/shard_map/ppermute | solution.py:660
  70.2 8.1 %collective-permute-start.26 = (bf16[32,2048]{1,0:T(8,128)(2,1)S(1)}, bf16[32,2048]{1,0:T(8,128)(2,1)S(1)}, u32[]{:S(2)}, u32[]{:S(2)}) collective-permute-start(bf16[32,2048]{1,0:T(8,128)(2,1)S(1)} %get-tuple-element.73), channel_id=1, source_target_pairs={{0,4},{1,5},{2,6},{3,7},{4,0},{5,1},{6,2},{7,3},{8,12},{9,13},{10,... | collective-permute-start | bytes 393224 | tf_op jit(solution)/shard_map/ppermute | solution.py:660
  71.7 6.5 %collective-permute-start.27 = (bf16[32,2048]{1,0:T(8,128)(2,1)S(1)}, bf16[32,2048]{1,0:T(8,128)(2,1)S(1)}, u32[]{:S(2)}, u32[]{:S(2)}) collective-permute-start(bf16[32,2048]{1,0:T(8,128)(2,1)S(1)} %get-tuple-element.74), channel_id=1, source_target_pairs={{0,5},{1,4},{2,7},{3,6},{4,1},{5,0},{6,3},{7,2},{8,13},{9,12},{10,... | collective-permute-start | bytes 393224 | tf_op jit(solution)/shard_map/ppermute | solution.py:660
  73.3 6.1 %collective-permute-start.22 = (bf16[24,2048]{1,0:T(8,128)(2,1)S(1)}, bf16[24,2048]{1,0:T(8,128)(2,1)S(1)}, u32[]{:S(2)}, u32[]{:S(2)}) collective-permute-start(bf16[24,2048]{1,0:T(8,128)(2,1)S(1)} %get-tuple-element.69), channel_id=1, source_target_pairs={{0,8},{1,9},{2,10},{3,11},{4,12},{5,13},{6,14},{7,15},{8,0},{9,1},... | collective-permute-start | bytes 294920 | tf_op jit(solution)/shard_map/ppermute | solution.py:660
  75.8 9.5 %collective-permute-start.23 = (bf16[24,2048]{1,0:T(8,128)(2,1)S(1)}, bf16[24,2048]{1,0:T(8,128)(2,1)S(1)}, u32[]{:S(2)}, u32[]{:S(2)}) collective-permute-start(bf16[24,2048]{1,0:T(8,128)(2,1)S(1)} %get-tuple-element.70), channel_id=1, source_target_pairs={{0,16},{1,17},{2,18},{3,19},{4,20},{5,21},{6,22},{7,23},{8,24},{9,... | collective-permute-start | bytes 294920 | tf_op jit(solution)/shard_map/ppermute | solution.py:660
  76.9 8.4 %collective-permute-start.24 = (bf16[24,2048]{1,0:T(8,128)(2,1)S(1)}, bf16[24,2048]{1,0:T(8,128)(2,1)S(1)}, u32[]{:S(2)}, u32[]{:S(2)}) collective-permute-start(bf16[24,2048]{1,0:T(8,128)(2,1)S(1)} %get-tuple-element.71), channel_id=1, source_target_pairs={{0,24},{1,25},{2,26},{3,27},{4,28},{5,29},{6,30},{7,31},{8,16},{9,... | collective-permute-start | bytes 294920 | tf_op jit(solution)/shard_map/ppermute | solution.py:660

commit v4 on v3

--- a/solution.py
+++ b/solution.py
@@ -536,23 +536,25 @@
 def piece_kernel(count, group_ref, *refs):
     pieces, (w0_ref, w1_ref, down_ref) = refs[:count], refs[count : count + 3]
     outs, (x_ref, h_ref) = refs[count + 3 : 2 * count + 3], refs[2 * count + 3 :]
-    height = pieces[0].shape[0]
-    for i, piece in enumerate(pieces):
-        x_ref[i * height : (i + 1) * height, :] = piece[...]
-    at = count * height
+    at = 0
+    for piece in pieces:
+        x_ref[at : at + piece.shape[0], :] = piece[...]
+        at += piece.shape[0]
     if at < x_ref.shape[0]:
         x_ref[at:, :] = jnp.zeros((x_ref.shape[0] - at, x_ref.shape[1]), jnp.bfloat16)
     hidden_units(group_ref, x_ref, (w0_ref, w1_ref), h_ref, lambda e: None)
     for col in range(0, down_ref.shape[1], DOWN_BLOCK):
         cols = slice(col, col + DOWN_BLOCK)
         down = jnp.dot(h_ref[...], down_ref[:, cols], preferred_element_type=jnp.float32)
-        for i, out in enumerate(outs):
-            out[:, cols] = down[i * height : (i + 1) * height].astype(jnp.bfloat16)
+        at = 0
+        for out in outs:
+            out[:, cols] = down[at : at + out.shape[0]].astype(jnp.bfloat16)
+            at += out.shape[0]
 
 
 def piece_rows(group, pieces, w0, w1, down):
     count = len(pieces)
-    height = count * pieces[0].shape[0]
+    height = sum(piece.shape[0] for piece in pieces)
     padded = -(-height // 16) * 16
     width, hidden = w0.shape[0], w0.shape[1] // 2
     return pl.pallas_call(
@@ -696,8 +698,8 @@
     z_pieces = swap_z((onward_z,) * 3)
     plane_pieces = swap_plane((onward_plane,) * 3)
     near, w0, w1, down = near_rows(group, plane_rows, z_rows, weights, partner_weights)
-    z_parts = piece_rows(group, z_pieces, w0, w1, down)
-    plane_parts = tuple(piece_rows(group, (piece,), w0, w1, down)[0] for piece in plane_pieces)
+    parts = piece_rows(group, z_pieces + plane_pieces, w0, w1, down)
+    z_parts, plane_parts = parts[:3], parts[3:]
     own, *near_sums = column_sum(near, swap_z(z_parts), half)
     far_sums = plane_sum(near, swap_plane(plane_parts))
     last_z, last_plane = barrier(swap_z(far_sums), swap_plane(near_sums))

time: 86.3 us -> 82.9 us (0.961)
  Pallas kernels: 20.5 us -> 14.9 us
  waiting for transfers between devices: 26 us -> 29.8 us
  starting transfers between devices: 38.3 us -> 36.6 us
    pallas_call x4 -> x1, Pallas kernels: 9.4 us -> 3.8 us  [piece_rows(): pl.pallas_call(functools.partial(piece_kernel, count), out_shape=tuple((j...]
    ppermute x28, waiting for transfers between devices: 26 us -> 29.8 us  [swap(): return lax.ppermute(value, ALL, pairs)]
    ppermute x28, starting transfers between devices: 38.3 us -> 36.6 us  [swap(): return lax.ppermute(value, ALL, pairs)]
  transfers between devices with their start and end apart: 28 -> 28, of which waited for: 6 -> 7; matrix products, arithmetic and copies ran while one was open for 0% -> 0% of each run, Pallas kernels for 23% -> 12%
where the time goes in v4:
time: 82.9 us; the launch traced here: 82.7 us
  starting transfers between devices  36.6 us (44%)
  waiting for transfers between devices  29.8 us (36%)
  Pallas kernels  14.9 us (18%)
  local copies, waits for them, and re-layouts  1.19 us (1%)
    ppermute x28, starting transfers between devices, swap(): return lax.ppermute(value, ALL, pairs)  36.6 us
    ppermute x28, waiting for transfers between devices, swap(): return lax.ppermute(value, ALL, pairs)  29.8 us
    pallas_call x1, Pallas kernels, near_rows(): pl.pallas_call(near_kernel, out_shape=(jax.ShapeDtypeStruct((height, widt...  5.43 us
    pallas_call x1, Pallas kernels, attention_terms(): pl.pallas_call(attention_kernel, out_shape=(jax.ShapeDtypeStruct((half, w...  4.33 us
    pallas_call x1, Pallas kernels, piece_rows(): pl.pallas_call(functools.partial(piece_kernel, count), out_shape=tuple((j...  3.8 us
  transfers between devices with their start and end apart: 28, of which 7 were waited for; matrix products, arithmetic and copies ran while one was open for 0% of the time, Pallas kernels for 12%

profile of v4, /device:TPU:0, one launch (start us, length us, event | category | flops | bytes accessed | tf_op | source)
XLA Modules:
  0.0 82.7 jit_solution(18237278572044093587)
XLA Ops:
  1.0 4.3 %attention_terms.1 = (f32[32,2048]{1,0:T(8,128)S(1)}, bf16[32,2048]{1,0:T(8,128)(2,1)S(1)}, bf16[32,128]{1,0:T(8,128)(2,1)S(1)}) custom-call(s32[4,9]{1,0:T(4,128)} %bitcast.21, s32[9]{0:T(128)} %lengths_ref.1, s32[1]{0:T(128)} %bitcast.1.tp_ref, s32[16]{0:T(128)} %home_ref.1, bf16[64,1024]{1,0:T(8,128)(2,1)} %q_hbm.1, bf16[64,512]{1,0:T(8,128)(2,1)} %fresh_hbm.1, ...), custom_call_target="tpu_custom_call" | custom-call | tf_op jit(solution)/shard_map/attention_terms/pallas_call | solution.py:364
  5.3 2.6 %collective-permute-start = (bf16[32,2048]{1,0:T(8,128)(2,1)S(1)}, bf16[32,2048]{1,0:T(8,128)(2,1)S(1)}, u32[]{:S(2)}, u32[]{:S(2)}) collective-permute-start(bf16[32,2048]{1,0:T(8,128)(2,1)S(1)} %get-tuple-element.47), channel_id=1, source_target_pairs={{0,1},{1,0},{2,3},{3,2},{4,5},{5,4},{6,7},{7,6},{8,9},{9,8},{10,11... | collective-permute-start | bytes 393224 | tf_op jit(solution)/shard_map/ppermute | solution.py:662
  7.9 4.2 %collective-permute-done.got_ref = bf16[32,2048]{1,0:T(8,128)(2,1)S(1)} collective-permute-done((bf16[32,2048]{1,0:T(8,128)(2,1)S(1)}, bf16[32,2048]{1,0:T(8,128)(2,1)S(1)}, u32[]{:S(2)}, u32[]{:S(2)}) %collective-permute-start) | collective-permute-done | bytes 131104 | tf_op jit(solution)/shard_map/ppermute | solution.py:662
  12.1 1.2 %copy-done.2 = bf16[2048,384]{1,0:T(8,128)(2,1)} copy-done((bf16[2048,384]{1,0:T(8,128)(2,1)}, bf16[2048,384]{1,0:T(8,128)(2,1)S(1)}, u32[]{:S(2)}) %copy-start.2) | copy-done | bytes 1572888
  13.4 1.9 %collective-permute-start.4 = (bf16[24,2176]{1,0:T(8,128)(2,1)S(1)}, bf16[24,2176]{1,0:T(8,128)(2,1)S(1)}, u32[]{:S(2)}, u32[]{:S(2)}) collective-permute-start(bf16[24,2176]{1,0:T(8,128)(2,1)S(1)} %get-tuple-element.52), channel_id=1, source_target_pairs={{0,8},{1,9},{2,10},{3,11},{4,12},{5,13},{6,14},{7,15},{8,0},{9,1},... | collective-permute-start | bytes 313352 | tf_op jit(solution)/shard_map/ppermute | solution.py:662
  15.3 1.5 %collective-permute-start.7 = (bf16[32,2176]{1,0:T(8,128)(2,1)S(1)}, bf16[32,2176]{1,0:T(8,128)(2,1)S(1)}, u32[]{:S(2)}, u32[]{:S(2)}) collective-permute-start(bf16[32,2176]{1,0:T(8,128)(2,1)S(1)} %get-tuple-element.51.r0), channel_id=1, source_target_pairs={{0,1},{1,0},{2,3},{3,2},{4,5},{5,4},{6,7},{7,6},{8,9},{9,8},{10,11... | collective-permute-start | bytes 417800 | tf_op jit(solution)/shard_map/ppermute | solution.py:662
  16.8 1.5 %collective-permute-start.8 = (bf16[32,2176]{1,0:T(8,128)(2,1)S(1)}, bf16[32,2176]{1,0:T(8,128)(2,1)S(1)}, u32[]{:S(2)}, u32[]{:S(2)}) collective-permute-start(bf16[32,2176]{1,0:T(8,128)(2,1)S(1)} %get-tuple-element.51.r0), channel_id=1, source_target_pairs={{0,4},{1,5},{2,6},{3,7},{4,0},{5,1},{6,2},{7,3},{8,12},{9,13},{10,... | collective-permute-start | bytes 417800 | tf_op jit(solution)/shard_map/ppermute | solution.py:662
  18.8 2.6 %collective-permute-start.5 = (bf16[24,2176]{1,0:T(8,128)(2,1)S(1)}, bf16[24,2176]{1,0:T(8,128)(2,1)S(1)}, u32[]{:S(2)}, u32[]{:S(2)}) collective-permute-start(bf16[24,2176]{1,0:T(8,128)(2,1)S(1)} %get-tuple-element.52), channel_id=1, source_target_pairs={{0,16},{1,17},{2,18},{3,19},{4,20},{5,21},{6,22},{7,23},{8,24},{9,... | collective-permute-start | bytes 313352 | tf_op jit(solution)/shard_map/ppermute | solution.py:662
  22.0 6.6 %collective-permute-done.5.z2 = bf16[24,2176]{1,0:T(8,128)(2,1)S(1)} collective-permute-done((bf16[24,2176]{1,0:T(8,128)(2,1)S(1)}, bf16[24,2176]{1,0:T(8,128)(2,1)S(1)}, u32[]{:S(2)}, u32[]{:S(2)}) %collective-permute-start.5) | collective-permute-done | bytes 104480 | tf_op jit(solution)/shard_map/ppermute | solution.py:662
  28.6 1.7 %collective-permute-start.10 = (bf16[32,2176]{1,0:T(8,128)(2,1)S(1)}, bf16[32,2176]{1,0:T(8,128)(2,1)S(1)}, u32[]{:S(2)}, u32[]{:S(2)}) collective-permute-start(bf16[32,2176]{1,0:T(8,128)(2,1)S(1)} %get-tuple-element.63), channel_id=1, source_target_pairs={{0,8},{1,9},{2,10},{3,11},{4,12},{5,13},{6,14},{7,15},{8,0},{9,1},... | collective-permute-start | bytes 417800 | tf_op jit(solution)/shard_map/ppermute | solution.py:662
  30.3 1.5 %collective-permute-start.13 = (bf16[72,2176]{1,0:T(8,128)(2,1)S(1)}, bf16[72,2176]{1,0:T(8,128)(2,1)S(1)}, u32[]{:S(2)}, u32[]{:S(2)}) collective-permute-start(bf16[72,2176]{1,0:T(8,128)(2,1)S(1)} %get-tuple-element.64), channel_id=1, source_target_pairs={{0,1},{1,0},{2,3},{3,2},{4,5},{5,4},{6,7},{7,6},{8,9},{9,8},{10,11... | collective-permute-start | bytes 940040 | tf_op jit(solution)/shard_map/ppermute | solution.py:662
  31.9 1.5 %collective-permute-start.14 = (bf16[72,2176]{1,0:T(8,128)(2,1)S(1)}, bf16[72,2176]{1,0:T(8,128)(2,1)S(1)}, u32[]{:S(2)}, u32[]{:S(2)}) collective-permute-start(bf16[72,2176]{1,0:T(8,128)(2,1)S(1)} %get-tuple-element.64), channel_id=1, source_target_pairs={{0,4},{1,5},{2,6},{3,7},{4,0},{5,1},{6,2},{7,3},{8,12},{9,13},{10,... | collective-permute-start | bytes 940040 | tf_op jit(solution)/shard_map/ppermute | solution.py:662
  33.9 1.5 %collective-permute-start.11 = (bf16[32,2176]{1,0:T(8,128)(2,1)S(1)}, bf16[32,2176]{1,0:T(8,128)(2,1)S(1)}, u32[]{:S(2)}, u32[]{:S(2)}) collective-permute-start(bf16[32,2176]{1,0:T(8,128)(2,1)S(1)} %get-tuple-element.63), channel_id=1, source_target_pairs={{0,16},{1,17},{2,18},{3,19},{4,20},{5,21},{6,22},{7,23},{8,24},{9,... | collective-permute-start | bytes 417800 | tf_op jit(solution)/shard_map/ppermute | solution.py:662
  35.4 1.3 %collective-permute-start.12 = (bf16[32,2176]{1,0:T(8,128)(2,1)S(1)}, bf16[32,2176]{1,0:T(8,128)(2,1)S(1)}, u32[]{:S(2)}, u32[]{:S(2)}) collective-permute-start(bf16[32,2176]{1,0:T(8,128)(2,1)S(1)} %get-tuple-element.63), channel_id=1, source_target_pairs={{0,24},{1,25},{2,26},{3,27},{4,28},{5,29},{6,30},{7,31},{8,16},{9,... | collective-permute-start | bytes 417800 | tf_op jit(solution)/shard_map/ppermute | solution.py:662
  36.7 5.4 %near_rows.1 = (f32[200,2048]{1,0:T(8,128)S(1)}, bf16[2048,768]{1,0:T(8,128)(2,1)S(1)}, bf16[2048,768]{1,0:T(8,128)(2,1)S(1)}, bf16[768,2048]{1,0:T(8,128)(2,1)S(1)}) custom-call(s32[3]{0:T(128)S(1)} %pad_add_fusion.group_ref, bf16[32,2176]{1,0:T(8,128)(2,1)S(1)} %get-tuple-element.51.r0, bf16[32,2176]{1,0:T(8,128)(2,1)S(1)} %collective-permute-done.7.r1, ...), custom_call_target="tpu_custom_call" | custom-call | flops 1887436800 | bytes 9437184 | tf_op jit(solution)/shard_map/near_rows/pallas_call | solution.py:515
  42.2 2.9 %collective-permute-done.11.refs_1_ = bf16[32,2176]{1,0:T(8,128)(2,1)S(1)} collective-permute-done((bf16[32,2176]{1,0:T(8,128)(2,1)S(1)}, bf16[32,2176]{1,0:T(8,128)(2,1)S(1)}, u32[]{:S(2)}, u32[]{:S(2)}) %collective-permute-start.11) | collective-permute-done | bytes 139296 | tf_op jit(solution)/shard_map/ppermute | solution.py:662
  45.8 3.8 %piece_rows.1 = (bf16[32,2048]{1,0:T(8,128)(2,1)S(1)}, bf16[32,2048]{1,0:T(8,128)(2,1)S(1)}, bf16[32,2048]{1,0:T(8,128)(2,1)S(1)}, bf16[72,2048]{1,0:T(8,128)(2,...) custom-call(s32[3]{0:T(128)S(1)} %pad_add_fusion.group_ref, ...), custom_call_target="tpu_custom_call" | custom-call | flops 2944401408 | bytes 9437184 | tf_op jit(solution)/shard_map/piece_rows/pallas_call | solution.py:560
  49.6 1.7 %collective-permute-start.16 = (bf16[32,2048]{1,0:T(8,128)(2,1)S(1)}, bf16[32,2048]{1,0:T(8,128)(2,1)S(1)}, u32[]{:S(2)}, u32[]{:S(2)}) collective-permute-start(bf16[32,2048]{1,0:T(8,128)(2,1)S(1)} %get-tuple-element.68), channel_id=1, source_target_pairs={{0,8},{1,9},{2,10},{3,11},{4,12},{5,13},{6,14},{7,15},{8,0},{9,1},... | collective-permute-start | bytes 393224 | tf_op jit(solution)/shard_map/ppermute | solution.py:662
  51.3 1.3 %collective-permute-start.19 = (bf16[72,2048]{1,0:T(8,128)(2,1)S(1)}, bf16[72,2048]{1,0:T(8,128)(2,1)S(1)}, u32[]{:S(2)}, u32[]{:S(2)}) collective-permute-start(bf16[72,2048]{1,0:T(8,128)(2,1)S(1)} %get-tuple-element.72), channel_id=1, source_target_pairs={{0,1},{1,0},{2,3},{3,2},{4,5},{5,4},{6,7},{7,6},{8,9},{9,8},{10,11... | collective-permute-start | bytes 884744 | tf_op jit(solution)/shard_map/ppermute | solution.py:662
  52.6 1.5 %collective-permute-start.20 = (bf16[72,2048]{1,0:T(8,128)(2,1)S(1)}, bf16[72,2048]{1,0:T(8,128)(2,1)S(1)}, u32[]{:S(2)}, u32[]{:S(2)}) collective-permute-start(bf16[72,2048]{1,0:T(8,128)(2,1)S(1)} %get-tuple-element.73), channel_id=1, source_target_pairs={{0,4},{1,5},{2,6},{3,7},{4,0},{5,1},{6,2},{7,3},{8,12},{9,13},{10,... | collective-permute-start | bytes 884744 | tf_op jit(solution)/shard_map/ppermute | solution.py:662
  54.8 1.7 %collective-permute-start.17 = (bf16[32,2048]{1,0:T(8,128)(2,1)S(1)}, bf16[32,2048]{1,0:T(8,128)(2,1)S(1)}, u32[]{:S(2)}, u32[]{:S(2)}) collective-permute-start(bf16[32,2048]{1,0:T(8,128)(2,1)S(1)} %get-tuple-element.69), channel_id=1, source_target_pairs={{0,16},{1,17},{2,18},{3,19},{4,20},{5,21},{6,22},{7,23},{8,24},{9,... | collective-permute-start | bytes 393224 | tf_op jit(solution)/shard_map/ppermute | solution.py:662
  56.5 1.0 %collective-permute-start.18 = (bf16[32,2048]{1,0:T(8,128)(2,1)S(1)}, bf16[32,2048]{1,0:T(8,128)(2,1)S(1)}, u32[]{:S(2)}, u32[]{:S(2)}) collective-permute-start(bf16[32,2048]{1,0:T(8,128)(2,1)S(1)} %get-tuple-element.70), channel_id=1, source_target_pairs={{0,24},{1,25},{2,26},{3,27},{4,28},{5,29},{6,30},{7,31},{8,16},{9,... | collective-permute-start | bytes 393224 | tf_op jit(solution)/shard_map/ppermute | solution.py:662
  57.5 8.4 %collective-permute-done.17.g2 = bf16[32,2048]{1,0:T(8,128)(2,1)S(1)} collective-permute-done((bf16[32,2048]{1,0:T(8,128)(2,1)S(1)}, bf16[32,2048]{1,0:T(8,128)(2,1)S(1)}, u32[]{:S(2)}, u32[]{:S(2)}) %collective-permute-start.17) | collective-permute-done | bytes 131104 | tf_op jit(solution)/shard_map/ppermute | solution.py:662
  66.0 1.3 %collective-permute-start.25 = (bf16[32,2048]{1,0:T(8,128)(2,1)S(1)}, bf16[32,2048]{1,0:T(8,128)(2,1)S(1)}, u32[]{:S(2)}, u32[]{:S(2)}) collective-permute-start(bf16[32,2048]{1,0:T(8,128)(2,1)S(1)} %get-tuple-element.78), channel_id=1, source_target_pairs={{0,1},{1,0},{2,3},{3,2},{4,5},{5,4},{6,7},{7,6},{8,9},{9,8},{10,11... | collective-permute-start | bytes 393224 | tf_op jit(solution)/shard_map/ppermute | solution.py:662
  67.3 1.5 %collective-permute-start.26 = (bf16[32,2048]{1,0:T(8,128)(2,1)S(1)}, bf16[32,2048]{1,0:T(8,128)(2,1)S(1)}, u32[]{:S(2)}, u32[]{:S(2)}) collective-permute-start(bf16[32,2048]{1,0:T(8,128)(2,1)S(1)} %get-tuple-element.79), channel_id=1, source_target_pairs={{0,4},{1,5},{2,6},{3,7},{4,0},{5,1},{6,2},{7,3},{8,12},{9,13},{10,... | collective-permute-start | bytes 393224 | tf_op jit(solution)/shard_map/ppermute | solution.py:662
  68.9 0.7 collective-permute-start.27
  69.7 2.0 %collective-permute-start.22 = (bf16[24,2048]{1,0:T(8,128)(2,1)S(1)}, bf16[24,2048]{1,0:T(8,128)(2,1)S(1)}, u32[]{:S(2)}, u32[]{:S(2)}) collective-permute-start(bf16[24,2048]{1,0:T(8,128)(2,1)S(1)} %get-tuple-element.75), channel_id=1, source_target_pairs={{0,8},{1,9},{2,10},{3,11},{4,12},{5,13},{6,14},{7,15},{8,0},{9,1},... | collective-permute-start | bytes 294920 | tf_op jit(solution)/shard_map/ppermute | solution.py:662
  71.8 1.5 %collective-permute-start.23 = (bf16[24,2048]{1,0:T(8,128)(2,1)S(1)}, bf16[24,2048]{1,0:T(8,128)(2,1)S(1)}, u32[]{:S(2)}, u32[]{:S(2)}) collective-permute-start(bf16[24,2048]{1,0:T(8,128)(2,1)S(1)} %get-tuple-element.76), channel_id=1, source_target_pairs={{0,16},{1,17},{2,18},{3,19},{4,20},{5,21},{6,22},{7,23},{8,24},{9,... | collective-permute-start | bytes 294920 | tf_op jit(solution)/shard_map/ppermute | solution.py:662
  73.3 1.4 %collective-permute-start.24 = (bf16[24,2048]{1,0:T(8,128)(2,1)S(1)}, bf16[24,2048]{1,0:T(8,128)(2,1)S(1)}, u32[]{:S(2)}, u32[]{:S(2)}) collective-permute-start(bf16[24,2048]{1,0:T(8,128)(2,1)S(1)} %get-tuple-element.77), channel_id=1, source_target_pairs={{0,24},{1,25},{2,26},{3,27},{4,28},{5,29},{6,30},{7,31},{8,16},{9,... | collective-permute-start | bytes 294920 | tf_op jit(solution)/shard_map/ppermute | solution.py:662
  74.7 0.7 collective-permute-done.22.z1
  75.5 6.3 %collective-permute-done.23.z2 = bf16[24,2048]{1,0:T(8,128)(2,1)S(1)} collective-permute-done((bf16[24,2048]{1,0:T(8,128)(2,1)S(1)}, bf16[24,2048]{1,0:T(8,128)(2,1)S(1)}, u32[]{:S(2)}, u32[]{:S(2)}) %collective-permute-start.23) | collective-permute-done | bytes 98336 | tf_op jit(solution)/shard_map/ppermute | solution.py:662
  81.8 0.9 %final_rows.1 = bf16[32,2048]{1,0:T(8,128)(2,1)} custom-call(f32[32,2048]{1,0:T(8,128)S(1)} %get-tuple-element.50.state_ref, f32[32,2048]{1,0:T(8,128)S(1)} %get-tuple-element.71.own_ref, bf16[32,2048]{1,0:T(8,128)(2,1)S(1)} %collective-permute-done.25.p1, bf16[32,2048]{1,0:T(8,128)(2,1)S(1)} %collective-permute-done.26.p2, ...), custom_call_target="tpu_custom_call" | custom-call | tf_op jit(solution)/shard_map/final_rows/pallas_call | solution.py:639
  (41 shorter events, 4.4 us)
Async XLA Ops:
  0.0 12.0 %collective-permute-start.1 = (bf16[2048,384]{1,0:T(8,128)(2,1)}, bf16[2048,384]{1,0:T(8,128)(2,1)S(1)}, u32[]{:S(2)}, u32[]{:S(2)}) collective-permute-start(bf16[2048,384]{1,0:T(8,128)(2,1)} %bitcast.13), channel_id=1, source_target_pairs={{0,2},{1,3},{2,0},{3,1},{4,6},{5,7},{6,4},{7,5},{8,10},{9,11},{10,... | collective-permute-start | bytes 4718600 | tf_op jit(solution)/shard_map/ppermute | solution.py:662
  0.5 11.6 %collective-permute-start.2 = (bf16[2048,384]{1,0:T(8,128)(2,1)}, bf16[2048,384]{1,0:T(8,128)(2,1)S(1)}, u32[]{:S(2)}, u32[]{:S(2)}) collective-permute-start(bf16[2048,384]{1,0:T(8,128)(2,1)} %bitcast.15), channel_id=1, source_target_pairs={{0,2},{1,3},{2,0},{3,1},{4,6},{5,7},{6,4},{7,5},{8,10},{9,11},{10,... | collective-permute-start | bytes 4718600 | tf_op jit(solution)/shard_map/ppermute | solution.py:662
  0.5 11.5 %collective-permute-start.3 = (bf16[384,2048]{1,0:T(8,128)(2,1)}, bf16[384,2048]{1,0:T(8,128)(2,1)}, u32[]{:S(2)}, u32[]{:S(2)}) collective-permute-start(bf16[384,2048]{1,0:T(8,128)(2,1)} %bitcast.17), channel_id=1, source_target_pairs={{0,2},{1,3},{2,0},{3,1},{4,6},{5,7},{6,4},{7,5},{8,10},{9,11},{10,... | collective-permute-start | bytes 4718600 | tf_op jit(solution)/shard_map/ppermute | solution.py:662
  1.0 12.3 %copy-start.1 = (f32[2048]{0:T(1024)S(1)}, f32[2048]{0:T(1024)}, u32[]{:S(2)}) copy-start(f32[2048]{0:T(1024)} %param.22) | copy-start | bytes 24580
  5.3 6.7 %collective-permute-start = (bf16[32,2048]{1,0:T(8,128)(2,1)S(1)}, bf16[32,2048]{1,0:T(8,128)(2,1)S(1)}, u32[]{:S(2)}, u32[]{:S(2)}) collective-permute-start(bf16[32,2048]{1,0:T(8,128)(2,1)S(1)} %get-tuple-element.47), channel_id=1, source_target_pairs={{0,1},{1,0},{2,3},{3,2},{4,5},{5,4},{6,7},{7,6},{8,9},{9,8},{10,11... | collective-permute-start | bytes 393224 | tf_op jit(solution)/shard_map/ppermute | solution.py:662
  12.0 1.2 %copy-start.2 = (bf16[2048,384]{1,0:T(8,128)(2,1)}, bf16[2048,384]{1,0:T(8,128)(2,1)S(1)}, u32[]{:S(2)}) copy-start(bf16[2048,384]{1,0:T(8,128)(2,1)S(1)} %collective-permute-done.1.wg1) | copy-start | bytes 4718596
  12.0 16.5 %copy-start.3 = (bf16[2048,384]{1,0:T(8,128)(2,1)}, bf16[2048,384]{1,0:T(8,128)(2,1)S(1)}, u32[]{:S(2)}) copy-start(bf16[2048,384]{1,0:T(8,128)(2,1)S(1)} %collective-permute-done.2.wu1) | copy-start | bytes 4718596
  13.4 8.0 %collective-permute-start.4 = (bf16[24,2176]{1,0:T(8,128)(2,1)S(1)}, bf16[24,2176]{1,0:T(8,128)(2,1)S(1)}, u32[]{:S(2)}, u32[]{:S(2)}) collective-permute-start(bf16[24,2176]{1,0:T(8,128)(2,1)S(1)} %get-tuple-element.52), channel_id=1, source_target_pairs={{0,8},{1,9},{2,10},{3,11},{4,12},{5,13},{6,14},{7,15},{8,0},{9,1},... | collective-permute-start | bytes 313352 | tf_op jit(solution)/shard_map/ppermute | solution.py:662
  15.3 13.3 %collective-permute-start.7 = (bf16[32,2176]{1,0:T(8,128)(2,1)S(1)}, bf16[32,2176]{1,0:T(8,128)(2,1)S(1)}, u32[]{:S(2)}, u32[]{:S(2)}) collective-permute-start(bf16[32,2176]{1,0:T(8,128)(2,1)S(1)} %get-tuple-element.51.r0), channel_id=1, source_target_pairs={{0,1},{1,0},{2,3},{3,2},{4,5},{5,4},{6,7},{7,6},{8,9},{9,8},{10,11... | collective-permute-start | bytes 417800 | tf_op jit(solution)/shard_map/ppermute | solution.py:662
  16.8 11.8 %collective-permute-start.8 = (bf16[32,2176]{1,0:T(8,128)(2,1)S(1)}, bf16[32,2176]{1,0:T(8,128)(2,1)S(1)}, u32[]{:S(2)}, u32[]{:S(2)}) collective-permute-start(bf16[32,2176]{1,0:T(8,128)(2,1)S(1)} %get-tuple-element.51.r0), channel_id=1, source_target_pairs={{0,4},{1,5},{2,6},{3,7},{4,0},{5,1},{6,2},{7,3},{8,12},{9,13},{10,... | collective-permute-start | bytes 417800 | tf_op jit(solution)/shard_map/ppermute | solution.py:662
  18.3 10.3 %collective-permute-start.9 = (bf16[32,2176]{1,0:T(8,128)(2,1)S(1)}, bf16[32,2176]{1,0:T(8,128)(2,1)S(1)}, u32[]{:S(2)}, u32[]{:S(2)}) collective-permute-start(bf16[32,2176]{1,0:T(8,128)(2,1)S(1)} %get-tuple-element.51.r0), channel_id=1, source_target_pairs={{0,5},{1,4},{2,7},{3,6},{4,1},{5,0},{6,3},{7,2},{8,13},{9,12},{10,... | collective-permute-start | bytes 417800 | tf_op jit(solution)/shard_map/ppermute | solution.py:662
  18.8 9.8 %collective-permute-start.5 = (bf16[24,2176]{1,0:T(8,128)(2,1)S(1)}, bf16[24,2176]{1,0:T(8,128)(2,1)S(1)}, u32[]{:S(2)}, u32[]{:S(2)}) collective-permute-start(bf16[24,2176]{1,0:T(8,128)(2,1)S(1)} %get-tuple-element.52), channel_id=1, source_target_pairs={{0,16},{1,17},{2,18},{3,19},{4,20},{5,21},{6,22},{7,23},{8,24},{9,... | collective-permute-start | bytes 313352 | tf_op jit(solution)/shard_map/ppermute | solution.py:662
  21.4 7.2 %collective-permute-start.6 = (bf16[24,2176]{1,0:T(8,128)(2,1)S(1)}, bf16[24,2176]{1,0:T(8,128)(2,1)S(1)}, u32[]{:S(2)}, u32[]{:S(2)}) collective-permute-start(bf16[24,2176]{1,0:T(8,128)(2,1)S(1)} %get-tuple-element.52), channel_id=1, source_target_pairs={{0,24},{1,25},{2,26},{3,27},{4,28},{5,29},{6,30},{7,31},{8,16},{9,... | collective-permute-start | bytes 313352 | tf_op jit(solution)/shard_map/ppermute | solution.py:662
  28.6 6.8 %collective-permute-start.10 = (bf16[32,2176]{1,0:T(8,128)(2,1)S(1)}, bf16[32,2176]{1,0:T(8,128)(2,1)S(1)}, u32[]{:S(2)}, u32[]{:S(2)}) collective-permute-start(bf16[32,2176]{1,0:T(8,128)(2,1)S(1)} %get-tuple-element.63), channel_id=1, source_target_pairs={{0,8},{1,9},{2,10},{3,11},{4,12},{5,13},{6,14},{7,15},{8,0},{9,1},... | collective-permute-start | bytes 417800 | tf_op jit(solution)/shard_map/ppermute | solution.py:662
  30.3 14.7 %collective-permute-start.13 = (bf16[72,2176]{1,0:T(8,128)(2,1)S(1)}, bf16[72,2176]{1,0:T(8,128)(2,1)S(1)}, u32[]{:S(2)}, u32[]{:S(2)}) collective-permute-start(bf16[72,2176]{1,0:T(8,128)(2,1)S(1)} %get-tuple-element.64), channel_id=1, source_target_pairs={{0,1},{1,0},{2,3},{3,2},{4,5},{5,4},{6,7},{7,6},{8,9},{9,8},{10,11... | collective-permute-start | bytes 940040 | tf_op jit(solution)/shard_map/ppermute | solution.py:662
  31.9 13.9 %collective-permute-start.14 = (bf16[72,2176]{1,0:T(8,128)(2,1)S(1)}, bf16[72,2176]{1,0:T(8,128)(2,1)S(1)}, u32[]{:S(2)}, u32[]{:S(2)}) collective-permute-start(bf16[72,2176]{1,0:T(8,128)(2,1)S(1)} %get-tuple-element.64), channel_id=1, source_target_pairs={{0,4},{1,5},{2,6},{3,7},{4,0},{5,1},{6,2},{7,3},{8,12},{9,13},{10,... | collective-permute-start | bytes 940040 | tf_op jit(solution)/shard_map/ppermute | solution.py:662
  33.4 12.4 %collective-permute-start.15 = (bf16[72,2176]{1,0:T(8,128)(2,1)S(1)}, bf16[72,2176]{1,0:T(8,128)(2,1)S(1)}, u32[]{:S(2)}, u32[]{:S(2)}) collective-permute-start(bf16[72,2176]{1,0:T(8,128)(2,1)S(1)} %get-tuple-element.64), channel_id=1, source_target_pairs={{0,5},{1,4},{2,7},{3,6},{4,1},{5,0},{6,3},{7,2},{8,13},{9,12},{10,... | collective-permute-start | bytes 940040 | tf_op jit(solution)/shard_map/ppermute | solution.py:662
  33.9 11.1 %collective-permute-start.11 = (bf16[32,2176]{1,0:T(8,128)(2,1)S(1)}, bf16[32,2176]{1,0:T(8,128)(2,1)S(1)}, u32[]{:S(2)}, u32[]{:S(2)}) collective-permute-start(bf16[32,2176]{1,0:T(8,128)(2,1)S(1)} %get-tuple-element.63), channel_id=1, source_target_pairs={{0,16},{1,17},{2,18},{3,19},{4,20},{5,21},{6,22},{7,23},{8,24},{9,... | collective-permute-start | bytes 417800 | tf_op jit(solution)/shard_map/ppermute | solution.py:662
  35.4 9.6 %collective-permute-start.12 = (bf16[32,2176]{1,0:T(8,128)(2,1)S(1)}, bf16[32,2176]{1,0:T(8,128)(2,1)S(1)}, u32[]{:S(2)}, u32[]{:S(2)}) collective-permute-start(bf16[32,2176]{1,0:T(8,128)(2,1)S(1)} %get-tuple-element.63), channel_id=1, source_target_pairs={{0,24},{1,25},{2,26},{3,27},{4,28},{5,29},{6,30},{7,31},{8,16},{9,... | collective-permute-start | bytes 417800 | tf_op jit(solution)/shard_map/ppermute | solution.py:662
  49.6 6.9 %collective-permute-start.16 = (bf16[32,2048]{1,0:T(8,128)(2,1)S(1)}, bf16[32,2048]{1,0:T(8,128)(2,1)S(1)}, u32[]{:S(2)}, u32[]{:S(2)}) collective-permute-start(bf16[32,2048]{1,0:T(8,128)(2,1)S(1)} %get-tuple-element.68), channel_id=1, source_target_pairs={{0,8},{1,9},{2,10},{3,11},{4,12},{5,13},{6,14},{7,15},{8,0},{9,1},... | collective-permute-start | bytes 393224 | tf_op jit(solution)/shard_map/ppermute | solution.py:662
  51.3 17.6 %collective-permute-start.19 = (bf16[72,2048]{1,0:T(8,128)(2,1)S(1)}, bf16[72,2048]{1,0:T(8,128)(2,1)S(1)}, u32[]{:S(2)}, u32[]{:S(2)}) collective-permute-start(bf16[72,2048]{1,0:T(8,128)(2,1)S(1)} %get-tuple-element.72), channel_id=1, source_target_pairs={{0,1},{1,0},{2,3},{3,2},{4,5},{5,4},{6,7},{7,6},{8,9},{9,8},{10,11... | collective-permute-start | bytes 884744 | tf_op jit(solution)/shard_map/ppermute | solution.py:662
  52.6 17.0 %collective-permute-start.20 = (bf16[72,2048]{1,0:T(8,128)(2,1)S(1)}, bf16[72,2048]{1,0:T(8,128)(2,1)S(1)}, u32[]{:S(2)}, u32[]{:S(2)}) collective-permute-start(bf16[72,2048]{1,0:T(8,128)(2,1)S(1)} %get-tuple-element.73), channel_id=1, source_target_pairs={{0,4},{1,5},{2,6},{3,7},{4,0},{5,1},{6,2},{7,3},{8,12},{9,13},{10,... | collective-permute-start | bytes 884744 | tf_op jit(solution)/shard_map/ppermute | solution.py:662
  54.1 15.4 %collective-permute-start.21 = (bf16[72,2048]{1,0:T(8,128)(2,1)S(1)}, bf16[72,2048]{1,0:T(8,128)(2,1)S(1)}, u32[]{:S(2)}, u32[]{:S(2)}) collective-permute-start(bf16[72,2048]{1,0:T(8,128)(2,1)S(1)} %get-tuple-element.74), channel_id=1, source_target_pairs={{0,5},{1,4},{2,7},{3,6},{4,1},{5,0},{6,3},{7,2},{8,13},{9,12},{10,... | collective-permute-start | bytes 884744 | tf_op jit(solution)/shard_map/ppermute | solution.py:662
  54.8 11.1 %collective-permute-start.17 = (bf16[32,2048]{1,0:T(8,128)(2,1)S(1)}, bf16[32,2048]{1,0:T(8,128)(2,1)S(1)}, u32[]{:S(2)}, u32[]{:S(2)}) collective-permute-start(bf16[32,2048]{1,0:T(8,128)(2,1)S(1)} %get-tuple-element.69), channel_id=1, source_target_pairs={{0,16},{1,17},{2,18},{3,19},{4,20},{5,21},{6,22},{7,23},{8,24},{9,... | collective-permute-start | bytes 393224 | tf_op jit(solution)/shard_map/ppermute | solution.py:662
  56.5 9.4 %collective-permute-start.18 = (bf16[32,2048]{1,0:T(8,128)(2,1)S(1)}, bf16[32,2048]{1,0:T(8,128)(2,1)S(1)}, u32[]{:S(2)}, u32[]{:S(2)}) collective-permute-start(bf16[32,2048]{1,0:T(8,128)(2,1)S(1)} %get-tuple-element.70), channel_id=1, source_target_pairs={{0,24},{1,25},{2,26},{3,27},{4,28},{5,29},{6,30},{7,31},{8,16},{9,... | collective-permute-start | bytes 393224 | tf_op jit(solution)/shard_map/ppermute | solution.py:662
  66.0 15.8 %copy-start = (f32[2048]{0:T(1024)S(1)}, f32[2048]{0:T(1024)}, u32[]{:S(2)}) copy-start(f32[2048]{0:T(1024)} %param.29) | copy-start | bytes 24580
  66.0 7.3 %collective-permute-start.25 = (bf16[32,2048]{1,0:T(8,128)(2,1)S(1)}, bf16[32,2048]{1,0:T(8,128)(2,1)S(1)}, u32[]{:S(2)}, u32[]{:S(2)}) collective-permute-start(bf16[32,2048]{1,0:T(8,128)(2,1)S(1)} %get-tuple-element.78), channel_id=1, source_target_pairs={{0,1},{1,0},{2,3},{3,2},{4,5},{5,4},{6,7},{7,6},{8,9},{9,8},{10,11... | collective-permute-start | bytes 393224 | tf_op jit(solution)/shard_map/ppermute | solution.py:662
  67.3 7.4 %collective-permute-start.26 = (bf16[32,2048]{1,0:T(8,128)(2,1)S(1)}, bf16[32,2048]{1,0:T(8,128)(2,1)S(1)}, u32[]{:S(2)}, u32[]{:S(2)}) collective-permute-start(bf16[32,2048]{1,0:T(8,128)(2,1)S(1)} %get-tuple-element.79), channel_id=1, source_target_pairs={{0,4},{1,5},{2,6},{3,7},{4,0},{5,1},{6,2},{7,3},{8,12},{9,13},{10,... | collective-permute-start | bytes 393224 | tf_op jit(solution)/shard_map/ppermute | solution.py:662
  68.9 5.9 %collective-permute-start.27 = (bf16[32,2048]{1,0:T(8,128)(2,1)S(1)}, bf16[32,2048]{1,0:T(8,128)(2,1)S(1)}, u32[]{:S(2)}, u32[]{:S(2)}) collective-permute-start(bf16[32,2048]{1,0:T(8,128)(2,1)S(1)} %get-tuple-element.80), channel_id=1, source_target_pairs={{0,5},{1,4},{2,7},{3,6},{4,1},{5,0},{6,3},{7,2},{8,13},{9,12},{10,... | collective-permute-start | bytes 393224 | tf_op jit(solution)/shard_map/ppermute | solution.py:662
  69.7 5.7 %collective-permute-start.22 = (bf16[24,2048]{1,0:T(8,128)(2,1)S(1)}, bf16[24,2048]{1,0:T(8,128)(2,1)S(1)}, u32[]{:S(2)}, u32[]{:S(2)}) collective-permute-start(bf16[24,2048]{1,0:T(8,128)(2,1)S(1)} %get-tuple-element.75), channel_id=1, source_target_pairs={{0,8},{1,9},{2,10},{3,11},{4,12},{5,13},{6,14},{7,15},{8,0},{9,1},... | collective-permute-start | bytes 294920 | tf_op jit(solution)/shard_map/ppermute | solution.py:662
  71.8 10.0 %collective-permute-start.23 = (bf16[24,2048]{1,0:T(8,128)(2,1)S(1)}, bf16[24,2048]{1,0:T(8,128)(2,1)S(1)}, u32[]{:S(2)}, u32[]{:S(2)}) collective-permute-start(bf16[24,2048]{1,0:T(8,128)(2,1)S(1)} %get-tuple-element.76), channel_id=1, source_target_pairs={{0,16},{1,17},{2,18},{3,19},{4,20},{5,21},{6,22},{7,23},{8,24},{9,... | collective-permute-start | bytes 294920 | tf_op jit(solution)/shard_map/ppermute | solution.py:662
  73.3 8.5 %collective-permute-start.24 = (bf16[24,2048]{1,0:T(8,128)(2,1)S(1)}, bf16[24,2048]{1,0:T(8,128)(2,1)S(1)}, u32[]{:S(2)}, u32[]{:S(2)}) collective-permute-start(bf16[24,2048]{1,0:T(8,128)(2,1)S(1)} %get-tuple-element.77), channel_id=1, source_target_pairs={{0,24},{1,25},{2,26},{3,27},{4,28},{5,29},{6,30},{7,31},{8,16},{9,... | collective-permute-start | bytes 294920 | tf_op jit(solution)/shard_map/ppermute | solution.py:662

commit v5 on v4

--- a/solution.py
+++ b/solution.py
@@ -237,7 +237,7 @@
 
 
 def attention_kernel(
-    pages_ref, lengths_ref, tp_ref, home_ref, q_hbm, fresh_hbm, cache_hbm, residual_hbm, ids_hbm,
+    pages_ref, lengths_ref, tp_ref, group_ref, home_ref, q_hbm, fresh_hbm, cache_hbm, residual_hbm, ids_hbm,
     routed_hbm, w_hbm, own_ref, send_ref, pack_ref,
     q_ref, fresh_ref, cache_ref, residual_ref, ids_ref, routed_ref, w_ref, context_ref, terms_ref,
     every_ref, sems,
@@ -356,7 +356,7 @@
 
 
 def attention_terms(
-    pages, lengths, tp_index, home, queries, fresh, cache, residual, ids, routed, w_out
+    pages, lengths, tp_index, group, home, queries, fresh, cache, residual, ids, routed, w_out
 ):
     tokens, width = residual.shape
     half = tokens // 2
@@ -368,7 +368,7 @@
             jax.ShapeDtypeStruct((half, width), jnp.bfloat16),
             jax.ShapeDtypeStruct((half, LANES), jnp.bfloat16),
         ),
-        in_specs=[smem()] * 4 + [hbm()] * 7,
+        in_specs=[smem()] * 5 + [hbm()] * 7,
         out_specs=(vmem(),) * 3,
         scratch_shapes=[pltpu.VMEM(v.shape, v.dtype) for v in moved]
         + [
@@ -379,19 +379,22 @@
         ],
         compiler_params=pltpu.CompilerParams(vmem_limit_bytes=40 * MIB),
         name="attention_terms",
-    )(stay(pages.T), stay(lengths), tp_index, stay(home), *[stay(v) for v in moved])
-
-
-def norm_kernel(own_ref, got_ref, pack_ref, gain_ref, state_ref, rows_ref, far_ref):
+    )(stay(pages.T), stay(lengths), tp_index, group, stay(home), *[stay(v) for v in moved])
+
+
+LATE = pl.CostEstimate(flops=3 * 10**10, bytes_accessed=1 << 20, transcendentals=0)
+
+
+def norm_kernel(own_ref, got_ref, pack_ref, gain_ref, state_ref, far_ref, near_ref):
     state = own_ref[...] + got_ref[...].astype(jnp.float32)
     state_ref[...] = state
     normed = rms_scale(state, gain_ref[...]).astype(jnp.bfloat16)
     width = state.shape[1]
     far = far_ref.shape[0]
-    rows_ref[:, :width] = normed
-    rows_ref[:, width:] = pack_ref[...]
     far_ref[:, :width] = normed[:far]
     far_ref[:, width:] = pack_ref[:far, :]
+    near_ref[:, :width] = normed[far:]
+    near_ref[:, width:] = pack_ref[far:, :]
 
 
 def norm_rows(own, got, pack, gain, far):
@@ -400,8 +403,8 @@
         norm_kernel,
         out_shape=(
             jax.ShapeDtypeStruct((rows, width), jnp.float32),
-            jax.ShapeDtypeStruct((rows, width + LANES), jnp.bfloat16),
             jax.ShapeDtypeStruct((far, width + LANES), jnp.bfloat16),
+            jax.ShapeDtypeStruct((rows - far, width + LANES), jnp.bfloat16),
         ),
         in_specs=[vmem()] * 4,
         out_specs=(vmem(),) * 3,
@@ -410,59 +413,69 @@
     )(own, got, pack, gain)
 
 
-def relay_kernel(r0, r1, r2, r3, z1, z2, z3, plane_ref, column_ref):
-    far = z1.shape[0]
-    near = r0.shape[0] - far
-    for j, piece in enumerate((z1, z2, z3)):
-        plane_ref[j * far : (j + 1) * far, :] = piece[...]
-    for i, piece in enumerate((r0, r1, r2, r3)):
-        column_ref[i * near : (i + 1) * near, :] = piece[far:, :]
-
-
-def relay_rows(rows, far):
-    height, width = far[0].shape
-    near = rows[0].shape[0] - height
-    return pl.pallas_call(
-        relay_kernel,
-        out_shape=(
-            jax.ShapeDtypeStruct((3 * height, width), jnp.bfloat16),
-            jax.ShapeDtypeStruct((4 * near, width), jnp.bfloat16),
-        ),
-        in_specs=[vmem()] * 7,
-        out_specs=(vmem(),) * 2,
+def join_kernel(starts, *refs):
+    out_ref = refs[-1]
+    at = 0
+    for start, piece in zip(starts, refs[:-1]):
+        height = piece.shape[0] - start
+        out_ref[at : at + height, :] = piece[start:, :]
+        at += height
+
+
+def join_rows(pieces, starts, cost, name):
+    height = sum(piece.shape[0] - start for piece, start in zip(pieces, starts))
+    return pl.pallas_call(
+        functools.partial(join_kernel, starts),
+        out_shape=jax.ShapeDtypeStruct((height, pieces[0].shape[1]), jnp.bfloat16),
+        in_specs=[vmem()] * len(pieces),
+        out_specs=vmem(),
         compiler_params=SMALL,
-        name="relay_rows",
-    )(*rows, *far)
-
-
-def hidden_units(group_ref, x_ref, w_refs, h_ref, ready):
+        cost_estimate=cost,
+        name=name,
+    )(*pieces)
+
+
+def hidden_units(groups, group_ref, x_ref, w0_ref, wg1_ref, wu1_ref, h_ref, ready):
     rows = x_ref.shape[0]
-    width = w_refs[0].shape[0]
-    hidden = h_ref.shape[1] // 2
-    groups = group_ref[2]
+    width, hidden = wg1_ref.shape
     lane = lax.broadcasted_iota(jnp.int32, (rows, LANES), 1)
     packed = x_ref[:, width:].astype(jnp.float32)
-    for e, w_ref in enumerate(w_refs):
-        group = group_ref[e]
+
+    def product(w_ref):
+        return jnp.dot(x_ref[:, :width], w_ref[...], preferred_element_type=jnp.float32)
+
+    def store(e, gate, up):
+        group = group_ref[0] ^ e
         share = jnp.sum(
             jnp.where((lane == group) | (lane == group + groups), packed, 0.0),
             axis=1,
             keepdims=True,
         )
-        ready(e)
-        both = jnp.dot(x_ref[:, :width], w_ref[...], preferred_element_type=jnp.float32)
-        gate, up = both[:, :hidden], both[:, hidden:]
         h_ref[:, e * hidden : (e + 1) * hidden] = (
             share * up * (gate / (1.0 + jnp.exp(-gate)))
         ).astype(jnp.bfloat16)
 
+    store(1, product(wg1_ref), product(wu1_ref))
+    ready()
+    both = product(w0_ref)
+    store(0, both[:, :hidden], both[:, hidden:])
+
 
 DOWN_BLOCK = 512
 
 
+def gather_pieces(pieces, x_ref):
+    at = 0
+    for piece in pieces:
+        x_ref[at : at + piece.shape[0], :] = piece[...]
+        at += piece.shape[0]
+    if at < x_ref.shape[0]:
+        x_ref[at:, :] = jnp.zeros((x_ref.shape[0] - at, x_ref.shape[1]), jnp.bfloat16)
+
+
 def near_kernel(
-    group_ref, r0, r1, r2, r3, z1, z2, z3, wg0, wu0, wd0, wg1, wu1, wd1,
-    out_ref, w0_ref, w1_ref, down_ref, x_ref, h_ref, sems,
+    groups, group_ref, r0, r1, r2, r3, far_ref, wg1_ref, wu1_ref, wg0, wu0, wd0, wd1,
+    out_ref, w0_ref, down_ref, x_ref, h_ref, sems,
 ):
     hidden = wg0.shape[1]
     fetches = [
@@ -471,8 +484,6 @@
             (
                 (wg0, w0_ref.at[:, :hidden]),
                 (wu0, w0_ref.at[:, hidden:]),
-                (wg1, w1_ref.at[:, :hidden]),
-                (wu1, w1_ref.at[:, hidden:]),
                 (wd0, down_ref.at[:hidden, :]),
                 (wd1, down_ref.at[hidden:, :]),
             )
@@ -480,24 +491,20 @@
     ]
     for fetch in fetches:
         fetch.start()
-    at = 0
-    for piece in (r0, r1, r2, r3, z1, z2, z3):
-        x_ref[at : at + piece.shape[0], :] = piece[...]
-        at += piece.shape[0]
-    if at < x_ref.shape[0]:
-        x_ref[at:, :] = jnp.zeros((x_ref.shape[0] - at, x_ref.shape[1]), jnp.bfloat16)
-
-    def ready(e):
-        fetches[2 * e].wait()
-        fetches[2 * e + 1].wait()
-
-    hidden_units(group_ref, x_ref, (w0_ref, w1_ref), h_ref, ready)
-    fetches[4].wait()
-    fetches[5].wait()
+    gather_pieces((r0, r1, r2, r3, far_ref), x_ref)
+
+    def ready():
+        fetches[0].wait()
+        fetches[1].wait()
+
+    hidden_units(groups, group_ref, x_ref, w0_ref, wg1_ref, wu1_ref, h_ref, ready)
+    fetches[2].wait()
+    fetches[3].wait()
+    height = out_ref.shape[0]
     for col in range(0, down_ref.shape[1], DOWN_BLOCK):
         cols = slice(col, col + DOWN_BLOCK)
         down = jnp.dot(h_ref[...], down_ref[:, cols], preferred_element_type=jnp.float32)
-        out_ref[:, cols] = down[:at]
+        out_ref[:, cols] = down[:height]
 
 
 def expert_cost(rows, width, hidden):
@@ -508,41 +515,37 @@
     )
 
 
-def near_rows(group, rows, far, weights, partner_weights):
-    height = 4 * rows[0].shape[0] + 3 * far[0].shape[0]
+def near_rows(groups, group, rows, far, weights, partner_weights):
+    height = 4 * rows[0].shape[0] + far.shape[0]
     padded = -(-height // 16) * 16
     width, hidden = weights[0].shape
-    return pl.pallas_call(
-        near_kernel,
+    wg0, wu0, wd0 = weights
+    wg1, wu1, wd1 = partner_weights
+    return pl.pallas_call(
+        functools.partial(near_kernel, groups),
         out_shape=(
             jax.ShapeDtypeStruct((height, width), jnp.float32),
             jax.ShapeDtypeStruct((width, 2 * hidden), jnp.bfloat16),
-            jax.ShapeDtypeStruct((width, 2 * hidden), jnp.bfloat16),
             jax.ShapeDtypeStruct((2 * hidden, width), jnp.bfloat16),
         ),
-        in_specs=[smem()] + [vmem()] * 7 + [hbm()] * 6,
-        out_specs=(vmem(),) * 4,
+        in_specs=[smem()] + [vmem()] * 7 + [hbm()] * 4,
+        out_specs=(vmem(),) * 3,
         scratch_shapes=[
             pltpu.VMEM((padded, width + LANES), jnp.bfloat16),
             pltpu.VMEM((padded, 2 * hidden), jnp.bfloat16),
-            pltpu.SemaphoreType.DMA((6,)),
+            pltpu.SemaphoreType.DMA((4,)),
         ],
         compiler_params=pltpu.CompilerParams(vmem_limit_bytes=24 * MIB),
         cost_estimate=expert_cost(height, width, hidden),
         name="near_rows",
-    )(group, *rows, *far, *[stay(w) for w in weights + partner_weights])
-
-
-def piece_kernel(count, group_ref, *refs):
-    pieces, (w0_ref, w1_ref, down_ref) = refs[:count], refs[count : count + 3]
-    outs, (x_ref, h_ref) = refs[count + 3 : 2 * count + 3], refs[2 * count + 3 :]
-    at = 0
-    for piece in pieces:
-        x_ref[at : at + piece.shape[0], :] = piece[...]
-        at += piece.shape[0]
-    if at < x_ref.shape[0]:
-        x_ref[at:, :] = jnp.zeros((x_ref.shape[0] - at, x_ref.shape[1]), jnp.bfloat16)
-    hidden_units(group_ref, x_ref, (w0_ref, w1_ref), h_ref, lambda e: None)
+    )(group, *rows, far, wg1, wu1, *[stay(w) for w in (wg0, wu0, wd0, wd1)])
+
+
+def piece_kernel(groups, count, group_ref, *refs):
+    pieces, (w0_ref, wg1_ref, wu1_ref, down_ref) = refs[:count], refs[count : count + 4]
+    outs, (x_ref, h_ref) = refs[count + 4 : 2 * count + 4], refs[2 * count + 4 :]
+    gather_pieces(pieces, x_ref)
+    hidden_units(groups, group_ref, x_ref, w0_ref, wg1_ref, wu1_ref, h_ref, lambda: None)
     for col in range(0, down_ref.shape[1], DOWN_BLOCK):
         cols = slice(col, col + DOWN_BLOCK)
         down = jnp.dot(h_ref[...], down_ref[:, cols], preferred_element_type=jnp.float32)
@@ -552,17 +555,17 @@
             at += out.shape[0]
 
 
-def piece_rows(group, pieces, w0, w1, down):
+def piece_rows(groups, group, pieces, w0, wg1, wu1, down):
     count = len(pieces)
     height = sum(piece.shape[0] for piece in pieces)
     padded = -(-height // 16) * 16
-    width, hidden = w0.shape[0], w0.shape[1] // 2
-    return pl.pallas_call(
-        functools.partial(piece_kernel, count),
+    width, hidden = wg1.shape
+    return pl.pallas_call(
+        functools.partial(piece_kernel, groups, count),
         out_shape=tuple(
             jax.ShapeDtypeStruct((piece.shape[0], width), jnp.bfloat16) for piece in pieces
         ),
-        in_specs=[smem()] + [vmem()] * (count + 3),
+        in_specs=[smem()] + [vmem()] * (count + 4),
         out_specs=(vmem(),) * count,
         scratch_shapes=[
             pltpu.VMEM((padded, width + LANES), jnp.bfloat16),
@@ -571,7 +574,7 @@
         compiler_params=pltpu.CompilerParams(vmem_limit_bytes=24 * MIB),
         cost_estimate=expert_cost(height, width, hidden),
         name="piece_rows",
-    )(group, *pieces, w0, w1, down)
+    )(group, *pieces, w0, wg1, wu1, down)
 
 
 def plane_sum_kernel(near_ref, g1, g2, g3, m1, m2, m3):
@@ -597,19 +600,40 @@
     )(near, *got)
 
 
-def column_sum_kernel(near_ref, g1, g2, g3, own_ref, m1, m2, m3):
+def first_sum_kernel(rows, near_ref, g1, out_ref):
+    near = g1.shape[0] // 4
+    for i in range(4):
+        there = slice(i * near, (i + 1) * near)
+        out_ref[there, :] = near_ref[(i + 1) * rows - near : (i + 1) * rows, :] + g1[
+            there, :
+        ].astype(jnp.float32)
+
+
+def first_sum(near, got, rows):
+    return pl.pallas_call(
+        functools.partial(first_sum_kernel, rows),
+        out_shape=jax.ShapeDtypeStruct(got.shape, jnp.float32),
+        in_specs=[vmem()] * 2,
+        out_specs=vmem(),
+        compiler_params=SMALL,
+        cost_estimate=LATE,
+        name="first_sum",
+    )(near, got)
+
+
+def column_sum_kernel(near_ref, first_ref, g2, g3, own_ref, m1, m2, m3):
     rows = own_ref.shape[0]
-    near = g1.shape[0] // 4
+    near = first_ref.shape[0] // 4
     far = rows - near
     for i, out in enumerate((own_ref, m1, m2, m3)):
         out[:far, :] = near_ref[i * rows : i * rows + far, :].astype(out.dtype)
-        total = near_ref[i * rows + far : (i + 1) * rows, :]
-        for got in (g1, g2, g3):
+        total = first_ref[i * near : (i + 1) * near, :]
+        for got in (g2, g3):
             total = total + got[i * near : (i + 1) * near, :].astype(jnp.float32)
         out[far:, :] = total.astype(out.dtype)
 
 
-def column_sum(near, got, rows):
+def column_sum(near, first, got, rows):
     width = near.shape[1]
     kinds = (jnp.float32, jnp.bfloat16, jnp.bfloat16, jnp.bfloat16)
     return pl.pallas_call(
@@ -618,33 +642,48 @@
         in_specs=[vmem()] * 4,
         out_specs=(vmem(),) * 4,
         compiler_params=SMALL,
+        cost_estimate=LATE,
         name="column_sum",
-    )(near, *got)
-
-
-def final_kernel(state_ref, own_ref, p1, p2, p3, z1, z2, z3, gain_ref, out_ref, total_ref):
-    total = state_ref[...] + own_ref[...]
-    for got in (p1, p2, p3):
-        total = total + got[...].astype(jnp.float32)
-    total_ref[...] = total
+    )(near, first, *got)
+
+
+def total_kernel(state_ref, own_ref, z1, z2, z3, total_ref):
+    total_ref[...] = state_ref[...] + own_ref[...]
     far = z1.shape[0]
     part = total_ref[:far, :]
     for got in (z1, z2, z3):
         part = part + got[...].astype(jnp.float32)
     total_ref[:far, :] = part
-    out_ref[...] = rms_scale(total_ref[...], gain_ref[...]).astype(jnp.bfloat16)
-
-
-def final_rows(state, own, plane, column, gain):
+
+
+def total_rows(state, own, column):
+    return pl.pallas_call(
+        total_kernel,
+        out_shape=jax.ShapeDtypeStruct(state.shape, jnp.float32),
+        in_specs=[vmem()] * 5,
+        out_specs=vmem(),
+        compiler_params=SMALL,
+        cost_estimate=LATE,
+        name="total_rows",
+    )(state, own, *column)
+
+
+def final_kernel(total_ref, p1, p2, p3, gain_ref, out_ref):
+    total = total_ref[...]
+    for got in (p1, p2, p3):
+        total = total + got[...].astype(jnp.float32)
+    out_ref[...] = rms_scale(total, gain_ref[...]).astype(jnp.bfloat16)
+
+
+def final_rows(total, plane, gain):
     return pl.pallas_call(
         final_kernel,
-        out_shape=jax.ShapeDtypeStruct(state.shape, jnp.bfloat16),
-        in_specs=[vmem()] * 9,
+        out_shape=jax.ShapeDtypeStruct(total.shape, jnp.bfloat16),
+        in_specs=[vmem()] * 5,
         out_specs=vmem(),
-        scratch_shapes=[pltpu.VMEM(state.shape, jnp.float32)],
         compiler_params=SMALL,
         name="final_rows",
-    )(state, own, *plane, *column, gain)
+    )(total, *plane, gain)
 
 
 def place(z, y, c, x):
@@ -685,25 +724,32 @@
     groups = expert_home.shape[0]
     weights = (w_gate[0], w_up[0], w_down[0])
     partner_weights = tuple(swap(w, 0, 0, 1, 0) for w in weights)
+    group = req_index.reshape(1)
     own_state, sent, pack = attention_terms(
-        request_page_index, cache_length_rows, tp_index.reshape(1).astype(jnp.int32), expert_home,
+        request_page_index, cache_length_rows, tp_index.reshape(1), group, expert_home,
         queries, fresh_key_value, key_value_cache, residual, route_ids, route_weights, w_out,
     )
     got, partner_weights = barrier(swap(sent, 0, 0, 0, 1), partner_weights)
-    group = jnp.stack([req_index, req_index ^ 1, groups]).astype(jnp.int32)
-    state, rows, far_rows = norm_rows(own_state, got, pack, gain_in[None, :], far)
-    z_rows, plane_rows = barrier(swap_z((far_rows,) * 3), swap_plane((rows,) * 3))
+    state, far_rows, last_rows = norm_rows(own_state, got, pack, gain_in[None, :], far)
+    rows = join_rows((far_rows, last_rows), (0, 0), LATE, "own_rows")
+    z_rows = swap_z((far_rows,) * 3)
+    onward_plane = join_rows(z_rows, (0, 0, 0), LATE, "onward_plane")
+    plane_rows, far_pieces = barrier(swap_plane((rows,) * 3), onward_plane)
     plane_rows = (rows,) + plane_rows
-    onward_plane, onward_z = relay_rows(plane_rows, z_rows)
+    onward_z = join_rows(plane_rows, (far,) * 4, None, "onward_z")
     z_pieces = swap_z((onward_z,) * 3)
     plane_pieces = swap_plane((onward_plane,) * 3)
-    near, w0, w1, down = near_rows(group, plane_rows, z_rows, weights, partner_weights)
-    parts = piece_rows(group, z_pieces + plane_pieces, w0, w1, down)
-    z_parts, plane_parts = parts[:3], parts[3:]
-    own, *near_sums = column_sum(near, swap_z(z_parts), half)
-    far_sums = plane_sum(near, swap_plane(plane_parts))
-    last_z, last_plane = barrier(swap_z(far_sums), swap_plane(near_sums))
-    return final_rows(state, own, last_plane, last_z, gain_out[None, :])
+    near, w0, down = near_rows(groups, group, plane_rows, far_pieces, weights, partner_weights)
+    parts = piece_rows(groups, group, z_pieces + plane_pieces, w0, *partner_weights[:2], down)
+    z_parts, plane_parts = swap_z(parts[:3]), swap_plane(parts[3:])
+    first = first_sum(near, z_parts[0], half)
+    plane_parts, first = barrier(plane_parts, first)
+    far_sums = plane_sum(near, plane_parts)
+    last_parts, far_sums = barrier(z_parts[1:], far_sums)
+    own, *near_sums = column_sum(near, first, last_parts, half)
+    total = total_rows(state, own, swap_z(far_sums))
+    last_plane, total = barrier(swap_plane(near_sums), total)
+    return final_rows(total, last_plane, gain_out[None, :])
 
 
 def solution(mesh):

time: 82.9 us -> 78.1 us (0.942)
  waiting for transfers between devices: 29.8 us -> 25.2 us
  starting transfers between devices: 36.6 us -> 37.8 us
  local copies, waits for them, and re-layouts: 1.19 us -> 0.01 us
    ppermute x28, waiting for transfers between devices: 29.8 us -> 25.2 us  [swap(): return lax.ppermute(value, ALL, pairs)]
    ppermute x28, starting transfers between devices: 36.6 us -> 37.8 us  [swap(): return lax.ppermute(value, ALL, pairs)]
    unnamed x8 -> x4, local copies, waits for them, and re-layouts: 1.19 us -> 0.01 us
    pallas_call x4 -> x8, Pallas kernels: 10.1 us -> 10 us  [the longest x1 4.87 us: near_rows(): pl.pallas_call(functools.partial(near_kernel, groups), out_shape=(jax.Sha...]
  transfers between devices with their start and end apart: 28 -> 28, of which waited for: 7 -> 9; matrix products, arithmetic and copies ran while one was open for 0% -> 0% of each run, Pallas kernels for 12% -> 12%
where the time goes in v5:
time: 78.1 us; the launch traced here: 78 us
  starting transfers between devices  37.8 us (48%)
  waiting for transfers between devices  25.2 us (32%)
  Pallas kernels  14.7 us (19%)
    ppermute x28, starting transfers between devices, swap(): return lax.ppermute(value, ALL, pairs)  37.8 us
    ppermute x28, waiting for transfers between devices, swap(): return lax.ppermute(value, ALL, pairs)  25.2 us
    pallas_call x1, Pallas kernels, near_rows(): pl.pallas_call(functools.partial(near_kernel, groups), out_shape=(jax.Sha...  4.87 us
    pallas_call x1, Pallas kernels, attention_terms(): pl.pallas_call(attention_kernel, out_shape=(jax.ShapeDtypeStruct((half, w...  4.33 us
    pallas_call x1, Pallas kernels, piece_rows(): pl.pallas_call(functools.partial(piece_kernel, groups, count), out_shape=...  4.18 us
  transfers between devices with their start and end apart: 28, of which 9 were waited for; matrix products, arithmetic and copies ran while one was open for 0% of the time, Pallas kernels for 12%

profile of v5, /device:TPU:0, one launch (start us, length us, event | category | flops | bytes accessed | tf_op | source)
XLA Modules:
  0.0 78.0 jit_solution(6619689499291559491)
XLA Ops:
  1.0 4.3 %attention_terms.1 = (f32[32,2048]{1,0:T(8,128)S(1)}, bf16[32,2048]{1,0:T(8,128)(2,1)S(1)}, bf16[32,128]{1,0:T(8,128)(2,1)S(1)}) custom-call(s32[4,9]{1,0:T(4,128)} %bitcast.20, s32[9]{0:T(128)} %lengths_ref.1, s32[1]{0:T(128)} %bitcast.2.tp_ref, s32[1]{0:T(128)} %bitcast.group_ref, s32[16]{0:T(128)} %home_ref.1, bf16[64,1024]{1,0:T(8,128)(2,1)} %q_hbm.1, ...), custom_call_target="tpu_custom_call" | custom-call | tf_op jit(solution)/shard_map/attention_terms/pallas_call | solution.py:364
  5.3 2.6 %collective-permute-start = (bf16[32,2048]{1,0:T(8,128)(2,1)S(1)}, bf16[32,2048]{1,0:T(8,128)(2,1)S(1)}, u32[]{:S(2)}, u32[]{:S(2)}) collective-permute-start(bf16[32,2048]{1,0:T(8,128)(2,1)S(1)} %get-tuple-element.49), channel_id=1, source_target_pairs={{0,1},{1,0},{2,3},{3,2},{4,5},{5,4},{6,7},{7,6},{8,9},{9,8},{10,11... | collective-permute-start | bytes 393224 | tf_op jit(solution)/shard_map/ppermute | solution.py:701
  7.9 4.2 %collective-permute-done.got_ref = bf16[32,2048]{1,0:T(8,128)(2,1)S(1)} collective-permute-done((bf16[32,2048]{1,0:T(8,128)(2,1)S(1)}, bf16[32,2048]{1,0:T(8,128)(2,1)S(1)}, u32[]{:S(2)}, u32[]{:S(2)}) %collective-permute-start) | collective-permute-done | bytes 131104 | tf_op jit(solution)/shard_map/ppermute | solution.py:701
  12.2 1.9 %collective-permute-start.7 = (bf16[24,2176]{1,0:T(8,128)(2,1)S(1)}, bf16[24,2176]{1,0:T(8,128)(2,1)S(1)}, u32[]{:S(2)}, u32[]{:S(2)}) collective-permute-start(bf16[24,2176]{1,0:T(8,128)(2,1)S(1)} %get-tuple-element.52.refs_0_), channel_id=1, source_target_pairs={{0,8},{1,9},{2,10},{3,11},{4,12},{5,13},{6,14},{7,15},{8,0},{9,1},... | collective-permute-start | bytes 313352 | tf_op jit(solution)/shard_map/ppermute | solution.py:701
  14.1 2.6 %collective-permute-start.8 = (bf16[24,2176]{1,0:T(8,128)(2,1)S(1)}, bf16[24,2176]{1,0:T(8,128)(2,1)S(1)}, u32[]{:S(2)}, u32[]{:S(2)}) collective-permute-start(bf16[24,2176]{1,0:T(8,128)(2,1)S(1)} %get-tuple-element.52.refs_0_), channel_id=1, source_target_pairs={{0,16},{1,17},{2,18},{3,19},{4,20},{5,21},{6,22},{7,23},{8,24},{9,... | collective-permute-start | bytes 313352 | tf_op jit(solution)/shard_map/ppermute | solution.py:701
  16.7 1.8 %collective-permute-start.4 = (bf16[32,2176]{1,0:T(8,128)(2,1)S(1)}, bf16[32,2176]{1,0:T(8,128)(2,1)S(1)}, u32[]{:S(2)}, u32[]{:S(2)}) collective-permute-start(bf16[32,2176]{1,0:T(8,128)(2,1)S(1)} %own_rows.1.r0.refs_0_), channel_id=1, source_target_pairs={{0,1},{1,0},{2,3},{3,2},{4,5},{5,4},{6,7},{7,6},{8,9},{9,8},{10,11... | collective-permute-start | bytes 417800 | tf_op jit(solution)/shard_map/ppermute | solution.py:701
  18.5 1.5 %collective-permute-start.5 = (bf16[32,2176]{1,0:T(8,128)(2,1)S(1)}, bf16[32,2176]{1,0:T(8,128)(2,1)S(1)}, u32[]{:S(2)}, u32[]{:S(2)}) collective-permute-start(bf16[32,2176]{1,0:T(8,128)(2,1)S(1)} %own_rows.1.r0.refs_0_), channel_id=1, source_target_pairs={{0,4},{1,5},{2,6},{3,7},{4,0},{5,1},{6,2},{7,3},{8,12},{9,13},{10,... | collective-permute-start | bytes 417800 | tf_op jit(solution)/shard_map/ppermute | solution.py:701
  20.7 4.2 %collective-permute-done.8.refs_1_ = bf16[24,2176]{1,0:T(8,128)(2,1)S(1)} collective-permute-done((bf16[24,2176]{1,0:T(8,128)(2,1)S(1)}, bf16[24,2176]{1,0:T(8,128)(2,1)S(1)}, u32[]{:S(2)}, u32[]{:S(2)}) %collective-permute-start.8) | collective-permute-done | bytes 104480 | tf_op jit(solution)/shard_map/ppermute | solution.py:701
  24.9 1.5 %collective-permute-done.5.r2.refs_2_ = bf16[32,2176]{1,0:T(8,128)(2,1)S(1)} collective-permute-done((bf16[32,2176]{1,0:T(8,128)(2,1)S(1)}, bf16[32,2176]{1,0:T(8,128)(2,1)S(1)}, u32[]{:S(2)}, u32[]{:S(2)}) %collective-permute-start.5) | collective-permute-done | bytes 139296 | tf_op jit(solution)/shard_map/ppermute | solution.py:701
  27.2 1.0 %collective-permute-start.13 = (bf16[72,2176]{1,0:T(8,128)(2,1)S(1)}, bf16[72,2176]{1,0:T(8,128)(2,1)S(1)}, u32[]{:S(2)}, u32[]{:S(2)}) collective-permute-start(bf16[72,2176]{1,0:T(8,128)(2,1)S(1)} %onward_plane.1.far_ref), channel_id=1, source_target_pairs={{0,1},{1,0},{2,3},{3,2},{4,5},{5,4},{6,7},{7,6},{8,9},{9,8},{10,11... | collective-permute-start | bytes 940040 | tf_op jit(solution)/shard_map/ppermute | solution.py:701
  28.2 1.5 %collective-permute-start.14 = (bf16[72,2176]{1,0:T(8,128)(2,1)S(1)}, bf16[72,2176]{1,0:T(8,128)(2,1)S(1)}, u32[]{:S(2)}, u32[]{:S(2)}) collective-permute-start(bf16[72,2176]{1,0:T(8,128)(2,1)S(1)} %onward_plane.1.far_ref), channel_id=1, source_target_pairs={{0,4},{1,5},{2,6},{3,7},{4,0},{5,1},{6,2},{7,3},{8,12},{9,13},{10,... | collective-permute-start | bytes 940040 | tf_op jit(solution)/shard_map/ppermute | solution.py:701
  29.7 1.0 %collective-permute-start.15 = (bf16[72,2176]{1,0:T(8,128)(2,1)S(1)}, bf16[72,2176]{1,0:T(8,128)(2,1)S(1)}, u32[]{:S(2)}, u32[]{:S(2)}) collective-permute-start(bf16[72,2176]{1,0:T(8,128)(2,1)S(1)} %onward_plane.1.far_ref), channel_id=1, source_target_pairs={{0,5},{1,4},{2,7},{3,6},{4,1},{5,0},{6,3},{7,2},{8,13},{9,12},{10,... | collective-permute-start | bytes 940040 | tf_op jit(solution)/shard_map/ppermute | solution.py:701
  30.7 3.5 %collective-permute-start.11 = (bf16[32,2176]{1,0:T(8,128)(2,1)S(1)}, bf16[32,2176]{1,0:T(8,128)(2,1)S(1)}, u32[]{:S(2)}, u32[]{:S(2)}) collective-permute-start(bf16[32,2176]{1,0:T(8,128)(2,1)S(1)} %onward_z.1), channel_id=1, source_target_pairs={{0,16},{1,17},{2,18},{3,19},{4,20},{5,21},{6,22},{7,23},{8,24},{9,... | collective-permute-start | bytes 417800 | tf_op jit(solution)/shard_map/ppermute | solution.py:701
  34.1 2.2 %collective-permute-start.12 = (bf16[32,2176]{1,0:T(8,128)(2,1)S(1)}, bf16[32,2176]{1,0:T(8,128)(2,1)S(1)}, u32[]{:S(2)}, u32[]{:S(2)}) collective-permute-start(bf16[32,2176]{1,0:T(8,128)(2,1)S(1)} %onward_z.1), channel_id=1, source_target_pairs={{0,24},{1,25},{2,26},{3,27},{4,28},{5,29},{6,30},{7,31},{8,16},{9,... | collective-permute-start | bytes 417800 | tf_op jit(solution)/shard_map/ppermute | solution.py:701
  36.3 4.9 %near_rows.1 = (f32[200,2048]{1,0:T(8,128)S(1)}, bf16[2048,768]{1,0:T(8,128)(2,1)S(1)}, bf16[768,2048]{1,0:T(8,128)(2,1)S(1)}) custom-call(s32[1]{0:T(128)} %bitcast.group_ref, bf16[32,2176]{1,0:T(8,128)(2,1)S(1)} %own_rows.1.r0.refs_0_, bf16[32,2176]{1,0:T(8,128)(2,1)S(1)} %collective-permute-done.4.r1.refs_1_, ...), custom_call_target="tpu_custom_call" | custom-call | flops 1887436800 | bytes 9437184 | tf_op jit(solution)/shard_map/near_rows/pallas_call | solution.py:524
  41.2 1.1 %collective-permute-done.11.refs_1_ = bf16[32,2176]{1,0:T(8,128)(2,1)S(1)} collective-permute-done((bf16[32,2176]{1,0:T(8,128)(2,1)S(1)}, bf16[32,2176]{1,0:T(8,128)(2,1)S(1)}, u32[]{:S(2)}, u32[]{:S(2)}) %collective-permute-start.11) | collective-permute-done | bytes 139296 | tf_op jit(solution)/shard_map/ppermute | solution.py:701
  42.5 4.2 %piece_rows.1 = (bf16[32,2048]{1,0:T(8,128)(2,1)S(1)}, bf16[32,2048]{1,0:T(8,128)(2,1)S(1)}, bf16[32,2048]{1,0:T(8,128)(2,1)S(1)}, bf16[72,2048]{1,0:T(8,128)(2,...) custom-call(s32[1]{0:T(128)} %bitcast.group_ref, ...), custom_call_target="tpu_custom_call" | custom-call | flops 2944401408 | bytes 9437184 | tf_op jit(solution)/shard_map/piece_rows/pallas_call | solution.py:563
  46.7 1.9 %collective-permute-start.19 = (bf16[32,2048]{1,0:T(8,128)(2,1)S(1)}, bf16[32,2048]{1,0:T(8,128)(2,1)S(1)}, u32[]{:S(2)}, u32[]{:S(2)}) collective-permute-start(bf16[32,2048]{1,0:T(8,128)(2,1)S(1)} %get-tuple-element.67), channel_id=1, source_target_pairs={{0,8},{1,9},{2,10},{3,11},{4,12},{5,13},{6,14},{7,15},{8,0},{9,1},... | collective-permute-start | bytes 393224 | tf_op jit(solution)/shard_map/ppermute | solution.py:701
  48.7 0.9 %collective-permute-start.16 = (bf16[72,2048]{1,0:T(8,128)(2,1)S(1)}, bf16[72,2048]{1,0:T(8,128)(2,1)S(1)}, u32[]{:S(2)}, u32[]{:S(2)}) collective-permute-start(bf16[72,2048]{1,0:T(8,128)(2,1)S(1)} %get-tuple-element.64), channel_id=1, source_target_pairs={{0,1},{1,0},{2,3},{3,2},{4,5},{5,4},{6,7},{7,6},{8,9},{9,8},{10,11... | collective-permute-start | bytes 884744 | tf_op jit(solution)/shard_map/ppermute | solution.py:701
  49.6 1.5 %collective-permute-start.17 = (bf16[72,2048]{1,0:T(8,128)(2,1)S(1)}, bf16[72,2048]{1,0:T(8,128)(2,1)S(1)}, u32[]{:S(2)}, u32[]{:S(2)}) collective-permute-start(bf16[72,2048]{1,0:T(8,128)(2,1)S(1)} %get-tuple-element.65), channel_id=1, source_target_pairs={{0,4},{1,5},{2,6},{3,7},{4,0},{5,1},{6,2},{7,3},{8,12},{9,13},{10,... | collective-permute-start | bytes 884744 | tf_op jit(solution)/shard_map/ppermute | solution.py:701
  51.1 1.0 %collective-permute-start.18 = (bf16[72,2048]{1,0:T(8,128)(2,1)S(1)}, bf16[72,2048]{1,0:T(8,128)(2,1)S(1)}, u32[]{:S(2)}, u32[]{:S(2)}) collective-permute-start(bf16[72,2048]{1,0:T(8,128)(2,1)S(1)} %get-tuple-element.66), channel_id=1, source_target_pairs={{0,5},{1,4},{2,7},{3,6},{4,1},{5,0},{6,3},{7,2},{8,13},{9,12},{10,... | collective-permute-start | bytes 884744 | tf_op jit(solution)/shard_map/ppermute | solution.py:701
  52.1 1.2 %collective-permute-start.20 = (bf16[32,2048]{1,0:T(8,128)(2,1)S(1)}, bf16[32,2048]{1,0:T(8,128)(2,1)S(1)}, u32[]{:S(2)}, u32[]{:S(2)}) collective-permute-start(bf16[32,2048]{1,0:T(8,128)(2,1)S(1)} %get-tuple-element.69), channel_id=1, source_target_pairs={{0,16},{1,17},{2,18},{3,19},{4,20},{5,21},{6,22},{7,23},{8,24},{9,... | collective-permute-start | bytes 393224 | tf_op jit(solution)/shard_map/ppermute | solution.py:701
  53.3 1.3 %collective-permute-start.21 = (bf16[32,2048]{1,0:T(8,128)(2,1)S(1)}, bf16[32,2048]{1,0:T(8,128)(2,1)S(1)}, u32[]{:S(2)}, u32[]{:S(2)}) collective-permute-start(bf16[32,2048]{1,0:T(8,128)(2,1)S(1)} %get-tuple-element.70), channel_id=1, source_target_pairs={{0,24},{1,25},{2,26},{3,27},{4,28},{5,29},{6,30},{7,31},{8,16},{9,... | collective-permute-start | bytes 393224 | tf_op jit(solution)/shard_map/ppermute | solution.py:701
  54.7 3.9 %collective-permute-done.16.g1 = bf16[72,2048]{1,0:T(8,128)(2,1)S(1)} collective-permute-done((bf16[72,2048]{1,0:T(8,128)(2,1)S(1)}, bf16[72,2048]{1,0:T(8,128)(2,1)S(1)}, u32[]{:S(2)}, u32[]{:S(2)}) %collective-permute-start.16) | collective-permute-done | bytes 294944 | tf_op jit(solution)/shard_map/ppermute | solution.py:701
  58.6 4.5 %collective-permute-done.17.g2 = bf16[72,2048]{1,0:T(8,128)(2,1)S(1)} collective-permute-done((bf16[72,2048]{1,0:T(8,128)(2,1)S(1)}, bf16[72,2048]{1,0:T(8,128)(2,1)S(1)}, u32[]{:S(2)}, u32[]{:S(2)}) %collective-permute-start.17) | collective-permute-done | bytes 294944 | tf_op jit(solution)/shard_map/ppermute | solution.py:701
  63.3 1.4 %collective-permute-start.25 = (bf16[24,2048]{1,0:T(8,128)(2,1)S(1)}, bf16[24,2048]{1,0:T(8,128)(2,1)S(1)}, u32[]{:S(2)}, u32[]{:S(2)}) collective-permute-start(bf16[24,2048]{1,0:T(8,128)(2,1)S(1)} %get-tuple-element.84), channel_id=1, source_target_pairs={{0,8},{1,9},{2,10},{3,11},{4,12},{5,13},{6,14},{7,15},{8,0},{9,1},... | collective-permute-start | bytes 294920 | tf_op jit(solution)/shard_map/ppermute | solution.py:701
  64.6 2.5 %collective-permute-start.26 = (bf16[24,2048]{1,0:T(8,128)(2,1)S(1)}, bf16[24,2048]{1,0:T(8,128)(2,1)S(1)}, u32[]{:S(2)}, u32[]{:S(2)}) collective-permute-start(bf16[24,2048]{1,0:T(8,128)(2,1)S(1)} %get-tuple-element.85), channel_id=1, source_target_pairs={{0,16},{1,17},{2,18},{3,19},{4,20},{5,21},{6,22},{7,23},{8,24},{9,... | collective-permute-start | bytes 294920 | tf_op jit(solution)/shard_map/ppermute | solution.py:701
  67.8 1.5 %collective-permute-start.22 = (bf16[32,2048]{1,0:T(8,128)(2,1)S(1)}, bf16[32,2048]{1,0:T(8,128)(2,1)S(1)}, u32[]{:S(2)}, u32[]{:S(2)}) collective-permute-start(bf16[32,2048]{1,0:T(8,128)(2,1)S(1)} %get-tuple-element.79), channel_id=1, source_target_pairs={{0,1},{1,0},{2,3},{3,2},{4,5},{5,4},{6,7},{7,6},{8,9},{9,8},{10,11... | collective-permute-start | bytes 393224 | tf_op jit(solution)/shard_map/ppermute | solution.py:701
  69.3 1.4 %collective-permute-start.23 = (bf16[32,2048]{1,0:T(8,128)(2,1)S(1)}, bf16[32,2048]{1,0:T(8,128)(2,1)S(1)}, u32[]{:S(2)}, u32[]{:S(2)}) collective-permute-start(bf16[32,2048]{1,0:T(8,128)(2,1)S(1)} %get-tuple-element.80), channel_id=1, source_target_pairs={{0,4},{1,5},{2,6},{3,7},{4,0},{5,1},{6,2},{7,3},{8,12},{9,13},{10,... | collective-permute-start | bytes 393224 | tf_op jit(solution)/shard_map/ppermute | solution.py:701
  71.4 3.8 %collective-permute-done.26.z2 = bf16[24,2048]{1,0:T(8,128)(2,1)S(1)} collective-permute-done((bf16[24,2048]{1,0:T(8,128)(2,1)S(1)}, bf16[24,2048]{1,0:T(8,128)(2,1)S(1)}, u32[]{:S(2)}, u32[]{:S(2)}) %collective-permute-start.26) | collective-permute-done | bytes 98336 | tf_op jit(solution)/shard_map/ppermute | solution.py:701
  75.3 1.8 %collective-permute-done.23.p2 = bf16[32,2048]{1,0:T(8,128)(2,1)S(1)} collective-permute-done((bf16[32,2048]{1,0:T(8,128)(2,1)S(1)}, bf16[32,2048]{1,0:T(8,128)(2,1)S(1)}, u32[]{:S(2)}, u32[]{:S(2)}) %collective-permute-start.23) | collective-permute-done | bytes 131104 | tf_op jit(solution)/shard_map/ppermute | solution.py:701
  77.1 0.8 %final_rows.1 = bf16[32,2048]{1,0:T(8,128)(2,1)} custom-call(f32[32,2048]{1,0:T(8,128)S(1)} %total_rows.1.total_ref, bf16[32,2048]{1,0:T(8,128)(2,1)S(1)} %collective-permute-done.22.p1, bf16[32,2048]{1,0:T(8,128)(2,1)S(1)} %collective-permute-done.23.p2, bf16[32,2048]{1,0:T(8,128)(2,1)S(1)} %collective-permute-done.24.p3, f32[1,2048]{1,0:T(1,128)S(1)} %bitcast.10), custom_call_target="tpu_custom_call" | custom-call | tf_op jit(solution)/shard_map/final_rows/pallas_call | solution.py:679
  (40 shorter events, 4.4 us)
Async XLA Ops:
  0.0 12.0 %collective-permute-start.1 = (bf16[2048,384]{1,0:T(8,128)(2,1)}, bf16[2048,384]{1,0:T(8,128)(2,1)S(1)}, u32[]{:S(2)}, u32[]{:S(2)}) collective-permute-start(bf16[2048,384]{1,0:T(8,128)(2,1)} %bitcast.12), channel_id=1, source_target_pairs={{0,2},{1,3},{2,0},{3,1},{4,6},{5,7},{6,4},{7,5},{8,10},{9,11},{10,... | collective-permute-start | bytes 4718600 | tf_op jit(solution)/shard_map/ppermute | solution.py:701
  0.5 11.6 %collective-permute-start.2 = (bf16[2048,384]{1,0:T(8,128)(2,1)}, bf16[2048,384]{1,0:T(8,128)(2,1)S(1)}, u32[]{:S(2)}, u32[]{:S(2)}) collective-permute-start(bf16[2048,384]{1,0:T(8,128)(2,1)} %bitcast.14), channel_id=1, source_target_pairs={{0,2},{1,3},{2,0},{3,1},{4,6},{5,7},{6,4},{7,5},{8,10},{9,11},{10,... | collective-permute-start | bytes 4718600 | tf_op jit(solution)/shard_map/ppermute | solution.py:701
  0.5 11.5 %collective-permute-start.3 = (bf16[384,2048]{1,0:T(8,128)(2,1)}, bf16[384,2048]{1,0:T(8,128)(2,1)}, u32[]{:S(2)}, u32[]{:S(2)}) collective-permute-start(bf16[384,2048]{1,0:T(8,128)(2,1)} %bitcast.16), channel_id=1, source_target_pairs={{0,2},{1,3},{2,0},{3,1},{4,6},{5,7},{6,4},{7,5},{8,10},{9,11},{10,... | collective-permute-start | bytes 4718600 | tf_op jit(solution)/shard_map/ppermute | solution.py:701
  1.0 11.1 %copy-start.1 = (f32[2048]{0:T(1024)S(1)}, f32[2048]{0:T(1024)}, u32[]{:S(2)}) copy-start(f32[2048]{0:T(1024)} %param.22) | copy-start | bytes 24580
  5.3 6.7 %collective-permute-start = (bf16[32,2048]{1,0:T(8,128)(2,1)S(1)}, bf16[32,2048]{1,0:T(8,128)(2,1)S(1)}, u32[]{:S(2)}, u32[]{:S(2)}) collective-permute-start(bf16[32,2048]{1,0:T(8,128)(2,1)S(1)} %get-tuple-element.49), channel_id=1, source_target_pairs={{0,1},{1,0},{2,3},{3,2},{4,5},{5,4},{6,7},{7,6},{8,9},{9,8},{10,11... | collective-permute-start | bytes 393224 | tf_op jit(solution)/shard_map/ppermute | solution.py:701
  12.2 7.8 %collective-permute-start.7 = (bf16[24,2176]{1,0:T(8,128)(2,1)S(1)}, bf16[24,2176]{1,0:T(8,128)(2,1)S(1)}, u32[]{:S(2)}, u32[]{:S(2)}) collective-permute-start(bf16[24,2176]{1,0:T(8,128)(2,1)S(1)} %get-tuple-element.52.refs_0_), channel_id=1, source_target_pairs={{0,8},{1,9},{2,10},{3,11},{4,12},{5,13},{6,14},{7,15},{8,0},{9,1},... | collective-permute-start | bytes 313352 | tf_op jit(solution)/shard_map/ppermute | solution.py:701
  14.1 10.8 %collective-permute-start.8 = (bf16[24,2176]{1,0:T(8,128)(2,1)S(1)}, bf16[24,2176]{1,0:T(8,128)(2,1)S(1)}, u32[]{:S(2)}, u32[]{:S(2)}) collective-permute-start(bf16[24,2176]{1,0:T(8,128)(2,1)S(1)} %get-tuple-element.52.refs_0_), channel_id=1, source_target_pairs={{0,16},{1,17},{2,18},{3,19},{4,20},{5,21},{6,22},{7,23},{8,24},{9,... | collective-permute-start | bytes 313352 | tf_op jit(solution)/shard_map/ppermute | solution.py:701
  16.7 8.2 %collective-permute-start.9 = (bf16[24,2176]{1,0:T(8,128)(2,1)S(1)}, bf16[24,2176]{1,0:T(8,128)(2,1)S(1)}, u32[]{:S(2)}, u32[]{:S(2)}) collective-permute-start(bf16[24,2176]{1,0:T(8,128)(2,1)S(1)} %get-tuple-element.52.refs_0_), channel_id=1, source_target_pairs={{0,24},{1,25},{2,26},{3,27},{4,28},{5,29},{6,30},{7,31},{8,16},{9,... | collective-permute-start | bytes 313352 | tf_op jit(solution)/shard_map/ppermute | solution.py:701
  16.7 8.2 %collective-permute-start.4 = (bf16[32,2176]{1,0:T(8,128)(2,1)S(1)}, bf16[32,2176]{1,0:T(8,128)(2,1)S(1)}, u32[]{:S(2)}, u32[]{:S(2)}) collective-permute-start(bf16[32,2176]{1,0:T(8,128)(2,1)S(1)} %own_rows.1.r0.refs_0_), channel_id=1, source_target_pairs={{0,1},{1,0},{2,3},{3,2},{4,5},{5,4},{6,7},{7,6},{8,9},{9,8},{10,11... | collective-permute-start | bytes 417800 | tf_op jit(solution)/shard_map/ppermute | solution.py:701
  18.5 7.9 %collective-permute-start.5 = (bf16[32,2176]{1,0:T(8,128)(2,1)S(1)}, bf16[32,2176]{1,0:T(8,128)(2,1)S(1)}, u32[]{:S(2)}, u32[]{:S(2)}) collective-permute-start(bf16[32,2176]{1,0:T(8,128)(2,1)S(1)} %own_rows.1.r0.refs_0_), channel_id=1, source_target_pairs={{0,4},{1,5},{2,6},{3,7},{4,0},{5,1},{6,2},{7,3},{8,12},{9,13},{10,... | collective-permute-start | bytes 417800 | tf_op jit(solution)/shard_map/ppermute | solution.py:701
  20.0 6.4 %collective-permute-start.6 = (bf16[32,2176]{1,0:T(8,128)(2,1)S(1)}, bf16[32,2176]{1,0:T(8,128)(2,1)S(1)}, u32[]{:S(2)}, u32[]{:S(2)}) collective-permute-start(bf16[32,2176]{1,0:T(8,128)(2,1)S(1)} %own_rows.1.r0.refs_0_), channel_id=1, source_target_pairs={{0,5},{1,4},{2,7},{3,6},{4,1},{5,0},{6,3},{7,2},{8,13},{9,12},{10,... | collective-permute-start | bytes 417800 | tf_op jit(solution)/shard_map/ppermute | solution.py:701
  26.4 7.7 %collective-permute-start.10 = (bf16[32,2176]{1,0:T(8,128)(2,1)S(1)}, bf16[32,2176]{1,0:T(8,128)(2,1)S(1)}, u32[]{:S(2)}, u32[]{:S(2)}) collective-permute-start(bf16[32,2176]{1,0:T(8,128)(2,1)S(1)} %onward_z.1), channel_id=1, source_target_pairs={{0,8},{1,9},{2,10},{3,11},{4,12},{5,13},{6,14},{7,15},{8,0},{9,1},... | collective-permute-start | bytes 417800 | tf_op jit(solution)/shard_map/ppermute | solution.py:701
  27.2 15.2 %collective-permute-start.13 = (bf16[72,2176]{1,0:T(8,128)(2,1)S(1)}, bf16[72,2176]{1,0:T(8,128)(2,1)S(1)}, u32[]{:S(2)}, u32[]{:S(2)}) collective-permute-start(bf16[72,2176]{1,0:T(8,128)(2,1)S(1)} %onward_plane.1.far_ref), channel_id=1, source_target_pairs={{0,1},{1,0},{2,3},{3,2},{4,5},{5,4},{6,7},{7,6},{8,9},{9,8},{10,11... | collective-permute-start | bytes 940040 | tf_op jit(solution)/shard_map/ppermute | solution.py:701
  28.2 14.3 %collective-permute-start.14 = (bf16[72,2176]{1,0:T(8,128)(2,1)S(1)}, bf16[72,2176]{1,0:T(8,128)(2,1)S(1)}, u32[]{:S(2)}, u32[]{:S(2)}) collective-permute-start(bf16[72,2176]{1,0:T(8,128)(2,1)S(1)} %onward_plane.1.far_ref), channel_id=1, source_target_pairs={{0,4},{1,5},{2,6},{3,7},{4,0},{5,1},{6,2},{7,3},{8,12},{9,13},{10,... | collective-permute-start | bytes 940040 | tf_op jit(solution)/shard_map/ppermute | solution.py:701
  29.7 12.8 %collective-permute-start.15 = (bf16[72,2176]{1,0:T(8,128)(2,1)S(1)}, bf16[72,2176]{1,0:T(8,128)(2,1)S(1)}, u32[]{:S(2)}, u32[]{:S(2)}) collective-permute-start(bf16[72,2176]{1,0:T(8,128)(2,1)S(1)} %onward_plane.1.far_ref), channel_id=1, source_target_pairs={{0,5},{1,4},{2,7},{3,6},{4,1},{5,0},{6,3},{7,2},{8,13},{9,12},{10,... | collective-permute-start | bytes 940040 | tf_op jit(solution)/shard_map/ppermute | solution.py:701
  30.7 11.7 %collective-permute-start.11 = (bf16[32,2176]{1,0:T(8,128)(2,1)S(1)}, bf16[32,2176]{1,0:T(8,128)(2,1)S(1)}, u32[]{:S(2)}, u32[]{:S(2)}) collective-permute-start(bf16[32,2176]{1,0:T(8,128)(2,1)S(1)} %onward_z.1), channel_id=1, source_target_pairs={{0,16},{1,17},{2,18},{3,19},{4,20},{5,21},{6,22},{7,23},{8,24},{9,... | collective-permute-start | bytes 417800 | tf_op jit(solution)/shard_map/ppermute | solution.py:701
  34.1 8.2 %collective-permute-start.12 = (bf16[32,2176]{1,0:T(8,128)(2,1)S(1)}, bf16[32,2176]{1,0:T(8,128)(2,1)S(1)}, u32[]{:S(2)}, u32[]{:S(2)}) collective-permute-start(bf16[32,2176]{1,0:T(8,128)(2,1)S(1)} %onward_z.1), channel_id=1, source_target_pairs={{0,24},{1,25},{2,26},{3,27},{4,28},{5,29},{6,30},{7,31},{8,16},{9,... | collective-permute-start | bytes 417800 | tf_op jit(solution)/shard_map/ppermute | solution.py:701
  46.7 6.6 %collective-permute-start.19 = (bf16[32,2048]{1,0:T(8,128)(2,1)S(1)}, bf16[32,2048]{1,0:T(8,128)(2,1)S(1)}, u32[]{:S(2)}, u32[]{:S(2)}) collective-permute-start(bf16[32,2048]{1,0:T(8,128)(2,1)S(1)} %get-tuple-element.67), channel_id=1, source_target_pairs={{0,8},{1,9},{2,10},{3,11},{4,12},{5,13},{6,14},{7,15},{8,0},{9,1},... | collective-permute-start | bytes 393224 | tf_op jit(solution)/shard_map/ppermute | solution.py:701
  48.7 9.9 %collective-permute-start.16 = (bf16[72,2048]{1,0:T(8,128)(2,1)S(1)}, bf16[72,2048]{1,0:T(8,128)(2,1)S(1)}, u32[]{:S(2)}, u32[]{:S(2)}) collective-permute-start(bf16[72,2048]{1,0:T(8,128)(2,1)S(1)} %get-tuple-element.64), channel_id=1, source_target_pairs={{0,1},{1,0},{2,3},{3,2},{4,5},{5,4},{6,7},{7,6},{8,9},{9,8},{10,11... | collective-permute-start | bytes 884744 | tf_op jit(solution)/shard_map/ppermute | solution.py:701
  49.6 13.5 %collective-permute-start.17 = (bf16[72,2048]{1,0:T(8,128)(2,1)S(1)}, bf16[72,2048]{1,0:T(8,128)(2,1)S(1)}, u32[]{:S(2)}, u32[]{:S(2)}) collective-permute-start(bf16[72,2048]{1,0:T(8,128)(2,1)S(1)} %get-tuple-element.65), channel_id=1, source_target_pairs={{0,4},{1,5},{2,6},{3,7},{4,0},{5,1},{6,2},{7,3},{8,12},{9,13},{10,... | collective-permute-start | bytes 884744 | tf_op jit(solution)/shard_map/ppermute | solution.py:701
  51.1 12.0 %collective-permute-start.18 = (bf16[72,2048]{1,0:T(8,128)(2,1)S(1)}, bf16[72,2048]{1,0:T(8,128)(2,1)S(1)}, u32[]{:S(2)}, u32[]{:S(2)}) collective-permute-start(bf16[72,2048]{1,0:T(8,128)(2,1)S(1)} %get-tuple-element.66), channel_id=1, source_target_pairs={{0,5},{1,4},{2,7},{3,6},{4,1},{5,0},{6,3},{7,2},{8,13},{9,12},{10,... | collective-permute-start | bytes 884744 | tf_op jit(solution)/shard_map/ppermute | solution.py:701
  52.1 11.1 %collective-permute-start.20 = (bf16[32,2048]{1,0:T(8,128)(2,1)S(1)}, bf16[32,2048]{1,0:T(8,128)(2,1)S(1)}, u32[]{:S(2)}, u32[]{:S(2)}) collective-permute-start(bf16[32,2048]{1,0:T(8,128)(2,1)S(1)} %get-tuple-element.69), channel_id=1, source_target_pairs={{0,16},{1,17},{2,18},{3,19},{4,20},{5,21},{6,22},{7,23},{8,24},{9,... | collective-permute-start | bytes 393224 | tf_op jit(solution)/shard_map/ppermute | solution.py:701
  53.3 9.9 %collective-permute-start.21 = (bf16[32,2048]{1,0:T(8,128)(2,1)S(1)}, bf16[32,2048]{1,0:T(8,128)(2,1)S(1)}, u32[]{:S(2)}, u32[]{:S(2)}) collective-permute-start(bf16[32,2048]{1,0:T(8,128)(2,1)S(1)} %get-tuple-element.70), channel_id=1, source_target_pairs={{0,24},{1,25},{2,26},{3,27},{4,28},{5,29},{6,30},{7,31},{8,16},{9,... | collective-permute-start | bytes 393224 | tf_op jit(solution)/shard_map/ppermute | solution.py:701
  63.3 7.5 %collective-permute-start.25 = (bf16[24,2048]{1,0:T(8,128)(2,1)S(1)}, bf16[24,2048]{1,0:T(8,128)(2,1)S(1)}, u32[]{:S(2)}, u32[]{:S(2)}) collective-permute-start(bf16[24,2048]{1,0:T(8,128)(2,1)S(1)} %get-tuple-element.84), channel_id=1, source_target_pairs={{0,8},{1,9},{2,10},{3,11},{4,12},{5,13},{6,14},{7,15},{8,0},{9,1},... | collective-permute-start | bytes 294920 | tf_op jit(solution)/shard_map/ppermute | solution.py:701
  64.6 10.6 %collective-permute-start.26 = (bf16[24,2048]{1,0:T(8,128)(2,1)S(1)}, bf16[24,2048]{1,0:T(8,128)(2,1)S(1)}, u32[]{:S(2)}, u32[]{:S(2)}) collective-permute-start(bf16[24,2048]{1,0:T(8,128)(2,1)S(1)} %get-tuple-element.85), channel_id=1, source_target_pairs={{0,16},{1,17},{2,18},{3,19},{4,20},{5,21},{6,22},{7,23},{8,24},{9,... | collective-permute-start | bytes 294920 | tf_op jit(solution)/shard_map/ppermute | solution.py:701
  67.2 8.0 %collective-permute-start.27 = (bf16[24,2048]{1,0:T(8,128)(2,1)S(1)}, bf16[24,2048]{1,0:T(8,128)(2,1)S(1)}, u32[]{:S(2)}, u32[]{:S(2)}) collective-permute-start(bf16[24,2048]{1,0:T(8,128)(2,1)S(1)} %get-tuple-element.86), channel_id=1, source_target_pairs={{0,24},{1,25},{2,26},{3,27},{4,28},{5,29},{6,30},{7,31},{8,16},{9,... | collective-permute-start | bytes 294920 | tf_op jit(solution)/shard_map/ppermute | solution.py:701
  67.8 7.5 %collective-permute-start.22 = (bf16[32,2048]{1,0:T(8,128)(2,1)S(1)}, bf16[32,2048]{1,0:T(8,128)(2,1)S(1)}, u32[]{:S(2)}, u32[]{:S(2)}) collective-permute-start(bf16[32,2048]{1,0:T(8,128)(2,1)S(1)} %get-tuple-element.79), channel_id=1, source_target_pairs={{0,1},{1,0},{2,3},{3,2},{4,5},{5,4},{6,7},{7,6},{8,9},{9,8},{10,11... | collective-permute-start | bytes 393224 | tf_op jit(solution)/shard_map/ppermute | solution.py:701
  69.3 7.8 %collective-permute-start.23 = (bf16[32,2048]{1,0:T(8,128)(2,1)S(1)}, bf16[32,2048]{1,0:T(8,128)(2,1)S(1)}, u32[]{:S(2)}, u32[]{:S(2)}) collective-permute-start(bf16[32,2048]{1,0:T(8,128)(2,1)S(1)} %get-tuple-element.80), channel_id=1, source_target_pairs={{0,4},{1,5},{2,6},{3,7},{4,0},{5,1},{6,2},{7,3},{8,12},{9,13},{10,... | collective-permute-start | bytes 393224 | tf_op jit(solution)/shard_map/ppermute | solution.py:701
  70.7 6.4 %collective-permute-start.24 = (bf16[32,2048]{1,0:T(8,128)(2,1)S(1)}, bf16[32,2048]{1,0:T(8,128)(2,1)S(1)}, u32[]{:S(2)}, u32[]{:S(2)}) collective-permute-start(bf16[32,2048]{1,0:T(8,128)(2,1)S(1)} %get-tuple-element.81), channel_id=1, source_target_pairs={{0,5},{1,4},{2,7},{3,6},{4,1},{5,0},{6,3},{7,2},{8,13},{9,12},{10,... | collective-permute-start | bytes 393224 | tf_op jit(solution)/shard_map/ppermute | solution.py:701
  75.2 1.9 %copy-start = (f32[2048]{0:T(1024)S(1)}, f32[2048]{0:T(1024)}, u32[]{:S(2)}) copy-start(f32[2048]{0:T(1024)} %param.29) | copy-start | bytes 24580

commit v6 on v5

--- a/solution.py
+++ b/solution.py
@@ -236,33 +236,8 @@
     return jnp.transpose(square)
 
 
-def attention_kernel(
-    pages_ref, lengths_ref, tp_ref, group_ref, home_ref, q_hbm, fresh_hbm, cache_hbm, residual_hbm, ids_hbm,
-    routed_hbm, w_hbm, own_ref, send_ref, pack_ref,
-    q_ref, fresh_ref, cache_ref, residual_ref, ids_ref, routed_ref, w_ref, context_ref, terms_ref,
-    every_ref, sems,
-):
-    fetches = [
-        pltpu.make_async_copy(source, target, sems.at[i])
-        for i, (source, target) in enumerate(
-            (
-                (q_hbm, q_ref),
-                (cache_hbm, cache_ref),
-                (fresh_hbm, fresh_ref),
-                (ids_hbm, ids_ref),
-                (routed_hbm, routed_ref),
-                (residual_hbm, residual_ref),
-                (w_hbm, w_ref),
-            )
-        )
-    ]
-    for fetch in fetches:
-        fetch.start()
-    tokens = q_ref.shape[0]
-    pool_pages, page_tokens, _ = cache_ref.shape
+def count_positions(pages_ref, lengths_ref, pool_pages, page_tokens, count_ref):
     slots, requests = pages_ref.shape
-    kv_heads = fresh_ref.shape[1] // (2 * HEAD_WIDTH)
-    group = q_ref.shape[1] // (HEAD_WIDTH * kv_heads)
     decodes = requests - 1
     row = lax.broadcasted_iota(jnp.int32, (decodes, page_tokens), 0)
 
@@ -282,23 +257,26 @@
         pool_pages,
         page_tokens,
     )
-    count = jnp.concatenate([first] * (PRE_DEV // decodes) + [later], axis=0)
-    query_place = lax.broadcasted_iota(jnp.int32, (tokens, tokens), 0)
-    key_place = lax.broadcasted_iota(jnp.int32, (tokens, tokens), 1)
+    count_ref[...] = jnp.concatenate([first] * (PRE_DEV // decodes) + [later], axis=0)
+
+
+def attend(start, q_ref, fresh_ref, cache_ref, count_ref, context_ref):
+    rows = context_ref.shape[0]
+    tokens = q_ref.shape[0]
+    kv_heads = fresh_ref.shape[1] // (2 * HEAD_WIDTH)
+    group = q_ref.shape[1] // (HEAD_WIDTH * kv_heads)
+    query_place = start + lax.broadcasted_iota(jnp.int32, (rows, tokens), 0)
+    key_place = lax.broadcasted_iota(jnp.int32, (rows, tokens), 1)
     seen = (key_place == query_place) | ((key_place <= query_place) & (query_place < PRE_DEV))
-    visible = jnp.concatenate([count] * group, axis=0)
     seen = jnp.concatenate([jnp.where(seen, 1.0, 0.0)] * group, axis=0)
+    visible = jnp.concatenate([count_ref[pl.ds(start, rows), :]] * group, axis=0)
     scale = HEAD_WIDTH**-0.5
-    for fetch in fetches[:3]:
-        fetch.wait()
     contract_last = (((1,), (1,)), ((), ()))
     for k in range(kv_heads):
         key_at, value_at = 2 * k * HEAD_WIDTH, (2 * k + 1) * HEAD_WIDTH
+        heads = [k * group + g for g in range(group)]
         query = jnp.concatenate(
-            [
-                q_ref[:, (k * group + g) * HEAD_WIDTH : (k * group + g + 1) * HEAD_WIDTH]
-                for g in range(group)
-            ],
+            [q_ref[pl.ds(start, rows), h * HEAD_WIDTH : (h + 1) * HEAD_WIDTH] for h in heads],
             axis=0,
         )
         keys = cache_ref[:, :, key_at : key_at + HEAD_WIDTH].reshape(-1, HEAD_WIDTH)
@@ -328,58 +306,115 @@
             preferred_element_type=jnp.float32,
         )
         mixed = mixed.astype(jnp.bfloat16)
-        for g in range(group):
-            h = k * group + g
-            context_ref[:, h * HEAD_WIDTH : (h + 1) * HEAD_WIDTH] = mixed[
-                g * tokens : (g + 1) * tokens
-            ]
-    half = tokens // 2
-    width = terms_ref.shape[1]
-    block = 512
-    own_at = pl.multiple_of(tp_ref[0] * half, half)
-    other_at = pl.multiple_of((1 - tp_ref[0]) * half, half)
-    for fetch in fetches[3:5]:
+        for g, h in enumerate(heads):
+            context_ref[:, h * HEAD_WIDTH : (h + 1) * HEAD_WIDTH] = mixed[g * rows : (g + 1) * rows]
+
+
+OUT_BLOCK = 512
+W_PIECES = 4
+
+
+def other_kernel(
+    pages_ref, lengths_ref, tp_ref, group_ref, q_hbm, fresh_hbm, cache_hbm, w_hbm,
+    send_ref, q_ref, fresh_ref, cache_ref, w_ref, count_ref, context_ref, terms_ref, sems,
+):
+    moves = [(q_hbm, q_ref), (fresh_hbm, fresh_ref), (cache_hbm, cache_ref)]
+    depth = w_ref.shape[0] // W_PIECES
+    parts = [slice(i * depth, (i + 1) * depth) for i in range(W_PIECES)]
+    moves += [(w_hbm.at[part, :], w_ref.at[part, :]) for part in parts]
+    fetches = [
+        pltpu.make_async_copy(source, target, sems.at[i])
+        for i, (source, target) in enumerate(moves)
+    ]
+    for fetch in fetches:
+        fetch.start()
+    half = context_ref.shape[0]
+    start = pl.multiple_of((1 - tp_ref[0]) * half, half)
+    count_positions(pages_ref, lengths_ref, cache_ref.shape[0], cache_ref.shape[1], count_ref)
+    for fetch in fetches[:3]:
+        fetch.wait()
+    attend(start, q_ref, fresh_ref, cache_ref, count_ref, context_ref)
+    for i, part in enumerate(parts):
+        fetches[3 + i].wait()
+        for at in range(0, w_ref.shape[1], OUT_BLOCK):
+            cols = slice(at, at + OUT_BLOCK)
+            terms = jnp.dot(
+                context_ref[:, part], w_ref[part, cols], preferred_element_type=jnp.float32
+            )
+            terms_ref[:, cols] = terms if i == 0 else terms_ref[:, cols] + terms
+    send_ref[...] = terms_ref[...].astype(jnp.bfloat16)
+
+
+def other_terms(pages, lengths, tp_index, group, queries, fresh, cache, w_out):
+    half = queries.shape[0] // 2
+    moved = (queries, fresh, cache, w_out)
+    return pl.pallas_call(
+        other_kernel,
+        out_shape=(jax.ShapeDtypeStruct((half, w_out.shape[1]), jnp.bfloat16),)
+        + tuple(jax.ShapeDtypeStruct(v.shape, v.dtype) for v in moved),
+        in_specs=[smem()] * 4 + [hbm()] * 4,
+        out_specs=(vmem(),) * 5,
+        scratch_shapes=[
+            pltpu.VMEM((queries.shape[0], cache.shape[0] * cache.shape[1]), jnp.float32),
+            pltpu.VMEM((half, queries.shape[1]), jnp.bfloat16),
+            pltpu.VMEM((half, w_out.shape[1]), jnp.float32),
+            pltpu.SemaphoreType.DMA((3 + W_PIECES,)),
+        ],
+        compiler_params=pltpu.CompilerParams(vmem_limit_bytes=16 * MIB),
+        name="other_terms",
+    )(stay(pages), stay(lengths), tp_index, group, *[stay(v) for v in moved])
+
+
+def own_kernel(
+    pages_ref, lengths_ref, tp_ref, home_ref, q_ref, fresh_ref, cache_ref, w_ref,
+    residual_hbm, ids_hbm, routed_hbm,
+    own_ref, pack_ref, residual_ref, ids_ref, routed_ref, count_ref, context_ref, every_ref, sems,
+):
+    moves = ((ids_hbm, ids_ref), (routed_hbm, routed_ref), (residual_hbm, residual_ref))
+    fetches = [
+        pltpu.make_async_copy(source, target, sems.at[i])
+        for i, (source, target) in enumerate(moves)
+    ]
+    for fetch in fetches:
+        fetch.start()
+    half = context_ref.shape[0]
+    start = pl.multiple_of(tp_ref[0] * half, half)
+    count_positions(pages_ref, lengths_ref, cache_ref.shape[0], cache_ref.shape[1], count_ref)
+    attend(start, q_ref, fresh_ref, cache_ref, count_ref, context_ref)
+    for fetch in fetches:
         fetch.wait()
     every_ref[...] = pack_shares(ids_ref[...], routed_ref[...], home_ref)
-    pack_ref[...] = every_ref[pl.ds(own_at, half), :].astype(jnp.bfloat16)
-    for fetch in fetches[5:]:
-        fetch.wait()
-    for at in range(0, width, block):
-        cols = slice(at, at + block)
-        terms_ref[:, cols] = jnp.dot(
+    pack_ref[...] = every_ref[pl.ds(start, half), :].astype(jnp.bfloat16)
+    for at in range(0, w_ref.shape[1], OUT_BLOCK):
+        cols = slice(at, at + OUT_BLOCK)
+        own_ref[:, cols] = residual_ref[pl.ds(start, half), cols].astype(jnp.float32) + jnp.dot(
             context_ref[...], w_ref[:, cols], preferred_element_type=jnp.float32
         )
-    own_ref[...] = terms_ref[pl.ds(own_at, half), :] + residual_ref[
-        pl.ds(own_at, half), :
-    ].astype(jnp.float32)
-    send_ref[...] = terms_ref[pl.ds(other_at, half), :].astype(jnp.bfloat16)
-
-
-def attention_terms(
-    pages, lengths, tp_index, group, home, queries, fresh, cache, residual, ids, routed, w_out
-):
+
+
+def own_terms(pages, lengths, tp_index, home, kept, residual, ids, routed):
     tokens, width = residual.shape
     half = tokens // 2
-    moved = (queries, fresh, cache, residual, ids.T, routed.T, w_out)
-    return pl.pallas_call(
-        attention_kernel,
+    queries, _, cache, _ = kept
+    moved = (residual, ids, routed)
+    return pl.pallas_call(
+        own_kernel,
         out_shape=(
             jax.ShapeDtypeStruct((half, width), jnp.float32),
-            jax.ShapeDtypeStruct((half, width), jnp.bfloat16),
             jax.ShapeDtypeStruct((half, LANES), jnp.bfloat16),
         ),
-        in_specs=[smem()] * 5 + [hbm()] * 7,
-        out_specs=(vmem(),) * 3,
+        in_specs=[smem()] * 4 + [vmem()] * 4 + [hbm()] * 3,
+        out_specs=(vmem(),) * 2,
         scratch_shapes=[pltpu.VMEM(v.shape, v.dtype) for v in moved]
         + [
-            pltpu.VMEM(queries.shape, jnp.bfloat16),
-            pltpu.VMEM((tokens, width), jnp.float32),
+            pltpu.VMEM((tokens, cache.shape[0] * cache.shape[1]), jnp.float32),
+            pltpu.VMEM((half, queries.shape[1]), jnp.bfloat16),
             pltpu.VMEM((LANES, LANES), jnp.float32),
-            pltpu.SemaphoreType.DMA((7,)),
+            pltpu.SemaphoreType.DMA((3,)),
         ],
-        compiler_params=pltpu.CompilerParams(vmem_limit_bytes=40 * MIB),
-        name="attention_terms",
-    )(stay(pages.T), stay(lengths), tp_index, group, stay(home), *[stay(v) for v in moved])
+        compiler_params=pltpu.CompilerParams(vmem_limit_bytes=16 * MIB),
+        name="own_terms",
+    )(stay(pages), stay(lengths), tp_index, stay(home), *kept, *[stay(v) for v in moved])
 
 
 LATE = pl.CostEstimate(flops=3 * 10**10, bytes_accessed=1 << 20, transcendentals=0)
@@ -435,30 +470,25 @@
     )(*pieces)
 
 
-def hidden_units(groups, group_ref, x_ref, w0_ref, wg1_ref, wu1_ref, h_ref, ready):
+def hidden_units(groups, group_ref, x_ref, w_refs, h_ref, ready):
     rows = x_ref.shape[0]
-    width, hidden = wg1_ref.shape
+    width = w_refs[0].shape[0]
+    hidden = h_ref.shape[1] // 2
     lane = lax.broadcasted_iota(jnp.int32, (rows, LANES), 1)
     packed = x_ref[:, width:].astype(jnp.float32)
-
-    def product(w_ref):
-        return jnp.dot(x_ref[:, :width], w_ref[...], preferred_element_type=jnp.float32)
-
-    def store(e, gate, up):
+    for e in (1, 0):
         group = group_ref[0] ^ e
         share = jnp.sum(
             jnp.where((lane == group) | (lane == group + groups), packed, 0.0),
             axis=1,
             keepdims=True,
         )
+        ready(e)
+        both = jnp.dot(x_ref[:, :width], w_refs[e][...], preferred_element_type=jnp.float32)
+        gate, up = both[:, :hidden], both[:, hidden:]
         h_ref[:, e * hidden : (e + 1) * hidden] = (
             share * up * (gate / (1.0 + jnp.exp(-gate)))
         ).astype(jnp.bfloat16)
-
-    store(1, product(wg1_ref), product(wu1_ref))
-    ready()
-    both = product(w0_ref)
-    store(0, both[:, :hidden], both[:, hidden:])
 
 
 DOWN_BLOCK = 512
@@ -474,8 +504,8 @@
 
 
 def near_kernel(
-    groups, group_ref, r0, r1, r2, r3, far_ref, wg1_ref, wu1_ref, wg0, wu0, wd0, wd1,
-    out_ref, w0_ref, down_ref, x_ref, h_ref, sems,
+    groups, group_ref, r0, r1, r2, r3, far_ref, wg1, wu1, wg0, wu0, wd0, wd1,
+    out_ref, w0_ref, w1_ref, down_ref, x_ref, h_ref, sems,
 ):
     hidden = wg0.shape[1]
     fetches = [
@@ -486,6 +516,8 @@
                 (wu0, w0_ref.at[:, hidden:]),
                 (wd0, down_ref.at[:hidden, :]),
                 (wd1, down_ref.at[hidden:, :]),
+                (wg1, w1_ref.at[:, :hidden]),
+                (wu1, w1_ref.at[:, hidden:]),
             )
         )
     ]
@@ -493,11 +525,11 @@
         fetch.start()
     gather_pieces((r0, r1, r2, r3, far_ref), x_ref)
 
-    def ready():
-        fetches[0].wait()
-        fetches[1].wait()
-
-    hidden_units(groups, group_ref, x_ref, w0_ref, wg1_ref, wu1_ref, h_ref, ready)
+    def ready(e):
+        for fetch in fetches[4:] if e else fetches[:2]:
+            fetch.wait()
+
+    hidden_units(groups, group_ref, x_ref, (w0_ref, w1_ref), h_ref, ready)
     fetches[2].wait()
     fetches[3].wait()
     height = out_ref.shape[0]
@@ -526,14 +558,15 @@
         out_shape=(
             jax.ShapeDtypeStruct((height, width), jnp.float32),
             jax.ShapeDtypeStruct((width, 2 * hidden), jnp.bfloat16),
+            jax.ShapeDtypeStruct((width, 2 * hidden), jnp.bfloat16),
             jax.ShapeDtypeStruct((2 * hidden, width), jnp.bfloat16),
         ),
         in_specs=[smem()] + [vmem()] * 7 + [hbm()] * 4,
-        out_specs=(vmem(),) * 3,
+        out_specs=(vmem(),) * 4,
         scratch_shapes=[
             pltpu.VMEM((padded, width + LANES), jnp.bfloat16),
             pltpu.VMEM((padded, 2 * hidden), jnp.bfloat16),
-            pltpu.SemaphoreType.DMA((4,)),
+            pltpu.SemaphoreType.DMA((6,)),
         ],
         compiler_params=pltpu.CompilerParams(vmem_limit_bytes=24 * MIB),
         cost_estimate=expert_cost(height, width, hidden),
@@ -542,10 +575,10 @@
 
 
 def piece_kernel(groups, count, group_ref, *refs):
-    pieces, (w0_ref, wg1_ref, wu1_ref, down_ref) = refs[:count], refs[count : count + 4]
-    outs, (x_ref, h_ref) = refs[count + 4 : 2 * count + 4], refs[2 * count + 4 :]
+    pieces, (w0_ref, w1_ref, down_ref) = refs[:count], refs[count : count + 3]
+    outs, (x_ref, h_ref) = refs[count + 3 : 2 * count + 3], refs[2 * count + 3 :]
     gather_pieces(pieces, x_ref)
-    hidden_units(groups, group_ref, x_ref, w0_ref, wg1_ref, wu1_ref, h_ref, lambda: None)
+    hidden_units(groups, group_ref, x_ref, (w0_ref, w1_ref), h_ref, lambda e: None)
     for col in range(0, down_ref.shape[1], DOWN_BLOCK):
         cols = slice(col, col + DOWN_BLOCK)
         down = jnp.dot(h_ref[...], down_ref[:, cols], preferred_element_type=jnp.float32)
@@ -555,17 +588,17 @@
             at += out.shape[0]
 
 
-def piece_rows(groups, group, pieces, w0, wg1, wu1, down):
+def piece_rows(groups, group, pieces, w0, w1, down):
     count = len(pieces)
     height = sum(piece.shape[0] for piece in pieces)
     padded = -(-height // 16) * 16
-    width, hidden = wg1.shape
+    width, hidden = w1.shape[0], w1.shape[1] // 2
     return pl.pallas_call(
         functools.partial(piece_kernel, groups, count),
         out_shape=tuple(
             jax.ShapeDtypeStruct((piece.shape[0], width), jnp.bfloat16) for piece in pieces
         ),
-        in_specs=[smem()] + [vmem()] * (count + 4),
+        in_specs=[smem()] + [vmem()] * (count + 3),
         out_specs=(vmem(),) * count,
         scratch_shapes=[
             pltpu.VMEM((padded, width + LANES), jnp.bfloat16),
@@ -574,7 +607,7 @@
         compiler_params=pltpu.CompilerParams(vmem_limit_bytes=24 * MIB),
         cost_estimate=expert_cost(height, width, hidden),
         name="piece_rows",
-    )(group, *pieces, w0, wg1, wu1, down)
+    )(group, *pieces, w0, w1, down)
 
 
 def plane_sum_kernel(near_ref, g1, g2, g3, m1, m2, m3):
@@ -701,7 +734,7 @@
     return lax.ppermute(value, ALL, pairs)
 
 
-PLANE = ((0, 0), (0, 1), (1, 0), (1, 1))
+PLANE = ((0, 0), (1, 1), (0, 1), (1, 0))
 
 
 def swap_z(pieces):
@@ -723,11 +756,15 @@
     far = half * 3 // 4
     groups = expert_home.shape[0]
     weights = (w_gate[0], w_up[0], w_down[0])
-    partner_weights = tuple(swap(w, 0, 0, 1, 0) for w in weights)
+    partner_weights = tuple(swap(stay(w), 0, 0, 1, 0) for w in weights)
     group = req_index.reshape(1)
-    own_state, sent, pack = attention_terms(
-        request_page_index, cache_length_rows, tp_index.reshape(1), group, expert_home,
-        queries, fresh_key_value, key_value_cache, residual, route_ids, route_weights, w_out,
+    tp_index, pages = tp_index.reshape(1), request_page_index.T
+    sent, *kept = other_terms(
+        pages, cache_length_rows, tp_index, group, queries, fresh_key_value, key_value_cache, w_out
+    )
+    own_state, pack = own_terms(
+        pages, cache_length_rows, tp_index, expert_home, kept, residual, route_ids.T,
+        route_weights.T,
     )
     got, partner_weights = barrier(swap(sent, 0, 0, 0, 1), partner_weights)
     state, far_rows, last_rows = norm_rows(own_state, got, pack, gain_in[None, :], far)
@@ -739,8 +776,8 @@
     onward_z = join_rows(plane_rows, (far,) * 4, None, "onward_z")
     z_pieces = swap_z((onward_z,) * 3)
     plane_pieces = swap_plane((onward_plane,) * 3)
-    near, w0, down = near_rows(groups, group, plane_rows, far_pieces, weights, partner_weights)
-    parts = piece_rows(groups, group, z_pieces + plane_pieces, w0, *partner_weights[:2], down)
+    near, *kept = near_rows(groups, group, plane_rows, far_pieces, weights, partner_weights)
+    parts = piece_rows(groups, group, z_pieces + plane_pieces, *kept)
     z_parts, plane_parts = swap_z(parts[:3]), swap_plane(parts[3:])
     first = first_sum(near, z_parts[0], half)
     plane_parts, first = barrier(plane_parts, first)

time: 78.1 us -> 76.7 us (0.982)
  waiting for transfers between devices: 25.2 us -> 21.2 us
  Pallas kernels: 14.7 us -> 17.7 us
    ppermute x28, waiting for transfers between devices: 25.2 us -> 21.2 us  [swap(): return lax.ppermute(value, ALL, pairs)]
    pallas_call x1 -> x2, Pallas kernels: 4.33 us -> 7.26 us  [the longest x1 3.75 us: other_terms(): pl.pallas_call(other_kernel, out_shape=(jax.ShapeDtypeStruct((half, w_out...]
    pallas_call x1, Pallas kernels: 4.87 us -> 5.72 us  [near_rows(): pl.pallas_call(functools.partial(near_kernel, groups), out_shape=(jax.Sha...]
  transfers between devices with their start and end apart: 28 -> 28, of which waited for: 9 -> 11; matrix products, arithmetic and copies ran while one was open for 0% -> 0% of each run, Pallas kernels for 12% -> 17%
where the time goes in v6:
time: 76.7 us; the launch traced here: 76.5 us
  starting transfers between devices  37.4 us (49%)
  waiting for transfers between devices  21.2 us (28%)
  Pallas kernels  17.7 us (23%)
    ppermute x28, starting transfers between devices, swap(): return lax.ppermute(value, ALL, pairs)  37.4 us
    ppermute x28, waiting for transfers between devices, swap(): return lax.ppermute(value, ALL, pairs)  21.2 us
    pallas_call x1, Pallas kernels, near_rows(): pl.pallas_call(functools.partial(near_kernel, groups), out_shape=(jax.Sha...  5.72 us
    pallas_call x1, Pallas kernels, other_terms(): pl.pallas_call(other_kernel, out_shape=(jax.ShapeDtypeStruct((half, w_out...  3.75 us
    pallas_call x1, Pallas kernels, own_terms(): pl.pallas_call(own_kernel, out_shape=(jax.ShapeDtypeStruct((half, width),...  3.5 us
    pallas_call x1, Pallas kernels, piece_rows(): pl.pallas_call(functools.partial(piece_kernel, groups, count), out_shape=...  3.42 us
  transfers between devices with their start and end apart: 28, of which 11 were waited for; matrix products, arithmetic and copies ran while one was open for 0% of the time, Pallas kernels for 17%

profile of v6, /device:TPU:0, one launch (start us, length us, event | category | flops | bytes accessed | tf_op | source)
XLA Modules:
  0.0 76.5 jit_solution(7171647210560369309)
XLA Ops:
  1.0 3.8 %other_terms.1 = (bf16[32,2048]{1,0:T(8,128)(2,1)S(1)}, bf16[64,1024]{1,0:T(8,128)(2,1)S(1)}, bf16[64,512]{1,0:T(8,128)(2,1)S(1)}, bf16[4,128,512]{2,1,0:T(8,128)(2,1)S(1)}, bf16[1024,2048]{1,0:T(8,128)(2,1)S(1)}) custom-call(s32[4,9]{1,0:T(4,128)} %bitcast.18, s32[9]{0:T(128)} %lengths_ref.3, s32[1]{0:T(128)} %bitcast.2.tp_ref, s32[1]{0:T(128)} %bitcast.group_ref, ...), custom_call_target="tpu_custom_call" | custom-call | tf_op jit(solution)/shard_map/other_terms/pallas_call | solution.py:351
  4.7 2.5 %collective-permute-start = (bf16[32,2048]{1,0:T(8,128)(2,1)S(1)}, bf16[32,2048]{1,0:T(8,128)(2,1)S(1)}, u32[]{:S(2)}, u32[]{:S(2)}) collective-permute-start(bf16[32,2048]{1,0:T(8,128)(2,1)S(1)} %get-tuple-element.58), channel_id=1, source_target_pairs={{0,1},{1,0},{2,3},{3,2},{4,5},{5,4},{6,7},{7,6},{8,9},{9,8},{10,11... | collective-permute-start | bytes 393224 | tf_op jit(solution)/shard_map/ppermute | solution.py:734
  7.3 3.5 %own_terms.1 = (f32[32,2048]{1,0:T(8,128)S(1)}, bf16[32,128]{1,0:T(8,128)(2,1)S(1)}) custom-call(s32[4,9]{1,0:T(4,128)} %bitcast.19, s32[9]{0:T(128)} %lengths_ref.3, s32[1]{0:T(128)} %bitcast.2.tp_ref, s32[16]{0:T(128)} %home_ref.1, bf16[64,1024]{1,0:T(8,128)(2,1)S(1)} %get-tuple-element.53.q_ref, bf16[64,512]{1,0:T(8,128)(2,1)S(1)} %get-tuple-element.54.fresh_ref, ...), custom_call_target="tpu_custom_call" | custom-call | tf_op jit(solution)/shard_map/own_terms/pallas_call | solution.py:400
  10.8 0.7 collective-permute-done.got_ref
  11.6 1.9 %collective-permute-start.7 = (bf16[24,2176]{1,0:T(8,128)(2,1)S(1)}, bf16[24,2176]{1,0:T(8,128)(2,1)S(1)}, u32[]{:S(2)}, u32[]{:S(2)}) collective-permute-start(bf16[24,2176]{1,0:T(8,128)(2,1)S(1)} %get-tuple-element.61.refs_0_), channel_id=1, source_target_pairs={{0,8},{1,9},{2,10},{3,11},{4,12},{5,13},{6,14},{7,15},{8,0},{9,1},... | collective-permute-start | bytes 313352 | tf_op jit(solution)/shard_map/ppermute | solution.py:734
  13.5 2.6 %collective-permute-start.8 = (bf16[24,2176]{1,0:T(8,128)(2,1)S(1)}, bf16[24,2176]{1,0:T(8,128)(2,1)S(1)}, u32[]{:S(2)}, u32[]{:S(2)}) collective-permute-start(bf16[24,2176]{1,0:T(8,128)(2,1)S(1)} %get-tuple-element.61.refs_0_), channel_id=1, source_target_pairs={{0,16},{1,17},{2,18},{3,19},{4,20},{5,21},{6,22},{7,23},{8,24},{9,... | collective-permute-start | bytes 313352 | tf_op jit(solution)/shard_map/ppermute | solution.py:734
  16.1 2.7 %collective-permute-start.4 = (bf16[32,2176]{1,0:T(8,128)(2,1)S(1)}, bf16[32,2176]{1,0:T(8,128)(2,1)S(1)}, u32[]{:S(2)}, u32[]{:S(2)}) collective-permute-start(bf16[32,2176]{1,0:T(8,128)(2,1)S(1)} %own_rows.1.r0.refs_0_), channel_id=1, source_target_pairs={{0,5},{1,4},{2,7},{3,6},{4,1},{5,0},{6,3},{7,2},{8,13},{9,12},{10,... | collective-permute-start | bytes 417800 | tf_op jit(solution)/shard_map/ppermute | solution.py:734
  18.9 0.5 collective-permute-start.5
  19.7 4.6 %collective-permute-done.8.refs_1_ = bf16[24,2176]{1,0:T(8,128)(2,1)S(1)} collective-permute-done((bf16[24,2176]{1,0:T(8,128)(2,1)S(1)}, bf16[24,2176]{1,0:T(8,128)(2,1)S(1)}, u32[]{:S(2)}, u32[]{:S(2)}) %collective-permute-start.8) | collective-permute-done | bytes 104480 | tf_op jit(solution)/shard_map/ppermute | solution.py:734
  24.3 0.6 collective-permute-done.5.r2.refs_2_
  24.9 1.2 %collective-permute-start.10 = (bf16[32,2176]{1,0:T(8,128)(2,1)S(1)}, bf16[32,2176]{1,0:T(8,128)(2,1)S(1)}, u32[]{:S(2)}, u32[]{:S(2)}) collective-permute-start(bf16[32,2176]{1,0:T(8,128)(2,1)S(1)} %onward_z.1), channel_id=1, source_target_pairs={{0,8},{1,9},{2,10},{3,11},{4,12},{5,13},{6,14},{7,15},{8,0},{9,1},... | collective-permute-start | bytes 417800 | tf_op jit(solution)/shard_map/ppermute | solution.py:734
  26.1 2.4 %collective-permute-start.13 = (bf16[72,2176]{1,0:T(8,128)(2,1)S(1)}, bf16[72,2176]{1,0:T(8,128)(2,1)S(1)}, u32[]{:S(2)}, u32[]{:S(2)}) collective-permute-start(bf16[72,2176]{1,0:T(8,128)(2,1)S(1)} %onward_plane.1.far_ref), channel_id=1, source_target_pairs={{0,5},{1,4},{2,7},{3,6},{4,1},{5,0},{6,3},{7,2},{8,13},{9,12},{10,... | collective-permute-start | bytes 940040 | tf_op jit(solution)/shard_map/ppermute | solution.py:734
  28.6 0.5 collective-permute-start.14
  29.6 3.0 %collective-permute-start.11 = (bf16[32,2176]{1,0:T(8,128)(2,1)S(1)}, bf16[32,2176]{1,0:T(8,128)(2,1)S(1)}, u32[]{:S(2)}, u32[]{:S(2)}) collective-permute-start(bf16[32,2176]{1,0:T(8,128)(2,1)S(1)} %onward_z.1), channel_id=1, source_target_pairs={{0,16},{1,17},{2,18},{3,19},{4,20},{5,21},{6,22},{7,23},{8,24},{9,... | collective-permute-start | bytes 417800 | tf_op jit(solution)/shard_map/ppermute | solution.py:734
  32.6 2.1 %collective-permute-start.12 = (bf16[32,2176]{1,0:T(8,128)(2,1)S(1)}, bf16[32,2176]{1,0:T(8,128)(2,1)S(1)}, u32[]{:S(2)}, u32[]{:S(2)}) collective-permute-start(bf16[32,2176]{1,0:T(8,128)(2,1)S(1)} %onward_z.1), channel_id=1, source_target_pairs={{0,24},{1,25},{2,26},{3,27},{4,28},{5,29},{6,30},{7,31},{8,16},{9,... | collective-permute-start | bytes 417800 | tf_op jit(solution)/shard_map/ppermute | solution.py:734
  34.7 5.7 %near_rows.1 = (f32[200,2048]{1,0:T(8,128)S(1)}, bf16[2048,768]{1,0:T(8,128)(2,1)S(1)}, bf16[2048,768]{1,0:T(8,128)(2,1)S(1)}, bf16[768,2048]{1,0:T(8,128)(2,1)S(1)}) custom-call(s32[1]{0:T(128)} %bitcast.group_ref, bf16[32,2176]{1,0:T(8,128)(2,1)S(1)} %own_rows.1.r0.refs_0_, bf16[32,2176]{1,0:T(8,128)(2,1)S(1)} %collective-permute-done.4.r1.refs_1_, ...), custom_call_target="tpu_custom_call" | custom-call | flops 1887436800 | bytes 9437184 | tf_op jit(solution)/shard_map/near_rows/pallas_call | solution.py:556
  40.4 1.0 %collective-permute-done.11.refs_1_ = bf16[32,2176]{1,0:T(8,128)(2,1)S(1)} collective-permute-done((bf16[32,2176]{1,0:T(8,128)(2,1)S(1)}, bf16[32,2176]{1,0:T(8,128)(2,1)S(1)}, u32[]{:S(2)}, u32[]{:S(2)}) %collective-permute-start.11) | collective-permute-done | bytes 139296 | tf_op jit(solution)/shard_map/ppermute | solution.py:734
  41.8 3.4 %piece_rows.1 = (bf16[32,2048]{1,0:T(8,128)(2,1)S(1)}, bf16[32,2048]{1,0:T(8,128)(2,1)S(1)}, bf16[32,2048]{1,0:T(8,128)(2,1)S(1)}, bf16[72,2048]{1,0:T(8,128)(2,...) custom-call(s32[1]{0:T(128)} %bitcast.group_ref, ...), custom_call_target="tpu_custom_call" | custom-call | flops 2944401408 | bytes 9437184 | tf_op jit(solution)/shard_map/piece_rows/pallas_call | solution.py:596
  45.2 1.8 %collective-permute-start.19 = (bf16[32,2048]{1,0:T(8,128)(2,1)S(1)}, bf16[32,2048]{1,0:T(8,128)(2,1)S(1)}, u32[]{:S(2)}, u32[]{:S(2)}) collective-permute-start(bf16[32,2048]{1,0:T(8,128)(2,1)S(1)} %get-tuple-element.77), channel_id=1, source_target_pairs={{0,8},{1,9},{2,10},{3,11},{4,12},{5,13},{6,14},{7,15},{8,0},{9,1},... | collective-permute-start | bytes 393224 | tf_op jit(solution)/shard_map/ppermute | solution.py:734
  47.0 2.7 %collective-permute-start.16 = (bf16[72,2048]{1,0:T(8,128)(2,1)S(1)}, bf16[72,2048]{1,0:T(8,128)(2,1)S(1)}, u32[]{:S(2)}, u32[]{:S(2)}) collective-permute-start(bf16[72,2048]{1,0:T(8,128)(2,1)S(1)} %get-tuple-element.74), channel_id=1, source_target_pairs={{0,5},{1,4},{2,7},{3,6},{4,1},{5,0},{6,3},{7,2},{8,13},{9,12},{10,... | collective-permute-start | bytes 884744 | tf_op jit(solution)/shard_map/ppermute | solution.py:734
  50.4 1.5 %collective-permute-start.20 = (bf16[32,2048]{1,0:T(8,128)(2,1)S(1)}, bf16[32,2048]{1,0:T(8,128)(2,1)S(1)}, u32[]{:S(2)}, u32[]{:S(2)}) collective-permute-start(bf16[32,2048]{1,0:T(8,128)(2,1)S(1)} %get-tuple-element.79), channel_id=1, source_target_pairs={{0,16},{1,17},{2,18},{3,19},{4,20},{5,21},{6,22},{7,23},{8,24},{9,... | collective-permute-start | bytes 393224 | tf_op jit(solution)/shard_map/ppermute | solution.py:734
  52.0 1.1 %collective-permute-start.21 = (bf16[32,2048]{1,0:T(8,128)(2,1)S(1)}, bf16[32,2048]{1,0:T(8,128)(2,1)S(1)}, u32[]{:S(2)}, u32[]{:S(2)}) collective-permute-start(bf16[32,2048]{1,0:T(8,128)(2,1)S(1)} %get-tuple-element.80), channel_id=1, source_target_pairs={{0,24},{1,25},{2,26},{3,27},{4,28},{5,29},{6,30},{7,31},{8,16},{9,... | collective-permute-start | bytes 393224 | tf_op jit(solution)/shard_map/ppermute | solution.py:734
  53.2 4.7 %collective-permute-done.16.g1 = bf16[72,2048]{1,0:T(8,128)(2,1)S(1)} collective-permute-done((bf16[72,2048]{1,0:T(8,128)(2,1)S(1)}, bf16[72,2048]{1,0:T(8,128)(2,1)S(1)}, u32[]{:S(2)}, u32[]{:S(2)}) %collective-permute-start.16) | collective-permute-done | bytes 294944 | tf_op jit(solution)/shard_map/ppermute | solution.py:734
  57.8 4.3 %collective-permute-done.17.g2 = bf16[72,2048]{1,0:T(8,128)(2,1)S(1)} collective-permute-done((bf16[72,2048]{1,0:T(8,128)(2,1)S(1)}, bf16[72,2048]{1,0:T(8,128)(2,1)S(1)}, u32[]{:S(2)}, u32[]{:S(2)}) %collective-permute-start.17) | collective-permute-done | bytes 294944 | tf_op jit(solution)/shard_map/ppermute | solution.py:734
  62.3 1.3 %collective-permute-start.25 = (bf16[24,2048]{1,0:T(8,128)(2,1)S(1)}, bf16[24,2048]{1,0:T(8,128)(2,1)S(1)}, u32[]{:S(2)}, u32[]{:S(2)}) collective-permute-start(bf16[24,2048]{1,0:T(8,128)(2,1)S(1)} %get-tuple-element.94), channel_id=1, source_target_pairs={{0,8},{1,9},{2,10},{3,11},{4,12},{5,13},{6,14},{7,15},{8,0},{9,1},... | collective-permute-start | bytes 294920 | tf_op jit(solution)/shard_map/ppermute | solution.py:734
  63.6 2.7 %collective-permute-start.26 = (bf16[24,2048]{1,0:T(8,128)(2,1)S(1)}, bf16[24,2048]{1,0:T(8,128)(2,1)S(1)}, u32[]{:S(2)}, u32[]{:S(2)}) collective-permute-start(bf16[24,2048]{1,0:T(8,128)(2,1)S(1)} %get-tuple-element.95), channel_id=1, source_target_pairs={{0,16},{1,17},{2,18},{3,19},{4,20},{5,21},{6,22},{7,23},{8,24},{9,... | collective-permute-start | bytes 294920 | tf_op jit(solution)/shard_map/ppermute | solution.py:734
  66.3 0.6 collective-permute-start.27
  67.0 2.6 %collective-permute-start.22 = (bf16[32,2048]{1,0:T(8,128)(2,1)S(1)}, bf16[32,2048]{1,0:T(8,128)(2,1)S(1)}, u32[]{:S(2)}, u32[]{:S(2)}) collective-permute-start(bf16[32,2048]{1,0:T(8,128)(2,1)S(1)} %get-tuple-element.89), channel_id=1, source_target_pairs={{0,5},{1,4},{2,7},{3,6},{4,1},{5,0},{6,3},{7,2},{8,13},{9,12},{10,... | collective-permute-start | bytes 393224 | tf_op jit(solution)/shard_map/ppermute | solution.py:734
  69.6 0.5 collective-permute-start.23
  70.5 3.4 %collective-permute-done.27.z3 = bf16[24,2048]{1,0:T(8,128)(2,1)S(1)} collective-permute-done((bf16[24,2048]{1,0:T(8,128)(2,1)S(1)}, bf16[24,2048]{1,0:T(8,128)(2,1)S(1)}, u32[]{:S(2)}, u32[]{:S(2)}) %collective-permute-start.27) | collective-permute-done | bytes 98336 | tf_op jit(solution)/shard_map/ppermute | solution.py:734
  74.3 1.3 %collective-permute-done.23.p2 = bf16[32,2048]{1,0:T(8,128)(2,1)S(1)} collective-permute-done((bf16[32,2048]{1,0:T(8,128)(2,1)S(1)}, bf16[32,2048]{1,0:T(8,128)(2,1)S(1)}, u32[]{:S(2)}, u32[]{:S(2)}) %collective-permute-start.23) | collective-permute-done | bytes 131104 | tf_op jit(solution)/shard_map/ppermute | solution.py:734
  75.7 0.8 %final_rows.1 = bf16[32,2048]{1,0:T(8,128)(2,1)} custom-call(f32[32,2048]{1,0:T(8,128)S(1)} %total_rows.1.total_ref, bf16[32,2048]{1,0:T(8,128)(2,1)S(1)} %collective-permute-done.22.p1, bf16[32,2048]{1,0:T(8,128)(2,1)S(1)} %collective-permute-done.23.p2, bf16[32,2048]{1,0:T(8,128)(2,1)S(1)} %collective-permute-done.24.p3, f32[1,2048]{1,0:T(1,128)S(1)} %bitcast.10), custom_call_target="tpu_custom_call" | custom-call | tf_op jit(solution)/shard_map/final_rows/pallas_call | solution.py:712
  (45 shorter events, 4.3 us)
Async XLA Ops:
  0.0 11.4 %collective-permute-start.1 = (bf16[2048,384]{1,0:T(8,128)(2,1)}, bf16[2048,384]{1,0:T(8,128)(2,1)S(1)}, u32[]{:S(2)}, u32[]{:S(2)}) collective-permute-start(bf16[2048,384]{1,0:T(8,128)(2,1)} %bitcast.12), channel_id=1, source_target_pairs={{0,2},{1,3},{2,0},{3,1},{4,6},{5,7},{6,4},{7,5},{8,10},{9,11},{10,... | collective-permute-start | bytes 4718600 | tf_op jit(solution)/shard_map/ppermute | solution.py:734
  0.5 11.0 %collective-permute-start.2 = (bf16[2048,384]{1,0:T(8,128)(2,1)}, bf16[2048,384]{1,0:T(8,128)(2,1)S(1)}, u32[]{:S(2)}, u32[]{:S(2)}) collective-permute-start(bf16[2048,384]{1,0:T(8,128)(2,1)} %bitcast.14), channel_id=1, source_target_pairs={{0,2},{1,3},{2,0},{3,1},{4,6},{5,7},{6,4},{7,5},{8,10},{9,11},{10,... | collective-permute-start | bytes 4718600 | tf_op jit(solution)/shard_map/ppermute | solution.py:734
  0.5 11.0 %collective-permute-start.3 = (bf16[384,2048]{1,0:T(8,128)(2,1)}, bf16[384,2048]{1,0:T(8,128)(2,1)}, u32[]{:S(2)}, u32[]{:S(2)}) collective-permute-start(bf16[384,2048]{1,0:T(8,128)(2,1)} %bitcast.16), channel_id=1, source_target_pairs={{0,2},{1,3},{2,0},{3,1},{4,6},{5,7},{6,4},{7,5},{8,10},{9,11},{10,... | collective-permute-start | bytes 4718600 | tf_op jit(solution)/shard_map/ppermute | solution.py:734
  4.7 6.7 %collective-permute-start = (bf16[32,2048]{1,0:T(8,128)(2,1)S(1)}, bf16[32,2048]{1,0:T(8,128)(2,1)S(1)}, u32[]{:S(2)}, u32[]{:S(2)}) collective-permute-start(bf16[32,2048]{1,0:T(8,128)(2,1)S(1)} %get-tuple-element.58), channel_id=1, source_target_pairs={{0,1},{1,0},{2,3},{3,2},{4,5},{5,4},{6,7},{7,6},{8,9},{9,8},{10,11... | collective-permute-start | bytes 393224 | tf_op jit(solution)/shard_map/ppermute | solution.py:734
  7.3 4.2 %copy-start.1 = (f32[2048]{0:T(1024)S(1)}, f32[2048]{0:T(1024)}, u32[]{:S(2)}) copy-start(f32[2048]{0:T(1024)} %param.22) | copy-start | bytes 24580
  11.5 4.7 %copy-start.2 = (bf16[2048,384]{1,0:T(8,128)(2,1)}, bf16[2048,384]{1,0:T(8,128)(2,1)S(1)}, u32[]{:S(2)}) copy-start(bf16[2048,384]{1,0:T(8,128)(2,1)S(1)} %collective-permute-done.1.wg1) | copy-start | bytes 4718596
  11.5 4.7 %copy-start.3 = (bf16[2048,384]{1,0:T(8,128)(2,1)}, bf16[2048,384]{1,0:T(8,128)(2,1)S(1)}, u32[]{:S(2)}) copy-start(bf16[2048,384]{1,0:T(8,128)(2,1)S(1)} %collective-permute-done.2.wu1) | copy-start | bytes 4718596
  11.6 7.8 %collective-permute-start.7 = (bf16[24,2176]{1,0:T(8,128)(2,1)S(1)}, bf16[24,2176]{1,0:T(8,128)(2,1)S(1)}, u32[]{:S(2)}, u32[]{:S(2)}) collective-permute-start(bf16[24,2176]{1,0:T(8,128)(2,1)S(1)} %get-tuple-element.61.refs_0_), channel_id=1, source_target_pairs={{0,8},{1,9},{2,10},{3,11},{4,12},{5,13},{6,14},{7,15},{8,0},{9,1},... | collective-permute-start | bytes 313352 | tf_op jit(solution)/shard_map/ppermute | solution.py:734
  13.5 10.8 %collective-permute-start.8 = (bf16[24,2176]{1,0:T(8,128)(2,1)S(1)}, bf16[24,2176]{1,0:T(8,128)(2,1)S(1)}, u32[]{:S(2)}, u32[]{:S(2)}) collective-permute-start(bf16[24,2176]{1,0:T(8,128)(2,1)S(1)} %get-tuple-element.61.refs_0_), channel_id=1, source_target_pairs={{0,16},{1,17},{2,18},{3,19},{4,20},{5,21},{6,22},{7,23},{8,24},{9,... | collective-permute-start | bytes 313352 | tf_op jit(solution)/shard_map/ppermute | solution.py:734
  16.1 8.2 %collective-permute-start.9 = (bf16[24,2176]{1,0:T(8,128)(2,1)S(1)}, bf16[24,2176]{1,0:T(8,128)(2,1)S(1)}, u32[]{:S(2)}, u32[]{:S(2)}) collective-permute-start(bf16[24,2176]{1,0:T(8,128)(2,1)S(1)} %get-tuple-element.61.refs_0_), channel_id=1, source_target_pairs={{0,24},{1,25},{2,26},{3,27},{4,28},{5,29},{6,30},{7,31},{8,16},{9,... | collective-permute-start | bytes 313352 | tf_op jit(solution)/shard_map/ppermute | solution.py:734
  16.1 8.2 %collective-permute-start.4 = (bf16[32,2176]{1,0:T(8,128)(2,1)S(1)}, bf16[32,2176]{1,0:T(8,128)(2,1)S(1)}, u32[]{:S(2)}, u32[]{:S(2)}) collective-permute-start(bf16[32,2176]{1,0:T(8,128)(2,1)S(1)} %own_rows.1.r0.refs_0_), channel_id=1, source_target_pairs={{0,5},{1,4},{2,7},{3,6},{4,1},{5,0},{6,3},{7,2},{8,13},{9,12},{10,... | collective-permute-start | bytes 417800 | tf_op jit(solution)/shard_map/ppermute | solution.py:734
  18.9 6.0 %collective-permute-start.5 = (bf16[32,2176]{1,0:T(8,128)(2,1)S(1)}, bf16[32,2176]{1,0:T(8,128)(2,1)S(1)}, u32[]{:S(2)}, u32[]{:S(2)}) collective-permute-start(bf16[32,2176]{1,0:T(8,128)(2,1)S(1)} %own_rows.1.r0.refs_0_), channel_id=1, source_target_pairs={{0,1},{1,0},{2,3},{3,2},{4,5},{5,4},{6,7},{7,6},{8,9},{9,8},{10,11... | collective-permute-start | bytes 417800 | tf_op jit(solution)/shard_map/ppermute | solution.py:734
  19.4 5.5 %collective-permute-start.6 = (bf16[32,2176]{1,0:T(8,128)(2,1)S(1)}, bf16[32,2176]{1,0:T(8,128)(2,1)S(1)}, u32[]{:S(2)}, u32[]{:S(2)}) collective-permute-start(bf16[32,2176]{1,0:T(8,128)(2,1)S(1)} %own_rows.1.r0.refs_0_), channel_id=1, source_target_pairs={{0,4},{1,5},{2,6},{3,7},{4,0},{5,1},{6,2},{7,3},{8,12},{9,13},{10,... | collective-permute-start | bytes 417800 | tf_op jit(solution)/shard_map/ppermute | solution.py:734
  24.9 7.7 %collective-permute-start.10 = (bf16[32,2176]{1,0:T(8,128)(2,1)S(1)}, bf16[32,2176]{1,0:T(8,128)(2,1)S(1)}, u32[]{:S(2)}, u32[]{:S(2)}) collective-permute-start(bf16[32,2176]{1,0:T(8,128)(2,1)S(1)} %onward_z.1), channel_id=1, source_target_pairs={{0,8},{1,9},{2,10},{3,11},{4,12},{5,13},{6,14},{7,15},{8,0},{9,1},... | collective-permute-start | bytes 417800 | tf_op jit(solution)/shard_map/ppermute | solution.py:734
  26.1 15.3 %collective-permute-start.13 = (bf16[72,2176]{1,0:T(8,128)(2,1)S(1)}, bf16[72,2176]{1,0:T(8,128)(2,1)S(1)}, u32[]{:S(2)}, u32[]{:S(2)}) collective-permute-start(bf16[72,2176]{1,0:T(8,128)(2,1)S(1)} %onward_plane.1.far_ref), channel_id=1, source_target_pairs={{0,5},{1,4},{2,7},{3,6},{4,1},{5,0},{6,3},{7,2},{8,13},{9,12},{10,... | collective-permute-start | bytes 940040 | tf_op jit(solution)/shard_map/ppermute | solution.py:734
  28.6 13.2 %collective-permute-start.14 = (bf16[72,2176]{1,0:T(8,128)(2,1)S(1)}, bf16[72,2176]{1,0:T(8,128)(2,1)S(1)}, u32[]{:S(2)}, u32[]{:S(2)}) collective-permute-start(bf16[72,2176]{1,0:T(8,128)(2,1)S(1)} %onward_plane.1.far_ref), channel_id=1, source_target_pairs={{0,1},{1,0},{2,3},{3,2},{4,5},{5,4},{6,7},{7,6},{8,9},{9,8},{10,11... | collective-permute-start | bytes 940040 | tf_op jit(solution)/shard_map/ppermute | solution.py:734
  29.1 12.6 %collective-permute-start.15 = (bf16[72,2176]{1,0:T(8,128)(2,1)S(1)}, bf16[72,2176]{1,0:T(8,128)(2,1)S(1)}, u32[]{:S(2)}, u32[]{:S(2)}) collective-permute-start(bf16[72,2176]{1,0:T(8,128)(2,1)S(1)} %onward_plane.1.far_ref), channel_id=1, source_target_pairs={{0,4},{1,5},{2,6},{3,7},{4,0},{5,1},{6,2},{7,3},{8,12},{9,13},{10,... | collective-permute-start | bytes 940040 | tf_op jit(solution)/shard_map/ppermute | solution.py:734
  29.6 11.8 %collective-permute-start.11 = (bf16[32,2176]{1,0:T(8,128)(2,1)S(1)}, bf16[32,2176]{1,0:T(8,128)(2,1)S(1)}, u32[]{:S(2)}, u32[]{:S(2)}) collective-permute-start(bf16[32,2176]{1,0:T(8,128)(2,1)S(1)} %onward_z.1), channel_id=1, source_target_pairs={{0,16},{1,17},{2,18},{3,19},{4,20},{5,21},{6,22},{7,23},{8,24},{9,... | collective-permute-start | bytes 417800 | tf_op jit(solution)/shard_map/ppermute | solution.py:734
  32.6 8.8 %collective-permute-start.12 = (bf16[32,2176]{1,0:T(8,128)(2,1)S(1)}, bf16[32,2176]{1,0:T(8,128)(2,1)S(1)}, u32[]{:S(2)}, u32[]{:S(2)}) collective-permute-start(bf16[32,2176]{1,0:T(8,128)(2,1)S(1)} %onward_z.1), channel_id=1, source_target_pairs={{0,24},{1,25},{2,26},{3,27},{4,28},{5,29},{6,30},{7,31},{8,16},{9,... | collective-permute-start | bytes 417800 | tf_op jit(solution)/shard_map/ppermute | solution.py:734
  45.2 6.8 %collective-permute-start.19 = (bf16[32,2048]{1,0:T(8,128)(2,1)S(1)}, bf16[32,2048]{1,0:T(8,128)(2,1)S(1)}, u32[]{:S(2)}, u32[]{:S(2)}) collective-permute-start(bf16[32,2048]{1,0:T(8,128)(2,1)S(1)} %get-tuple-element.77), channel_id=1, source_target_pairs={{0,8},{1,9},{2,10},{3,11},{4,12},{5,13},{6,14},{7,15},{8,0},{9,1},... | collective-permute-start | bytes 393224 | tf_op jit(solution)/shard_map/ppermute | solution.py:734
  47.0 10.9 %collective-permute-start.16 = (bf16[72,2048]{1,0:T(8,128)(2,1)S(1)}, bf16[72,2048]{1,0:T(8,128)(2,1)S(1)}, u32[]{:S(2)}, u32[]{:S(2)}) collective-permute-start(bf16[72,2048]{1,0:T(8,128)(2,1)S(1)} %get-tuple-element.74), channel_id=1, source_target_pairs={{0,5},{1,4},{2,7},{3,6},{4,1},{5,0},{6,3},{7,2},{8,13},{9,12},{10,... | collective-permute-start | bytes 884744 | tf_op jit(solution)/shard_map/ppermute | solution.py:734
  49.6 12.5 %collective-permute-start.17 = (bf16[72,2048]{1,0:T(8,128)(2,1)S(1)}, bf16[72,2048]{1,0:T(8,128)(2,1)S(1)}, u32[]{:S(2)}, u32[]{:S(2)}) collective-permute-start(bf16[72,2048]{1,0:T(8,128)(2,1)S(1)} %get-tuple-element.75), channel_id=1, source_target_pairs={{0,1},{1,0},{2,3},{3,2},{4,5},{5,4},{6,7},{7,6},{8,9},{9,8},{10,11... | collective-permute-start | bytes 884744 | tf_op jit(solution)/shard_map/ppermute | solution.py:734
  50.1 12.0 %collective-permute-start.18 = (bf16[72,2048]{1,0:T(8,128)(2,1)S(1)}, bf16[72,2048]{1,0:T(8,128)(2,1)S(1)}, u32[]{:S(2)}, u32[]{:S(2)}) collective-permute-start(bf16[72,2048]{1,0:T(8,128)(2,1)S(1)} %get-tuple-element.76), channel_id=1, source_target_pairs={{0,4},{1,5},{2,6},{3,7},{4,0},{5,1},{6,2},{7,3},{8,12},{9,13},{10,... | collective-permute-start | bytes 884744 | tf_op jit(solution)/shard_map/ppermute | solution.py:734
  50.4 11.8 %collective-permute-start.20 = (bf16[32,2048]{1,0:T(8,128)(2,1)S(1)}, bf16[32,2048]{1,0:T(8,128)(2,1)S(1)}, u32[]{:S(2)}, u32[]{:S(2)}) collective-permute-start(bf16[32,2048]{1,0:T(8,128)(2,1)S(1)} %get-tuple-element.79), channel_id=1, source_target_pairs={{0,16},{1,17},{2,18},{3,19},{4,20},{5,21},{6,22},{7,23},{8,24},{9,... | collective-permute-start | bytes 393224 | tf_op jit(solution)/shard_map/ppermute | solution.py:734
  52.0 10.3 %collective-permute-start.21 = (bf16[32,2048]{1,0:T(8,128)(2,1)S(1)}, bf16[32,2048]{1,0:T(8,128)(2,1)S(1)}, u32[]{:S(2)}, u32[]{:S(2)}) collective-permute-start(bf16[32,2048]{1,0:T(8,128)(2,1)S(1)} %get-tuple-element.80), channel_id=1, source_target_pairs={{0,24},{1,25},{2,26},{3,27},{4,28},{5,29},{6,30},{7,31},{8,16},{9,... | collective-permute-start | bytes 393224 | tf_op jit(solution)/shard_map/ppermute | solution.py:734
  62.3 7.8 %collective-permute-start.25 = (bf16[24,2048]{1,0:T(8,128)(2,1)S(1)}, bf16[24,2048]{1,0:T(8,128)(2,1)S(1)}, u32[]{:S(2)}, u32[]{:S(2)}) collective-permute-start(bf16[24,2048]{1,0:T(8,128)(2,1)S(1)} %get-tuple-element.94), channel_id=1, source_target_pairs={{0,8},{1,9},{2,10},{3,11},{4,12},{5,13},{6,14},{7,15},{8,0},{9,1},... | collective-permute-start | bytes 294920 | tf_op jit(solution)/shard_map/ppermute | solution.py:734
  63.6 6.9 %collective-permute-start.26 = (bf16[24,2048]{1,0:T(8,128)(2,1)S(1)}, bf16[24,2048]{1,0:T(8,128)(2,1)S(1)}, u32[]{:S(2)}, u32[]{:S(2)}) collective-permute-start(bf16[24,2048]{1,0:T(8,128)(2,1)S(1)} %get-tuple-element.95), channel_id=1, source_target_pairs={{0,16},{1,17},{2,18},{3,19},{4,20},{5,21},{6,22},{7,23},{8,24},{9,... | collective-permute-start | bytes 294920 | tf_op jit(solution)/shard_map/ppermute | solution.py:734
  66.3 7.6 %collective-permute-start.27 = (bf16[24,2048]{1,0:T(8,128)(2,1)S(1)}, bf16[24,2048]{1,0:T(8,128)(2,1)S(1)}, u32[]{:S(2)}, u32[]{:S(2)}) collective-permute-start(bf16[24,2048]{1,0:T(8,128)(2,1)S(1)} %get-tuple-element.96), channel_id=1, source_target_pairs={{0,24},{1,25},{2,26},{3,27},{4,28},{5,29},{6,30},{7,31},{8,16},{9,... | collective-permute-start | bytes 294920 | tf_op jit(solution)/shard_map/ppermute | solution.py:734
  67.0 7.3 %collective-permute-start.22 = (bf16[32,2048]{1,0:T(8,128)(2,1)S(1)}, bf16[32,2048]{1,0:T(8,128)(2,1)S(1)}, u32[]{:S(2)}, u32[]{:S(2)}) collective-permute-start(bf16[32,2048]{1,0:T(8,128)(2,1)S(1)} %get-tuple-element.89), channel_id=1, source_target_pairs={{0,5},{1,4},{2,7},{3,6},{4,1},{5,0},{6,3},{7,2},{8,13},{9,12},{10,... | collective-permute-start | bytes 393224 | tf_op jit(solution)/shard_map/ppermute | solution.py:734
  69.6 6.0 %collective-permute-start.23 = (bf16[32,2048]{1,0:T(8,128)(2,1)S(1)}, bf16[32,2048]{1,0:T(8,128)(2,1)S(1)}, u32[]{:S(2)}, u32[]{:S(2)}) collective-permute-start(bf16[32,2048]{1,0:T(8,128)(2,1)S(1)} %get-tuple-element.90), channel_id=1, source_target_pairs={{0,1},{1,0},{2,3},{3,2},{4,5},{5,4},{6,7},{7,6},{8,9},{9,8},{10,11... | collective-permute-start | bytes 393224 | tf_op jit(solution)/shard_map/ppermute | solution.py:734
  70.1 5.6 %collective-permute-start.24 = (bf16[32,2048]{1,0:T(8,128)(2,1)S(1)}, bf16[32,2048]{1,0:T(8,128)(2,1)S(1)}, u32[]{:S(2)}, u32[]{:S(2)}) collective-permute-start(bf16[32,2048]{1,0:T(8,128)(2,1)S(1)} %get-tuple-element.91), channel_id=1, source_target_pairs={{0,4},{1,5},{2,6},{3,7},{4,0},{5,1},{6,2},{7,3},{8,12},{9,13},{10,... | collective-permute-start | bytes 393224 | tf_op jit(solution)/shard_map/ppermute | solution.py:734
  73.9 1.8 %copy-start = (f32[2048]{0:T(1024)S(1)}, f32[2048]{0:T(1024)}, u32[]{:S(2)}) copy-start(f32[2048]{0:T(1024)} %param.29) | copy-start | bytes 24580

commit v7 on v6

--- a/solution.py
+++ b/solution.py
@@ -504,8 +504,8 @@
 
 
 def near_kernel(
-    groups, group_ref, r0, r1, r2, r3, far_ref, wg1, wu1, wg0, wu0, wd0, wd1,
-    out_ref, w0_ref, w1_ref, down_ref, x_ref, h_ref, sems,
+    groups, group_ref, r0, r1, r2, r3, far_ref, z1_ref, wg1, wu1, wg0, wu0, wd0, wd1,
+    out_ref, z1_out_ref, w0_ref, w1_ref, down_ref, x_ref, h_ref, sems,
 ):
     hidden = wg0.shape[1]
     fetches = [
@@ -523,7 +523,7 @@
     ]
     for fetch in fetches:
         fetch.start()
-    gather_pieces((r0, r1, r2, r3, far_ref), x_ref)
+    gather_pieces((r0, r1, r2, r3, far_ref, z1_ref), x_ref)
 
     def ready(e):
         for fetch in fetches[4:] if e else fetches[:2]:
@@ -537,6 +537,7 @@
         cols = slice(col, col + DOWN_BLOCK)
         down = jnp.dot(h_ref[...], down_ref[:, cols], preferred_element_type=jnp.float32)
         out_ref[:, cols] = down[:height]
+        z1_out_ref[:, cols] = down[height : height + z1_ref.shape[0]].astype(jnp.bfloat16)
 
 
 def expert_cost(rows, width, hidden):
@@ -547,9 +548,9 @@
     )
 
 
-def near_rows(groups, group, rows, far, weights, partner_weights):
+def near_rows(groups, group, rows, far, near_z, weights, partner_weights):
     height = 4 * rows[0].shape[0] + far.shape[0]
-    padded = -(-height // 16) * 16
+    padded = -(-(height + near_z.shape[0]) // 16) * 16
     width, hidden = weights[0].shape
     wg0, wu0, wd0 = weights
     wg1, wu1, wd1 = partner_weights
@@ -557,12 +558,13 @@
         functools.partial(near_kernel, groups),
         out_shape=(
             jax.ShapeDtypeStruct((height, width), jnp.float32),
+            jax.ShapeDtypeStruct((near_z.shape[0], width), jnp.bfloat16),
             jax.ShapeDtypeStruct((width, 2 * hidden), jnp.bfloat16),
             jax.ShapeDtypeStruct((width, 2 * hidden), jnp.bfloat16),
             jax.ShapeDtypeStruct((2 * hidden, width), jnp.bfloat16),
         ),
-        in_specs=[smem()] + [vmem()] * 7 + [hbm()] * 4,
-        out_specs=(vmem(),) * 4,
+        in_specs=[smem()] + [vmem()] * 8 + [hbm()] * 4,
+        out_specs=(vmem(),) * 5,
         scratch_shapes=[
             pltpu.VMEM((padded, width + LANES), jnp.bfloat16),
             pltpu.VMEM((padded, 2 * hidden), jnp.bfloat16),
@@ -571,7 +573,7 @@
         compiler_params=pltpu.CompilerParams(vmem_limit_bytes=24 * MIB),
         cost_estimate=expert_cost(height, width, hidden),
         name="near_rows",
-    )(group, *rows, far, wg1, wu1, *[stay(w) for w in (wg0, wu0, wd0, wd1)])
+    )(group, *rows, far, near_z, wg1, wu1, *[stay(w) for w in (wg0, wu0, wd0, wd1)])
 
 
 def piece_kernel(groups, count, group_ref, *refs):
@@ -776,9 +778,11 @@
     onward_z = join_rows(plane_rows, (far,) * 4, None, "onward_z")
     z_pieces = swap_z((onward_z,) * 3)
     plane_pieces = swap_plane((onward_plane,) * 3)
-    near, *kept = near_rows(groups, group, plane_rows, far_pieces, weights, partner_weights)
-    parts = piece_rows(groups, group, z_pieces + plane_pieces, *kept)
-    z_parts, plane_parts = swap_z(parts[:3]), swap_plane(parts[3:])
+    near, near_part, *kept = near_rows(
+        groups, group, plane_rows, far_pieces, z_pieces[0], weights, partner_weights
+    )
+    parts = piece_rows(groups, group, z_pieces[1:] + plane_pieces, *kept)
+    z_parts, plane_parts = swap_z((near_part,) + parts[:2]), swap_plane(parts[2:])
     first = first_sum(near, z_parts[0], half)
     plane_parts, first = barrier(plane_parts, first)
     far_sums = plane_sum(near, plane_parts)

time: 76.7 us -> 75.3 us (0.982)
  transfers between devices with their start and end apart: 28 -> 28, of which waited for: 11 -> 10; matrix products, arithmetic and copies ran while one was open for 0% -> 0% of each run, Pallas kernels for 17% -> 22%
where the time goes in v7:
time: 75.3 us; the launch traced here: 75.1 us
  starting transfers between devices  36.9 us (49%)
  waiting for transfers between devices  20.5 us (27%)
  Pallas kernels  17.5 us (23%)
    ppermute x28, starting transfers between devices, swap(): return lax.ppermute(value, ALL, pairs)  36.9 us
    ppermute x28, waiting for transfers between devices, swap(): return lax.ppermute(value, ALL, pairs)  20.5 us
    pallas_call x1, Pallas kernels, near_rows(): pl.pallas_call(functools.partial(near_kernel, groups), out_shape=(jax.Sha...  5.93 us
    pallas_call x1, Pallas kernels, other_terms(): pl.pallas_call(other_kernel, out_shape=(jax.ShapeDtypeStruct((half, w_out...  3.75 us
    pallas_call x1, Pallas kernels, own_terms(): pl.pallas_call(own_kernel, out_shape=(jax.ShapeDtypeStruct((half, width),...  3.5 us
    pallas_call x1, Pallas kernels, piece_rows(): pl.pallas_call(functools.partial(piece_kernel, groups, count), out_shape=...  3.01 us
  transfers between devices with their start and end apart: 28, of which 10 were waited for; matrix products, arithmetic and copies ran while one was open for 0% of the time, Pallas kernels for 22%

profile of v7, /device:TPU:0, one launch (start us, length us, event | category | flops | bytes accessed | tf_op | source)
XLA Modules:
  0.0 75.1 jit_solution(14100663472161092434)
XLA Ops:
  1.0 3.8 %other_terms.1 = (bf16[32,2048]{1,0:T(8,128)(2,1)S(1)}, bf16[64,1024]{1,0:T(8,128)(2,1)S(1)}, bf16[64,512]{1,0:T(8,128)(2,1)S(1)}, bf16[4,128,512]{2,1,0:T(8,128)(2,1)S(1)}, bf16[1024,2048]{1,0:T(8,128)(2,1)S(1)}) custom-call(s32[4,9]{1,0:T(4,128)} %bitcast.18, s32[9]{0:T(128)} %lengths_ref.3, s32[1]{0:T(128)} %bitcast.2.tp_ref, s32[1]{0:T(128)} %bitcast.group_ref, ...), custom_call_target="tpu_custom_call" | custom-call | tf_op jit(solution)/shard_map/other_terms/pallas_call | solution.py:351
  4.7 2.5 %collective-permute-start = (bf16[32,2048]{1,0:T(8,128)(2,1)S(1)}, bf16[32,2048]{1,0:T(8,128)(2,1)S(1)}, u32[]{:S(2)}, u32[]{:S(2)}) collective-permute-start(bf16[32,2048]{1,0:T(8,128)(2,1)S(1)} %get-tuple-element.58), channel_id=1, source_target_pairs={{0,1},{1,0},{2,3},{3,2},{4,5},{5,4},{6,7},{7,6},{8,9},{9,8},{10,11... | collective-permute-start | bytes 393224 | tf_op jit(solution)/shard_map/ppermute | solution.py:736
  7.3 3.5 %own_terms.1 = (f32[32,2048]{1,0:T(8,128)S(1)}, bf16[32,128]{1,0:T(8,128)(2,1)S(1)}) custom-call(s32[4,9]{1,0:T(4,128)} %bitcast.19, s32[9]{0:T(128)} %lengths_ref.3, s32[1]{0:T(128)} %bitcast.2.tp_ref, s32[16]{0:T(128)} %home_ref.1, bf16[64,1024]{1,0:T(8,128)(2,1)S(1)} %get-tuple-element.53.q_ref, bf16[64,512]{1,0:T(8,128)(2,1)S(1)} %get-tuple-element.54.fresh_ref, ...), custom_call_target="tpu_custom_call" | custom-call | tf_op jit(solution)/shard_map/own_terms/pallas_call | solution.py:400
  10.8 0.7 collective-permute-done.got_ref
  11.6 1.9 %collective-permute-start.7 = (bf16[24,2176]{1,0:T(8,128)(2,1)S(1)}, bf16[24,2176]{1,0:T(8,128)(2,1)S(1)}, u32[]{:S(2)}, u32[]{:S(2)}) collective-permute-start(bf16[24,2176]{1,0:T(8,128)(2,1)S(1)} %get-tuple-element.61.refs_0_), channel_id=1, source_target_pairs={{0,8},{1,9},{2,10},{3,11},{4,12},{5,13},{6,14},{7,15},{8,0},{9,1},... | collective-permute-start | bytes 313352 | tf_op jit(solution)/shard_map/ppermute | solution.py:736
  13.5 2.6 %collective-permute-start.8 = (bf16[24,2176]{1,0:T(8,128)(2,1)S(1)}, bf16[24,2176]{1,0:T(8,128)(2,1)S(1)}, u32[]{:S(2)}, u32[]{:S(2)}) collective-permute-start(bf16[24,2176]{1,0:T(8,128)(2,1)S(1)} %get-tuple-element.61.refs_0_), channel_id=1, source_target_pairs={{0,16},{1,17},{2,18},{3,19},{4,20},{5,21},{6,22},{7,23},{8,24},{9,... | collective-permute-start | bytes 313352 | tf_op jit(solution)/shard_map/ppermute | solution.py:736
  16.1 2.7 %collective-permute-start.4 = (bf16[32,2176]{1,0:T(8,128)(2,1)S(1)}, bf16[32,2176]{1,0:T(8,128)(2,1)S(1)}, u32[]{:S(2)}, u32[]{:S(2)}) collective-permute-start(bf16[32,2176]{1,0:T(8,128)(2,1)S(1)} %own_rows.1.refs_0_.r0), channel_id=1, source_target_pairs={{0,5},{1,4},{2,7},{3,6},{4,1},{5,0},{6,3},{7,2},{8,13},{9,12},{10,... | collective-permute-start | bytes 417800 | tf_op jit(solution)/shard_map/ppermute | solution.py:736
  18.9 0.5 collective-permute-start.5
  19.7 4.6 %collective-permute-done.8.refs_1_ = bf16[24,2176]{1,0:T(8,128)(2,1)S(1)} collective-permute-done((bf16[24,2176]{1,0:T(8,128)(2,1)S(1)}, bf16[24,2176]{1,0:T(8,128)(2,1)S(1)}, u32[]{:S(2)}, u32[]{:S(2)}) %collective-permute-start.8) | collective-permute-done | bytes 104480 | tf_op jit(solution)/shard_map/ppermute | solution.py:736
  24.3 0.6 collective-permute-done.5.refs_2_.r2
  24.9 1.2 %collective-permute-start.10 = (bf16[32,2176]{1,0:T(8,128)(2,1)S(1)}, bf16[32,2176]{1,0:T(8,128)(2,1)S(1)}, u32[]{:S(2)}, u32[]{:S(2)}) collective-permute-start(bf16[32,2176]{1,0:T(8,128)(2,1)S(1)} %onward_z.1), channel_id=1, source_target_pairs={{0,8},{1,9},{2,10},{3,11},{4,12},{5,13},{6,14},{7,15},{8,0},{9,1},... | collective-permute-start | bytes 417800 | tf_op jit(solution)/shard_map/ppermute | solution.py:736
  26.1 2.4 %collective-permute-start.13 = (bf16[72,2176]{1,0:T(8,128)(2,1)S(1)}, bf16[72,2176]{1,0:T(8,128)(2,1)S(1)}, u32[]{:S(2)}, u32[]{:S(2)}) collective-permute-start(bf16[72,2176]{1,0:T(8,128)(2,1)S(1)} %onward_plane.1.far_ref), channel_id=1, source_target_pairs={{0,5},{1,4},{2,7},{3,6},{4,1},{5,0},{6,3},{7,2},{8,13},{9,12},{10,... | collective-permute-start | bytes 940040 | tf_op jit(solution)/shard_map/ppermute | solution.py:736
  28.6 0.5 collective-permute-start.14
  29.6 3.0 %collective-permute-start.11 = (bf16[32,2176]{1,0:T(8,128)(2,1)S(1)}, bf16[32,2176]{1,0:T(8,128)(2,1)S(1)}, u32[]{:S(2)}, u32[]{:S(2)}) collective-permute-start(bf16[32,2176]{1,0:T(8,128)(2,1)S(1)} %onward_z.1), channel_id=1, source_target_pairs={{0,16},{1,17},{2,18},{3,19},{4,20},{5,21},{6,22},{7,23},{8,24},{9,... | collective-permute-start | bytes 417800 | tf_op jit(solution)/shard_map/ppermute | solution.py:736
  32.6 2.1 %collective-permute-start.12 = (bf16[32,2176]{1,0:T(8,128)(2,1)S(1)}, bf16[32,2176]{1,0:T(8,128)(2,1)S(1)}, u32[]{:S(2)}, u32[]{:S(2)}) collective-permute-start(bf16[32,2176]{1,0:T(8,128)(2,1)S(1)} %onward_z.1), channel_id=1, source_target_pairs={{0,24},{1,25},{2,26},{3,27},{4,28},{5,29},{6,30},{7,31},{8,16},{9,... | collective-permute-start | bytes 417800 | tf_op jit(solution)/shard_map/ppermute | solution.py:736
  34.7 5.9 %near_rows.1 = (f32[200,2048]{1,0:T(8,128)S(1)}, bf16[32,2048]{1,0:T(8,128)(2,1)S(1)}, bf16[2048,768]{1,0:T(8,128)(2,1)S(1)}, bf16[2048,768]{1,0:T(8,128)(2,1)S(1)}, bf16[768,2048]{1,0:T(8,128)(2,1)S(1)}) custom-call(s32[1]{0:T(128)} %bitcast.group_ref, bf16[32,2176]{1,0:T(8,128)(2,1)S(1)} %own_rows.1.refs_0_.r0, ...), custom_call_target="tpu_custom_call" | custom-call | flops 1887436800 | bytes 9437184 | tf_op jit(solution)/shard_map/near_rows/pallas_call | solution.py:557
  40.6 0.8 %collective-permute-done.11.refs_0_ = bf16[32,2176]{1,0:T(8,128)(2,1)S(1)} collective-permute-done((bf16[32,2176]{1,0:T(8,128)(2,1)S(1)}, bf16[32,2176]{1,0:T(8,128)(2,1)S(1)}, u32[]{:S(2)}, u32[]{:S(2)}) %collective-permute-start.11) | collective-permute-done | bytes 139296 | tf_op jit(solution)/shard_map/ppermute | solution.py:736
  41.8 3.0 %piece_rows.1 = (bf16[32,2048]{1,0:T(8,128)(2,1)S(1)}, bf16[32,2048]{1,0:T(8,128)(2,1)S(1)}, bf16[72,2048]{1,0:T(8,128)(2,1)S(1)}, bf16[72,2048]{1,0:T(8,128)(2,1)S(1)}, bf16[72,2048]{1,0:T(8,128)(2,1)S(1)}) custom-call(s32[1]{0:T(128)} %bitcast.group_ref, bf16[32,2176]{1,0:T(8,128)(2,1)S(1)} %collective-permute-done.11.refs_0_, ...), custom_call_target="tpu_custom_call" | custom-call | flops 2642411520 | bytes 9437184 | tf_op jit(solution)/shard_map/piece_rows/pallas_call | solution.py:598
  44.8 2.5 %collective-permute-start.16 = (bf16[72,2048]{1,0:T(8,128)(2,1)S(1)}, bf16[72,2048]{1,0:T(8,128)(2,1)S(1)}, u32[]{:S(2)}, u32[]{:S(2)}) collective-permute-start(bf16[72,2048]{1,0:T(8,128)(2,1)S(1)} %get-tuple-element.74), channel_id=1, source_target_pairs={{0,5},{1,4},{2,7},{3,6},{4,1},{5,0},{6,3},{7,2},{8,13},{9,12},{10,... | collective-permute-start | bytes 884744 | tf_op jit(solution)/shard_map/ppermute | solution.py:736
  47.8 0.6 collective-permute-start.18
  48.3 2.9 %collective-permute-start.20 = (bf16[32,2048]{1,0:T(8,128)(2,1)S(1)}, bf16[32,2048]{1,0:T(8,128)(2,1)S(1)}, u32[]{:S(2)}, u32[]{:S(2)}) collective-permute-start(bf16[32,2048]{1,0:T(8,128)(2,1)S(1)} %get-tuple-element.79), channel_id=1, source_target_pairs={{0,16},{1,17},{2,18},{3,19},{4,20},{5,21},{6,22},{7,23},{8,24},{9,... | collective-permute-start | bytes 393224 | tf_op jit(solution)/shard_map/ppermute | solution.py:736
  51.2 1.2 %collective-permute-start.21 = (bf16[32,2048]{1,0:T(8,128)(2,1)S(1)}, bf16[32,2048]{1,0:T(8,128)(2,1)S(1)}, u32[]{:S(2)}, u32[]{:S(2)}) collective-permute-start(bf16[32,2048]{1,0:T(8,128)(2,1)S(1)} %get-tuple-element.80), channel_id=1, source_target_pairs={{0,24},{1,25},{2,26},{3,27},{4,28},{5,29},{6,30},{7,31},{8,16},{9,... | collective-permute-start | bytes 393224 | tf_op jit(solution)/shard_map/ppermute | solution.py:736
  52.4 3.2 %collective-permute-done.16.g1 = bf16[72,2048]{1,0:T(8,128)(2,1)S(1)} collective-permute-done((bf16[72,2048]{1,0:T(8,128)(2,1)S(1)}, bf16[72,2048]{1,0:T(8,128)(2,1)S(1)}, u32[]{:S(2)}, u32[]{:S(2)}) %collective-permute-start.16) | collective-permute-done | bytes 294944 | tf_op jit(solution)/shard_map/ppermute | solution.py:736
  55.7 5.3 %collective-permute-done.17.g2 = bf16[72,2048]{1,0:T(8,128)(2,1)S(1)} collective-permute-done((bf16[72,2048]{1,0:T(8,128)(2,1)S(1)}, bf16[72,2048]{1,0:T(8,128)(2,1)S(1)}, u32[]{:S(2)}, u32[]{:S(2)}) %collective-permute-start.17) | collective-permute-done | bytes 294944 | tf_op jit(solution)/shard_map/ppermute | solution.py:736
  61.1 1.7 %collective-permute-start.25 = (bf16[24,2048]{1,0:T(8,128)(2,1)S(1)}, bf16[24,2048]{1,0:T(8,128)(2,1)S(1)}, u32[]{:S(2)}, u32[]{:S(2)}) collective-permute-start(bf16[24,2048]{1,0:T(8,128)(2,1)S(1)} %get-tuple-element.94), channel_id=1, source_target_pairs={{0,8},{1,9},{2,10},{3,11},{4,12},{5,13},{6,14},{7,15},{8,0},{9,1},... | collective-permute-start | bytes 294920 | tf_op jit(solution)/shard_map/ppermute | solution.py:736
  62.8 1.6 %collective-permute-start.26 = (bf16[24,2048]{1,0:T(8,128)(2,1)S(1)}, bf16[24,2048]{1,0:T(8,128)(2,1)S(1)}, u32[]{:S(2)}, u32[]{:S(2)}) collective-permute-start(bf16[24,2048]{1,0:T(8,128)(2,1)S(1)} %get-tuple-element.95), channel_id=1, source_target_pairs={{0,16},{1,17},{2,18},{3,19},{4,20},{5,21},{6,22},{7,23},{8,24},{9,... | collective-permute-start | bytes 294920 | tf_op jit(solution)/shard_map/ppermute | solution.py:736
  64.5 1.1 %collective-permute-start.27 = (bf16[24,2048]{1,0:T(8,128)(2,1)S(1)}, bf16[24,2048]{1,0:T(8,128)(2,1)S(1)}, u32[]{:S(2)}, u32[]{:S(2)}) collective-permute-start(bf16[24,2048]{1,0:T(8,128)(2,1)S(1)} %get-tuple-element.96), channel_id=1, source_target_pairs={{0,24},{1,25},{2,26},{3,27},{4,28},{5,29},{6,30},{7,31},{8,16},{9,... | collective-permute-start | bytes 294920 | tf_op jit(solution)/shard_map/ppermute | solution.py:736
  65.7 2.4 %collective-permute-start.22 = (bf16[32,2048]{1,0:T(8,128)(2,1)S(1)}, bf16[32,2048]{1,0:T(8,128)(2,1)S(1)}, u32[]{:S(2)}, u32[]{:S(2)}) collective-permute-start(bf16[32,2048]{1,0:T(8,128)(2,1)S(1)} %get-tuple-element.89), channel_id=1, source_target_pairs={{0,5},{1,4},{2,7},{3,6},{4,1},{5,0},{6,3},{7,2},{8,13},{9,12},{10,... | collective-permute-start | bytes 393224 | tf_op jit(solution)/shard_map/ppermute | solution.py:736
  68.6 0.6 collective-permute-start.24
  69.2 4.1 %collective-permute-done.26.z2 = bf16[24,2048]{1,0:T(8,128)(2,1)S(1)} collective-permute-done((bf16[24,2048]{1,0:T(8,128)(2,1)S(1)}, bf16[24,2048]{1,0:T(8,128)(2,1)S(1)}, u32[]{:S(2)}, u32[]{:S(2)}) %collective-permute-start.26) | collective-permute-done | bytes 98336 | tf_op jit(solution)/shard_map/ppermute | solution.py:736
  73.4 0.8 %collective-permute-done.23.p2 = bf16[32,2048]{1,0:T(8,128)(2,1)S(1)} collective-permute-done((bf16[32,2048]{1,0:T(8,128)(2,1)S(1)}, bf16[32,2048]{1,0:T(8,128)(2,1)S(1)}, u32[]{:S(2)}, u32[]{:S(2)}) %collective-permute-start.23) | collective-permute-done | bytes 131104 | tf_op jit(solution)/shard_map/ppermute | solution.py:736
  74.3 0.8 %final_rows.1 = bf16[32,2048]{1,0:T(8,128)(2,1)} custom-call(f32[32,2048]{1,0:T(8,128)S(1)} %total_rows.1.total_ref, bf16[32,2048]{1,0:T(8,128)(2,1)S(1)} %collective-permute-done.22.p1, bf16[32,2048]{1,0:T(8,128)(2,1)S(1)} %collective-permute-done.23.p2, bf16[32,2048]{1,0:T(8,128)(2,1)S(1)} %collective-permute-done.24.p3, f32[1,2048]{1,0:T(1,128)S(1)} %bitcast.10), custom_call_target="tpu_custom_call" | custom-call | tf_op jit(solution)/shard_map/final_rows/pallas_call | solution.py:714
  (45 shorter events, 3.8 us)
Async XLA Ops:
  0.0 11.4 %collective-permute-start.1 = (bf16[2048,384]{1,0:T(8,128)(2,1)}, bf16[2048,384]{1,0:T(8,128)(2,1)S(1)}, u32[]{:S(2)}, u32[]{:S(2)}) collective-permute-start(bf16[2048,384]{1,0:T(8,128)(2,1)} %bitcast.12), channel_id=1, source_target_pairs={{0,2},{1,3},{2,0},{3,1},{4,6},{5,7},{6,4},{7,5},{8,10},{9,11},{10,... | collective-permute-start | bytes 4718600 | tf_op jit(solution)/shard_map/ppermute | solution.py:736
  0.5 11.0 %collective-permute-start.2 = (bf16[2048,384]{1,0:T(8,128)(2,1)}, bf16[2048,384]{1,0:T(8,128)(2,1)S(1)}, u32[]{:S(2)}, u32[]{:S(2)}) collective-permute-start(bf16[2048,384]{1,0:T(8,128)(2,1)} %bitcast.14), channel_id=1, source_target_pairs={{0,2},{1,3},{2,0},{3,1},{4,6},{5,7},{6,4},{7,5},{8,10},{9,11},{10,... | collective-permute-start | bytes 4718600 | tf_op jit(solution)/shard_map/ppermute | solution.py:736
  0.5 11.0 %collective-permute-start.3 = (bf16[384,2048]{1,0:T(8,128)(2,1)}, bf16[384,2048]{1,0:T(8,128)(2,1)}, u32[]{:S(2)}, u32[]{:S(2)}) collective-permute-start(bf16[384,2048]{1,0:T(8,128)(2,1)} %bitcast.16), channel_id=1, source_target_pairs={{0,2},{1,3},{2,0},{3,1},{4,6},{5,7},{6,4},{7,5},{8,10},{9,11},{10,... | collective-permute-start | bytes 4718600 | tf_op jit(solution)/shard_map/ppermute | solution.py:736
  4.7 6.7 %collective-permute-start = (bf16[32,2048]{1,0:T(8,128)(2,1)S(1)}, bf16[32,2048]{1,0:T(8,128)(2,1)S(1)}, u32[]{:S(2)}, u32[]{:S(2)}) collective-permute-start(bf16[32,2048]{1,0:T(8,128)(2,1)S(1)} %get-tuple-element.58), channel_id=1, source_target_pairs={{0,1},{1,0},{2,3},{3,2},{4,5},{5,4},{6,7},{7,6},{8,9},{9,8},{10,11... | collective-permute-start | bytes 393224 | tf_op jit(solution)/shard_map/ppermute | solution.py:736
  7.3 4.2 %copy-start.1 = (f32[2048]{0:T(1024)S(1)}, f32[2048]{0:T(1024)}, u32[]{:S(2)}) copy-start(f32[2048]{0:T(1024)} %param.22) | copy-start | bytes 24580
  11.5 4.7 %copy-start.2 = (bf16[2048,384]{1,0:T(8,128)(2,1)}, bf16[2048,384]{1,0:T(8,128)(2,1)S(1)}, u32[]{:S(2)}) copy-start(bf16[2048,384]{1,0:T(8,128)(2,1)S(1)} %collective-permute-done.1.wg1) | copy-start | bytes 4718596
  11.5 4.7 %copy-start.3 = (bf16[2048,384]{1,0:T(8,128)(2,1)}, bf16[2048,384]{1,0:T(8,128)(2,1)S(1)}, u32[]{:S(2)}) copy-start(bf16[2048,384]{1,0:T(8,128)(2,1)S(1)} %collective-permute-done.2.wu1) | copy-start | bytes 4718596
  11.6 7.8 %collective-permute-start.7 = (bf16[24,2176]{1,0:T(8,128)(2,1)S(1)}, bf16[24,2176]{1,0:T(8,128)(2,1)S(1)}, u32[]{:S(2)}, u32[]{:S(2)}) collective-permute-start(bf16[24,2176]{1,0:T(8,128)(2,1)S(1)} %get-tuple-element.61.refs_0_), channel_id=1, source_target_pairs={{0,8},{1,9},{2,10},{3,11},{4,12},{5,13},{6,14},{7,15},{8,0},{9,1},... | collective-permute-start | bytes 313352 | tf_op jit(solution)/shard_map/ppermute | solution.py:736
  13.5 10.8 %collective-permute-start.8 = (bf16[24,2176]{1,0:T(8,128)(2,1)S(1)}, bf16[24,2176]{1,0:T(8,128)(2,1)S(1)}, u32[]{:S(2)}, u32[]{:S(2)}) collective-permute-start(bf16[24,2176]{1,0:T(8,128)(2,1)S(1)} %get-tuple-element.61.refs_0_), channel_id=1, source_target_pairs={{0,16},{1,17},{2,18},{3,19},{4,20},{5,21},{6,22},{7,23},{8,24},{9,... | collective-permute-start | bytes 313352 | tf_op jit(solution)/shard_map/ppermute | solution.py:736
  16.1 8.2 %collective-permute-start.9 = (bf16[24,2176]{1,0:T(8,128)(2,1)S(1)}, bf16[24,2176]{1,0:T(8,128)(2,1)S(1)}, u32[]{:S(2)}, u32[]{:S(2)}) collective-permute-start(bf16[24,2176]{1,0:T(8,128)(2,1)S(1)} %get-tuple-element.61.refs_0_), channel_id=1, source_target_pairs={{0,24},{1,25},{2,26},{3,27},{4,28},{5,29},{6,30},{7,31},{8,16},{9,... | collective-permute-start | bytes 313352 | tf_op jit(solution)/shard_map/ppermute | solution.py:736
  16.1 8.2 %collective-permute-start.4 = (bf16[32,2176]{1,0:T(8,128)(2,1)S(1)}, bf16[32,2176]{1,0:T(8,128)(2,1)S(1)}, u32[]{:S(2)}, u32[]{:S(2)}) collective-permute-start(bf16[32,2176]{1,0:T(8,128)(2,1)S(1)} %own_rows.1.refs_0_.r0), channel_id=1, source_target_pairs={{0,5},{1,4},{2,7},{3,6},{4,1},{5,0},{6,3},{7,2},{8,13},{9,12},{10,... | collective-permute-start | bytes 417800 | tf_op jit(solution)/shard_map/ppermute | solution.py:736
  18.9 6.0 %collective-permute-start.5 = (bf16[32,2176]{1,0:T(8,128)(2,1)S(1)}, bf16[32,2176]{1,0:T(8,128)(2,1)S(1)}, u32[]{:S(2)}, u32[]{:S(2)}) collective-permute-start(bf16[32,2176]{1,0:T(8,128)(2,1)S(1)} %own_rows.1.refs_0_.r0), channel_id=1, source_target_pairs={{0,1},{1,0},{2,3},{3,2},{4,5},{5,4},{6,7},{7,6},{8,9},{9,8},{10,11... | collective-permute-start | bytes 417800 | tf_op jit(solution)/shard_map/ppermute | solution.py:736
  19.4 5.5 %collective-permute-start.6 = (bf16[32,2176]{1,0:T(8,128)(2,1)S(1)}, bf16[32,2176]{1,0:T(8,128)(2,1)S(1)}, u32[]{:S(2)}, u32[]{:S(2)}) collective-permute-start(bf16[32,2176]{1,0:T(8,128)(2,1)S(1)} %own_rows.1.refs_0_.r0), channel_id=1, source_target_pairs={{0,4},{1,5},{2,6},{3,7},{4,0},{5,1},{6,2},{7,3},{8,12},{9,13},{10,... | collective-permute-start | bytes 417800 | tf_op jit(solution)/shard_map/ppermute | solution.py:736
  24.9 7.7 %collective-permute-start.10 = (bf16[32,2176]{1,0:T(8,128)(2,1)S(1)}, bf16[32,2176]{1,0:T(8,128)(2,1)S(1)}, u32[]{:S(2)}, u32[]{:S(2)}) collective-permute-start(bf16[32,2176]{1,0:T(8,128)(2,1)S(1)} %onward_z.1), channel_id=1, source_target_pairs={{0,8},{1,9},{2,10},{3,11},{4,12},{5,13},{6,14},{7,15},{8,0},{9,1},... | collective-permute-start | bytes 417800 | tf_op jit(solution)/shard_map/ppermute | solution.py:736
  26.1 15.3 %collective-permute-start.13 = (bf16[72,2176]{1,0:T(8,128)(2,1)S(1)}, bf16[72,2176]{1,0:T(8,128)(2,1)S(1)}, u32[]{:S(2)}, u32[]{:S(2)}) collective-permute-start(bf16[72,2176]{1,0:T(8,128)(2,1)S(1)} %onward_plane.1.far_ref), channel_id=1, source_target_pairs={{0,5},{1,4},{2,7},{3,6},{4,1},{5,0},{6,3},{7,2},{8,13},{9,12},{10,... | collective-permute-start | bytes 940040 | tf_op jit(solution)/shard_map/ppermute | solution.py:736
  28.6 13.2 %collective-permute-start.14 = (bf16[72,2176]{1,0:T(8,128)(2,1)S(1)}, bf16[72,2176]{1,0:T(8,128)(2,1)S(1)}, u32[]{:S(2)}, u32[]{:S(2)}) collective-permute-start(bf16[72,2176]{1,0:T(8,128)(2,1)S(1)} %onward_plane.1.far_ref), channel_id=1, source_target_pairs={{0,1},{1,0},{2,3},{3,2},{4,5},{5,4},{6,7},{7,6},{8,9},{9,8},{10,11... | collective-permute-start | bytes 940040 | tf_op jit(solution)/shard_map/ppermute | solution.py:736
  29.1 12.6 %collective-permute-start.15 = (bf16[72,2176]{1,0:T(8,128)(2,1)S(1)}, bf16[72,2176]{1,0:T(8,128)(2,1)S(1)}, u32[]{:S(2)}, u32[]{:S(2)}) collective-permute-start(bf16[72,2176]{1,0:T(8,128)(2,1)S(1)} %onward_plane.1.far_ref), channel_id=1, source_target_pairs={{0,4},{1,5},{2,6},{3,7},{4,0},{5,1},{6,2},{7,3},{8,12},{9,13},{10,... | collective-permute-start | bytes 940040 | tf_op jit(solution)/shard_map/ppermute | solution.py:736
  29.6 11.8 %collective-permute-start.11 = (bf16[32,2176]{1,0:T(8,128)(2,1)S(1)}, bf16[32,2176]{1,0:T(8,128)(2,1)S(1)}, u32[]{:S(2)}, u32[]{:S(2)}) collective-permute-start(bf16[32,2176]{1,0:T(8,128)(2,1)S(1)} %onward_z.1), channel_id=1, source_target_pairs={{0,16},{1,17},{2,18},{3,19},{4,20},{5,21},{6,22},{7,23},{8,24},{9,... | collective-permute-start | bytes 417800 | tf_op jit(solution)/shard_map/ppermute | solution.py:736
  32.6 8.8 %collective-permute-start.12 = (bf16[32,2176]{1,0:T(8,128)(2,1)S(1)}, bf16[32,2176]{1,0:T(8,128)(2,1)S(1)}, u32[]{:S(2)}, u32[]{:S(2)}) collective-permute-start(bf16[32,2176]{1,0:T(8,128)(2,1)S(1)} %onward_z.1), channel_id=1, source_target_pairs={{0,24},{1,25},{2,26},{3,27},{4,28},{5,29},{6,30},{7,31},{8,16},{9,... | collective-permute-start | bytes 417800 | tf_op jit(solution)/shard_map/ppermute | solution.py:736
  41.4 9.8 %collective-permute-start.19 = (bf16[32,2048]{1,0:T(8,128)(2,1)S(1)}, bf16[32,2048]{1,0:T(8,128)(2,1)S(1)}, u32[]{:S(2)}, u32[]{:S(2)}) collective-permute-start(bf16[32,2048]{1,0:T(8,128)(2,1)S(1)} %get-tuple-element.77), channel_id=1, source_target_pairs={{0,8},{1,9},{2,10},{3,11},{4,12},{5,13},{6,14},{7,15},{8,0},{9,1},... | collective-permute-start | bytes 393224 | tf_op jit(solution)/shard_map/ppermute | solution.py:736
  44.8 10.9 %collective-permute-start.16 = (bf16[72,2048]{1,0:T(8,128)(2,1)S(1)}, bf16[72,2048]{1,0:T(8,128)(2,1)S(1)}, u32[]{:S(2)}, u32[]{:S(2)}) collective-permute-start(bf16[72,2048]{1,0:T(8,128)(2,1)S(1)} %get-tuple-element.74), channel_id=1, source_target_pairs={{0,5},{1,4},{2,7},{3,6},{4,1},{5,0},{6,3},{7,2},{8,13},{9,12},{10,... | collective-permute-start | bytes 884744 | tf_op jit(solution)/shard_map/ppermute | solution.py:736
  47.3 13.7 %collective-permute-start.17 = (bf16[72,2048]{1,0:T(8,128)(2,1)S(1)}, bf16[72,2048]{1,0:T(8,128)(2,1)S(1)}, u32[]{:S(2)}, u32[]{:S(2)}) collective-permute-start(bf16[72,2048]{1,0:T(8,128)(2,1)S(1)} %get-tuple-element.75), channel_id=1, source_target_pairs={{0,1},{1,0},{2,3},{3,2},{4,5},{5,4},{6,7},{7,6},{8,9},{9,8},{10,11... | collective-permute-start | bytes 884744 | tf_op jit(solution)/shard_map/ppermute | solution.py:736
  47.8 13.2 %collective-permute-start.18 = (bf16[72,2048]{1,0:T(8,128)(2,1)S(1)}, bf16[72,2048]{1,0:T(8,128)(2,1)S(1)}, u32[]{:S(2)}, u32[]{:S(2)}) collective-permute-start(bf16[72,2048]{1,0:T(8,128)(2,1)S(1)} %get-tuple-element.76), channel_id=1, source_target_pairs={{0,4},{1,5},{2,6},{3,7},{4,0},{5,1},{6,2},{7,3},{8,12},{9,13},{10,... | collective-permute-start | bytes 884744 | tf_op jit(solution)/shard_map/ppermute | solution.py:736
  48.3 12.8 %collective-permute-start.20 = (bf16[32,2048]{1,0:T(8,128)(2,1)S(1)}, bf16[32,2048]{1,0:T(8,128)(2,1)S(1)}, u32[]{:S(2)}, u32[]{:S(2)}) collective-permute-start(bf16[32,2048]{1,0:T(8,128)(2,1)S(1)} %get-tuple-element.79), channel_id=1, source_target_pairs={{0,16},{1,17},{2,18},{3,19},{4,20},{5,21},{6,22},{7,23},{8,24},{9,... | collective-permute-start | bytes 393224 | tf_op jit(solution)/shard_map/ppermute | solution.py:736
  51.2 9.9 %collective-permute-start.21 = (bf16[32,2048]{1,0:T(8,128)(2,1)S(1)}, bf16[32,2048]{1,0:T(8,128)(2,1)S(1)}, u32[]{:S(2)}, u32[]{:S(2)}) collective-permute-start(bf16[32,2048]{1,0:T(8,128)(2,1)S(1)} %get-tuple-element.80), channel_id=1, source_target_pairs={{0,24},{1,25},{2,26},{3,27},{4,28},{5,29},{6,30},{7,31},{8,16},{9,... | collective-permute-start | bytes 393224 | tf_op jit(solution)/shard_map/ppermute | solution.py:736
  61.1 7.5 %collective-permute-start.25 = (bf16[24,2048]{1,0:T(8,128)(2,1)S(1)}, bf16[24,2048]{1,0:T(8,128)(2,1)S(1)}, u32[]{:S(2)}, u32[]{:S(2)}) collective-permute-start(bf16[24,2048]{1,0:T(8,128)(2,1)S(1)} %get-tuple-element.94), channel_id=1, source_target_pairs={{0,8},{1,9},{2,10},{3,11},{4,12},{5,13},{6,14},{7,15},{8,0},{9,1},... | collective-permute-start | bytes 294920 | tf_op jit(solution)/shard_map/ppermute | solution.py:736
  62.8 10.5 %collective-permute-start.26 = (bf16[24,2048]{1,0:T(8,128)(2,1)S(1)}, bf16[24,2048]{1,0:T(8,128)(2,1)S(1)}, u32[]{:S(2)}, u32[]{:S(2)}) collective-permute-start(bf16[24,2048]{1,0:T(8,128)(2,1)S(1)} %get-tuple-element.95), channel_id=1, source_target_pairs={{0,16},{1,17},{2,18},{3,19},{4,20},{5,21},{6,22},{7,23},{8,24},{9,... | collective-permute-start | bytes 294920 | tf_op jit(solution)/shard_map/ppermute | solution.py:736
  64.5 8.8 %collective-permute-start.27 = (bf16[24,2048]{1,0:T(8,128)(2,1)S(1)}, bf16[24,2048]{1,0:T(8,128)(2,1)S(1)}, u32[]{:S(2)}, u32[]{:S(2)}) collective-permute-start(bf16[24,2048]{1,0:T(8,128)(2,1)S(1)} %get-tuple-element.96), channel_id=1, source_target_pairs={{0,24},{1,25},{2,26},{3,27},{4,28},{5,29},{6,30},{7,31},{8,16},{9,... | collective-permute-start | bytes 294920 | tf_op jit(solution)/shard_map/ppermute | solution.py:736
  65.7 7.7 %collective-permute-start.22 = (bf16[32,2048]{1,0:T(8,128)(2,1)S(1)}, bf16[32,2048]{1,0:T(8,128)(2,1)S(1)}, u32[]{:S(2)}, u32[]{:S(2)}) collective-permute-start(bf16[32,2048]{1,0:T(8,128)(2,1)S(1)} %get-tuple-element.89), channel_id=1, source_target_pairs={{0,5},{1,4},{2,7},{3,6},{4,1},{5,0},{6,3},{7,2},{8,13},{9,12},{10,... | collective-permute-start | bytes 393224 | tf_op jit(solution)/shard_map/ppermute | solution.py:736
  68.1 6.2 %collective-permute-start.23 = (bf16[32,2048]{1,0:T(8,128)(2,1)S(1)}, bf16[32,2048]{1,0:T(8,128)(2,1)S(1)}, u32[]{:S(2)}, u32[]{:S(2)}) collective-permute-start(bf16[32,2048]{1,0:T(8,128)(2,1)S(1)} %get-tuple-element.90), channel_id=1, source_target_pairs={{0,1},{1,0},{2,3},{3,2},{4,5},{5,4},{6,7},{7,6},{8,9},{9,8},{10,11... | collective-permute-start | bytes 393224 | tf_op jit(solution)/shard_map/ppermute | solution.py:736
  68.6 5.7 %collective-permute-start.24 = (bf16[32,2048]{1,0:T(8,128)(2,1)S(1)}, bf16[32,2048]{1,0:T(8,128)(2,1)S(1)}, u32[]{:S(2)}, u32[]{:S(2)}) collective-permute-start(bf16[32,2048]{1,0:T(8,128)(2,1)S(1)} %get-tuple-element.91), channel_id=1, source_target_pairs={{0,4},{1,5},{2,6},{3,7},{4,0},{5,1},{6,2},{7,3},{8,12},{9,13},{10,... | collective-permute-start | bytes 393224 | tf_op jit(solution)/shard_map/ppermute | solution.py:736
  73.3 1.0 %copy-start = (f32[2048]{0:T(1024)S(1)}, f32[2048]{0:T(1024)}, u32[]{:S(2)}) copy-start(f32[2048]{0:T(1024)} %param.29) | copy-start | bytes 24580

commit v8 on v7

--- a/solution.py
+++ b/solution.py
@@ -367,10 +367,13 @@
 
 def own_kernel(
     pages_ref, lengths_ref, tp_ref, home_ref, q_ref, fresh_ref, cache_ref, w_ref,
-    residual_hbm, ids_hbm, routed_hbm,
-    own_ref, pack_ref, residual_ref, ids_ref, routed_ref, count_ref, context_ref, every_ref, sems,
+    residual_hbm, ids_hbm, routed_hbm, gain_hbm,
+    own_ref, pack_ref, gain_ref, residual_ref, ids_ref, routed_ref, count_ref, context_ref, every_ref, sems,
 ):
-    moves = ((ids_hbm, ids_ref), (routed_hbm, routed_ref), (residual_hbm, residual_ref))
+    moves = (
+        (ids_hbm, ids_ref), (routed_hbm, routed_ref), (residual_hbm, residual_ref),
+        (gain_hbm, gain_ref),
+    )
     fetches = [
         pltpu.make_async_copy(source, target, sems.at[i])
         for i, (source, target) in enumerate(moves)
@@ -392,7 +395,7 @@
         )
 
 
-def own_terms(pages, lengths, tp_index, home, kept, residual, ids, routed):
+def own_terms(pages, lengths, tp_index, home, kept, residual, ids, routed, gain):
     tokens, width = residual.shape
     half = tokens // 2
     queries, _, cache, _ = kept
@@ -402,19 +405,20 @@
         out_shape=(
             jax.ShapeDtypeStruct((half, width), jnp.float32),
             jax.ShapeDtypeStruct((half, LANES), jnp.bfloat16),
+            jax.ShapeDtypeStruct(gain.shape, gain.dtype),
         ),
-        in_specs=[smem()] * 4 + [vmem()] * 4 + [hbm()] * 3,
-        out_specs=(vmem(),) * 2,
+        in_specs=[smem()] * 4 + [vmem()] * 4 + [hbm()] * 4,
+        out_specs=(vmem(),) * 3,
         scratch_shapes=[pltpu.VMEM(v.shape, v.dtype) for v in moved]
         + [
             pltpu.VMEM((tokens, cache.shape[0] * cache.shape[1]), jnp.float32),
             pltpu.VMEM((half, queries.shape[1]), jnp.bfloat16),
             pltpu.VMEM((LANES, LANES), jnp.float32),
-            pltpu.SemaphoreType.DMA((3,)),
+            pltpu.SemaphoreType.DMA((4,)),
         ],
         compiler_params=pltpu.CompilerParams(vmem_limit_bytes=16 * MIB),
         name="own_terms",
-    )(stay(pages), stay(lengths), tp_index, stay(home), *kept, *[stay(v) for v in moved])
+    )(stay(pages), stay(lengths), tp_index, stay(home), *kept, *[stay(v) for v in moved + (gain,)])
 
 
 LATE = pl.CostEstimate(flops=3 * 10**10, bytes_accessed=1 << 20, transcendentals=0)
@@ -764,9 +768,9 @@
     sent, *kept = other_terms(
         pages, cache_length_rows, tp_index, group, queries, fresh_key_value, key_value_cache, w_out
     )
-    own_state, pack = own_terms(
+    own_state, pack, last_gain = own_terms(
         pages, cache_length_rows, tp_index, expert_home, kept, residual, route_ids.T,
-        route_weights.T,
+        route_weights.T, gain_out[None, :],
     )
     got, partner_weights = barrier(swap(sent, 0, 0, 0, 1), partner_weights)
     state, far_rows, last_rows = norm_rows(own_state, got, pack, gain_in[None, :], far)
@@ -790,7 +794,7 @@
     own, *near_sums = column_sum(near, first, last_parts, half)
     total = total_rows(state, own, swap_z(far_sums))
     last_plane, total = barrier(swap_plane(near_sums), total)
-    return final_rows(total, last_plane, gain_out[None, :])
+    return final_rows(total, last_plane, last_gain)
 
 
 def solution(mesh):

time: 75.3 us -> 75.3 us (level)
  no operation moved by 1% of the time
where the time goes in v8:
time: 75.3 us; the launch traced here: 75.1 us
  starting transfers between devices  36.9 us (49%)
  waiting for transfers between devices  20.5 us (27%)
  Pallas kernels  17.5 us (23%)
    ppermute x28, starting transfers between devices, swap(): return lax.ppermute(value, ALL, pairs)  36.9 us
    ppermute x28, waiting for transfers between devices, swap(): return lax.ppermute(value, ALL, pairs)  20.5 us
    pallas_call x1, Pallas kernels, near_rows(): pl.pallas_call(functools.partial(near_kernel, groups), out_shape=(jax.Sha...  5.93 us
    pallas_call x1, Pallas kernels, other_terms(): pl.pallas_call(other_kernel, out_shape=(jax.ShapeDtypeStruct((half, w_out...  3.76 us
    pallas_call x1, Pallas kernels, own_terms(): pl.pallas_call(own_kernel, out_shape=(jax.ShapeDtypeStruct((half, width),...  3.51 us
    pallas_call x1, Pallas kernels, piece_rows(): pl.pallas_call(functools.partial(piece_kernel, groups, count), out_shape=...  3.01 us
  transfers between devices with their start and end apart: 28, of which 10 were waited for; matrix products, arithmetic and copies ran while one was open for 0% of the time, Pallas kernels for 22%

profile of v8, /device:TPU:0, one launch (start us, length us, event | category | flops | bytes accessed | tf_op | source)
XLA Modules:
  0.0 75.1 jit_solution(17239515094193192668)
XLA Ops:
  1.0 3.8 %other_terms.1 = (bf16[32,2048]{1,0:T(8,128)(2,1)S(1)}, bf16[64,1024]{1,0:T(8,128)(2,1)S(1)}, bf16[64,512]{1,0:T(8,128)(2,1)S(1)}, bf16[4,128,512]{2,1,0:T(8,128)(2,1)S(1)}, bf16[1024,2048]{1,0:T(8,128)(2,1)S(1)}) custom-call(s32[4,9]{1,0:T(4,128)} %bitcast.18, s32[9]{0:T(128)} %lengths_ref.3, s32[1]{0:T(128)} %bitcast.2.tp_ref, s32[1]{0:T(128)} %bitcast.group_ref, ...), custom_call_target="tpu_custom_call" | custom-call | tf_op jit(solution)/shard_map/other_terms/pallas_call | solution.py:351
  4.7 2.5 %collective-permute-start = (bf16[32,2048]{1,0:T(8,128)(2,1)S(1)}, bf16[32,2048]{1,0:T(8,128)(2,1)S(1)}, u32[]{:S(2)}, u32[]{:S(2)}) collective-permute-start(bf16[32,2048]{1,0:T(8,128)(2,1)S(1)} %get-tuple-element.59), channel_id=1, source_target_pairs={{0,1},{1,0},{2,3},{3,2},{4,5},{5,4},{6,7},{7,6},{8,9},{9,8},{10,11... | collective-permute-start | bytes 393224 | tf_op jit(solution)/shard_map/ppermute | solution.py:740
  7.3 3.5 %own_terms.1 = (f32[32,2048]{1,0:T(8,128)S(1)}, bf16[32,128]{1,0:T(8,128)(2,1)S(1)}, f32[1,2048]{1,0:T(1,128)S(1)}) custom-call(s32[4,9]{1,0:T(4,128)} %bitcast.19, s32[9]{0:T(128)} %lengths_ref.3, s32[1]{0:T(128)} %bitcast.2.tp_ref, s32[16]{0:T(128)} %home_ref.1, bf16[64,1024]{1,0:T(8,128)(2,1)S(1)} %get-tuple-element.54.q_ref, ...), custom_call_target="tpu_custom_call" | custom-call | tf_op jit(solution)/shard_map/own_terms/pallas_call | solution.py:403
  10.8 0.6 collective-permute-done.got_ref
  11.6 1.9 %collective-permute-start.7 = (bf16[24,2176]{1,0:T(8,128)(2,1)S(1)}, bf16[24,2176]{1,0:T(8,128)(2,1)S(1)}, u32[]{:S(2)}, u32[]{:S(2)}) collective-permute-start(bf16[24,2176]{1,0:T(8,128)(2,1)S(1)} %get-tuple-element.62.refs_0_), channel_id=1, source_target_pairs={{0,8},{1,9},{2,10},{3,11},{4,12},{5,13},{6,14},{7,15},{8,0},{9,1},... | collective-permute-start | bytes 313352 | tf_op jit(solution)/shard_map/ppermute | solution.py:740
  13.5 2.6 %collective-permute-start.8 = (bf16[24,2176]{1,0:T(8,128)(2,1)S(1)}, bf16[24,2176]{1,0:T(8,128)(2,1)S(1)}, u32[]{:S(2)}, u32[]{:S(2)}) collective-permute-start(bf16[24,2176]{1,0:T(8,128)(2,1)S(1)} %get-tuple-element.62.refs_0_), channel_id=1, source_target_pairs={{0,16},{1,17},{2,18},{3,19},{4,20},{5,21},{6,22},{7,23},{8,24},{9,... | collective-permute-start | bytes 313352 | tf_op jit(solution)/shard_map/ppermute | solution.py:740
  16.1 2.7 %collective-permute-start.4 = (bf16[32,2176]{1,0:T(8,128)(2,1)S(1)}, bf16[32,2176]{1,0:T(8,128)(2,1)S(1)}, u32[]{:S(2)}, u32[]{:S(2)}) collective-permute-start(bf16[32,2176]{1,0:T(8,128)(2,1)S(1)} %own_rows.1.refs_0_.r0), channel_id=1, source_target_pairs={{0,5},{1,4},{2,7},{3,6},{4,1},{5,0},{6,3},{7,2},{8,13},{9,12},{10,... | collective-permute-start | bytes 417800 | tf_op jit(solution)/shard_map/ppermute | solution.py:740
  19.7 4.6 %collective-permute-done.8.refs_1_ = bf16[24,2176]{1,0:T(8,128)(2,1)S(1)} collective-permute-done((bf16[24,2176]{1,0:T(8,128)(2,1)S(1)}, bf16[24,2176]{1,0:T(8,128)(2,1)S(1)}, u32[]{:S(2)}, u32[]{:S(2)}) %collective-permute-start.8) | collective-permute-done | bytes 104480 | tf_op jit(solution)/shard_map/ppermute | solution.py:740
  24.3 0.6 collective-permute-done.5.refs_2_.r2
  24.9 1.2 %collective-permute-start.10 = (bf16[32,2176]{1,0:T(8,128)(2,1)S(1)}, bf16[32,2176]{1,0:T(8,128)(2,1)S(1)}, u32[]{:S(2)}, u32[]{:S(2)}) collective-permute-start(bf16[32,2176]{1,0:T(8,128)(2,1)S(1)} %onward_z.1), channel_id=1, source_target_pairs={{0,8},{1,9},{2,10},{3,11},{4,12},{5,13},{6,14},{7,15},{8,0},{9,1},... | collective-permute-start | bytes 417800 | tf_op jit(solution)/shard_map/ppermute | solution.py:740
  26.1 2.4 %collective-permute-start.13 = (bf16[72,2176]{1,0:T(8,128)(2,1)S(1)}, bf16[72,2176]{1,0:T(8,128)(2,1)S(1)}, u32[]{:S(2)}, u32[]{:S(2)}) collective-permute-start(bf16[72,2176]{1,0:T(8,128)(2,1)S(1)} %onward_plane.1.far_ref), channel_id=1, source_target_pairs={{0,5},{1,4},{2,7},{3,6},{4,1},{5,0},{6,3},{7,2},{8,13},{9,12},{10,... | collective-permute-start | bytes 940040 | tf_op jit(solution)/shard_map/ppermute | solution.py:740
  28.6 0.5 collective-permute-start.14
  29.6 3.0 %collective-permute-start.11 = (bf16[32,2176]{1,0:T(8,128)(2,1)S(1)}, bf16[32,2176]{1,0:T(8,128)(2,1)S(1)}, u32[]{:S(2)}, u32[]{:S(2)}) collective-permute-start(bf16[32,2176]{1,0:T(8,128)(2,1)S(1)} %onward_z.1), channel_id=1, source_target_pairs={{0,16},{1,17},{2,18},{3,19},{4,20},{5,21},{6,22},{7,23},{8,24},{9,... | collective-permute-start | bytes 417800 | tf_op jit(solution)/shard_map/ppermute | solution.py:740
  32.6 2.1 %collective-permute-start.12 = (bf16[32,2176]{1,0:T(8,128)(2,1)S(1)}, bf16[32,2176]{1,0:T(8,128)(2,1)S(1)}, u32[]{:S(2)}, u32[]{:S(2)}) collective-permute-start(bf16[32,2176]{1,0:T(8,128)(2,1)S(1)} %onward_z.1), channel_id=1, source_target_pairs={{0,24},{1,25},{2,26},{3,27},{4,28},{5,29},{6,30},{7,31},{8,16},{9,... | collective-permute-start | bytes 417800 | tf_op jit(solution)/shard_map/ppermute | solution.py:740
  34.7 5.9 %near_rows.1 = (f32[200,2048]{1,0:T(8,128)S(1)}, bf16[32,2048]{1,0:T(8,128)(2,1)S(1)}, bf16[2048,768]{1,0:T(8,128)(2,1)S(1)}, bf16[2048,768]{1,0:T(8,128)(2,1)S(1)}, bf16[768,2048]{1,0:T(8,128)(2,1)S(1)}) custom-call(s32[1]{0:T(128)} %bitcast.group_ref, bf16[32,2176]{1,0:T(8,128)(2,1)S(1)} %own_rows.1.refs_0_.r0, ...), custom_call_target="tpu_custom_call" | custom-call | flops 1887436800 | bytes 9437184 | tf_op jit(solution)/shard_map/near_rows/pallas_call | solution.py:561
  40.6 0.8 %collective-permute-done.11.refs_0_ = bf16[32,2176]{1,0:T(8,128)(2,1)S(1)} collective-permute-done((bf16[32,2176]{1,0:T(8,128)(2,1)S(1)}, bf16[32,2176]{1,0:T(8,128)(2,1)S(1)}, u32[]{:S(2)}, u32[]{:S(2)}) %collective-permute-start.11) | collective-permute-done | bytes 139296 | tf_op jit(solution)/shard_map/ppermute | solution.py:740
  41.8 3.0 %piece_rows.1 = (bf16[32,2048]{1,0:T(8,128)(2,1)S(1)}, bf16[32,2048]{1,0:T(8,128)(2,1)S(1)}, bf16[72,2048]{1,0:T(8,128)(2,1)S(1)}, bf16[72,2048]{1,0:T(8,128)(2,1)S(1)}, bf16[72,2048]{1,0:T(8,128)(2,1)S(1)}) custom-call(s32[1]{0:T(128)} %bitcast.group_ref, bf16[32,2176]{1,0:T(8,128)(2,1)S(1)} %collective-permute-done.11.refs_0_, ...), custom_call_target="tpu_custom_call" | custom-call | flops 2642411520 | bytes 9437184 | tf_op jit(solution)/shard_map/piece_rows/pallas_call | solution.py:602
  44.8 2.5 %collective-permute-start.16 = (bf16[72,2048]{1,0:T(8,128)(2,1)S(1)}, bf16[72,2048]{1,0:T(8,128)(2,1)S(1)}, u32[]{:S(2)}, u32[]{:S(2)}) collective-permute-start(bf16[72,2048]{1,0:T(8,128)(2,1)S(1)} %get-tuple-element.75), channel_id=1, source_target_pairs={{0,5},{1,4},{2,7},{3,6},{4,1},{5,0},{6,3},{7,2},{8,13},{9,12},{10,... | collective-permute-start | bytes 884744 | tf_op jit(solution)/shard_map/ppermute | solution.py:740
  47.8 0.6 collective-permute-start.18
  48.3 2.9 %collective-permute-start.20 = (bf16[32,2048]{1,0:T(8,128)(2,1)S(1)}, bf16[32,2048]{1,0:T(8,128)(2,1)S(1)}, u32[]{:S(2)}, u32[]{:S(2)}) collective-permute-start(bf16[32,2048]{1,0:T(8,128)(2,1)S(1)} %get-tuple-element.80), channel_id=1, source_target_pairs={{0,16},{1,17},{2,18},{3,19},{4,20},{5,21},{6,22},{7,23},{8,24},{9,... | collective-permute-start | bytes 393224 | tf_op jit(solution)/shard_map/ppermute | solution.py:740
  51.2 1.2 %collective-permute-start.21 = (bf16[32,2048]{1,0:T(8,128)(2,1)S(1)}, bf16[32,2048]{1,0:T(8,128)(2,1)S(1)}, u32[]{:S(2)}, u32[]{:S(2)}) collective-permute-start(bf16[32,2048]{1,0:T(8,128)(2,1)S(1)} %get-tuple-element.81), channel_id=1, source_target_pairs={{0,24},{1,25},{2,26},{3,27},{4,28},{5,29},{6,30},{7,31},{8,16},{9,... | collective-permute-start | bytes 393224 | tf_op jit(solution)/shard_map/ppermute | solution.py:740
  52.4 3.2 %collective-permute-done.16.g1 = bf16[72,2048]{1,0:T(8,128)(2,1)S(1)} collective-permute-done((bf16[72,2048]{1,0:T(8,128)(2,1)S(1)}, bf16[72,2048]{1,0:T(8,128)(2,1)S(1)}, u32[]{:S(2)}, u32[]{:S(2)}) %collective-permute-start.16) | collective-permute-done | bytes 294944 | tf_op jit(solution)/shard_map/ppermute | solution.py:740
  55.7 5.3 %collective-permute-done.17.g2 = bf16[72,2048]{1,0:T(8,128)(2,1)S(1)} collective-permute-done((bf16[72,2048]{1,0:T(8,128)(2,1)S(1)}, bf16[72,2048]{1,0:T(8,128)(2,1)S(1)}, u32[]{:S(2)}, u32[]{:S(2)}) %collective-permute-start.17) | collective-permute-done | bytes 294944 | tf_op jit(solution)/shard_map/ppermute | solution.py:740
  61.1 1.7 %collective-permute-start.25 = (bf16[24,2048]{1,0:T(8,128)(2,1)S(1)}, bf16[24,2048]{1,0:T(8,128)(2,1)S(1)}, u32[]{:S(2)}, u32[]{:S(2)}) collective-permute-start(bf16[24,2048]{1,0:T(8,128)(2,1)S(1)} %get-tuple-element.95), channel_id=1, source_target_pairs={{0,8},{1,9},{2,10},{3,11},{4,12},{5,13},{6,14},{7,15},{8,0},{9,1},... | collective-permute-start | bytes 294920 | tf_op jit(solution)/shard_map/ppermute | solution.py:740
  62.8 1.6 %collective-permute-start.26 = (bf16[24,2048]{1,0:T(8,128)(2,1)S(1)}, bf16[24,2048]{1,0:T(8,128)(2,1)S(1)}, u32[]{:S(2)}, u32[]{:S(2)}) collective-permute-start(bf16[24,2048]{1,0:T(8,128)(2,1)S(1)} %get-tuple-element.96), channel_id=1, source_target_pairs={{0,16},{1,17},{2,18},{3,19},{4,20},{5,21},{6,22},{7,23},{8,24},{9,... | collective-permute-start | bytes 294920 | tf_op jit(solution)/shard_map/ppermute | solution.py:740
  64.5 1.1 %collective-permute-start.27 = (bf16[24,2048]{1,0:T(8,128)(2,1)S(1)}, bf16[24,2048]{1,0:T(8,128)(2,1)S(1)}, u32[]{:S(2)}, u32[]{:S(2)}) collective-permute-start(bf16[24,2048]{1,0:T(8,128)(2,1)S(1)} %get-tuple-element.97), channel_id=1, source_target_pairs={{0,24},{1,25},{2,26},{3,27},{4,28},{5,29},{6,30},{7,31},{8,16},{9,... | collective-permute-start | bytes 294920 | tf_op jit(solution)/shard_map/ppermute | solution.py:740
  65.7 2.4 %collective-permute-start.22 = (bf16[32,2048]{1,0:T(8,128)(2,1)S(1)}, bf16[32,2048]{1,0:T(8,128)(2,1)S(1)}, u32[]{:S(2)}, u32[]{:S(2)}) collective-permute-start(bf16[32,2048]{1,0:T(8,128)(2,1)S(1)} %get-tuple-element.90), channel_id=1, source_target_pairs={{0,5},{1,4},{2,7},{3,6},{4,1},{5,0},{6,3},{7,2},{8,13},{9,12},{10,... | collective-permute-start | bytes 393224 | tf_op jit(solution)/shard_map/ppermute | solution.py:740
  68.1 0.5 collective-permute-start.23
  68.6 0.6 collective-permute-start.24
  69.2 4.1 %collective-permute-done.26.z2 = bf16[24,2048]{1,0:T(8,128)(2,1)S(1)} collective-permute-done((bf16[24,2048]{1,0:T(8,128)(2,1)S(1)}, bf16[24,2048]{1,0:T(8,128)(2,1)S(1)}, u32[]{:S(2)}, u32[]{:S(2)}) %collective-permute-start.26) | collective-permute-done | bytes 98336 | tf_op jit(solution)/shard_map/ppermute | solution.py:740
  73.4 0.8 %collective-permute-done.23.p2 = bf16[32,2048]{1,0:T(8,128)(2,1)S(1)} collective-permute-done((bf16[32,2048]{1,0:T(8,128)(2,1)S(1)}, bf16[32,2048]{1,0:T(8,128)(2,1)S(1)}, u32[]{:S(2)}, u32[]{:S(2)}) %collective-permute-start.23) | collective-permute-done | bytes 131104 | tf_op jit(solution)/shard_map/ppermute | solution.py:740
  74.3 0.8 %final_rows.1 = bf16[32,2048]{1,0:T(8,128)(2,1)} custom-call(f32[32,2048]{1,0:T(8,128)S(1)} %total_rows.1.total_ref, bf16[32,2048]{1,0:T(8,128)(2,1)S(1)} %collective-permute-done.22.p1, bf16[32,2048]{1,0:T(8,128)(2,1)S(1)} %collective-permute-done.23.p2, bf16[32,2048]{1,0:T(8,128)(2,1)S(1)} %collective-permute-done.24.p3, ...), custom_call_target="tpu_custom_call" | custom-call | tf_op jit(solution)/shard_map/final_rows/pallas_call | solution.py:718
  (43 shorter events, 3.8 us)
Async XLA Ops:
  0.0 11.5 %collective-permute-start.1 = (bf16[2048,384]{1,0:T(8,128)(2,1)}, bf16[2048,384]{1,0:T(8,128)(2,1)S(1)}, u32[]{:S(2)}, u32[]{:S(2)}) collective-permute-start(bf16[2048,384]{1,0:T(8,128)(2,1)} %bitcast.11), channel_id=1, source_target_pairs={{0,2},{1,3},{2,0},{3,1},{4,6},{5,7},{6,4},{7,5},{8,10},{9,11},{10,... | collective-permute-start | bytes 4718600 | tf_op jit(solution)/shard_map/ppermute | solution.py:740
  0.5 11.0 %collective-permute-start.2 = (bf16[2048,384]{1,0:T(8,128)(2,1)}, bf16[2048,384]{1,0:T(8,128)(2,1)S(1)}, u32[]{:S(2)}, u32[]{:S(2)}) collective-permute-start(bf16[2048,384]{1,0:T(8,128)(2,1)} %bitcast.13), channel_id=1, source_target_pairs={{0,2},{1,3},{2,0},{3,1},{4,6},{5,7},{6,4},{7,5},{8,10},{9,11},{10,... | collective-permute-start | bytes 4718600 | tf_op jit(solution)/shard_map/ppermute | solution.py:740
  0.5 11.0 %collective-permute-start.3 = (bf16[384,2048]{1,0:T(8,128)(2,1)}, bf16[384,2048]{1,0:T(8,128)(2,1)}, u32[]{:S(2)}, u32[]{:S(2)}) collective-permute-start(bf16[384,2048]{1,0:T(8,128)(2,1)} %bitcast.15), channel_id=1, source_target_pairs={{0,2},{1,3},{2,0},{3,1},{4,6},{5,7},{6,4},{7,5},{8,10},{9,11},{10,... | collective-permute-start | bytes 4718600 | tf_op jit(solution)/shard_map/ppermute | solution.py:740
  4.7 6.7 %collective-permute-start = (bf16[32,2048]{1,0:T(8,128)(2,1)S(1)}, bf16[32,2048]{1,0:T(8,128)(2,1)S(1)}, u32[]{:S(2)}, u32[]{:S(2)}) collective-permute-start(bf16[32,2048]{1,0:T(8,128)(2,1)S(1)} %get-tuple-element.59), channel_id=1, source_target_pairs={{0,1},{1,0},{2,3},{3,2},{4,5},{5,4},{6,7},{7,6},{8,9},{9,8},{10,11... | collective-permute-start | bytes 393224 | tf_op jit(solution)/shard_map/ppermute | solution.py:740
  7.3 4.2 %copy-start = (f32[2048]{0:T(1024)S(1)}, f32[2048]{0:T(1024)}, u32[]{:S(2)}) copy-start(f32[2048]{0:T(1024)} %param.22) | copy-start | bytes 24580
  11.5 4.7 %copy-start.1 = (bf16[2048,384]{1,0:T(8,128)(2,1)}, bf16[2048,384]{1,0:T(8,128)(2,1)S(1)}, u32[]{:S(2)}) copy-start(bf16[2048,384]{1,0:T(8,128)(2,1)S(1)} %collective-permute-done.1.wg1) | copy-start | bytes 4718596
  11.5 4.7 %copy-start.2 = (bf16[2048,384]{1,0:T(8,128)(2,1)}, bf16[2048,384]{1,0:T(8,128)(2,1)S(1)}, u32[]{:S(2)}) copy-start(bf16[2048,384]{1,0:T(8,128)(2,1)S(1)} %collective-permute-done.2.wu1) | copy-start | bytes 4718596
  11.6 7.8 %collective-permute-start.7 = (bf16[24,2176]{1,0:T(8,128)(2,1)S(1)}, bf16[24,2176]{1,0:T(8,128)(2,1)S(1)}, u32[]{:S(2)}, u32[]{:S(2)}) collective-permute-start(bf16[24,2176]{1,0:T(8,128)(2,1)S(1)} %get-tuple-element.62.refs_0_), channel_id=1, source_target_pairs={{0,8},{1,9},{2,10},{3,11},{4,12},{5,13},{6,14},{7,15},{8,0},{9,1},... | collective-permute-start | bytes 313352 | tf_op jit(solution)/shard_map/ppermute | solution.py:740
  13.5 10.8 %collective-permute-start.8 = (bf16[24,2176]{1,0:T(8,128)(2,1)S(1)}, bf16[24,2176]{1,0:T(8,128)(2,1)S(1)}, u32[]{:S(2)}, u32[]{:S(2)}) collective-permute-start(bf16[24,2176]{1,0:T(8,128)(2,1)S(1)} %get-tuple-element.62.refs_0_), channel_id=1, source_target_pairs={{0,16},{1,17},{2,18},{3,19},{4,20},{5,21},{6,22},{7,23},{8,24},{9,... | collective-permute-start | bytes 313352 | tf_op jit(solution)/shard_map/ppermute | solution.py:740
  16.1 8.2 %collective-permute-start.9 = (bf16[24,2176]{1,0:T(8,128)(2,1)S(1)}, bf16[24,2176]{1,0:T(8,128)(2,1)S(1)}, u32[]{:S(2)}, u32[]{:S(2)}) collective-permute-start(bf16[24,2176]{1,0:T(8,128)(2,1)S(1)} %get-tuple-element.62.refs_0_), channel_id=1, source_target_pairs={{0,24},{1,25},{2,26},{3,27},{4,28},{5,29},{6,30},{7,31},{8,16},{9,... | collective-permute-start | bytes 313352 | tf_op jit(solution)/shard_map/ppermute | solution.py:740
  16.1 8.2 %collective-permute-start.4 = (bf16[32,2176]{1,0:T(8,128)(2,1)S(1)}, bf16[32,2176]{1,0:T(8,128)(2,1)S(1)}, u32[]{:S(2)}, u32[]{:S(2)}) collective-permute-start(bf16[32,2176]{1,0:T(8,128)(2,1)S(1)} %own_rows.1.refs_0_.r0), channel_id=1, source_target_pairs={{0,5},{1,4},{2,7},{3,6},{4,1},{5,0},{6,3},{7,2},{8,13},{9,12},{10,... | collective-permute-start | bytes 417800 | tf_op jit(solution)/shard_map/ppermute | solution.py:740
  18.9 6.0 %collective-permute-start.5 = (bf16[32,2176]{1,0:T(8,128)(2,1)S(1)}, bf16[32,2176]{1,0:T(8,128)(2,1)S(1)}, u32[]{:S(2)}, u32[]{:S(2)}) collective-permute-start(bf16[32,2176]{1,0:T(8,128)(2,1)S(1)} %own_rows.1.refs_0_.r0), channel_id=1, source_target_pairs={{0,1},{1,0},{2,3},{3,2},{4,5},{5,4},{6,7},{7,6},{8,9},{9,8},{10,11... | collective-permute-start | bytes 417800 | tf_op jit(solution)/shard_map/ppermute | solution.py:740
  19.4 5.5 %collective-permute-start.6 = (bf16[32,2176]{1,0:T(8,128)(2,1)S(1)}, bf16[32,2176]{1,0:T(8,128)(2,1)S(1)}, u32[]{:S(2)}, u32[]{:S(2)}) collective-permute-start(bf16[32,2176]{1,0:T(8,128)(2,1)S(1)} %own_rows.1.refs_0_.r0), channel_id=1, source_target_pairs={{0,4},{1,5},{2,6},{3,7},{4,0},{5,1},{6,2},{7,3},{8,12},{9,13},{10,... | collective-permute-start | bytes 417800 | tf_op jit(solution)/shard_map/ppermute | solution.py:740
  24.9 7.7 %collective-permute-start.10 = (bf16[32,2176]{1,0:T(8,128)(2,1)S(1)}, bf16[32,2176]{1,0:T(8,128)(2,1)S(1)}, u32[]{:S(2)}, u32[]{:S(2)}) collective-permute-start(bf16[32,2176]{1,0:T(8,128)(2,1)S(1)} %onward_z.1), channel_id=1, source_target_pairs={{0,8},{1,9},{2,10},{3,11},{4,12},{5,13},{6,14},{7,15},{8,0},{9,1},... | collective-permute-start | bytes 417800 | tf_op jit(solution)/shard_map/ppermute | solution.py:740
  26.1 15.3 %collective-permute-start.13 = (bf16[72,2176]{1,0:T(8,128)(2,1)S(1)}, bf16[72,2176]{1,0:T(8,128)(2,1)S(1)}, u32[]{:S(2)}, u32[]{:S(2)}) collective-permute-start(bf16[72,2176]{1,0:T(8,128)(2,1)S(1)} %onward_plane.1.far_ref), channel_id=1, source_target_pairs={{0,5},{1,4},{2,7},{3,6},{4,1},{5,0},{6,3},{7,2},{8,13},{9,12},{10,... | collective-permute-start | bytes 940040 | tf_op jit(solution)/shard_map/ppermute | solution.py:740
  28.6 13.2 %collective-permute-start.14 = (bf16[72,2176]{1,0:T(8,128)(2,1)S(1)}, bf16[72,2176]{1,0:T(8,128)(2,1)S(1)}, u32[]{:S(2)}, u32[]{:S(2)}) collective-permute-start(bf16[72,2176]{1,0:T(8,128)(2,1)S(1)} %onward_plane.1.far_ref), channel_id=1, source_target_pairs={{0,1},{1,0},{2,3},{3,2},{4,5},{5,4},{6,7},{7,6},{8,9},{9,8},{10,11... | collective-permute-start | bytes 940040 | tf_op jit(solution)/shard_map/ppermute | solution.py:740
  29.1 12.6 %collective-permute-start.15 = (bf16[72,2176]{1,0:T(8,128)(2,1)S(1)}, bf16[72,2176]{1,0:T(8,128)(2,1)S(1)}, u32[]{:S(2)}, u32[]{:S(2)}) collective-permute-start(bf16[72,2176]{1,0:T(8,128)(2,1)S(1)} %onward_plane.1.far_ref), channel_id=1, source_target_pairs={{0,4},{1,5},{2,6},{3,7},{4,0},{5,1},{6,2},{7,3},{8,12},{9,13},{10,... | collective-permute-start | bytes 940040 | tf_op jit(solution)/shard_map/ppermute | solution.py:740
  29.6 11.8 %collective-permute-start.11 = (bf16[32,2176]{1,0:T(8,128)(2,1)S(1)}, bf16[32,2176]{1,0:T(8,128)(2,1)S(1)}, u32[]{:S(2)}, u32[]{:S(2)}) collective-permute-start(bf16[32,2176]{1,0:T(8,128)(2,1)S(1)} %onward_z.1), channel_id=1, source_target_pairs={{0,16},{1,17},{2,18},{3,19},{4,20},{5,21},{6,22},{7,23},{8,24},{9,... | collective-permute-start | bytes 417800 | tf_op jit(solution)/shard_map/ppermute | solution.py:740
  32.6 8.8 %collective-permute-start.12 = (bf16[32,2176]{1,0:T(8,128)(2,1)S(1)}, bf16[32,2176]{1,0:T(8,128)(2,1)S(1)}, u32[]{:S(2)}, u32[]{:S(2)}) collective-permute-start(bf16[32,2176]{1,0:T(8,128)(2,1)S(1)} %onward_z.1), channel_id=1, source_target_pairs={{0,24},{1,25},{2,26},{3,27},{4,28},{5,29},{6,30},{7,31},{8,16},{9,... | collective-permute-start | bytes 417800 | tf_op jit(solution)/shard_map/ppermute | solution.py:740
  41.4 9.8 %collective-permute-start.19 = (bf16[32,2048]{1,0:T(8,128)(2,1)S(1)}, bf16[32,2048]{1,0:T(8,128)(2,1)S(1)}, u32[]{:S(2)}, u32[]{:S(2)}) collective-permute-start(bf16[32,2048]{1,0:T(8,128)(2,1)S(1)} %get-tuple-element.78), channel_id=1, source_target_pairs={{0,8},{1,9},{2,10},{3,11},{4,12},{5,13},{6,14},{7,15},{8,0},{9,1},... | collective-permute-start | bytes 393224 | tf_op jit(solution)/shard_map/ppermute | solution.py:740
  44.8 10.9 %collective-permute-start.16 = (bf16[72,2048]{1,0:T(8,128)(2,1)S(1)}, bf16[72,2048]{1,0:T(8,128)(2,1)S(1)}, u32[]{:S(2)}, u32[]{:S(2)}) collective-permute-start(bf16[72,2048]{1,0:T(8,128)(2,1)S(1)} %get-tuple-element.75), channel_id=1, source_target_pairs={{0,5},{1,4},{2,7},{3,6},{4,1},{5,0},{6,3},{7,2},{8,13},{9,12},{10,... | collective-permute-start | bytes 884744 | tf_op jit(solution)/shard_map/ppermute | solution.py:740
  47.3 13.7 %collective-permute-start.17 = (bf16[72,2048]{1,0:T(8,128)(2,1)S(1)}, bf16[72,2048]{1,0:T(8,128)(2,1)S(1)}, u32[]{:S(2)}, u32[]{:S(2)}) collective-permute-start(bf16[72,2048]{1,0:T(8,128)(2,1)S(1)} %get-tuple-element.76), channel_id=1, source_target_pairs={{0,1},{1,0},{2,3},{3,2},{4,5},{5,4},{6,7},{7,6},{8,9},{9,8},{10,11... | collective-permute-start | bytes 884744 | tf_op jit(solution)/shard_map/ppermute | solution.py:740
  47.8 13.2 %collective-permute-start.18 = (bf16[72,2048]{1,0:T(8,128)(2,1)S(1)}, bf16[72,2048]{1,0:T(8,128)(2,1)S(1)}, u32[]{:S(2)}, u32[]{:S(2)}) collective-permute-start(bf16[72,2048]{1,0:T(8,128)(2,1)S(1)} %get-tuple-element.77), channel_id=1, source_target_pairs={{0,4},{1,5},{2,6},{3,7},{4,0},{5,1},{6,2},{7,3},{8,12},{9,13},{10,... | collective-permute-start | bytes 884744 | tf_op jit(solution)/shard_map/ppermute | solution.py:740
  48.3 12.8 %collective-permute-start.20 = (bf16[32,2048]{1,0:T(8,128)(2,1)S(1)}, bf16[32,2048]{1,0:T(8,128)(2,1)S(1)}, u32[]{:S(2)}, u32[]{:S(2)}) collective-permute-start(bf16[32,2048]{1,0:T(8,128)(2,1)S(1)} %get-tuple-element.80), channel_id=1, source_target_pairs={{0,16},{1,17},{2,18},{3,19},{4,20},{5,21},{6,22},{7,23},{8,24},{9,... | collective-permute-start | bytes 393224 | tf_op jit(solution)/shard_map/ppermute | solution.py:740
  51.2 9.9 %collective-permute-start.21 = (bf16[32,2048]{1,0:T(8,128)(2,1)S(1)}, bf16[32,2048]{1,0:T(8,128)(2,1)S(1)}, u32[]{:S(2)}, u32[]{:S(2)}) collective-permute-start(bf16[32,2048]{1,0:T(8,128)(2,1)S(1)} %get-tuple-element.81), channel_id=1, source_target_pairs={{0,24},{1,25},{2,26},{3,27},{4,28},{5,29},{6,30},{7,31},{8,16},{9,... | collective-permute-start | bytes 393224 | tf_op jit(solution)/shard_map/ppermute | solution.py:740
  61.1 7.5 %collective-permute-start.25 = (bf16[24,2048]{1,0:T(8,128)(2,1)S(1)}, bf16[24,2048]{1,0:T(8,128)(2,1)S(1)}, u32[]{:S(2)}, u32[]{:S(2)}) collective-permute-start(bf16[24,2048]{1,0:T(8,128)(2,1)S(1)} %get-tuple-element.95), channel_id=1, source_target_pairs={{0,8},{1,9},{2,10},{3,11},{4,12},{5,13},{6,14},{7,15},{8,0},{9,1},... | collective-permute-start | bytes 294920 | tf_op jit(solution)/shard_map/ppermute | solution.py:740
  62.8 10.5 %collective-permute-start.26 = (bf16[24,2048]{1,0:T(8,128)(2,1)S(1)}, bf16[24,2048]{1,0:T(8,128)(2,1)S(1)}, u32[]{:S(2)}, u32[]{:S(2)}) collective-permute-start(bf16[24,2048]{1,0:T(8,128)(2,1)S(1)} %get-tuple-element.96), channel_id=1, source_target_pairs={{0,16},{1,17},{2,18},{3,19},{4,20},{5,21},{6,22},{7,23},{8,24},{9,... | collective-permute-start | bytes 294920 | tf_op jit(solution)/shard_map/ppermute | solution.py:740
  64.5 8.8 %collective-permute-start.27 = (bf16[24,2048]{1,0:T(8,128)(2,1)S(1)}, bf16[24,2048]{1,0:T(8,128)(2,1)S(1)}, u32[]{:S(2)}, u32[]{:S(2)}) collective-permute-start(bf16[24,2048]{1,0:T(8,128)(2,1)S(1)} %get-tuple-element.97), channel_id=1, source_target_pairs={{0,24},{1,25},{2,26},{3,27},{4,28},{5,29},{6,30},{7,31},{8,16},{9,... | collective-permute-start | bytes 294920 | tf_op jit(solution)/shard_map/ppermute | solution.py:740
  65.7 7.7 %collective-permute-start.22 = (bf16[32,2048]{1,0:T(8,128)(2,1)S(1)}, bf16[32,2048]{1,0:T(8,128)(2,1)S(1)}, u32[]{:S(2)}, u32[]{:S(2)}) collective-permute-start(bf16[32,2048]{1,0:T(8,128)(2,1)S(1)} %get-tuple-element.90), channel_id=1, source_target_pairs={{0,5},{1,4},{2,7},{3,6},{4,1},{5,0},{6,3},{7,2},{8,13},{9,12},{10,... | collective-permute-start | bytes 393224 | tf_op jit(solution)/shard_map/ppermute | solution.py:740
  68.1 6.2 %collective-permute-start.23 = (bf16[32,2048]{1,0:T(8,128)(2,1)S(1)}, bf16[32,2048]{1,0:T(8,128)(2,1)S(1)}, u32[]{:S(2)}, u32[]{:S(2)}) collective-permute-start(bf16[32,2048]{1,0:T(8,128)(2,1)S(1)} %get-tuple-element.91), channel_id=1, source_target_pairs={{0,1},{1,0},{2,3},{3,2},{4,5},{5,4},{6,7},{7,6},{8,9},{9,8},{10,11... | collective-permute-start | bytes 393224 | tf_op jit(solution)/shard_map/ppermute | solution.py:740
  68.6 5.7 %collective-permute-start.24 = (bf16[32,2048]{1,0:T(8,128)(2,1)S(1)}, bf16[32,2048]{1,0:T(8,128)(2,1)S(1)}, u32[]{:S(2)}, u32[]{:S(2)}) collective-permute-start(bf16[32,2048]{1,0:T(8,128)(2,1)S(1)} %get-tuple-element.92), channel_id=1, source_target_pairs={{0,4},{1,5},{2,6},{3,7},{4,0},{5,1},{6,2},{7,3},{8,12},{9,13},{10,... | collective-permute-start | bytes 393224 | tf_op jit(solution)/shard_map/ppermute | solution.py:740

commit v9 on v8

--- a/solution.py
+++ b/solution.py
@@ -507,10 +507,7 @@
         x_ref[at:, :] = jnp.zeros((x_ref.shape[0] - at, x_ref.shape[1]), jnp.bfloat16)
 
 
-def near_kernel(
-    groups, group_ref, r0, r1, r2, r3, far_ref, z1_ref, wg1, wu1, wg0, wu0, wd0, wd1,
-    out_ref, z1_out_ref, w0_ref, w1_ref, down_ref, x_ref, h_ref, sems,
-):
+def merge_kernel(wg1, wu1, wg0, wu0, wd0, wd1, w0_ref, w1_ref, down_ref, sems):
     hidden = wg0.shape[1]
     fetches = [
         pltpu.make_async_copy(source, target, sems.at[i])
@@ -527,15 +524,38 @@
     ]
     for fetch in fetches:
         fetch.start()
+    for fetch in fetches:
+        fetch.wait()
+
+
+def merge_weights(weights, partner_weights):
+    wg0, wu0, wd0 = weights
+    wg1, wu1, wd1 = partner_weights
+    width, hidden = wg0.shape
+    return pl.pallas_call(
+        merge_kernel,
+        out_shape=(
+            jax.ShapeDtypeStruct((width, 2 * hidden), jnp.bfloat16),
+            jax.ShapeDtypeStruct((width, 2 * hidden), jnp.bfloat16),
+            jax.ShapeDtypeStruct((2 * hidden, width), jnp.bfloat16),
+        ),
+        in_specs=[pl.BlockSpec(memory_space=pl.ANY)] * 2 + [hbm()] * 4,
+        out_specs=(vmem(),) * 3,
+        scratch_shapes=[pltpu.SemaphoreType.DMA((6,))],
+        compiler_params=SMALL,
+        cost_estimate=pl.CostEstimate(
+            flops=0, bytes_accessed=24 * width * hidden, transcendentals=0
+        ),
+        name="merge_weights",
+    )(wg1, wu1, *[stay(w) for w in (wg0, wu0, wd0, wd1)])
+
+
+def near_kernel(
+    groups, group_ref, r0, r1, r2, r3, far_ref, z1_ref, w0_ref, w1_ref, down_ref,
+    out_ref, z1_out_ref, x_ref, h_ref,
+):
     gather_pieces((r0, r1, r2, r3, far_ref, z1_ref), x_ref)
-
-    def ready(e):
-        for fetch in fetches[4:] if e else fetches[:2]:
-            fetch.wait()
-
-    hidden_units(groups, group_ref, x_ref, (w0_ref, w1_ref), h_ref, ready)
-    fetches[2].wait()
-    fetches[3].wait()
+    hidden_units(groups, group_ref, x_ref, (w0_ref, w1_ref), h_ref, lambda e: None)
     height = out_ref.shape[0]
     for col in range(0, down_ref.shape[1], DOWN_BLOCK):
         cols = slice(col, col + DOWN_BLOCK)
@@ -552,32 +572,26 @@
     )
 
 
-def near_rows(groups, group, rows, far, near_z, weights, partner_weights):
+def near_rows(groups, group, rows, far, near_z, w0, w1, down):
     height = 4 * rows[0].shape[0] + far.shape[0]
     padded = -(-(height + near_z.shape[0]) // 16) * 16
-    width, hidden = weights[0].shape
-    wg0, wu0, wd0 = weights
-    wg1, wu1, wd1 = partner_weights
+    width, hidden = w1.shape[0], w1.shape[1] // 2
     return pl.pallas_call(
         functools.partial(near_kernel, groups),
         out_shape=(
             jax.ShapeDtypeStruct((height, width), jnp.float32),
             jax.ShapeDtypeStruct((near_z.shape[0], width), jnp.bfloat16),
-            jax.ShapeDtypeStruct((width, 2 * hidden), jnp.bfloat16),
-            jax.ShapeDtypeStruct((width, 2 * hidden), jnp.bfloat16),
-            jax.ShapeDtypeStruct((2 * hidden, width), jnp.bfloat16),
         ),
-        in_specs=[smem()] + [vmem()] * 8 + [hbm()] * 4,
-        out_specs=(vmem(),) * 5,
+        in_specs=[smem()] + [vmem()] * 9,
+        out_specs=(vmem(),) * 2,
         scratch_shapes=[
             pltpu.VMEM((padded, width + LANES), jnp.bfloat16),
             pltpu.VMEM((padded, 2 * hidden), jnp.bfloat16),
-            pltpu.SemaphoreType.DMA((6,)),
         ],
         compiler_params=pltpu.CompilerParams(vmem_limit_bytes=24 * MIB),
         cost_estimate=expert_cost(height, width, hidden),
         name="near_rows",
-    )(group, *rows, far, near_z, wg1, wu1, *[stay(w) for w in (wg0, wu0, wd0, wd1)])
+    )(group, *rows, far, near_z, w0, w1, down)
 
 
 def piece_kernel(groups, count, group_ref, *refs):
@@ -776,15 +790,17 @@
     state, far_rows, last_rows = norm_rows(own_state, got, pack, gain_in[None, :], far)
     rows = join_rows((far_rows, last_rows), (0, 0), LATE, "own_rows")
     z_rows = swap_z((far_rows,) * 3)
+    nearest, partner_weights = barrier(z_rows[0], partner_weights)
+    kept = merge_weights(weights, partner_weights)
+    far_rows, kept = barrier(z_rows[1:], kept)
+    z_rows = (nearest,) + far_rows
     onward_plane = join_rows(z_rows, (0, 0, 0), LATE, "onward_plane")
     plane_rows, far_pieces = barrier(swap_plane((rows,) * 3), onward_plane)
     plane_rows = (rows,) + plane_rows
     onward_z = join_rows(plane_rows, (far,) * 4, None, "onward_z")
     z_pieces = swap_z((onward_z,) * 3)
     plane_pieces = swap_plane((onward_plane,) * 3)
-    near, near_part, *kept = near_rows(
-        groups, group, plane_rows, far_pieces, z_pieces[0], weights, partner_weights
-    )
+    near, near_part = near_rows(groups, group, plane_rows, far_pieces, z_pieces[0], *kept)
     parts = piece_rows(groups, group, z_pieces[1:] + plane_pieces, *kept)
     z_parts, plane_parts = swap_z((near_part,) + parts[:2]), swap_plane(parts[2:])
     first = first_sum(near, z_parts[0], half)

time: 75.3 us -> 75.4 us (level)
    pallas_call x0 -> x1, Pallas kernels: none -> 3.79 us  [merge_weights(): pl.pallas_call(merge_kernel, out_shape=(jax.ShapeDtypeStruct((width, 2 *...]
    pallas_call x1, Pallas kernels: 5.93 us -> 2.57 us  [near_rows(): pl.pallas_call(functools.partial(near_kernel, groups), out_shape=(jax.Sha...]
  transfers between devices with their start and end apart: 28 -> 28, of which waited for: 10 -> 10; matrix products, arithmetic and copies ran while one was open for 0% -> 0% of each run, Pallas kernels for 22% -> 23%
where the time goes in v9:
time: 75.4 us; the launch traced here: 75.2 us
  starting transfers between devices  36.9 us (49%)
  waiting for transfers between devices  20.1 us (27%)
  Pallas kernels  18 us (24%)
    ppermute x28, starting transfers between devices, swap(): return lax.ppermute(value, ALL, pairs)  36.9 us
    ppermute x28, waiting for transfers between devices, swap(): return lax.ppermute(value, ALL, pairs)  20.1 us
    pallas_call x1, Pallas kernels, merge_weights(): pl.pallas_call(merge_kernel, out_shape=(jax.ShapeDtypeStruct((width, 2 *...  3.79 us
    pallas_call x1, Pallas kernels, other_terms(): pl.pallas_call(other_kernel, out_shape=(jax.ShapeDtypeStruct((half, w_out...  3.76 us
    pallas_call x1, Pallas kernels, own_terms(): pl.pallas_call(own_kernel, out_shape=(jax.ShapeDtypeStruct((half, width),...  3.51 us
    pallas_call x1, Pallas kernels, piece_rows(): pl.pallas_call(functools.partial(piece_kernel, groups, count), out_shape=...  3.04 us
    pallas_call x1, Pallas kernels, near_rows(): pl.pallas_call(functools.partial(near_kernel, groups), out_shape=(jax.Sha...  2.57 us
  transfers between devices with their start and end apart: 28, of which 10 were waited for; matrix products, arithmetic and copies ran while one was open for 0% of the time, Pallas kernels for 23%

profile of v9, /device:TPU:0, one launch (start us, length us, event | category | flops | bytes accessed | tf_op | source)
XLA Modules:
  0.0 75.2 jit_solution(756075849796081055)
XLA Ops:
  1.0 3.8 %other_terms.1 = (bf16[32,2048]{1,0:T(8,128)(2,1)S(1)}, bf16[64,1024]{1,0:T(8,128)(2,1)S(1)}, bf16[64,512]{1,0:T(8,128)(2,1)S(1)}, bf16[4,128,512]{2,1,0:T(8,128)(2,1)S(1)}, bf16[1024,2048]{1,0:T(8,128)(2,1)S(1)}) custom-call(s32[4,9]{1,0:T(4,128)} %bitcast.18, s32[9]{0:T(128)} %lengths_ref.3, s32[1]{0:T(128)} %bitcast.2.tp_ref, s32[1]{0:T(128)} %bitcast.group_ref, ...), custom_call_target="tpu_custom_call" | custom-call | tf_op jit(solution)/shard_map/other_terms/pallas_call | solution.py:351
  4.7 2.5 %collective-permute-start = (bf16[32,2048]{1,0:T(8,128)(2,1)S(1)}, bf16[32,2048]{1,0:T(8,128)(2,1)S(1)}, u32[]{:S(2)}, u32[]{:S(2)}) collective-permute-start(bf16[32,2048]{1,0:T(8,128)(2,1)S(1)} %get-tuple-element.68), channel_id=1, source_target_pairs={{0,1},{1,0},{2,3},{3,2},{4,5},{5,4},{6,7},{7,6},{8,9},{9,8},{10,11... | collective-permute-start | bytes 393224 | tf_op jit(solution)/shard_map/ppermute | solution.py:754
  7.3 3.5 %own_terms.1 = (f32[32,2048]{1,0:T(8,128)S(1)}, bf16[32,128]{1,0:T(8,128)(2,1)S(1)}, f32[1,2048]{1,0:T(1,128)S(1)}) custom-call(s32[4,9]{1,0:T(4,128)} %bitcast.19, s32[9]{0:T(128)} %lengths_ref.3, s32[1]{0:T(128)} %bitcast.2.tp_ref, s32[16]{0:T(128)} %home_ref.1, bf16[64,1024]{1,0:T(8,128)(2,1)S(1)} %get-tuple-element.63.q_ref, ...), custom_call_target="tpu_custom_call" | custom-call | tf_op jit(solution)/shard_map/own_terms/pallas_call | solution.py:403
  10.8 0.6 collective-permute-done.got_ref
  11.6 1.9 %collective-permute-start.7 = (bf16[24,2176]{1,0:T(8,128)(2,1)S(1)}, bf16[24,2176]{1,0:T(8,128)(2,1)S(1)}, u32[]{:S(2)}, u32[]{:S(2)}) collective-permute-start(bf16[24,2176]{1,0:T(8,128)(2,1)S(1)} %get-tuple-element.71.refs_0_), channel_id=1, source_target_pairs={{0,8},{1,9},{2,10},{3,11},{4,12},{5,13},{6,14},{7,15},{8,0},{9,1},... | collective-permute-start | bytes 313352 | tf_op jit(solution)/shard_map/ppermute | solution.py:754
  13.5 2.6 %collective-permute-start.8 = (bf16[24,2176]{1,0:T(8,128)(2,1)S(1)}, bf16[24,2176]{1,0:T(8,128)(2,1)S(1)}, u32[]{:S(2)}, u32[]{:S(2)}) collective-permute-start(bf16[24,2176]{1,0:T(8,128)(2,1)S(1)} %get-tuple-element.71.refs_0_), channel_id=1, source_target_pairs={{0,16},{1,17},{2,18},{3,19},{4,20},{5,21},{6,22},{7,23},{8,24},{9,... | collective-permute-start | bytes 313352 | tf_op jit(solution)/shard_map/ppermute | solution.py:754
  16.1 2.7 %collective-permute-start.4 = (bf16[32,2176]{1,0:T(8,128)(2,1)S(1)}, bf16[32,2176]{1,0:T(8,128)(2,1)S(1)}, u32[]{:S(2)}, u32[]{:S(2)}) collective-permute-start(bf16[32,2176]{1,0:T(8,128)(2,1)S(1)} %own_rows.1.refs_0_.r0), channel_id=1, source_target_pairs={{0,5},{1,4},{2,7},{3,6},{4,1},{5,0},{6,3},{7,2},{8,13},{9,12},{10,... | collective-permute-start | bytes 417800 | tf_op jit(solution)/shard_map/ppermute | solution.py:754
  18.9 0.5 collective-permute-start.5
  19.7 3.8 %merge_weights.1 = (bf16[2048,768]{1,0:T(8,128)(2,1)S(1)}, bf16[2048,768]{1,0:T(8,128)(2,1)S(1)}, bf16[768,2048]{1,0:T(8,128)(2,1)S(1)}) custom-call(bf16[2048,384]{1,0:T(8,128)(2,1)} %copy-done.1, bf16[2048,384]{1,0:T(8,128)(2,1)} %copy-done.2, bf16[2048,384]{1,0:T(8,128)(2,1)} %bitcast.12, bf16[2048,384]{1,0:T(8,128)(2,1)} %bitcast.14, ...), custom_call_target="tpu_custom_call" | custom-call | bytes 18874368 | tf_op jit(solution)/shard_map/merge_weights/pallas_call | solution.py:535
  23.5 0.8 %collective-permute-done.8.refs_1_ = bf16[24,2176]{1,0:T(8,128)(2,1)S(1)} collective-permute-done((bf16[24,2176]{1,0:T(8,128)(2,1)S(1)}, bf16[24,2176]{1,0:T(8,128)(2,1)S(1)}, u32[]{:S(2)}, u32[]{:S(2)}) %collective-permute-start.8) | collective-permute-done | bytes 104480 | tf_op jit(solution)/shard_map/ppermute | solution.py:754
  24.3 0.6 collective-permute-done.5.refs_2_.r2
  24.9 1.2 %collective-permute-start.10 = (bf16[32,2176]{1,0:T(8,128)(2,1)S(1)}, bf16[32,2176]{1,0:T(8,128)(2,1)S(1)}, u32[]{:S(2)}, u32[]{:S(2)}) collective-permute-start(bf16[32,2176]{1,0:T(8,128)(2,1)S(1)} %onward_z.1), channel_id=1, source_target_pairs={{0,8},{1,9},{2,10},{3,11},{4,12},{5,13},{6,14},{7,15},{8,0},{9,1},... | collective-permute-start | bytes 417800 | tf_op jit(solution)/shard_map/ppermute | solution.py:754
  26.1 2.4 %collective-permute-start.13 = (bf16[72,2176]{1,0:T(8,128)(2,1)S(1)}, bf16[72,2176]{1,0:T(8,128)(2,1)S(1)}, u32[]{:S(2)}, u32[]{:S(2)}) collective-permute-start(bf16[72,2176]{1,0:T(8,128)(2,1)S(1)} %onward_plane.1.far_ref), channel_id=1, source_target_pairs={{0,5},{1,4},{2,7},{3,6},{4,1},{5,0},{6,3},{7,2},{8,13},{9,12},{10,... | collective-permute-start | bytes 940040 | tf_op jit(solution)/shard_map/ppermute | solution.py:754
  29.6 3.0 %collective-permute-start.11 = (bf16[32,2176]{1,0:T(8,128)(2,1)S(1)}, bf16[32,2176]{1,0:T(8,128)(2,1)S(1)}, u32[]{:S(2)}, u32[]{:S(2)}) collective-permute-start(bf16[32,2176]{1,0:T(8,128)(2,1)S(1)} %onward_z.1), channel_id=1, source_target_pairs={{0,16},{1,17},{2,18},{3,19},{4,20},{5,21},{6,22},{7,23},{8,24},{9,... | collective-permute-start | bytes 417800 | tf_op jit(solution)/shard_map/ppermute | solution.py:754
  32.6 2.1 %collective-permute-start.12 = (bf16[32,2176]{1,0:T(8,128)(2,1)S(1)}, bf16[32,2176]{1,0:T(8,128)(2,1)S(1)}, u32[]{:S(2)}, u32[]{:S(2)}) collective-permute-start(bf16[32,2176]{1,0:T(8,128)(2,1)S(1)} %onward_z.1), channel_id=1, source_target_pairs={{0,24},{1,25},{2,26},{3,27},{4,28},{5,29},{6,30},{7,31},{8,16},{9,... | collective-permute-start | bytes 417800 | tf_op jit(solution)/shard_map/ppermute | solution.py:754
  34.7 2.6 %near_rows.1 = (f32[200,2048]{1,0:T(8,128)S(1)}, bf16[32,2048]{1,0:T(8,128)(2,1)S(1)}) custom-call(s32[1]{0:T(128)} %bitcast.group_ref, bf16[32,2176]{1,0:T(8,128)(2,1)S(1)} %own_rows.1.refs_0_.r0, bf16[32,2176]{1,0:T(8,128)(2,1)S(1)} %collective-permute-done.4.refs_1_.r1, bf16[32,2176]{1,0:T(8,128)(2,1)S(1)} %collective-permute-done.5.refs_2_.r2, ...), custom_call_target="tpu_custom_call" | custom-call | flops 1887436800 | bytes 9437184 | tf_op jit(solution)/shard_map/near_rows/pallas_call | solution.py:579
  37.2 4.2 %collective-permute-done.11.refs_0_ = bf16[32,2176]{1,0:T(8,128)(2,1)S(1)} collective-permute-done((bf16[32,2176]{1,0:T(8,128)(2,1)S(1)}, bf16[32,2176]{1,0:T(8,128)(2,1)S(1)}, u32[]{:S(2)}, u32[]{:S(2)}) %collective-permute-start.11) | collective-permute-done | bytes 139296 | tf_op jit(solution)/shard_map/ppermute | solution.py:754
  41.8 3.0 %piece_rows.1 = (bf16[32,2048]{1,0:T(8,128)(2,1)S(1)}, bf16[32,2048]{1,0:T(8,128)(2,1)S(1)}, bf16[72,2048]{1,0:T(8,128)(2,1)S(1)}, bf16[72,2048]{1,0:T(8,128)(2,1)S(1)}, bf16[72,2048]{1,0:T(8,128)(2,1)S(1)}) custom-call(s32[1]{0:T(128)} %bitcast.group_ref, bf16[32,2176]{1,0:T(8,128)(2,1)S(1)} %collective-permute-done.11.refs_0_, ...), custom_call_target="tpu_custom_call" | custom-call | flops 2642411520 | bytes 9437184 | tf_op jit(solution)/shard_map/piece_rows/pallas_call | solution.py:616
  44.8 2.4 %collective-permute-start.16 = (bf16[72,2048]{1,0:T(8,128)(2,1)S(1)}, bf16[72,2048]{1,0:T(8,128)(2,1)S(1)}, u32[]{:S(2)}, u32[]{:S(2)}) collective-permute-start(bf16[72,2048]{1,0:T(8,128)(2,1)S(1)} %get-tuple-element.93), channel_id=1, source_target_pairs={{0,5},{1,4},{2,7},{3,6},{4,1},{5,0},{6,3},{7,2},{8,13},{9,12},{10,... | collective-permute-start | bytes 884744 | tf_op jit(solution)/shard_map/ppermute | solution.py:754
  47.8 0.6 collective-permute-start.18
  48.4 2.9 %collective-permute-start.20 = (bf16[32,2048]{1,0:T(8,128)(2,1)S(1)}, bf16[32,2048]{1,0:T(8,128)(2,1)S(1)}, u32[]{:S(2)}, u32[]{:S(2)}) collective-permute-start(bf16[32,2048]{1,0:T(8,128)(2,1)S(1)} %get-tuple-element.98), channel_id=1, source_target_pairs={{0,16},{1,17},{2,18},{3,19},{4,20},{5,21},{6,22},{7,23},{8,24},{9,... | collective-permute-start | bytes 393224 | tf_op jit(solution)/shard_map/ppermute | solution.py:754
  51.3 1.2 %collective-permute-start.21 = (bf16[32,2048]{1,0:T(8,128)(2,1)S(1)}, bf16[32,2048]{1,0:T(8,128)(2,1)S(1)}, u32[]{:S(2)}, u32[]{:S(2)}) collective-permute-start(bf16[32,2048]{1,0:T(8,128)(2,1)S(1)} %get-tuple-element.99), channel_id=1, source_target_pairs={{0,24},{1,25},{2,26},{3,27},{4,28},{5,29},{6,30},{7,31},{8,16},{9,... | collective-permute-start | bytes 393224 | tf_op jit(solution)/shard_map/ppermute | solution.py:754
  52.5 3.2 %collective-permute-done.16.g1 = bf16[72,2048]{1,0:T(8,128)(2,1)S(1)} collective-permute-done((bf16[72,2048]{1,0:T(8,128)(2,1)S(1)}, bf16[72,2048]{1,0:T(8,128)(2,1)S(1)}, u32[]{:S(2)}, u32[]{:S(2)}) %collective-permute-start.16) | collective-permute-done | bytes 294944 | tf_op jit(solution)/shard_map/ppermute | solution.py:754
  55.7 5.3 %collective-permute-done.17.g2 = bf16[72,2048]{1,0:T(8,128)(2,1)S(1)} collective-permute-done((bf16[72,2048]{1,0:T(8,128)(2,1)S(1)}, bf16[72,2048]{1,0:T(8,128)(2,1)S(1)}, u32[]{:S(2)}, u32[]{:S(2)}) %collective-permute-start.17) | collective-permute-done | bytes 294944 | tf_op jit(solution)/shard_map/ppermute | solution.py:754
  61.2 1.7 %collective-permute-start.25 = (bf16[24,2048]{1,0:T(8,128)(2,1)S(1)}, bf16[24,2048]{1,0:T(8,128)(2,1)S(1)}, u32[]{:S(2)}, u32[]{:S(2)}) collective-permute-start(bf16[24,2048]{1,0:T(8,128)(2,1)S(1)} %get-tuple-element.113), channel_id=1, source_target_pairs={{0,8},{1,9},{2,10},{3,11},{4,12},{5,13},{6,14},{7,15},{8,0},{9,1},... | collective-permute-start | bytes 294920 | tf_op jit(solution)/shard_map/ppermute | solution.py:754
  62.9 1.6 %collective-permute-start.26 = (bf16[24,2048]{1,0:T(8,128)(2,1)S(1)}, bf16[24,2048]{1,0:T(8,128)(2,1)S(1)}, u32[]{:S(2)}, u32[]{:S(2)}) collective-permute-start(bf16[24,2048]{1,0:T(8,128)(2,1)S(1)} %get-tuple-element.114), channel_id=1, source_target_pairs={{0,16},{1,17},{2,18},{3,19},{4,20},{5,21},{6,22},{7,23},{8,24},{9,... | collective-permute-start | bytes 294920 | tf_op jit(solution)/shard_map/ppermute | solution.py:754
  64.5 1.1 %collective-permute-start.27 = (bf16[24,2048]{1,0:T(8,128)(2,1)S(1)}, bf16[24,2048]{1,0:T(8,128)(2,1)S(1)}, u32[]{:S(2)}, u32[]{:S(2)}) collective-permute-start(bf16[24,2048]{1,0:T(8,128)(2,1)S(1)} %get-tuple-element.115), channel_id=1, source_target_pairs={{0,24},{1,25},{2,26},{3,27},{4,28},{5,29},{6,30},{7,31},{8,16},{9,... | collective-permute-start | bytes 294920 | tf_op jit(solution)/shard_map/ppermute | solution.py:754
  65.7 2.4 %collective-permute-start.22 = (bf16[32,2048]{1,0:T(8,128)(2,1)S(1)}, bf16[32,2048]{1,0:T(8,128)(2,1)S(1)}, u32[]{:S(2)}, u32[]{:S(2)}) collective-permute-start(bf16[32,2048]{1,0:T(8,128)(2,1)S(1)} %get-tuple-element.108), channel_id=1, source_target_pairs={{0,5},{1,4},{2,7},{3,6},{4,1},{5,0},{6,3},{7,2},{8,13},{9,12},{10,... | collective-permute-start | bytes 393224 | tf_op jit(solution)/shard_map/ppermute | solution.py:754
  68.7 0.6 collective-permute-start.24
  69.3 4.1 %collective-permute-done.26.z2 = bf16[24,2048]{1,0:T(8,128)(2,1)S(1)} collective-permute-done((bf16[24,2048]{1,0:T(8,128)(2,1)S(1)}, bf16[24,2048]{1,0:T(8,128)(2,1)S(1)}, u32[]{:S(2)}, u32[]{:S(2)}) %collective-permute-start.26) | collective-permute-done | bytes 98336 | tf_op jit(solution)/shard_map/ppermute | solution.py:754
  73.4 0.8 %collective-permute-done.23.p2 = bf16[32,2048]{1,0:T(8,128)(2,1)S(1)} collective-permute-done((bf16[32,2048]{1,0:T(8,128)(2,1)S(1)}, bf16[32,2048]{1,0:T(8,128)(2,1)S(1)}, u32[]{:S(2)}, u32[]{:S(2)}) %collective-permute-start.23) | collective-permute-done | bytes 131104 | tf_op jit(solution)/shard_map/ppermute | solution.py:754
  74.3 0.8 %final_rows.1 = bf16[32,2048]{1,0:T(8,128)(2,1)} custom-call(f32[32,2048]{1,0:T(8,128)S(1)} %total_rows.1.total_ref, bf16[32,2048]{1,0:T(8,128)(2,1)S(1)} %collective-permute-done.22.p1, bf16[32,2048]{1,0:T(8,128)(2,1)S(1)} %collective-permute-done.23.p2, bf16[32,2048]{1,0:T(8,128)(2,1)S(1)} %collective-permute-done.24.p3, ...), custom_call_target="tpu_custom_call" | custom-call | tf_op jit(solution)/shard_map/final_rows/pallas_call | solution.py:732
  (44 shorter events, 4.3 us)
Async XLA Ops:
  0.0 11.5 %collective-permute-start.1 = (bf16[2048,384]{1,0:T(8,128)(2,1)}, bf16[2048,384]{1,0:T(8,128)(2,1)S(1)}, u32[]{:S(2)}, u32[]{:S(2)}) collective-permute-start(bf16[2048,384]{1,0:T(8,128)(2,1)} %bitcast.11), channel_id=1, source_target_pairs={{0,2},{1,3},{2,0},{3,1},{4,6},{5,7},{6,4},{7,5},{8,10},{9,11},{10,... | collective-permute-start | bytes 4718600 | tf_op jit(solution)/shard_map/ppermute | solution.py:754
  0.5 11.0 %collective-permute-start.2 = (bf16[2048,384]{1,0:T(8,128)(2,1)}, bf16[2048,384]{1,0:T(8,128)(2,1)S(1)}, u32[]{:S(2)}, u32[]{:S(2)}) collective-permute-start(bf16[2048,384]{1,0:T(8,128)(2,1)} %bitcast.13), channel_id=1, source_target_pairs={{0,2},{1,3},{2,0},{3,1},{4,6},{5,7},{6,4},{7,5},{8,10},{9,11},{10,... | collective-permute-start | bytes 4718600 | tf_op jit(solution)/shard_map/ppermute | solution.py:754
  0.5 11.0 %collective-permute-start.3 = (bf16[384,2048]{1,0:T(8,128)(2,1)}, bf16[384,2048]{1,0:T(8,128)(2,1)}, u32[]{:S(2)}, u32[]{:S(2)}) collective-permute-start(bf16[384,2048]{1,0:T(8,128)(2,1)} %bitcast.15), channel_id=1, source_target_pairs={{0,2},{1,3},{2,0},{3,1},{4,6},{5,7},{6,4},{7,5},{8,10},{9,11},{10,... | collective-permute-start | bytes 4718600 | tf_op jit(solution)/shard_map/ppermute | solution.py:754
  4.7 6.7 %collective-permute-start = (bf16[32,2048]{1,0:T(8,128)(2,1)S(1)}, bf16[32,2048]{1,0:T(8,128)(2,1)S(1)}, u32[]{:S(2)}, u32[]{:S(2)}) collective-permute-start(bf16[32,2048]{1,0:T(8,128)(2,1)S(1)} %get-tuple-element.68), channel_id=1, source_target_pairs={{0,1},{1,0},{2,3},{3,2},{4,5},{5,4},{6,7},{7,6},{8,9},{9,8},{10,11... | collective-permute-start | bytes 393224 | tf_op jit(solution)/shard_map/ppermute | solution.py:754
  7.3 4.2 %copy-start = (f32[2048]{0:T(1024)S(1)}, f32[2048]{0:T(1024)}, u32[]{:S(2)}) copy-start(f32[2048]{0:T(1024)} %param.22) | copy-start | bytes 24580
  11.5 4.7 %copy-start.1 = (bf16[2048,384]{1,0:T(8,128)(2,1)}, bf16[2048,384]{1,0:T(8,128)(2,1)S(1)}, u32[]{:S(2)}) copy-start(bf16[2048,384]{1,0:T(8,128)(2,1)S(1)} %collective-permute-done.1.wg1) | copy-start | bytes 4718596
  11.5 4.7 %copy-start.2 = (bf16[2048,384]{1,0:T(8,128)(2,1)}, bf16[2048,384]{1,0:T(8,128)(2,1)S(1)}, u32[]{:S(2)}) copy-start(bf16[2048,384]{1,0:T(8,128)(2,1)S(1)} %collective-permute-done.2.wu1) | copy-start | bytes 4718596
  11.6 7.8 %collective-permute-start.7 = (bf16[24,2176]{1,0:T(8,128)(2,1)S(1)}, bf16[24,2176]{1,0:T(8,128)(2,1)S(1)}, u32[]{:S(2)}, u32[]{:S(2)}) collective-permute-start(bf16[24,2176]{1,0:T(8,128)(2,1)S(1)} %get-tuple-element.71.refs_0_), channel_id=1, source_target_pairs={{0,8},{1,9},{2,10},{3,11},{4,12},{5,13},{6,14},{7,15},{8,0},{9,1},... | collective-permute-start | bytes 313352 | tf_op jit(solution)/shard_map/ppermute | solution.py:754
  13.5 10.8 %collective-permute-start.8 = (bf16[24,2176]{1,0:T(8,128)(2,1)S(1)}, bf16[24,2176]{1,0:T(8,128)(2,1)S(1)}, u32[]{:S(2)}, u32[]{:S(2)}) collective-permute-start(bf16[24,2176]{1,0:T(8,128)(2,1)S(1)} %get-tuple-element.71.refs_0_), channel_id=1, source_target_pairs={{0,16},{1,17},{2,18},{3,19},{4,20},{5,21},{6,22},{7,23},{8,24},{9,... | collective-permute-start | bytes 313352 | tf_op jit(solution)/shard_map/ppermute | solution.py:754
  16.1 8.2 %collective-permute-start.9 = (bf16[24,2176]{1,0:T(8,128)(2,1)S(1)}, bf16[24,2176]{1,0:T(8,128)(2,1)S(1)}, u32[]{:S(2)}, u32[]{:S(2)}) collective-permute-start(bf16[24,2176]{1,0:T(8,128)(2,1)S(1)} %get-tuple-element.71.refs_0_), channel_id=1, source_target_pairs={{0,24},{1,25},{2,26},{3,27},{4,28},{5,29},{6,30},{7,31},{8,16},{9,... | collective-permute-start | bytes 313352 | tf_op jit(solution)/shard_map/ppermute | solution.py:754
  16.1 8.2 %collective-permute-start.4 = (bf16[32,2176]{1,0:T(8,128)(2,1)S(1)}, bf16[32,2176]{1,0:T(8,128)(2,1)S(1)}, u32[]{:S(2)}, u32[]{:S(2)}) collective-permute-start(bf16[32,2176]{1,0:T(8,128)(2,1)S(1)} %own_rows.1.refs_0_.r0), channel_id=1, source_target_pairs={{0,5},{1,4},{2,7},{3,6},{4,1},{5,0},{6,3},{7,2},{8,13},{9,12},{10,... | collective-permute-start | bytes 417800 | tf_op jit(solution)/shard_map/ppermute | solution.py:754
  18.9 6.0 %collective-permute-start.5 = (bf16[32,2176]{1,0:T(8,128)(2,1)S(1)}, bf16[32,2176]{1,0:T(8,128)(2,1)S(1)}, u32[]{:S(2)}, u32[]{:S(2)}) collective-permute-start(bf16[32,2176]{1,0:T(8,128)(2,1)S(1)} %own_rows.1.refs_0_.r0), channel_id=1, source_target_pairs={{0,1},{1,0},{2,3},{3,2},{4,5},{5,4},{6,7},{7,6},{8,9},{9,8},{10,11... | collective-permute-start | bytes 417800 | tf_op jit(solution)/shard_map/ppermute | solution.py:754
  19.4 5.5 %collective-permute-start.6 = (bf16[32,2176]{1,0:T(8,128)(2,1)S(1)}, bf16[32,2176]{1,0:T(8,128)(2,1)S(1)}, u32[]{:S(2)}, u32[]{:S(2)}) collective-permute-start(bf16[32,2176]{1,0:T(8,128)(2,1)S(1)} %own_rows.1.refs_0_.r0), channel_id=1, source_target_pairs={{0,4},{1,5},{2,6},{3,7},{4,0},{5,1},{6,2},{7,3},{8,12},{9,13},{10,... | collective-permute-start | bytes 417800 | tf_op jit(solution)/shard_map/ppermute | solution.py:754
  24.9 7.7 %collective-permute-start.10 = (bf16[32,2176]{1,0:T(8,128)(2,1)S(1)}, bf16[32,2176]{1,0:T(8,128)(2,1)S(1)}, u32[]{:S(2)}, u32[]{:S(2)}) collective-permute-start(bf16[32,2176]{1,0:T(8,128)(2,1)S(1)} %onward_z.1), channel_id=1, source_target_pairs={{0,8},{1,9},{2,10},{3,11},{4,12},{5,13},{6,14},{7,15},{8,0},{9,1},... | collective-permute-start | bytes 417800 | tf_op jit(solution)/shard_map/ppermute | solution.py:754
  26.1 15.3 %collective-permute-start.13 = (bf16[72,2176]{1,0:T(8,128)(2,1)S(1)}, bf16[72,2176]{1,0:T(8,128)(2,1)S(1)}, u32[]{:S(2)}, u32[]{:S(2)}) collective-permute-start(bf16[72,2176]{1,0:T(8,128)(2,1)S(1)} %onward_plane.1.far_ref), channel_id=1, source_target_pairs={{0,5},{1,4},{2,7},{3,6},{4,1},{5,0},{6,3},{7,2},{8,13},{9,12},{10,... | collective-permute-start | bytes 940040 | tf_op jit(solution)/shard_map/ppermute | solution.py:754
  28.6 13.2 %collective-permute-start.14 = (bf16[72,2176]{1,0:T(8,128)(2,1)S(1)}, bf16[72,2176]{1,0:T(8,128)(2,1)S(1)}, u32[]{:S(2)}, u32[]{:S(2)}) collective-permute-start(bf16[72,2176]{1,0:T(8,128)(2,1)S(1)} %onward_plane.1.far_ref), channel_id=1, source_target_pairs={{0,1},{1,0},{2,3},{3,2},{4,5},{5,4},{6,7},{7,6},{8,9},{9,8},{10,11... | collective-permute-start | bytes 940040 | tf_op jit(solution)/shard_map/ppermute | solution.py:754
  29.1 12.6 %collective-permute-start.15 = (bf16[72,2176]{1,0:T(8,128)(2,1)S(1)}, bf16[72,2176]{1,0:T(8,128)(2,1)S(1)}, u32[]{:S(2)}, u32[]{:S(2)}) collective-permute-start(bf16[72,2176]{1,0:T(8,128)(2,1)S(1)} %onward_plane.1.far_ref), channel_id=1, source_target_pairs={{0,4},{1,5},{2,6},{3,7},{4,0},{5,1},{6,2},{7,3},{8,12},{9,13},{10,... | collective-permute-start | bytes 940040 | tf_op jit(solution)/shard_map/ppermute | solution.py:754
  29.6 11.8 %collective-permute-start.11 = (bf16[32,2176]{1,0:T(8,128)(2,1)S(1)}, bf16[32,2176]{1,0:T(8,128)(2,1)S(1)}, u32[]{:S(2)}, u32[]{:S(2)}) collective-permute-start(bf16[32,2176]{1,0:T(8,128)(2,1)S(1)} %onward_z.1), channel_id=1, source_target_pairs={{0,16},{1,17},{2,18},{3,19},{4,20},{5,21},{6,22},{7,23},{8,24},{9,... | collective-permute-start | bytes 417800 | tf_op jit(solution)/shard_map/ppermute | solution.py:754
  32.6 8.8 %collective-permute-start.12 = (bf16[32,2176]{1,0:T(8,128)(2,1)S(1)}, bf16[32,2176]{1,0:T(8,128)(2,1)S(1)}, u32[]{:S(2)}, u32[]{:S(2)}) collective-permute-start(bf16[32,2176]{1,0:T(8,128)(2,1)S(1)} %onward_z.1), channel_id=1, source_target_pairs={{0,24},{1,25},{2,26},{3,27},{4,28},{5,29},{6,30},{7,31},{8,16},{9,... | collective-permute-start | bytes 417800 | tf_op jit(solution)/shard_map/ppermute | solution.py:754
  41.4 9.8 %collective-permute-start.19 = (bf16[32,2048]{1,0:T(8,128)(2,1)S(1)}, bf16[32,2048]{1,0:T(8,128)(2,1)S(1)}, u32[]{:S(2)}, u32[]{:S(2)}) collective-permute-start(bf16[32,2048]{1,0:T(8,128)(2,1)S(1)} %get-tuple-element.96), channel_id=1, source_target_pairs={{0,8},{1,9},{2,10},{3,11},{4,12},{5,13},{6,14},{7,15},{8,0},{9,1},... | collective-permute-start | bytes 393224 | tf_op jit(solution)/shard_map/ppermute | solution.py:754
  44.8 10.9 %collective-permute-start.16 = (bf16[72,2048]{1,0:T(8,128)(2,1)S(1)}, bf16[72,2048]{1,0:T(8,128)(2,1)S(1)}, u32[]{:S(2)}, u32[]{:S(2)}) collective-permute-start(bf16[72,2048]{1,0:T(8,128)(2,1)S(1)} %get-tuple-element.93), channel_id=1, source_target_pairs={{0,5},{1,4},{2,7},{3,6},{4,1},{5,0},{6,3},{7,2},{8,13},{9,12},{10,... | collective-permute-start | bytes 884744 | tf_op jit(solution)/shard_map/ppermute | solution.py:754
  47.2 13.8 %collective-permute-start.17 = (bf16[72,2048]{1,0:T(8,128)(2,1)S(1)}, bf16[72,2048]{1,0:T(8,128)(2,1)S(1)}, u32[]{:S(2)}, u32[]{:S(2)}) collective-permute-start(bf16[72,2048]{1,0:T(8,128)(2,1)S(1)} %get-tuple-element.94), channel_id=1, source_target_pairs={{0,1},{1,0},{2,3},{3,2},{4,5},{5,4},{6,7},{7,6},{8,9},{9,8},{10,11... | collective-permute-start | bytes 884744 | tf_op jit(solution)/shard_map/ppermute | solution.py:754
  47.8 13.3 %collective-permute-start.18 = (bf16[72,2048]{1,0:T(8,128)(2,1)S(1)}, bf16[72,2048]{1,0:T(8,128)(2,1)S(1)}, u32[]{:S(2)}, u32[]{:S(2)}) collective-permute-start(bf16[72,2048]{1,0:T(8,128)(2,1)S(1)} %get-tuple-element.95), channel_id=1, source_target_pairs={{0,4},{1,5},{2,6},{3,7},{4,0},{5,1},{6,2},{7,3},{8,12},{9,13},{10,... | collective-permute-start | bytes 884744 | tf_op jit(solution)/shard_map/ppermute | solution.py:754
  48.4 12.8 %collective-permute-start.20 = (bf16[32,2048]{1,0:T(8,128)(2,1)S(1)}, bf16[32,2048]{1,0:T(8,128)(2,1)S(1)}, u32[]{:S(2)}, u32[]{:S(2)}) collective-permute-start(bf16[32,2048]{1,0:T(8,128)(2,1)S(1)} %get-tuple-element.98), channel_id=1, source_target_pairs={{0,16},{1,17},{2,18},{3,19},{4,20},{5,21},{6,22},{7,23},{8,24},{9,... | collective-permute-start | bytes 393224 | tf_op jit(solution)/shard_map/ppermute | solution.py:754
  51.3 9.9 %collective-permute-start.21 = (bf16[32,2048]{1,0:T(8,128)(2,1)S(1)}, bf16[32,2048]{1,0:T(8,128)(2,1)S(1)}, u32[]{:S(2)}, u32[]{:S(2)}) collective-permute-start(bf16[32,2048]{1,0:T(8,128)(2,1)S(1)} %get-tuple-element.99), channel_id=1, source_target_pairs={{0,24},{1,25},{2,26},{3,27},{4,28},{5,29},{6,30},{7,31},{8,16},{9,... | collective-permute-start | bytes 393224 | tf_op jit(solution)/shard_map/ppermute | solution.py:754
  61.2 7.5 %collective-permute-start.25 = (bf16[24,2048]{1,0:T(8,128)(2,1)S(1)}, bf16[24,2048]{1,0:T(8,128)(2,1)S(1)}, u32[]{:S(2)}, u32[]{:S(2)}) collective-permute-start(bf16[24,2048]{1,0:T(8,128)(2,1)S(1)} %get-tuple-element.113), channel_id=1, source_target_pairs={{0,8},{1,9},{2,10},{3,11},{4,12},{5,13},{6,14},{7,15},{8,0},{9,1},... | collective-permute-start | bytes 294920 | tf_op jit(solution)/shard_map/ppermute | solution.py:754
  62.9 10.5 %collective-permute-start.26 = (bf16[24,2048]{1,0:T(8,128)(2,1)S(1)}, bf16[24,2048]{1,0:T(8,128)(2,1)S(1)}, u32[]{:S(2)}, u32[]{:S(2)}) collective-permute-start(bf16[24,2048]{1,0:T(8,128)(2,1)S(1)} %get-tuple-element.114), channel_id=1, source_target_pairs={{0,16},{1,17},{2,18},{3,19},{4,20},{5,21},{6,22},{7,23},{8,24},{9,... | collective-permute-start | bytes 294920 | tf_op jit(solution)/shard_map/ppermute | solution.py:754
  64.5 8.8 %collective-permute-start.27 = (bf16[24,2048]{1,0:T(8,128)(2,1)S(1)}, bf16[24,2048]{1,0:T(8,128)(2,1)S(1)}, u32[]{:S(2)}, u32[]{:S(2)}) collective-permute-start(bf16[24,2048]{1,0:T(8,128)(2,1)S(1)} %get-tuple-element.115), channel_id=1, source_target_pairs={{0,24},{1,25},{2,26},{3,27},{4,28},{5,29},{6,30},{7,31},{8,16},{9,... | collective-permute-start | bytes 294920 | tf_op jit(solution)/shard_map/ppermute | solution.py:754
  65.7 7.7 %collective-permute-start.22 = (bf16[32,2048]{1,0:T(8,128)(2,1)S(1)}, bf16[32,2048]{1,0:T(8,128)(2,1)S(1)}, u32[]{:S(2)}, u32[]{:S(2)}) collective-permute-start(bf16[32,2048]{1,0:T(8,128)(2,1)S(1)} %get-tuple-element.108), channel_id=1, source_target_pairs={{0,5},{1,4},{2,7},{3,6},{4,1},{5,0},{6,3},{7,2},{8,13},{9,12},{10,... | collective-permute-start | bytes 393224 | tf_op jit(solution)/shard_map/ppermute | solution.py:754
  68.1 6.2 %collective-permute-start.23 = (bf16[32,2048]{1,0:T(8,128)(2,1)S(1)}, bf16[32,2048]{1,0:T(8,128)(2,1)S(1)}, u32[]{:S(2)}, u32[]{:S(2)}) collective-permute-start(bf16[32,2048]{1,0:T(8,128)(2,1)S(1)} %get-tuple-element.109), channel_id=1, source_target_pairs={{0,1},{1,0},{2,3},{3,2},{4,5},{5,4},{6,7},{7,6},{8,9},{9,8},{10,11... | collective-permute-start | bytes 393224 | tf_op jit(solution)/shard_map/ppermute | solution.py:754
  68.7 5.7 %collective-permute-start.24 = (bf16[32,2048]{1,0:T(8,128)(2,1)S(1)}, bf16[32,2048]{1,0:T(8,128)(2,1)S(1)}, u32[]{:S(2)}, u32[]{:S(2)}) collective-permute-start(bf16[32,2048]{1,0:T(8,128)(2,1)S(1)} %get-tuple-element.110), channel_id=1, source_target_pairs={{0,4},{1,5},{2,6},{3,7},{4,0},{5,1},{6,2},{7,3},{8,12},{9,13},{10,... | collective-permute-start | bytes 393224 | tf_op jit(solution)/shard_map/ppermute | solution.py:754

commit v10 on v8

--- a/solution.py
+++ b/solution.py
@@ -311,7 +311,7 @@
 
 
 OUT_BLOCK = 512
-W_PIECES = 4
+W_PIECES = 8
 
 
 def other_kernel(

time: 75.3 us -> 75.3 us (level)
  no operation moved by 1% of the time
where the time goes in v10:
time: 75.3 us; the launch traced here: 75.1 us
  starting transfers between devices  36.8 us (49%)
  waiting for transfers between devices  20.6 us (27%)
  Pallas kernels  17.5 us (23%)
    ppermute x28, starting transfers between devices, swap(): return lax.ppermute(value, ALL, pairs)  36.8 us
    ppermute x28, waiting for transfers between devices, swap(): return lax.ppermute(value, ALL, pairs)  20.6 us
    pallas_call x1, Pallas kernels, near_rows(): pl.pallas_call(functools.partial(near_kernel, groups), out_shape=(jax.Sha...  5.93 us
    pallas_call x1, Pallas kernels, other_terms(): pl.pallas_call(other_kernel, out_shape=(jax.ShapeDtypeStruct((half, w_out...  3.7 us
    pallas_call x1, Pallas kernels, own_terms(): pl.pallas_call(own_kernel, out_shape=(jax.ShapeDtypeStruct((half, width),...  3.51 us
    pallas_call x1, Pallas kernels, piece_rows(): pl.pallas_call(functools.partial(piece_kernel, groups, count), out_shape=...  3 us
  transfers between devices with their start and end apart: 28, of which 10 were waited for; matrix products, arithmetic and copies ran while one was open for 0% of the time, Pallas kernels for 22%

profile of v10, /device:TPU:0, one launch (start us, length us, event | category | flops | bytes accessed | tf_op | source)
XLA Modules:
  0.0 75.1 jit_solution(18080369297236606184)
XLA Ops:
  1.0 3.7 %other_terms.1 = (bf16[32,2048]{1,0:T(8,128)(2,1)S(1)}, bf16[64,1024]{1,0:T(8,128)(2,1)S(1)}, bf16[64,512]{1,0:T(8,128)(2,1)S(1)}, bf16[4,128,512]{2,1,0:T(8,128)(2,1)S(1)}, bf16[1024,2048]{1,0:T(8,128)(2,1)S(1)}) custom-call(s32[4,9]{1,0:T(4,128)} %bitcast.18, s32[9]{0:T(128)} %lengths_ref.3, s32[1]{0:T(128)} %bitcast.2.tp_ref, s32[1]{0:T(128)} %bitcast.group_ref, ...), custom_call_target="tpu_custom_call" | custom-call | tf_op jit(solution)/shard_map/other_terms/pallas_call | solution.py:351
  4.7 2.5 %collective-permute-start = (bf16[32,2048]{1,0:T(8,128)(2,1)S(1)}, bf16[32,2048]{1,0:T(8,128)(2,1)S(1)}, u32[]{:S(2)}, u32[]{:S(2)}) collective-permute-start(bf16[32,2048]{1,0:T(8,128)(2,1)S(1)} %get-tuple-element.59), channel_id=1, source_target_pairs={{0,1},{1,0},{2,3},{3,2},{4,5},{5,4},{6,7},{7,6},{8,9},{9,8},{10,11... | collective-permute-start | bytes 393224 | tf_op jit(solution)/shard_map/ppermute | solution.py:740
  7.2 3.5 %own_terms.1 = (f32[32,2048]{1,0:T(8,128)S(1)}, bf16[32,128]{1,0:T(8,128)(2,1)S(1)}, f32[1,2048]{1,0:T(1,128)S(1)}) custom-call(s32[4,9]{1,0:T(4,128)} %bitcast.19, s32[9]{0:T(128)} %lengths_ref.3, s32[1]{0:T(128)} %bitcast.2.tp_ref, s32[16]{0:T(128)} %home_ref.1, bf16[64,1024]{1,0:T(8,128)(2,1)S(1)} %get-tuple-element.54.q_ref, ...), custom_call_target="tpu_custom_call" | custom-call | tf_op jit(solution)/shard_map/own_terms/pallas_call | solution.py:403
  10.7 0.6 collective-permute-done.got_ref
  11.6 1.9 %collective-permute-start.7 = (bf16[24,2176]{1,0:T(8,128)(2,1)S(1)}, bf16[24,2176]{1,0:T(8,128)(2,1)S(1)}, u32[]{:S(2)}, u32[]{:S(2)}) collective-permute-start(bf16[24,2176]{1,0:T(8,128)(2,1)S(1)} %get-tuple-element.62.refs_0_), channel_id=1, source_target_pairs={{0,8},{1,9},{2,10},{3,11},{4,12},{5,13},{6,14},{7,15},{8,0},{9,1},... | collective-permute-start | bytes 313352 | tf_op jit(solution)/shard_map/ppermute | solution.py:740
  13.5 2.6 %collective-permute-start.8 = (bf16[24,2176]{1,0:T(8,128)(2,1)S(1)}, bf16[24,2176]{1,0:T(8,128)(2,1)S(1)}, u32[]{:S(2)}, u32[]{:S(2)}) collective-permute-start(bf16[24,2176]{1,0:T(8,128)(2,1)S(1)} %get-tuple-element.62.refs_0_), channel_id=1, source_target_pairs={{0,16},{1,17},{2,18},{3,19},{4,20},{5,21},{6,22},{7,23},{8,24},{9,... | collective-permute-start | bytes 313352 | tf_op jit(solution)/shard_map/ppermute | solution.py:740
  16.1 2.7 %collective-permute-start.4 = (bf16[32,2176]{1,0:T(8,128)(2,1)S(1)}, bf16[32,2176]{1,0:T(8,128)(2,1)S(1)}, u32[]{:S(2)}, u32[]{:S(2)}) collective-permute-start(bf16[32,2176]{1,0:T(8,128)(2,1)S(1)} %own_rows.1.refs_0_.r0), channel_id=1, source_target_pairs={{0,5},{1,4},{2,7},{3,6},{4,1},{5,0},{6,3},{7,2},{8,13},{9,12},{10,... | collective-permute-start | bytes 417800 | tf_op jit(solution)/shard_map/ppermute | solution.py:740
  18.8 0.5 collective-permute-start.5
  19.6 4.6 %collective-permute-done.8.refs_1_ = bf16[24,2176]{1,0:T(8,128)(2,1)S(1)} collective-permute-done((bf16[24,2176]{1,0:T(8,128)(2,1)S(1)}, bf16[24,2176]{1,0:T(8,128)(2,1)S(1)}, u32[]{:S(2)}, u32[]{:S(2)}) %collective-permute-start.8) | collective-permute-done | bytes 104480 | tf_op jit(solution)/shard_map/ppermute | solution.py:740
  24.3 0.5 collective-permute-done.5.refs_2_.r2
  24.9 1.2 %collective-permute-start.10 = (bf16[32,2176]{1,0:T(8,128)(2,1)S(1)}, bf16[32,2176]{1,0:T(8,128)(2,1)S(1)}, u32[]{:S(2)}, u32[]{:S(2)}) collective-permute-start(bf16[32,2176]{1,0:T(8,128)(2,1)S(1)} %onward_z.1), channel_id=1, source_target_pairs={{0,8},{1,9},{2,10},{3,11},{4,12},{5,13},{6,14},{7,15},{8,0},{9,1},... | collective-permute-start | bytes 417800 | tf_op jit(solution)/shard_map/ppermute | solution.py:740
  26.1 2.4 %collective-permute-start.13 = (bf16[72,2176]{1,0:T(8,128)(2,1)S(1)}, bf16[72,2176]{1,0:T(8,128)(2,1)S(1)}, u32[]{:S(2)}, u32[]{:S(2)}) collective-permute-start(bf16[72,2176]{1,0:T(8,128)(2,1)S(1)} %onward_plane.1.far_ref), channel_id=1, source_target_pairs={{0,5},{1,4},{2,7},{3,6},{4,1},{5,0},{6,3},{7,2},{8,13},{9,12},{10,... | collective-permute-start | bytes 940040 | tf_op jit(solution)/shard_map/ppermute | solution.py:740
  28.5 0.5 collective-permute-start.14
  29.6 2.9 %collective-permute-start.11 = (bf16[32,2176]{1,0:T(8,128)(2,1)S(1)}, bf16[32,2176]{1,0:T(8,128)(2,1)S(1)}, u32[]{:S(2)}, u32[]{:S(2)}) collective-permute-start(bf16[32,2176]{1,0:T(8,128)(2,1)S(1)} %onward_z.1), channel_id=1, source_target_pairs={{0,16},{1,17},{2,18},{3,19},{4,20},{5,21},{6,22},{7,23},{8,24},{9,... | collective-permute-start | bytes 417800 | tf_op jit(solution)/shard_map/ppermute | solution.py:740
  32.5 2.0 %collective-permute-start.12 = (bf16[32,2176]{1,0:T(8,128)(2,1)S(1)}, bf16[32,2176]{1,0:T(8,128)(2,1)S(1)}, u32[]{:S(2)}, u32[]{:S(2)}) collective-permute-start(bf16[32,2176]{1,0:T(8,128)(2,1)S(1)} %onward_z.1), channel_id=1, source_target_pairs={{0,24},{1,25},{2,26},{3,27},{4,28},{5,29},{6,30},{7,31},{8,16},{9,... | collective-permute-start | bytes 417800 | tf_op jit(solution)/shard_map/ppermute | solution.py:740
  34.5 5.9 %near_rows.1 = (f32[200,2048]{1,0:T(8,128)S(1)}, bf16[32,2048]{1,0:T(8,128)(2,1)S(1)}, bf16[2048,768]{1,0:T(8,128)(2,1)S(1)}, bf16[2048,768]{1,0:T(8,128)(2,1)S(1)}, bf16[768,2048]{1,0:T(8,128)(2,1)S(1)}) custom-call(s32[1]{0:T(128)} %bitcast.group_ref, bf16[32,2176]{1,0:T(8,128)(2,1)S(1)} %own_rows.1.refs_0_.r0, ...), custom_call_target="tpu_custom_call" | custom-call | flops 1887436800 | bytes 9437184 | tf_op jit(solution)/shard_map/near_rows/pallas_call | solution.py:561
  40.4 0.9 %collective-permute-done.11.refs_0_ = bf16[32,2176]{1,0:T(8,128)(2,1)S(1)} collective-permute-done((bf16[32,2176]{1,0:T(8,128)(2,1)S(1)}, bf16[32,2176]{1,0:T(8,128)(2,1)S(1)}, u32[]{:S(2)}, u32[]{:S(2)}) %collective-permute-start.11) | collective-permute-done | bytes 139296 | tf_op jit(solution)/shard_map/ppermute | solution.py:740
  41.7 3.0 %piece_rows.1 = (bf16[32,2048]{1,0:T(8,128)(2,1)S(1)}, bf16[32,2048]{1,0:T(8,128)(2,1)S(1)}, bf16[72,2048]{1,0:T(8,128)(2,1)S(1)}, bf16[72,2048]{1,0:T(8,128)(2,1)S(1)}, bf16[72,2048]{1,0:T(8,128)(2,1)S(1)}) custom-call(s32[1]{0:T(128)} %bitcast.group_ref, bf16[32,2176]{1,0:T(8,128)(2,1)S(1)} %collective-permute-done.11.refs_0_, ...), custom_call_target="tpu_custom_call" | custom-call | flops 2642411520 | bytes 9437184 | tf_op jit(solution)/shard_map/piece_rows/pallas_call | solution.py:602
  44.7 2.5 %collective-permute-start.16 = (bf16[72,2048]{1,0:T(8,128)(2,1)S(1)}, bf16[72,2048]{1,0:T(8,128)(2,1)S(1)}, u32[]{:S(2)}, u32[]{:S(2)}) collective-permute-start(bf16[72,2048]{1,0:T(8,128)(2,1)S(1)} %get-tuple-element.75), channel_id=1, source_target_pairs={{0,5},{1,4},{2,7},{3,6},{4,1},{5,0},{6,3},{7,2},{8,13},{9,12},{10,... | collective-permute-start | bytes 884744 | tf_op jit(solution)/shard_map/ppermute | solution.py:740
  47.7 0.6 collective-permute-start.18
  48.3 2.9 %collective-permute-start.20 = (bf16[32,2048]{1,0:T(8,128)(2,1)S(1)}, bf16[32,2048]{1,0:T(8,128)(2,1)S(1)}, u32[]{:S(2)}, u32[]{:S(2)}) collective-permute-start(bf16[32,2048]{1,0:T(8,128)(2,1)S(1)} %get-tuple-element.80), channel_id=1, source_target_pairs={{0,16},{1,17},{2,18},{3,19},{4,20},{5,21},{6,22},{7,23},{8,24},{9,... | collective-permute-start | bytes 393224 | tf_op jit(solution)/shard_map/ppermute | solution.py:740
  51.2 1.2 %collective-permute-start.21 = (bf16[32,2048]{1,0:T(8,128)(2,1)S(1)}, bf16[32,2048]{1,0:T(8,128)(2,1)S(1)}, u32[]{:S(2)}, u32[]{:S(2)}) collective-permute-start(bf16[32,2048]{1,0:T(8,128)(2,1)S(1)} %get-tuple-element.81), channel_id=1, source_target_pairs={{0,24},{1,25},{2,26},{3,27},{4,28},{5,29},{6,30},{7,31},{8,16},{9,... | collective-permute-start | bytes 393224 | tf_op jit(solution)/shard_map/ppermute | solution.py:740
  52.4 3.2 %collective-permute-done.16.g1 = bf16[72,2048]{1,0:T(8,128)(2,1)S(1)} collective-permute-done((bf16[72,2048]{1,0:T(8,128)(2,1)S(1)}, bf16[72,2048]{1,0:T(8,128)(2,1)S(1)}, u32[]{:S(2)}, u32[]{:S(2)}) %collective-permute-start.16) | collective-permute-done | bytes 294944 | tf_op jit(solution)/shard_map/ppermute | solution.py:740
  55.6 5.3 %collective-permute-done.17.g2 = bf16[72,2048]{1,0:T(8,128)(2,1)S(1)} collective-permute-done((bf16[72,2048]{1,0:T(8,128)(2,1)S(1)}, bf16[72,2048]{1,0:T(8,128)(2,1)S(1)}, u32[]{:S(2)}, u32[]{:S(2)}) %collective-permute-start.17) | collective-permute-done | bytes 294944 | tf_op jit(solution)/shard_map/ppermute | solution.py:740
  61.1 1.7 %collective-permute-start.25 = (bf16[24,2048]{1,0:T(8,128)(2,1)S(1)}, bf16[24,2048]{1,0:T(8,128)(2,1)S(1)}, u32[]{:S(2)}, u32[]{:S(2)}) collective-permute-start(bf16[24,2048]{1,0:T(8,128)(2,1)S(1)} %get-tuple-element.95), channel_id=1, source_target_pairs={{0,8},{1,9},{2,10},{3,11},{4,12},{5,13},{6,14},{7,15},{8,0},{9,1},... | collective-permute-start | bytes 294920 | tf_op jit(solution)/shard_map/ppermute | solution.py:740
  62.8 1.6 %collective-permute-start.26 = (bf16[24,2048]{1,0:T(8,128)(2,1)S(1)}, bf16[24,2048]{1,0:T(8,128)(2,1)S(1)}, u32[]{:S(2)}, u32[]{:S(2)}) collective-permute-start(bf16[24,2048]{1,0:T(8,128)(2,1)S(1)} %get-tuple-element.96), channel_id=1, source_target_pairs={{0,16},{1,17},{2,18},{3,19},{4,20},{5,21},{6,22},{7,23},{8,24},{9,... | collective-permute-start | bytes 294920 | tf_op jit(solution)/shard_map/ppermute | solution.py:740
  64.4 1.1 %collective-permute-start.27 = (bf16[24,2048]{1,0:T(8,128)(2,1)S(1)}, bf16[24,2048]{1,0:T(8,128)(2,1)S(1)}, u32[]{:S(2)}, u32[]{:S(2)}) collective-permute-start(bf16[24,2048]{1,0:T(8,128)(2,1)S(1)} %get-tuple-element.97), channel_id=1, source_target_pairs={{0,24},{1,25},{2,26},{3,27},{4,28},{5,29},{6,30},{7,31},{8,16},{9,... | collective-permute-start | bytes 294920 | tf_op jit(solution)/shard_map/ppermute | solution.py:740
  65.6 2.4 %collective-permute-start.22 = (bf16[32,2048]{1,0:T(8,128)(2,1)S(1)}, bf16[32,2048]{1,0:T(8,128)(2,1)S(1)}, u32[]{:S(2)}, u32[]{:S(2)}) collective-permute-start(bf16[32,2048]{1,0:T(8,128)(2,1)S(1)} %get-tuple-element.90), channel_id=1, source_target_pairs={{0,5},{1,4},{2,7},{3,6},{4,1},{5,0},{6,3},{7,2},{8,13},{9,12},{10,... | collective-permute-start | bytes 393224 | tf_op jit(solution)/shard_map/ppermute | solution.py:740
  68.6 0.6 collective-permute-start.24
  69.2 4.1 %collective-permute-done.26.z2 = bf16[24,2048]{1,0:T(8,128)(2,1)S(1)} collective-permute-done((bf16[24,2048]{1,0:T(8,128)(2,1)S(1)}, bf16[24,2048]{1,0:T(8,128)(2,1)S(1)}, u32[]{:S(2)}, u32[]{:S(2)}) %collective-permute-start.26) | collective-permute-done | bytes 98336 | tf_op jit(solution)/shard_map/ppermute | solution.py:740
  73.4 0.8 %collective-permute-done.23.p2 = bf16[32,2048]{1,0:T(8,128)(2,1)S(1)} collective-permute-done((bf16[32,2048]{1,0:T(8,128)(2,1)S(1)}, bf16[32,2048]{1,0:T(8,128)(2,1)S(1)}, u32[]{:S(2)}, u32[]{:S(2)}) %collective-permute-start.23) | collective-permute-done | bytes 131104 | tf_op jit(solution)/shard_map/ppermute | solution.py:740
  74.2 0.8 %final_rows.1 = bf16[32,2048]{1,0:T(8,128)(2,1)} custom-call(f32[32,2048]{1,0:T(8,128)S(1)} %total_rows.1.total_ref, bf16[32,2048]{1,0:T(8,128)(2,1)S(1)} %collective-permute-done.22.p1, bf16[32,2048]{1,0:T(8,128)(2,1)S(1)} %collective-permute-done.23.p2, bf16[32,2048]{1,0:T(8,128)(2,1)S(1)} %collective-permute-done.24.p3, ...), custom_call_target="tpu_custom_call" | custom-call | tf_op jit(solution)/shard_map/final_rows/pallas_call | solution.py:718
  (43 shorter events, 3.8 us)
Async XLA Ops:
  0.0 11.4 %collective-permute-start.1 = (bf16[2048,384]{1,0:T(8,128)(2,1)}, bf16[2048,384]{1,0:T(8,128)(2,1)S(1)}, u32[]{:S(2)}, u32[]{:S(2)}) collective-permute-start(bf16[2048,384]{1,0:T(8,128)(2,1)} %bitcast.11), channel_id=1, source_target_pairs={{0,2},{1,3},{2,0},{3,1},{4,6},{5,7},{6,4},{7,5},{8,10},{9,11},{10,... | collective-permute-start | bytes 4718600 | tf_op jit(solution)/shard_map/ppermute | solution.py:740
  0.5 10.9 %collective-permute-start.2 = (bf16[2048,384]{1,0:T(8,128)(2,1)}, bf16[2048,384]{1,0:T(8,128)(2,1)S(1)}, u32[]{:S(2)}, u32[]{:S(2)}) collective-permute-start(bf16[2048,384]{1,0:T(8,128)(2,1)} %bitcast.13), channel_id=1, source_target_pairs={{0,2},{1,3},{2,0},{3,1},{4,6},{5,7},{6,4},{7,5},{8,10},{9,11},{10,... | collective-permute-start | bytes 4718600 | tf_op jit(solution)/shard_map/ppermute | solution.py:740
  0.5 10.9 %collective-permute-start.3 = (bf16[384,2048]{1,0:T(8,128)(2,1)}, bf16[384,2048]{1,0:T(8,128)(2,1)}, u32[]{:S(2)}, u32[]{:S(2)}) collective-permute-start(bf16[384,2048]{1,0:T(8,128)(2,1)} %bitcast.15), channel_id=1, source_target_pairs={{0,2},{1,3},{2,0},{3,1},{4,6},{5,7},{6,4},{7,5},{8,10},{9,11},{10,... | collective-permute-start | bytes 4718600 | tf_op jit(solution)/shard_map/ppermute | solution.py:740
  4.7 6.7 %collective-permute-start = (bf16[32,2048]{1,0:T(8,128)(2,1)S(1)}, bf16[32,2048]{1,0:T(8,128)(2,1)S(1)}, u32[]{:S(2)}, u32[]{:S(2)}) collective-permute-start(bf16[32,2048]{1,0:T(8,128)(2,1)S(1)} %get-tuple-element.59), channel_id=1, source_target_pairs={{0,1},{1,0},{2,3},{3,2},{4,5},{5,4},{6,7},{7,6},{8,9},{9,8},{10,11... | collective-permute-start | bytes 393224 | tf_op jit(solution)/shard_map/ppermute | solution.py:740
  7.2 4.2 %copy-start = (f32[2048]{0:T(1024)S(1)}, f32[2048]{0:T(1024)}, u32[]{:S(2)}) copy-start(f32[2048]{0:T(1024)} %param.22) | copy-start | bytes 24580
  11.4 4.7 %copy-start.1 = (bf16[2048,384]{1,0:T(8,128)(2,1)}, bf16[2048,384]{1,0:T(8,128)(2,1)S(1)}, u32[]{:S(2)}) copy-start(bf16[2048,384]{1,0:T(8,128)(2,1)S(1)} %collective-permute-done.1.wg1) | copy-start | bytes 4718596
  11.4 4.7 %copy-start.2 = (bf16[2048,384]{1,0:T(8,128)(2,1)}, bf16[2048,384]{1,0:T(8,128)(2,1)S(1)}, u32[]{:S(2)}) copy-start(bf16[2048,384]{1,0:T(8,128)(2,1)S(1)} %collective-permute-done.2.wu1) | copy-start | bytes 4718596
  11.6 7.8 %collective-permute-start.7 = (bf16[24,2176]{1,0:T(8,128)(2,1)S(1)}, bf16[24,2176]{1,0:T(8,128)(2,1)S(1)}, u32[]{:S(2)}, u32[]{:S(2)}) collective-permute-start(bf16[24,2176]{1,0:T(8,128)(2,1)S(1)} %get-tuple-element.62.refs_0_), channel_id=1, source_target_pairs={{0,8},{1,9},{2,10},{3,11},{4,12},{5,13},{6,14},{7,15},{8,0},{9,1},... | collective-permute-start | bytes 313352 | tf_op jit(solution)/shard_map/ppermute | solution.py:740
  13.5 10.8 %collective-permute-start.8 = (bf16[24,2176]{1,0:T(8,128)(2,1)S(1)}, bf16[24,2176]{1,0:T(8,128)(2,1)S(1)}, u32[]{:S(2)}, u32[]{:S(2)}) collective-permute-start(bf16[24,2176]{1,0:T(8,128)(2,1)S(1)} %get-tuple-element.62.refs_0_), channel_id=1, source_target_pairs={{0,16},{1,17},{2,18},{3,19},{4,20},{5,21},{6,22},{7,23},{8,24},{9,... | collective-permute-start | bytes 313352 | tf_op jit(solution)/shard_map/ppermute | solution.py:740
  16.1 8.2 %collective-permute-start.9 = (bf16[24,2176]{1,0:T(8,128)(2,1)S(1)}, bf16[24,2176]{1,0:T(8,128)(2,1)S(1)}, u32[]{:S(2)}, u32[]{:S(2)}) collective-permute-start(bf16[24,2176]{1,0:T(8,128)(2,1)S(1)} %get-tuple-element.62.refs_0_), channel_id=1, source_target_pairs={{0,24},{1,25},{2,26},{3,27},{4,28},{5,29},{6,30},{7,31},{8,16},{9,... | collective-permute-start | bytes 313352 | tf_op jit(solution)/shard_map/ppermute | solution.py:740
  16.1 8.2 %collective-permute-start.4 = (bf16[32,2176]{1,0:T(8,128)(2,1)S(1)}, bf16[32,2176]{1,0:T(8,128)(2,1)S(1)}, u32[]{:S(2)}, u32[]{:S(2)}) collective-permute-start(bf16[32,2176]{1,0:T(8,128)(2,1)S(1)} %own_rows.1.refs_0_.r0), channel_id=1, source_target_pairs={{0,5},{1,4},{2,7},{3,6},{4,1},{5,0},{6,3},{7,2},{8,13},{9,12},{10,... | collective-permute-start | bytes 417800 | tf_op jit(solution)/shard_map/ppermute | solution.py:740
  18.8 6.0 %collective-permute-start.5 = (bf16[32,2176]{1,0:T(8,128)(2,1)S(1)}, bf16[32,2176]{1,0:T(8,128)(2,1)S(1)}, u32[]{:S(2)}, u32[]{:S(2)}) collective-permute-start(bf16[32,2176]{1,0:T(8,128)(2,1)S(1)} %own_rows.1.refs_0_.r0), channel_id=1, source_target_pairs={{0,1},{1,0},{2,3},{3,2},{4,5},{5,4},{6,7},{7,6},{8,9},{9,8},{10,11... | collective-permute-start | bytes 417800 | tf_op jit(solution)/shard_map/ppermute | solution.py:740
  19.4 5.5 %collective-permute-start.6 = (bf16[32,2176]{1,0:T(8,128)(2,1)S(1)}, bf16[32,2176]{1,0:T(8,128)(2,1)S(1)}, u32[]{:S(2)}, u32[]{:S(2)}) collective-permute-start(bf16[32,2176]{1,0:T(8,128)(2,1)S(1)} %own_rows.1.refs_0_.r0), channel_id=1, source_target_pairs={{0,4},{1,5},{2,6},{3,7},{4,0},{5,1},{6,2},{7,3},{8,12},{9,13},{10,... | collective-permute-start | bytes 417800 | tf_op jit(solution)/shard_map/ppermute | solution.py:740
  24.9 7.7 %collective-permute-start.10 = (bf16[32,2176]{1,0:T(8,128)(2,1)S(1)}, bf16[32,2176]{1,0:T(8,128)(2,1)S(1)}, u32[]{:S(2)}, u32[]{:S(2)}) collective-permute-start(bf16[32,2176]{1,0:T(8,128)(2,1)S(1)} %onward_z.1), channel_id=1, source_target_pairs={{0,8},{1,9},{2,10},{3,11},{4,12},{5,13},{6,14},{7,15},{8,0},{9,1},... | collective-permute-start | bytes 417800 | tf_op jit(solution)/shard_map/ppermute | solution.py:740
  26.1 15.3 %collective-permute-start.13 = (bf16[72,2176]{1,0:T(8,128)(2,1)S(1)}, bf16[72,2176]{1,0:T(8,128)(2,1)S(1)}, u32[]{:S(2)}, u32[]{:S(2)}) collective-permute-start(bf16[72,2176]{1,0:T(8,128)(2,1)S(1)} %onward_plane.1.far_ref), channel_id=1, source_target_pairs={{0,5},{1,4},{2,7},{3,6},{4,1},{5,0},{6,3},{7,2},{8,13},{9,12},{10,... | collective-permute-start | bytes 940040 | tf_op jit(solution)/shard_map/ppermute | solution.py:740
  28.5 13.2 %collective-permute-start.14 = (bf16[72,2176]{1,0:T(8,128)(2,1)S(1)}, bf16[72,2176]{1,0:T(8,128)(2,1)S(1)}, u32[]{:S(2)}, u32[]{:S(2)}) collective-permute-start(bf16[72,2176]{1,0:T(8,128)(2,1)S(1)} %onward_plane.1.far_ref), channel_id=1, source_target_pairs={{0,1},{1,0},{2,3},{3,2},{4,5},{5,4},{6,7},{7,6},{8,9},{9,8},{10,11... | collective-permute-start | bytes 940040 | tf_op jit(solution)/shard_map/ppermute | solution.py:740
  29.1 12.6 %collective-permute-start.15 = (bf16[72,2176]{1,0:T(8,128)(2,1)S(1)}, bf16[72,2176]{1,0:T(8,128)(2,1)S(1)}, u32[]{:S(2)}, u32[]{:S(2)}) collective-permute-start(bf16[72,2176]{1,0:T(8,128)(2,1)S(1)} %onward_plane.1.far_ref), channel_id=1, source_target_pairs={{0,4},{1,5},{2,6},{3,7},{4,0},{5,1},{6,2},{7,3},{8,12},{9,13},{10,... | collective-permute-start | bytes 940040 | tf_op jit(solution)/shard_map/ppermute | solution.py:740
  29.6 11.8 %collective-permute-start.11 = (bf16[32,2176]{1,0:T(8,128)(2,1)S(1)}, bf16[32,2176]{1,0:T(8,128)(2,1)S(1)}, u32[]{:S(2)}, u32[]{:S(2)}) collective-permute-start(bf16[32,2176]{1,0:T(8,128)(2,1)S(1)} %onward_z.1), channel_id=1, source_target_pairs={{0,16},{1,17},{2,18},{3,19},{4,20},{5,21},{6,22},{7,23},{8,24},{9,... | collective-permute-start | bytes 417800 | tf_op jit(solution)/shard_map/ppermute | solution.py:740
  32.5 8.9 %collective-permute-start.12 = (bf16[32,2176]{1,0:T(8,128)(2,1)S(1)}, bf16[32,2176]{1,0:T(8,128)(2,1)S(1)}, u32[]{:S(2)}, u32[]{:S(2)}) collective-permute-start(bf16[32,2176]{1,0:T(8,128)(2,1)S(1)} %onward_z.1), channel_id=1, source_target_pairs={{0,24},{1,25},{2,26},{3,27},{4,28},{5,29},{6,30},{7,31},{8,16},{9,... | collective-permute-start | bytes 417800 | tf_op jit(solution)/shard_map/ppermute | solution.py:740
  41.4 9.8 %collective-permute-start.19 = (bf16[32,2048]{1,0:T(8,128)(2,1)S(1)}, bf16[32,2048]{1,0:T(8,128)(2,1)S(1)}, u32[]{:S(2)}, u32[]{:S(2)}) collective-permute-start(bf16[32,2048]{1,0:T(8,128)(2,1)S(1)} %get-tuple-element.78), channel_id=1, source_target_pairs={{0,8},{1,9},{2,10},{3,11},{4,12},{5,13},{6,14},{7,15},{8,0},{9,1},... | collective-permute-start | bytes 393224 | tf_op jit(solution)/shard_map/ppermute | solution.py:740
  44.7 10.9 %collective-permute-start.16 = (bf16[72,2048]{1,0:T(8,128)(2,1)S(1)}, bf16[72,2048]{1,0:T(8,128)(2,1)S(1)}, u32[]{:S(2)}, u32[]{:S(2)}) collective-permute-start(bf16[72,2048]{1,0:T(8,128)(2,1)S(1)} %get-tuple-element.75), channel_id=1, source_target_pairs={{0,5},{1,4},{2,7},{3,6},{4,1},{5,0},{6,3},{7,2},{8,13},{9,12},{10,... | collective-permute-start | bytes 884744 | tf_op jit(solution)/shard_map/ppermute | solution.py:740
  47.2 13.7 %collective-permute-start.17 = (bf16[72,2048]{1,0:T(8,128)(2,1)S(1)}, bf16[72,2048]{1,0:T(8,128)(2,1)S(1)}, u32[]{:S(2)}, u32[]{:S(2)}) collective-permute-start(bf16[72,2048]{1,0:T(8,128)(2,1)S(1)} %get-tuple-element.76), channel_id=1, source_target_pairs={{0,1},{1,0},{2,3},{3,2},{4,5},{5,4},{6,7},{7,6},{8,9},{9,8},{10,11... | collective-permute-start | bytes 884744 | tf_op jit(solution)/shard_map/ppermute | solution.py:740
  47.7 13.2 %collective-permute-start.18 = (bf16[72,2048]{1,0:T(8,128)(2,1)S(1)}, bf16[72,2048]{1,0:T(8,128)(2,1)S(1)}, u32[]{:S(2)}, u32[]{:S(2)}) collective-permute-start(bf16[72,2048]{1,0:T(8,128)(2,1)S(1)} %get-tuple-element.77), channel_id=1, source_target_pairs={{0,4},{1,5},{2,6},{3,7},{4,0},{5,1},{6,2},{7,3},{8,12},{9,13},{10,... | collective-permute-start | bytes 884744 | tf_op jit(solution)/shard_map/ppermute | solution.py:740
  48.3 12.8 %collective-permute-start.20 = (bf16[32,2048]{1,0:T(8,128)(2,1)S(1)}, bf16[32,2048]{1,0:T(8,128)(2,1)S(1)}, u32[]{:S(2)}, u32[]{:S(2)}) collective-permute-start(bf16[32,2048]{1,0:T(8,128)(2,1)S(1)} %get-tuple-element.80), channel_id=1, source_target_pairs={{0,16},{1,17},{2,18},{3,19},{4,20},{5,21},{6,22},{7,23},{8,24},{9,... | collective-permute-start | bytes 393224 | tf_op jit(solution)/shard_map/ppermute | solution.py:740
  51.2 9.9 %collective-permute-start.21 = (bf16[32,2048]{1,0:T(8,128)(2,1)S(1)}, bf16[32,2048]{1,0:T(8,128)(2,1)S(1)}, u32[]{:S(2)}, u32[]{:S(2)}) collective-permute-start(bf16[32,2048]{1,0:T(8,128)(2,1)S(1)} %get-tuple-element.81), channel_id=1, source_target_pairs={{0,24},{1,25},{2,26},{3,27},{4,28},{5,29},{6,30},{7,31},{8,16},{9,... | collective-permute-start | bytes 393224 | tf_op jit(solution)/shard_map/ppermute | solution.py:740
  61.1 7.5 %collective-permute-start.25 = (bf16[24,2048]{1,0:T(8,128)(2,1)S(1)}, bf16[24,2048]{1,0:T(8,128)(2,1)S(1)}, u32[]{:S(2)}, u32[]{:S(2)}) collective-permute-start(bf16[24,2048]{1,0:T(8,128)(2,1)S(1)} %get-tuple-element.95), channel_id=1, source_target_pairs={{0,8},{1,9},{2,10},{3,11},{4,12},{5,13},{6,14},{7,15},{8,0},{9,1},... | collective-permute-start | bytes 294920 | tf_op jit(solution)/shard_map/ppermute | solution.py:740
  62.8 10.5 %collective-permute-start.26 = (bf16[24,2048]{1,0:T(8,128)(2,1)S(1)}, bf16[24,2048]{1,0:T(8,128)(2,1)S(1)}, u32[]{:S(2)}, u32[]{:S(2)}) collective-permute-start(bf16[24,2048]{1,0:T(8,128)(2,1)S(1)} %get-tuple-element.96), channel_id=1, source_target_pairs={{0,16},{1,17},{2,18},{3,19},{4,20},{5,21},{6,22},{7,23},{8,24},{9,... | collective-permute-start | bytes 294920 | tf_op jit(solution)/shard_map/ppermute | solution.py:740
  64.4 8.9 %collective-permute-start.27 = (bf16[24,2048]{1,0:T(8,128)(2,1)S(1)}, bf16[24,2048]{1,0:T(8,128)(2,1)S(1)}, u32[]{:S(2)}, u32[]{:S(2)}) collective-permute-start(bf16[24,2048]{1,0:T(8,128)(2,1)S(1)} %get-tuple-element.97), channel_id=1, source_target_pairs={{0,24},{1,25},{2,26},{3,27},{4,28},{5,29},{6,30},{7,31},{8,16},{9,... | collective-permute-start | bytes 294920 | tf_op jit(solution)/shard_map/ppermute | solution.py:740
  65.6 7.7 %collective-permute-start.22 = (bf16[32,2048]{1,0:T(8,128)(2,1)S(1)}, bf16[32,2048]{1,0:T(8,128)(2,1)S(1)}, u32[]{:S(2)}, u32[]{:S(2)}) collective-permute-start(bf16[32,2048]{1,0:T(8,128)(2,1)S(1)} %get-tuple-element.90), channel_id=1, source_target_pairs={{0,5},{1,4},{2,7},{3,6},{4,1},{5,0},{6,3},{7,2},{8,13},{9,12},{10,... | collective-permute-start | bytes 393224 | tf_op jit(solution)/shard_map/ppermute | solution.py:740
  68.0 6.1 %collective-permute-start.23 = (bf16[32,2048]{1,0:T(8,128)(2,1)S(1)}, bf16[32,2048]{1,0:T(8,128)(2,1)S(1)}, u32[]{:S(2)}, u32[]{:S(2)}) collective-permute-start(bf16[32,2048]{1,0:T(8,128)(2,1)S(1)} %get-tuple-element.91), channel_id=1, source_target_pairs={{0,1},{1,0},{2,3},{3,2},{4,5},{5,4},{6,7},{7,6},{8,9},{9,8},{10,11... | collective-permute-start | bytes 393224 | tf_op jit(solution)/shard_map/ppermute | solution.py:740
  68.6 5.7 %collective-permute-start.24 = (bf16[32,2048]{1,0:T(8,128)(2,1)S(1)}, bf16[32,2048]{1,0:T(8,128)(2,1)S(1)}, u32[]{:S(2)}, u32[]{:S(2)}) collective-permute-start(bf16[32,2048]{1,0:T(8,128)(2,1)S(1)} %get-tuple-element.92), channel_id=1, source_target_pairs={{0,4},{1,5},{2,6},{3,7},{4,0},{5,1},{6,2},{7,3},{8,12},{9,13},{10,... | collective-permute-start | bytes 393224 | tf_op jit(solution)/shard_map/ppermute | solution.py:740
